TPU v7x, 128 devices: a whole 4x4x4 slice. The times are simulated.
128 devices in a mesh: sy: 8 (over x, y_lo), sz: 16 (over z, y_hi, core).
Axes of the slice: x: 4, y: 4 (y_hi: 2, y_lo: 2; y = y_hi * 2 + y_lo), z: 4, core: 2. Of those that a mesh axis runs over, the one named last changes fastest.
Arguments:
- labels: int32 [16, 512, 512], P(None, 'sy', 'sz'), may hold values from 0 to 3
- wall_dist: bfloat16 [16, 512, 512], P(None, 'sy', 'sz'), may hold values from -5 to 5
- material_table: bfloat16 [4, 16], replicated, may hold values from -4 to 4
- dist_weight: bfloat16 [16], replicated, may hold values from -4 to 4
- conv_weight: bfloat16 [27, 16, 16], replicated, may hold values from -0.3125 to 0.3125
- down_weight: bfloat16 [8, 64, 16], replicated, may hold values from -0.5 to 0.5
- mix_weight: bfloat16 [64, 256, 256], P('sz'), may hold values from -0.375 to 0.375
- cotangent: bfloat16 [64, 8, 256, 256], P('sz', None, 'sy'), may hold values from -6 to 6
Outputs:
- mid_features: bfloat16 [64, 8, 256, 256], P('sz', None, 'sy')
- mix_grad: float32 [64, 256, 256], P('sz', 'sy')
- down_grad: float32 [8, 64, 16], replicated
- conv_grad: float32 [27, 16, 16], replicated
All inputs are finite; a program needn't handle non-finite values.
Results may differ from a plain program's by a relative error of at most 0.0084.
Values may be sent and summed in bfloat16 or wider, within the bound.
No kernel may reach another device: no remote copies, remote signals or barrier semaphores. Data moves between devices by JAX's collectives and lax.ppermute only.
A program may use at most 192 MiB of HBM per device.

v0:
```python
import math

import jax
import jax.numpy as jnp
from jax import lax
from jax.sharding import PartitionSpec as P


def extended(value, sides, width):
    for axis, dim in sides:
        size, length = (lax.axis_size(axis), value.shape[dim])
        up = [(i, (i + 1) % size) for i in range(size - 1)]
        down = [(j, i) for i, j in up]
        last = lax.slice_in_dim(value, length - width, length, axis=dim)
        first = lax.slice_in_dim(value, 0, width, axis=dim)
        before = lax.ppermute(last, axis, up)
        after = lax.ppermute(first, axis, down)
        value = jnp.concatenate([before, value, after], axis=dim)
    return value


def silu_slope(values):
    sigma = jax.nn.sigmoid(values)
    return sigma * (1.0 + values * (1.0 - sigma))


def embed_cells(materials, distance, material_table, dist_weight):
    total = (
        dist_weight.astype(jnp.float32)[:, None, None, None] * distance.astype(jnp.float32)[None]
    )
    for entry in range(material_table.shape[0]):
        column = material_table[entry].astype(jnp.float32)[:, None, None, None]
        total = total + jnp.where(materials[None] == entry, column, 0.0)
    return total.astype(jnp.bfloat16)


def per_device(
    labels, wall_dist, material_table, dist_weight, conv_weight, down_weight, mix_weight, cotangent
):
    depth, rows_y, rows_z = labels.shape
    channels = material_table.shape[1]
    wide_channels = down_weight.shape[1]
    count_y = lax.axis_size("sy")
    count_z = lax.axis_size("sz")
    numbers = ("NCDHW", "OIDHW", "NCDHW")
    embedded = embed_cells(labels, wall_dist, material_table, dist_weight)
    bordered = extended(embedded, (("sy", 2), ("sz", 3)), 1)
    padded = jnp.pad(bordered, ((0, 0), (1, 1), (0, 0), (0, 0)))
    kernel = jnp.transpose(conv_weight.reshape(3, 3, 3, channels, channels), (3, 4, 0, 1, 2))
    pre_act = lax.conv_general_dilated(
        padded[None],
        kernel,
        (1, 1, 1),
        "VALID",
        dimension_numbers=numbers,
        preferred_element_type=jnp.float32,
    )[0]
    hidden = jax.nn.silu(pre_act).astype(jnp.bfloat16)
    half_x = depth // 2
    half_y = rows_y // 2
    down_kernel = jnp.transpose(
        down_weight.reshape(2, 2, 2, wide_channels, channels), (3, 4, 0, 1, 2)
    )
    coarse = lax.conv_general_dilated(
        hidden[None],
        down_kernel,
        (2, 2, 2),
        "VALID",
        dimension_numbers=numbers,
        preferred_element_type=jnp.float32,
    )[0].astype(jnp.bfloat16)
    channel_coarse = lax.all_to_all(coarse, "sz", split_axis=0, concat_axis=3, tiled=True)
    mixed_pre = jnp.einsum(
        "czw,cxyw->cxyz", mix_weight, channel_coarse, preferred_element_type=jnp.float32
    )
    mid_features = jax.nn.silu(mixed_pre).astype(jnp.bfloat16)
    mixed_grad = (cotangent.astype(jnp.float32) * silu_slope(mixed_pre)).astype(jnp.bfloat16)
    mix_partial = jnp.einsum(
        "cxyz,cxyw->czw", mixed_grad, channel_coarse, preferred_element_type=jnp.float32
    )
    mix_grad = lax.psum_scatter(mix_partial, "sy", scatter_dimension=1, tiled=True) / math.sqrt(
        half_x * half_y * count_y
    )
    channel_grad = jnp.einsum(
        "czw,cxyz->cxyw", mix_weight, mixed_grad, preferred_element_type=jnp.float32
    ).astype(jnp.bfloat16)
    coarse_grad = lax.all_to_all(channel_grad, "sz", split_axis=3, concat_axis=0, tiled=True)
    down_corr = lax.conv_general_dilated(
        hidden[:, None],
        coarse_grad[:, None],
        (1, 1, 1),
        "VALID",
        rhs_dilation=(2, 2, 2),
        dimension_numbers=numbers,
        preferred_element_type=jnp.float32,
    )
    down_partial = jnp.transpose(down_corr, (2, 3, 4, 1, 0)).reshape(8, wide_channels, channels)
    hidden_grad = lax.conv_transpose(
        coarse_grad[None],
        down_kernel,
        (2, 2, 2),
        "VALID",
        dimension_numbers=numbers,
        transpose_kernel=True,
        preferred_element_type=jnp.float32,
    )[0]
    pre_grad = (hidden_grad * silu_slope(pre_act)).astype(jnp.bfloat16)
    correlated = lax.conv_general_dilated(
        padded[:, None],
        pre_grad[:, None],
        (1, 1, 1),
        "VALID",
        dimension_numbers=numbers,
        preferred_element_type=jnp.float32,
    )
    conv_partial = jnp.transpose(correlated, (2, 3, 4, 1, 0)).reshape(27, channels, channels)
    conv_total, down_total = lax.psum((conv_partial, down_partial), ("sy", "sz"))
    cells_fine = depth * rows_y * count_y * rows_z * count_z
    cells_coarse = cells_fine // 8
    conv_grad = conv_total / math.sqrt(cells_fine)
    down_grad = down_total / math.sqrt(cells_coarse)
    return (mid_features, mix_grad, down_grad, conv_grad)


def solution(mesh):
    in_specs = (
        P(None, "sy", "sz"),
        P(None, "sy", "sz"),
        P(),
        P(),
        P(),
        P(),
        P("sz", None, None),
        P("sz", None, "sy", None),
    )
    out_specs = (P("sz", None, "sy", None), P("sz", "sy", None), P(), P())
    return jax.shard_map(
        per_device, mesh=mesh, in_specs=in_specs, out_specs=out_specs, check_vma=False
    )
```

profile of v0, /device:TPU:0, one launch (start us, length us, event | category | flops | bytes accessed | tf_op | source)
XLA Modules:
  0.0 650.5 jit_solution(8956671132373303856)
XLA Ops:
  7.2 0.7 convert_element_type.92
  7.9 0.8 bitcast_convert_fusion.3
  8.7 0.9 convert_element_type.93
  9.7 1.1 broadcast_compare_fusion.3
  10.8 2.8 add_convert_fusion
  13.5 2.9 fusion.34
  16.5 3.1 copy.73
  19.6 3.6 collective-permute-start
  23.2 3.1 copy.74
  26.3 1.3 collective-permute-start.1
  27.6 2.9 copy.75
  30.5 1.9 collective-permute-done.1
  32.5 2.9 copy.76
  35.3 1.1 pad_maximum_fusion.2
  36.4 1.3 collective-permute-start.2
  37.7 1.5 collective-permute-start.3
  39.2 0.2 copy.79
  39.4 4.6 collective-permute-done.3
  44.0 3.7 fusion.49
  47.7 2.3 pad.5
  50.1 11.2 %copy.78 = bf16[16,18,66,1,8,5]{0,4,5,2,1,3:T(8,128)(2,1)} copy(bf16[16,18,66,1,8,5]{2,0,5,4,1,3:T(8,128)(2,1)} %bitcast.107) | data formatting | bytes 3041280 | tf_op jit(solution)/shard_map/conv_general_dilated | solution.py:50
  61.2 3.7 slice.40
  64.9 33.2 %fusion.10 = (bf16[16,64,8,5,16]{4,2,3,1,0:T(8,128)(2,1)}, f32[16,64,8,5,16]{4,2,3,1,0:T(8,128)}) fusion(pred[8,5]{0,1:T(8,128)(4,1)S(1)} %copy-done.15, bf16[3,3,3,16,16]{4,3,2,1,0:T(8,128)(2,1)S(1)} %bitcast.119, bf16[16,18,66,1,7,2]{0,4,5,2,1,3:T(8,128)(2,1)S(1)} %slice.40, bf16[16,18,66,1,8,5]{0,4,5,2,1,3:T(8,128)(2,1)} %copy.78), kind=kOutput, calls=%fused_computation.13 | convolution fusion | flops 577205248 | bytes 5998888 | tf_op jit(solution)/shard_map/conv_general_dilated | solution.py:50
  98.1 10.9 %copy.80 = bf16[16,64,8,5,16]{1,4,3,2,0:T(8,128)(2,1)} copy(bf16[16,64,8,5,16]{4,2,3,1,0:T(8,128)(2,1)} %get-tuple-element.22) | data formatting | bytes 2621440 | tf_op jit(solution)/shard_map/convert_element_type | solution.py:58
  109.1 2.0 slice.41
  111.1 0.1 slice.42
  111.2 2.3 fusion.18
  113.5 10.2 %copy.81 = bf16[16,64,1,8,5,16]{5,3,4,1,0,2:T(8,128)(2,1)} copy(bf16[16,64,1,8,5,16]{1,5,4,3,2,0:T(8,128)(2,1)} %fusion.18) | data formatting | bytes 2621440 | tf_op jit(solution)/shard_map/convert_element_type | solution.py:58
  123.6 6.7 %fusion.25 = bf16[8,32,8,2,64]{4,2,3,1,0:T(8,128)(2,1)S(1)} fusion(bf16[2,2,2,64,16]{3,4,2,1,0:T(8,128)(2,1)S(1)} %bitcast.121, bf16[16,64,1,8,5,16]{5,3,4,1,0,2:T(8,128)(2,1)} %copy.81), kind=kOutput, calls=%fused_computation.36 | convolution fusion | flops 67371008 | bytes 1851392 | tf_op jit(solution)/shard_map/conv_general_dilated | solution.py:64
  130.3 1.2 copy.82
  131.6 4.9 copy.83
  136.5 3.8 reshape.175
  140.3 23.6 %all_to_all.33 = bf16[16,2,8192]{2,1,0:T(2,128)(2,1)} all-to-all(bf16[16,2,8192]{2,1,0:T(2,128)(2,1)S(1)} %reshape.175), channel_id=1, replica_groups=mesh['sy'=8,'sz'=16] {'sz'}, dimensions={0} | all-to-all | bytes 1048576 | tf_op jit(solution)/shard_map/all_to_all | solution.py:72
  163.9 4.0 reshape.176
  168.0 2.2 copy.84
  170.2 1.7 multiply_convert_fusion.2
  171.9 1.1 convolution_convert_fusion
  173.0 4.6 copy.88
  177.6 4.5 reshape.177
  182.1 3.6 all-to-all-start.1
  185.7 0.0 reduce-scatter.2.cloned.1.call-start
  185.8 4.9 fusion.48
  190.7 14.2 %copy.87 = f32[16,64,8,5,16]{1,4,3,2,0:T(8,128)} copy(f32[16,64,8,5,16]{4,2,3,1,0:T(8,128)} %get-tuple-element.23) | data formatting | bytes 5242880 | tf_op jit(solution)/shard_map/conv_general_dilated | solution.py:50
  205.0 32.5 %copy.98 = bf16[16,1,18,66,34]{0,1,4,3,2:T(2,128)(2,1)} copy(bf16[16,1,18,66,34]{3,0,4,2,1:T(8,128)(2,1)S(1)} %copy-done.3) | data formatting | bytes 2585088 | tf_op jit(solution)/shard_map/broadcast_in_dim | solution.py:109
  237.5 3.5 convolution_bitcast_fusion
  241.0 0.0 reduce-scatter.2.cloned.1.call-update
  241.0 2.0 reshape.178
  243.0 3.1 copy.90
  246.1 1.3 copy-done.2
  247.4 3.0 copy.107
  250.4 1.5 pad.8.clone
  252.0 7.6 %copy.92 = bf16[64,1,8,32,16]{0,1,4,3,2:T(2,128)(2,1)} copy(bf16[64,1,8,32,16]{3,4,2,0,1:T(8,128)(2,1)} %bitcast.104) | data formatting | bytes 1048576 | tf_op jit(solution)/shard_map/broadcast_in_dim | solution.py:90
  259.5 10.5 %broadcast_select_fusion = f32[16,64,8,6,16]{4,2,3,1,0:T(8,128)} fusion(pred[8,6]{0,1:T(8,128)(4,1)S(1)} %copy-done.13, bf16[2,2,2,64,16]{3,4,2,1,0:T(8,128)(2,1)S(1)} %bitcast.122, bf16[64,8,32,8,3]{0,2,4,3,1:T(8,128)(2,1)S(1)} %bitcast.102), kind=kOutput, calls=%fused_computation.9 | convolution fusion | flops 101449728 | bytes 3948592 | tf_op jit(solution)/shard_map/conv_general_dilated | solution.py:98
  270.1 17.6 %copy.96 = f32[16,64,8,6,16]{1,4,3,2,0:T(8,128)} copy(f32[16,64,8,6,16]{4,2,3,1,0:T(8,128)} %broadcast_select_fusion) | data formatting | bytes 6291456 | tf_op jit(solution)/shard_map/conv_general_dilated | solution.py:98
  287.6 5.5 fusion.17
  293.2 29.4 %copy.99 = bf16[16,1,16,64,32]{0,1,4,3,2:T(2,128)(2,1)} copy(bf16[16,1,16,64,32]{3,0,4,2,1:T(8,128)(2,1)} %get-tuple-element.8) | data formatting | bytes 2097152 | tf_op jit(solution)/shard_map/convert_element_type | solution.py:107
  322.6 24.8 %copy.91 = bf16[16,1,16,64,32]{0,1,4,3,2:T(2,128)(2,1)} copy(bf16[16,1,16,64,32]{3,0,4,2,1:T(8,128)(2,1)S(1)} %get-tuple-element.9) | data formatting | bytes 2097152 | tf_op jit(solution)/shard_map/convert_element_type | solution.py:58
  347.3 191.6 %fusion.36 = f32[3,3,3,16,16]{3,4,2,1,0:T(8,128)S(1)} fusion(bf16[16,1,18,66,34]{0,1,4,3,2:T(2,128)(2,1)} %copy.98, bf16[16,1,16,64,32]{0,1,4,3,2:T(2,128)(2,1)} %copy.99), kind=kOutput, calls=%fused_computation.64 | convolution fusion | flops 452984832 | bytes 2368768 | tf_op jit(solution)/shard_map/transpose | solution.py:116
  539.0 32.6 %fusion.35 = f32[2,2,2,64,16]{3,4,2,1,0:T(8,128)S(1)} fusion(bf16[16,1,16,64,32]{0,1,4,3,2:T(2,128)(2,1)} %copy.91, bf16[64,1,8,32,16]{0,1,4,3,2:T(2,128)(2,1)S(1)} %copy-done.5), kind=kOutput, calls=%fused_computation.63 | convolution fusion | flops 67108864 | bytes 1605632 | tf_op jit(solution)/shard_map/transpose | solution.py:97
  571.6 0.2 copy.100
  571.8 68.7 %all-reduce.1 = (f32[8,64,16]{1,2,0:T(8,128)S(1)}, f32[27,16,16]{0,2,1:T(8,128)S(1)}) all-reduce(f32[8,64,16]{1,2,0:T(8,128)S(1)} %bitcast.120, f32[27,16,16]{0,2,1:T(8,128)S(1)} %copy.100), channel_id=1, replica_groups=mesh['sy'=8,'sz'=16] {'sy','sz'}, use_global_device_ids=true, to_apply=%region_1.2 | all-reduce | flops 15104 | bytes 120832 | tf_op jit(solution)/shard_map/psum | solution.py:117
  640.5 0.6 broadcast_multiply_fusion.2
  641.1 0.7 broadcast_multiply_fusion
  641.8 1.6 broadcast_multiply_fusion.1
  (35 shorter events, 0.1 us)
Async XLA Ops:
  7.2 163.0 %copy-start = (bf16[4,256,256]{2,1,0:T(8,128)(2,1)S(1)}, bf16[4,256,256]{2,1,0:T(8,128)(2,1)}, u32[]{:S(2)}) copy-start(bf16[4,256,256]{2,1,0:T(8,128)(2,1)} %param.14) | copy-start | bytes 1572868
  19.6 8.0 %collective-permute-start = (bf16[16,16,1,32]{3,1,2,0:T(8,128)(2,1)S(1)}, bf16[16,16,1,32]{3,1,2,0:T(8,128)(2,1)S(1)}, u32[]{:S(2)}, u32[]{:S(2)}) collective-permute-start(bf16[16,16,1,32]{3,1,2,0:T(8,128)(2,1)S(1)} %copy.73), channel_id=1, source_target_pairs={{0,16},{16,32},{32,48},{48,64},{64,80},{80,96},{96,112},{1,17},{17... | collective-permute-start | bytes 49160 | tf_op jit(solution)/shard_map/ppermute | solution.py:16
  26.3 6.2 collective-permute-start.1
  30.5 8.7 %copy-start.10 = (bf16[27,16,16]{0,2,1:T(8,128)(2,1)S(1)}, bf16[27,16,16]{0,2,1:T(8,128)(2,1)}, u32[]{:S(2)}) copy-start(bf16[27,16,16]{0,2,1:T(8,128)(2,1)} %param.12) | copy-start | bytes 41476
  36.4 3.0 collective-permute-start.2
  37.7 6.3 collective-permute-start.3
  39.4 8.3 %copy-start.6 = (bf16[16,16,66,1]{2,0,3,1:T(8,128)(2,1)}, bf16[16,16,66,1]{2,0,3,1:T(8,128)(2,1)S(1)}, u32[]{:S(2)}) copy-start(bf16[16,16,66,1]{2,0,3,1:T(8,128)(2,1)S(1)} %collective-permute-done.2) | copy-start | bytes 101380
  44.0 3.7 copy-start.8
  61.2 3.7 copy-start.15
  113.5 10.2 %copy-start.11 = (bf16[8,64,16]{1,2,0:T(8,128)(2,1)S(1)}, bf16[8,64,16]{1,2,0:T(8,128)(2,1)}, u32[]{:S(2)}) copy-start(bf16[8,64,16]{1,2,0:T(8,128)(2,1)} %param.13) | copy-start | bytes 49156
  168.0 2.2 copy-start.14
  170.2 1.8 copy-start.4
  171.9 13.8 %copy-start.7 = (bf16[16,16,66,1]{2,0,3,1:T(8,128)(2,1)S(1)}, bf16[16,16,66,1]{2,0,3,1:T(8,128)(2,1)}, u32[]{:S(2)}) copy-start(bf16[16,16,66,1]{2,0,3,1:T(8,128)(2,1)} %copy-done.6) | copy-start | bytes 101380
  171.9 13.9 %copy-start.9 = (bf16[16,16,66,1]{2,0,3,1:T(8,128)(2,1)S(1)}, bf16[16,16,66,1]{2,0,3,1:T(8,128)(2,1)}, u32[]{:S(2)}) copy-start(bf16[16,16,66,1]{2,0,3,1:T(8,128)(2,1)} %copy-done.8) | copy-start | bytes 101380
  182.1 58.8 %all-to-all-start.1 = ((bf16[16,2,8192]{2,1,0:T(2,128)(2,1)}), bf16[16,2,8192]{2,1,0:T(2,128)(2,1)S(1)}, u32[]{:S(2)}, u32[]{:S(2)}) async-start(bf16[16,2,8192]{2,1,0:T(2,128)(2,1)} %reshape.177), calls=%async_computation.2 | async-start | bytes 1048576 | tf_op jit(solution)/shard_map/all_to_all | solution.py:87
  185.7 456.1 %reduce-scatter.2.cloned.1.call-start = ((), (), s32[]{:S(2)}) async-start(), calls=%async_computation.3 | async-start | bytes 1179648 | tf_op jit(solution)/shard_map/reduce_scatter | solution.py:81
  190.7 14.3 %copy-start.3 = (bf16[16,1,18,66,34]{3,0,4,2,1:T(8,128)(2,1)S(1)}, bf16[16,1,18,66,34]{3,0,4,2,1:T(8,128)(2,1)}, u32[]{:S(2)}) copy-start(bf16[16,1,18,66,34]{3,0,4,2,1:T(8,128)(2,1)} %fusion.48) | copy-start | bytes 3877636
  246.1 1.3 copy-start.2
  250.4 9.1 %copy-start.12 = (bf16[8,64,16]{1,2,0:T(8,128)(2,1)S(1)}, bf16[8,64,16]{1,2,0:T(8,128)(2,1)}, u32[]{:S(2)}) copy-start(bf16[8,64,16]{1,2,0:T(8,128)(2,1)} %param.13) | copy-start | bytes 49156
  250.4 9.1 %copy-start.13 = (pred[8,6]{0,1:T(8,128)(4,1)S(1)}, pred[8,6]{0,1:T(8,128)(4,1)}, u32[]{:S(2)}) copy-start(pred[8,6]{0,1:T(8,128)(4,1)} %constant.46) | copy-start | bytes 148
  347.3 191.7 %copy-start.5 = (bf16[64,1,8,32,16]{0,1,4,3,2:T(2,128)(2,1)S(1)}, bf16[64,1,8,32,16]{0,1,4,3,2:T(2,128)(2,1)}, u32[]{:S(2)}) copy-start(bf16[64,1,8,32,16]{0,1,4,3,2:T(2,128)(2,1)} %copy.92) | copy-start | bytes 1572868
  539.0 104.4 %copy-start.1 = (bf16[4,256,256]{2,1,0:T(8,128)(2,1)S(1)}, bf16[4,256,256]{2,1,0:T(8,128)(2,1)}, u32[]{:S(2)}) copy-start(bf16[4,256,256]{2,1,0:T(8,128)(2,1)} %param.14) | copy-start | bytes 1572868
Sparse Core Ops, SparseCore 0:
  241.1 42.0 reduce-scatter.1
where the time goes:
time: 661 us; the launch traced here: 650 us
  matrix products  281 us (43%)
  local copies, waits for them, and re-layouts  218 us (33%)
  blocking collectives  92.3 us (14%)
  other arithmetic  26.7 us (4%)
  between operations  14.6 us (2%)
  starting transfers between devices  11.2 us (2%)
    transpose x1, matrix products, per_device(): jnp.transpose(correlated, (2, 3, 4, 1, 0)).reshape(27, channels, channels)  192 us
    psum x1, blocking collectives, per_device(): lax.psum((conv_partial, down_partial), ('sy', 'sz'))  68.7 us
    convert_element_type x5, local copies, waits for them, and re-layouts, per_device(): hidden = jax.nn.silu(pre_act).astype(jnp.bfloat16)  48 us
    conv_general_dilated x1, matrix products, per_device(): lax.conv_general_dilated(padded[None], kernel, (1, 1, 1), 'VALID', dimens...  33.2 us
    transpose x1, matrix products, per_device(): jnp.transpose(down_corr, (2, 3, 4, 1, 0))  32.6 us
    broadcast_in_dim x1, local copies, waits for them, and re-layouts, per_device(): padded[:, None]  32.5 us
    convert_element_type x1, local copies, waits for them, and re-layouts, per_device(): pre_grad = (hidden_grad * silu_slope(pre_act)).astype(jnp.bfloat16)  29.4 us
    conv_general_dilated x3, local copies, waits for them, and re-layouts, per_device(): lax.conv_general_dilated(padded[None], kernel, (1, 1, 1), 'VALID', dimens...  29.1 us
  transfers between devices with their start and end apart: 6, of which 2 were waited for; matrix products, arithmetic and copies ran while one was open for 60% of the time, Pallas kernels for 0%

commit v1 on v0

v1 whole, which is shorter than its diff:
```python
import math

import jax
import jax.numpy as jnp
from jax import lax
from jax.experimental import pallas as pl
from jax.experimental.pallas import tpu as pltpu
from jax.sharding import PartitionSpec as P

F32 = jnp.float32
BF16 = jnp.bfloat16
VMEM = pl.BlockSpec(memory_space=pltpu.VMEM)


def dot(a, b, ca, cb):
    return lax.dot_general(a, b, (((ca,), (cb,)), ((), ())), preferred_element_type=F32)


def iota(shape, dim):
    return lax.broadcasted_iota(jnp.int32, shape, dim)


def feature_kernel(lab_ref, wd_ref, out_ref, lab_s, wd_s):
    lab_s[...] = lab_ref[...]
    wd_s[...] = wd_ref[...].astype(F32)
    row = iota((128, 64), 0)
    run, r = row // 32, row % 32
    y = jnp.where(run == 0, 2 * r, jnp.where(run == 1, 2 * r + 1, jnp.where(run == 2, 2 * r - 1, 2 * r + 2)))
    pick = (y == iota((128, 64), 1)).astype(BF16)
    for z in range(out_ref.shape[0]):
        lab = lab_s[:, z, :]
        parts = [(lab == m).astype(F32).astype(BF16) for m in range(4)]
        parts.append(wd_s[:, z, :].astype(BF16))
        out_ref[z] = dot(pick, jnp.concatenate(parts, axis=0), 1, 1).astype(BF16)


def weight_kernel(conv_ref, down_ref, emb_ref, band_ref, dband_ref, table_ref):
    spread = (iota((256, 16), 0) % 16 == iota((256, 16), 1)).astype(BF16)
    wide = dot(spread, conv_ref[...], 1, 0).astype(BF16)
    offset = iota((256, 256), 0) // 16 - iota((256, 256), 1) // 16 + 1
    for t in range(9):
        total = jnp.zeros((256, 256), F32)
        for tx in range(3):
            at = (tx * 9 + t) * 16
            tile = dot(wide[:, at : at + 16], spread, 1, 1)
            total = jnp.where(offset == tx, tile, total)
        band_ref[t] = total.astype(BF16)
    lane_x = iota((64, 256), 1) // 16
    for bc in range(4):
        tiles = [dot(down_ref[4 * a + bc], spread, 0, 1) for a in range(2)]
        both = jnp.where(lane_x % 2 == 0, tiles[0], tiles[1])
        for x2 in range(8):
            dband_ref[bc, 64 * x2 : 64 * x2 + 64, :] = jnp.where(lane_x // 2 == x2, both, 0.0).astype(BF16)
    lane_e = iota((16, 256), 1) // 16
    row_e = iota((16, 256), 0)
    rows = dot(emb_ref[...], spread, 1, 1)
    for m in range(5):
        line = jnp.broadcast_to(rows[m : m + 1, :], (16, 256))
        table_ref[16 * m : 16 * m + 16, :] = jnp.where(lane_e == row_e, line, 0.0).astype(BF16)


def forward_kernel(
    feat_ref, zlo_ref, zhi_ref, ylo_ref, yhi_ref, table_ref, band_ref, dband_ref,
    emb_ref, slope_ref, hidden_ref, coarse_ref, turn_a, turn_b,
):
    table = table_ref[...]
    row = iota((128, 80), 0)
    emb_ref[0] = dot(zlo_ref[...], table, 1, 0).astype(BF16)
    emb_ref[33] = dot(zhi_ref[...], table, 1, 0).astype(BF16)
    ylo = ylo_ref[...].astype(F32)
    yhi = yhi_ref[...].astype(F32)
    for z in range(32):
        f = feat_ref[z].astype(F32)
        f = jnp.where(row == 64, ylo[z : z + 1, :], f)
        f = jnp.where(row == 127, yhi[z : z + 1, :], f)
        emb_ref[z + 1] = dot(f.astype(BF16), table, 1, 0).astype(BF16)
    chunk = 8
    for b in range(2):
        runs = (2, 0, 1) if b == 0 else (0, 1, 3)
        for z0 in range(0, 32, chunk):
            acc = None
            for ty in range(3):
                for tz in range(3):
                    run = 32 * runs[ty]
                    rows = emb_ref[z0 + tz : z0 + tz + chunk, run : run + 32, :].reshape(32 * chunk, 256)
                    part = dot(rows, band_ref[3 * ty + tz], 1, 0)
                    acc = part if acc is None else acc + part
            sigma = jax.nn.sigmoid(acc)
            hid = (acc * sigma).astype(BF16).reshape(chunk, 32, 256)
            slope = (sigma * (1.0 + acc * (1.0 - sigma))).reshape(chunk, 32, 256)
            for k in range(chunk):
                z2, c = (z0 + k) // 2, k % 2
                hidden_ref[2 * b + c, 32 * z2 : 32 * z2 + 32, :] = hid[k]
                slope_ref[2 * b + c, 32 * z2 : 32 * z2 + 32, :] = slope[k]
    for x2 in range(8):
        at = slice(64 * x2, 64 * x2 + 64)
        acc = None
        for bc in range(4):
            part = dot(dband_ref[bc, at, :], hidden_ref[bc], 1, 1)
            acc = part if acc is None else acc + part
        turn_a[at, :] = acc
    for z2 in range(16):
        for half in range(2):
            pieces = [
                turn_a[64 * x2 : 64 * x2 + 64, 32 * z2 : 32 * z2 + 32]
                for x2 in range(4 * half, 4 * half + 4)
            ]
            turn_b[half, pl.ds(z2, 64, stride=16), :] = jnp.concatenate(pieces, axis=1)
    for half in range(2):
        coarse_ref[:, 128 * half : 128 * half + 128] = turn_b[half].astype(BF16)


def mix_kernel(scale, coarse_ref, mix_ref, cot_ref, mid_ref, mixg_ref, grad_ref):
    width = mix_ref.shape[1]
    coarse = coarse_ref[...].reshape(width, 256)
    mix = mix_ref[0]
    flat = coarse.T
    pre = dot(flat, mix, 1, 1)
    sigma = jax.nn.sigmoid(pre)
    mid_ref[0] = (pre * sigma).astype(BF16)
    grad = (cot_ref[0].astype(F32) * (sigma * (1.0 + pre * (1.0 - sigma)))).astype(BF16)
    turned = grad.T
    mixg_ref[0] = dot(turned, flat, 1, 0) * scale
    out = dot(mix.T, turned, 1, 0)
    grad_ref[...] = out.astype(BF16).reshape(grad_ref.shape)


def fold(value, step):
    lanes = value.shape[-1]
    if lanes == 256:
        value = value[:, :128] + value[:, 128:]
    shift = 64
    while shift >= step:
        value = value + pltpu.roll(value, shift, 1)
        shift //= 2
    return value


def backward_kernel(
    down_scale, conv_scale, cgrad_ref, emb_ref, slope_ref, hidden_ref, dband_ref,
    out_ref, turn_a, turn_b, turned_pg,
):
    for half in range(2):
        turn_b[half] = cgrad_ref[:, 128 * half : 128 * half + 128].astype(F32)
    for half in range(2):
        for quad in range(4):
            pieces = [turn_b[half, pl.ds(4 * quad + k, 64, stride=16), :] for k in range(4)]
            for k in range(4):
                x2 = 4 * half + k
                turn_a[64 * x2 : 64 * x2 + 64, 128 * quad : 128 * quad + 128] = jnp.concatenate(
                    [p[:, 32 * k : 32 * k + 32] for p in pieces], axis=1
                )
    cg_t = turn_a[...].astype(BF16)
    cg = cg_t.T
    lane = iota((64, 256), 1)
    low = iota((64, 128), 1)
    down = jnp.zeros((64, 128), F32)
    for bc in range(4):
        total = jnp.zeros((64, 256), F32)
        for x2 in range(8):
            part = dot(cg_t[64 * x2 : 64 * x2 + 64, :], hidden_ref[bc], 1, 0)
            total = jnp.where(lane // 32 == x2, part, total)
        down = jnp.where(low // 32 == bc, fold(total, 32), down)
    out_ref[0:64, :] = down * down_scale
    for bc in range(4):
        hgrad = dot(cg, dband_ref[bc], 1, 0)
        pgrad = (hgrad * slope_ref[bc]).astype(BF16)
        turned_pg[bc] = pgrad.T
    lane_x = iota((16, 256), 1) // 16
    group = iota((16, 128), 1) // 16
    blocks = [jnp.zeros((16, 128), F32) for _ in range(4)]
    for ty in range(3):
        for tz in range(3):
            acc = None
            for bc in range(4):
                b, c = bc // 2, bc % 2
                run = 32 * ((2, 0, 1) if b == 0 else (0, 1, 3))[ty]
                q, p = (c + tz) // 2, (c + tz) % 2
                rows = emb_ref[q : q + 16, p, run : run + 32, :].reshape(512, 256)
                part = dot(turned_pg[bc], rows, 1, 0)
                acc = part if acc is None else acc + part
            for tx in range(3):
                total = jnp.zeros((16, 256), F32)
                for x in range(16):
                    if 0 <= x + tx - 1 < 16:
                        total = jnp.where(lane_x == x + tx - 1, acc[16 * x : 16 * x + 16, :], total)
                tap = 9 * tx + 3 * ty + tz
                blocks[tap // 8] = jnp.where(group == tap % 8, fold(total, 16), blocks[tap // 8])
    for k in range(4):
        out_ref[64 + 16 * k : 80 + 16 * k, :] = blocks[k] * conv_scale


def params(mib):
    return pltpu.CompilerParams(vmem_limit_bytes=mib << 20)


def cost(flops, nbytes):
    return pl.CostEstimate(flops=flops, bytes_accessed=nbytes, transcendentals=0)


def shape(dims, dtype):
    return jax.ShapeDtypeStruct(dims, dtype)


def sum_everywhere(value, axes):
    for axis in axes:
        size = lax.axis_size(axis)
        step = 1
        while step < size:
            value = value + lax.ppermute(value, axis, [(i, i ^ step) for i in range(size)])
            step *= 2
    return value


def per_device(
    labels, wall_dist, material_table, dist_weight, conv_weight, down_weight, mix_weight, cotangent
):
    count_y = lax.axis_size("sy")
    count_z = lax.axis_size("sz")
    mine = 64 // count_z
    width = mix_weight.shape[1]
    features = pl.pallas_call(
        feature_kernel,
        out_shape=shape((32, 128, 80), BF16),
        in_specs=[VMEM] * 2,
        out_specs=VMEM,
        scratch_shapes=[pltpu.VMEM((16, 32, 64), jnp.int32), pltpu.VMEM((16, 32, 64), F32)],
        compiler_params=params(16),
        cost_estimate=cost(32 * 128 * 64 * 80 * 2, 2 << 20),
        name="features",
    )(jnp.transpose(labels, (0, 2, 1)), jnp.transpose(wall_dist, (0, 2, 1)))
    up_y = [(i, i + 1) for i in range(count_y - 1)]
    up_z = [(i, i + 1) for i in range(count_z - 1)]
    ylo = lax.ppermute(features[:, 63, :], "sy", up_y)
    yhi = lax.ppermute(features[:, 0, :], "sy", [(j, i) for i, j in up_y])

    def whole(z):
        row = lax.broadcasted_iota(jnp.int32, (128, 80), 0)
        face = jnp.where(row == 64, ylo[z][None], features[z])
        return jnp.where(row == 127, yhi[z][None], face)

    zlo = lax.ppermute(whole(31), "sz", up_z)
    zhi = lax.ppermute(whole(0), "sz", [(j, i) for i, j in up_z])

    flat_conv = jnp.transpose(conv_weight, (2, 0, 1)).reshape(16, 432)
    rows = jnp.concatenate([material_table, dist_weight[None], jnp.zeros((3, 16), BF16)], axis=0)
    band, dband, table = pl.pallas_call(
        weight_kernel,
        out_shape=(shape((9, 256, 256), BF16), shape((4, 512, 256), BF16), shape((80, 256), BF16)),
        in_specs=[VMEM] * 3,
        out_specs=(VMEM,) * 3,
        compiler_params=params(16),
        cost_estimate=cost(27 * 256 * 16 * 256 * 2, 3 << 20),
        name="weights",
    )(flat_conv, jnp.transpose(down_weight, (0, 2, 1)), rows)

    embedded, slope, hidden, coarse = pl.pallas_call(
        forward_kernel,
        out_shape=(
            shape((34, 128, 256), BF16),
            shape((4, 512, 256), F32),
            shape((4, 512, 256), BF16),
            shape((1024, 256), BF16),
        ),
        in_specs=[VMEM] * 8,
        out_specs=(VMEM,) * 4,
        scratch_shapes=[pltpu.VMEM((512, 512), F32), pltpu.VMEM((2, 1024, 128), F32)],
        compiler_params=params(32),
        cost_estimate=cost(3 << 30, 10 << 20),
        name="forward",
    )(features, zlo, zhi, ylo, yhi, table, band, dband)

    sent = lax.all_to_all(
        coarse.reshape(count_z, mine * 16, 256), "sz", split_axis=0, concat_axis=0, tiled=True
    )
    block = lambda *dims: pl.BlockSpec(dims, lambda c: (c,) + (0,) * (len(dims) - 1))
    mid, mix_partial, back = pl.pallas_call(
        lambda *refs: mix_kernel(1.0 / math.sqrt(8 * 32 * count_y), *refs),
        grid=(mine,),
        out_shape=(
            shape((mine, 256, width), BF16),
            shape((mine, width, width), F32),
            shape((count_z, mine * 16, 256), BF16),
        ),
        in_specs=[
            pl.BlockSpec((count_z, 16, 256), lambda c: (0, c, 0)),
            block(1, width, width),
            block(1, 256, width),
        ],
        out_specs=(
            block(1, 256, width),
            block(1, width, width),
            pl.BlockSpec((count_z, 16, 256), lambda c: (0, c, 0)),
        ),
        compiler_params=params(16),
        cost_estimate=cost(mine * 3 * 2 * 256 * width * width, 5 << 20),
        name="mix",
    )(sent, mix_weight, cotangent.reshape(mine, 256, width))
    coarse_grad = lax.all_to_all(back, "sz", split_axis=0, concat_axis=0, tiled=True)
    mix_grad = lax.psum_scatter(mix_partial, "sy", scatter_dimension=1, tiled=True)

    cells = 16 * 64 * count_y * 32 * count_z
    sums = pl.pallas_call(
        lambda *refs: backward_kernel(
            1.0 / math.sqrt(cells // 8), 1.0 / math.sqrt(cells), *refs
        ),
        out_shape=shape((128, 128), F32),
        in_specs=[VMEM] * 5,
        out_specs=VMEM,
        scratch_shapes=[
            pltpu.VMEM((512, 512), F32),
            pltpu.VMEM((2, 1024, 128), F32),
            pltpu.VMEM((4, 256, 512), BF16),
        ],
        compiler_params=params(32),
        cost_estimate=cost(4 << 30, 8 << 20),
        name="backward",
    )(coarse_grad.reshape(1024, 256), embedded.reshape(17, 2, 128, 256), slope, hidden, dband)
    sums = sum_everywhere(sums, ("sz", "sy"))
    down_grad = jnp.transpose(sums[:64].reshape(64, 4, 2, 16), (2, 1, 0, 3)).reshape(8, 64, 16)
    conv_grad = jnp.transpose(sums[64:].reshape(4, 16, 8, 16), (0, 2, 1, 3)).reshape(32, 16, 16)[:27]
    return (mid.reshape(cotangent.shape), mix_grad, down_grad, conv_grad)


def solution(mesh):
    in_specs = (
        P(None, "sy", "sz"),
        P(None, "sy", "sz"),
        P(),
        P(),
        P(),
        P(),
        P("sz", None, None),
        P("sz", None, "sy", None),
    )
    out_specs = (P("sz", None, "sy", None), P("sz", "sy", None), P(), P())
    return jax.shard_map(
        per_device, mesh=mesh, in_specs=in_specs, out_specs=out_specs, check_vma=False
    )
```

time: 661 us -> 136 us (0.21); the launches traced: 650 us -> 135 us
  matrix products: 281 us -> 0 us
  local copies, waits for them, and re-layouts: 218 us -> 10.8 us
  blocking collectives: 92.3 us -> 41.1 us
  other arithmetic: 26.7 us -> 0.94 us
  waiting for transfers between devices: 6.54 us -> 25.5 us
  Pallas kernels: 0 us -> 18.4 us
  starting transfers between devices: 11.2 us -> 23.9 us
    transpose x2 -> x0, matrix products: 224 us -> none  [the longest x1 192 us: per_device(): jnp.transpose(correlated, (2, 3, 4, 1, 0)).reshape(27, channels, channels)]
    convert_element_type x9 -> x0, local copies, waits for them, and re-layouts: 88.1 us -> none  [the longest x5 48 us: per_device(): hidden = jax.nn.silu(pre_act).astype(jnp.bfloat16)]
    psum x1 -> x0, blocking collectives: 68.7 us -> none  [per_device(): lax.psum((conv_partial, down_partial), ('sy', 'sz'))]
    conv_general_dilated x3 -> x0, matrix products: 50.4 us -> none  [the longest x1 33.2 us: per_device(): lax.conv_general_dilated(padded[None], kernel, (1, 1, 1), 'VALID', dimens...]
    conv_general_dilated x4 -> x0, local copies, waits for them, and re-layouts: 46.7 us -> none  [the longest x3 29.1 us: per_device(): lax.conv_general_dilated(padded[None], kernel, (1, 1, 1), 'VALID', dimens...]
    broadcast_in_dim x4 -> x3, local copies, waits for them, and re-layouts: 43.9 us -> 0.02 us  [the longest x1 0.01 us: whole(): face = jnp.where(row == 64, ylo[z][None], features[z])]
    ppermute x4 -> x11, waiting for transfers between devices: 6.52 us -> 25.5 us  [the longest x7 21.4 us: sum_everywhere(): lax.ppermute(value, axis, [(i, i ^ step) for i in range(size)])]
    pallas_call x0 -> x5, Pallas kernels: none -> 18.4 us  [the longest x1 6.03 us: per_device(): pl.pallas_call(forward_kernel, out_shape=(shape((34, 128, 256), BF16), sh...]
  transfers between devices with their start and end apart: 6 -> 12, of which waited for: 2 -> 8; matrix products, arithmetic and copies ran while one was open for 60% -> 3% of each run, Pallas kernels for 0% -> 5%
where the time goes in v1:
time: 136 us; the launch traced here: 135 us
  blocking collectives  41.1 us (30%)
  waiting for transfers between devices  25.5 us (19%)
  starting transfers between devices  23.9 us (18%)
  Pallas kernels  18.4 us (14%)
  between operations  14.3 us (11%)
  local copies, waits for them, and re-layouts  10.8 us (8%)
    all_to_all x1, blocking collectives, per_device(): lax.all_to_all(coarse.reshape(count_z, mine * 16, 256), 'sz', split_axis=...  21.4 us
    ppermute x7, waiting for transfers between devices, sum_everywhere(): lax.ppermute(value, axis, [(i, i ^ step) for i in range(size)])  21.4 us
    all_to_all x1, blocking collectives, per_device(): lax.all_to_all(back, 'sz', split_axis=0, concat_axis=0, tiled=True)  19.7 us
    ppermute x7, starting transfers between devices, sum_everywhere(): lax.ppermute(value, axis, [(i, i ^ step) for i in range(size)])  14.7 us
    unnamed x25, local copies, waits for them, and re-layouts  8.51 us
    pallas_call x1, Pallas kernels, per_device(): pl.pallas_call(forward_kernel, out_shape=(shape((34, 128, 256), BF16), sh...  6.03 us
    pallas_call x1, Pallas kernels, per_device(): pl.pallas_call(lambda *refs: backward_kernel(1.0 / math.sqrt(cells // 8),...  5.39 us
    ppermute x1, waiting for transfers between devices, per_device(): yhi = lax.ppermute(features[:, 0, :], 'sy', [(j, i) for i, j in up_y])  4.13 us
  transfers between devices with their start and end apart: 12, of which 8 were waited for; matrix products, arithmetic and copies ran while one was open for 3% of the time, Pallas kernels for 5%

profile of v1, /device:TPU:0, one launch (start us, length us, event | category | flops | bytes accessed | tf_op | source)
XLA Modules:
  0.0 134.9 jit_solution(12720293601670238338)
XLA Ops:
  7.2 0.0 reduce-scatter.2.cloned.1.call-start
  7.2 0.0 copy-start.2
  7.2 0.9 copy-done.2
  8.2 0.0 copy-start.3
  8.2 0.9 copy-done.3
  9.1 2.5 %features.1.feat_ref = bf16[32,128,80]{2,1,0:T(8,128)(2,1)S(1)} custom-call(s32[16,32,64]{2,1,0:T(8,128)S(1)} %bitcast.46, bf16[16,32,64]{2,1,0:T(8,128)(2,1)S(1)} %bitcast.47), custom_call_target="tpu_custom_call" | custom-call | flops 41943040 | bytes 2097152 | tf_op jit(solution)/shard_map/features/pallas_call | solution.py:222
  11.6 3.6 %collective-permute-start.1 = (bf16[32,80]{1,0:T(8,128)(2,1)S(1)}, bf16[32,80]{1,0:T(8,128)(2,1)S(1)}, u32[]{:S(2)}, u32[]{:S(2)}) collective-permute-start(bf16[32,80]{1,0:T(8,128)(2,1)S(1)} %bitcast.54), channel_id=1, source_target_pairs={{0,16},{16,32},{32,48},{48,64},{64,80},{80,96},{96,112},{1,17},{17... | collective-permute-start | bytes 15368 | tf_op jit(solution)/shard_map/ppermute | solution.py:234
  15.2 1.3 collective-permute-start
  16.5 0.1 pad.2.clone
  16.6 0.0 collective-permute-done.1.ylo_ref
  16.6 4.1 %collective-permute-done.yhi_ref = bf16[32,80]{1,0:T(8,128)(2,1)S(1)} collective-permute-done((bf16[32,80]{1,0:T(8,128)(2,1)S(1)}, bf16[32,80]{1,0:T(8,128)(2,1)S(1)}, u32[]{:S(2)}, u32[]{:S(2)}) %collective-permute-start) | collective-permute-done | bytes 5152 | tf_op jit(solution)/shard_map/ppermute | solution.py:235
  20.8 0.1 fusion.1
  20.9 1.3 collective-permute-start.3
  22.2 3.0 %collective-permute-start.2 = (bf16[128,80]{1,0:T(8,128)(2,1)S(1)}, bf16[128,80]{1,0:T(8,128)(2,1)S(1)}, u32[]{:S(2)}, u32[]{:S(2)}) collective-permute-start(bf16[128,80]{1,0:T(8,128)(2,1)S(1)} %get-tuple-element.33), channel_id=1, source_target_pairs={{0,1},{1,2},{2,3},{3,4},{4,5},{5,6},{6,7},{7,8},{8,9},{9,10},{10,1... | collective-permute-start | bytes 61448 | tf_op jit(solution)/shard_map/ppermute | solution.py:242
  25.2 0.8 maximum_maximum_fusion.emb_ref
  26.0 1.0 copy.25
  27.0 0.2 reshape.38.conv_ref
  27.2 0.0 copy-start.4
  27.2 0.8 copy-done.4
  28.0 1.4 %weights.1 = (bf16[9,256,256]{2,1,0:T(8,128)(2,1)S(1)}, bf16[4,512,256]{2,1,0:T(8,128)(2,1)S(1)}, bf16[80,256]{1,0:T(8,128)(2,1)S(1)}) custom-call(bf16[16,432]{1,0:T(8,128)(2,1)S(1)} %reshape.38.conv_ref, bf16[8,16,64]{2,1,0:T(8,128)(2,1)S(1)} %bitcast.48, bf16[8,16]{1,0:T(8,128)(2,1)S(1)} %maximum_maximum_fusion.emb_ref), custom_call_target="tpu_custom_call" | custom-call | flops 56623104 | bytes 3145728 | tf_op jit(solution)/shard_map/weights/pallas_call | solution.py:247
  29.4 0.0 copy-start.5
  29.4 0.0 collective-permute-done.3.zhi_ref
  29.4 0.0 collective-permute-done.2.zlo_ref
  29.4 0.0 copy-start
  29.4 0.0 copy-start.1
  29.4 6.0 %forward.1 = (bf16[34,128,256]{2,1,0:T(8,128)(2,1)S(1)}, f32[4,512,256]{2,1,0:T(8,128)S(1)}, bf16[4,512,256]{2,1,0:T(8,128)(2,1)S(1)}, bf16[1024,256]{1,0:T(8,128)(2,1)S(1)}) custom-call(bf16[32,128,80]{2,1,0:T(8,128)(2,1)S(1)} %features.1.feat_ref, bf16[128,80]{1,0:T(8,128)(2,1)S(1)} %collective-permute-done.2.zlo_ref, ...), custom_call_target="tpu_custom_call" | custom-call | flops 3221225472 | bytes 10485760 | tf_op jit(solution)/shard_map/forward/pallas_call | solution.py:257
  35.4 0.0 copy-done.5
  35.5 0.0 copy-start.9
  35.5 1.0 copy-done.9
  36.5 0.0 copy-start.7
  36.5 21.4 %all_to_all.10.refs_0_ = bf16[16,64,256]{2,1,0:T(8,128)(2,1)S(1)} all-to-all(bf16[16,64,256]{2,1,0:T(8,128)(2,1)S(1)} %bitcast.44), channel_id=1, replica_groups=mesh['sy'=8,'sz'=16] {'sz'}, dimensions={0} | all-to-all | bytes 1048576 | tf_op jit(solution)/shard_map/all_to_all | solution.py:273
  57.9 0.0 copy-done
  57.9 0.0 copy-done.1
  57.9 3.0 %mix.1 = (bf16[4,256,256]{2,1,0:T(8,128)(2,1)}, f32[4,256,256]{2,1,0:T(8,128)}, bf16[16,64,256]{2,1,0:T(8,128)(2,1)S(1)}) custom-call(bf16[16,64,256]{2,1,0:T(8,128)(2,1)S(1)} %all_to_all.10.refs_0_, bf16[4,256,256]{2,1,0:T(8,128)(2,1)S(1)} %copy-done, bf16[4,256,256]{2,1,0:T(8,128)(2,1)S(1)} %bitcast.43), custom_call_target="tpu_custom_call" | custom-call | flops 402653184 | bytes 5242880 | tf_op jit(solution)/shard_map/mix/pallas_call | solution.py:277
  60.9 0.0 copy-done.7
  60.9 0.0 reduce-scatter.2.cloned.1.call-update
  60.9 19.7 %all_to_all.11 = bf16[16,64,256]{2,1,0:T(8,128)(2,1)S(1)} all-to-all(bf16[16,64,256]{2,1,0:T(8,128)(2,1)S(1)} %get-tuple-element.20), channel_id=1, replica_groups=mesh['sy'=8,'sz'=16] {'sz'}, dimensions={0} | all-to-all | bytes 1048576 | tf_op jit(solution)/shard_map/all_to_all | solution.py:299
  80.6 0.0 copy-start.6
  80.7 1.2 copy-done.6
  81.9 0.0 copy-start.8
  81.9 1.6 %copy-done.8 = f32[4,512,256]{2,1,0:T(8,128)S(1)} copy-done((f32[4,512,256]{2,1,0:T(8,128)S(1)}, f32[4,512,256]{2,1,0:T(8,128)}, u32[]{:S(2)}) %copy-start.8) | copy-done | bytes 2097176
  83.5 0.0 copy-start.10
  83.5 1.2 copy-done.10
  84.7 5.4 %backward.1 = f32[128,128]{1,0:T(8,128)S(1)} custom-call(bf16[1024,256]{1,0:T(8,128)(2,1)S(1)} %bitcast.45, bf16[17,2,128,256]{3,2,1,0:T(8,128)(2,1)S(1)} %bitcast.49, f32[4,512,256]{2,1,0:T(8,128)S(1)} %copy-done.8, bf16[4,512,256]{2,1,0:T(8,128)(2,1)S(1)} %copy-done.10, bf16[4,512,256]{2,1,0:T(8,128)(2,1)S(1)} %copy-done.6), custom_call_target="tpu_custom_call" | custom-call | flops 4294967296 | bytes 8388608 | tf_op jit(solution)/shard_map/backward/pallas_call | solution.py:303
  90.1 0.1 collective-permute-start.4
  90.2 1.2 collective-permute-done.4
  91.4 0.1 collective-permute-start.5
  91.5 6.6 %collective-permute-done.5 = f32[128,128]{1,0:T(8,128)S(1)} collective-permute-done((f32[128,128]{1,0:T(8,128)S(1)}, f32[128,128]{1,0:T(8,128)S(1)}, u32[]{:S(2)}, u32[]{:S(2)}) %collective-permute-start.5) | collective-permute-done | bytes 65568 | tf_op jit(solution)/shard_map/ppermute | solution.py:210
  98.2 1.3 collective-permute-start.6
  99.5 3.0 %collective-permute-done.6 = f32[128,128]{1,0:T(8,128)S(1)} collective-permute-done((f32[128,128]{1,0:T(8,128)S(1)}, f32[128,128]{1,0:T(8,128)S(1)}, u32[]{:S(2)}, u32[]{:S(2)}) %collective-permute-start.6) | collective-permute-done | bytes 65568 | tf_op jit(solution)/shard_map/ppermute | solution.py:210
  102.5 2.7 %collective-permute-start.7 = (f32[128,128]{1,0:T(8,128)S(1)}, f32[128,128]{1,0:T(8,128)S(1)}, u32[]{:S(2)}, u32[]{:S(2)}) collective-permute-start(f32[128,128]{1,0:T(8,128)S(1)} %add.25), channel_id=1, source_target_pairs={{0,8},{1,9},{2,10},{3,11},{4,12},{5,13},{6,14},{7,15},{8,0},{9,1},... | collective-permute-start | bytes 196616 | tf_op jit(solution)/shard_map/ppermute | solution.py:210
  105.3 3.1 %collective-permute-done.7 = f32[128,128]{1,0:T(8,128)S(1)} collective-permute-done((f32[128,128]{1,0:T(8,128)S(1)}, f32[128,128]{1,0:T(8,128)S(1)}, u32[]{:S(2)}, u32[]{:S(2)}) %collective-permute-start.7) | collective-permute-done | bytes 65568 | tf_op jit(solution)/shard_map/ppermute | solution.py:210
  108.4 3.9 %collective-permute-start.8 = (f32[128,128]{1,0:T(8,128)S(1)}, f32[128,128]{1,0:T(8,128)S(1)}, u32[]{:S(2)}, u32[]{:S(2)}) collective-permute-start(f32[128,128]{1,0:T(8,128)S(1)} %add.26), channel_id=1, source_target_pairs={{0,16},{16,0},{32,48},{48,32},{64,80},{80,64},{96,112},{112,96},{1... | collective-permute-start | bytes 196616 | tf_op jit(solution)/shard_map/ppermute | solution.py:210
  112.3 2.2 %collective-permute-done.8 = f32[128,128]{1,0:T(8,128)S(1)} collective-permute-done((f32[128,128]{1,0:T(8,128)S(1)}, f32[128,128]{1,0:T(8,128)S(1)}, u32[]{:S(2)}, u32[]{:S(2)}) %collective-permute-start.8) | collective-permute-done | bytes 65568 | tf_op jit(solution)/shard_map/ppermute | solution.py:210
  114.5 3.7 %collective-permute-start.9 = (f32[128,128]{1,0:T(8,128)S(1)}, f32[128,128]{1,0:T(8,128)S(1)}, u32[]{:S(2)}, u32[]{:S(2)}) collective-permute-start(f32[128,128]{1,0:T(8,128)S(1)} %add.27), channel_id=1, source_target_pairs={{0,32},{16,48},{32,0},{48,16},{64,96},{80,112},{96,64},{112,80},{1... | collective-permute-start | bytes 196616 | tf_op jit(solution)/shard_map/ppermute | solution.py:210
  118.2 2.2 %collective-permute-done.9 = f32[128,128]{1,0:T(8,128)S(1)} collective-permute-done((f32[128,128]{1,0:T(8,128)S(1)}, f32[128,128]{1,0:T(8,128)S(1)}, u32[]{:S(2)}, u32[]{:S(2)}) %collective-permute-start.9) | collective-permute-done | bytes 65568 | tf_op jit(solution)/shard_map/ppermute | solution.py:210
  120.4 3.0 %collective-permute-start.10 = (f32[128,128]{1,0:T(8,128)S(1)}, f32[128,128]{1,0:T(8,128)S(1)}, u32[]{:S(2)}, u32[]{:S(2)}) collective-permute-start(f32[128,128]{1,0:T(8,128)S(1)} %add.28), channel_id=1, source_target_pairs={{0,64},{16,80},{32,96},{48,112},{64,0},{80,16},{96,32},{112,48},{1... | collective-permute-start | bytes 196616 | tf_op jit(solution)/shard_map/ppermute | solution.py:210
  123.4 2.9 %collective-permute-done.10 = f32[128,128]{1,0:T(8,128)S(1)} collective-permute-done((f32[128,128]{1,0:T(8,128)S(1)}, f32[128,128]{1,0:T(8,128)S(1)}, u32[]{:S(2)}, u32[]{:S(2)}) %collective-permute-start.10) | collective-permute-done | bytes 65568 | tf_op jit(solution)/shard_map/ppermute | solution.py:210
  126.3 0.1 copy.26
  126.4 0.6 copy.27
  127.1 0.1 reshape.46
  127.3 0.8 copy.29
  128.1 0.0 reduce-scatter.2.cloned.1.call-done
  (17 shorter events, 0.2 us)
Async XLA Ops:
  7.2 120.9 %reduce-scatter.2.cloned.1.call-start = ((), (), s32[]{:S(2)}) async-start(), calls=%async_computation.3 | async-start | bytes 1179648 | tf_op jit(solution)/shard_map/reduce_scatter | solution.py:300
  7.2 1.0 copy-start.2
  8.2 0.9 copy-start.3
  11.6 5.0 %collective-permute-start.1 = (bf16[32,80]{1,0:T(8,128)(2,1)S(1)}, bf16[32,80]{1,0:T(8,128)(2,1)S(1)}, u32[]{:S(2)}, u32[]{:S(2)}) collective-permute-start(bf16[32,80]{1,0:T(8,128)(2,1)S(1)} %bitcast.54), channel_id=1, source_target_pairs={{0,16},{16,32},{32,48},{48,64},{64,80},{80,96},{96,112},{1,17},{17... | collective-permute-start | bytes 15368 | tf_op jit(solution)/shard_map/ppermute | solution.py:234
  15.2 5.5 %collective-permute-start = (bf16[32,80]{1,0:T(8,128)(2,1)S(1)}, bf16[32,80]{1,0:T(8,128)(2,1)S(1)}, u32[]{:S(2)}, u32[]{:S(2)}) collective-permute-start(bf16[32,80]{1,0:T(8,128)(2,1)S(1)} %bitcast.55), channel_id=1, source_target_pairs={{16,0},{32,16},{48,32},{64,48},{80,64},{96,80},{112,96},{17,1},{33... | collective-permute-start | bytes 15368 | tf_op jit(solution)/shard_map/ppermute | solution.py:235
  20.9 8.5 %collective-permute-start.3 = (bf16[128,80]{1,0:T(8,128)(2,1)S(1)}, bf16[128,80]{1,0:T(8,128)(2,1)S(1)}, u32[]{:S(2)}, u32[]{:S(2)}) collective-permute-start(bf16[128,80]{1,0:T(8,128)(2,1)S(1)} %get-tuple-element.32), channel_id=1, source_target_pairs={{1,0},{2,1},{3,2},{4,3},{5,4},{6,5},{7,6},{8,7},{9,8},{10,9},{11,1... | collective-permute-start | bytes 61448 | tf_op jit(solution)/shard_map/ppermute | solution.py:243
  22.2 7.2 %collective-permute-start.2 = (bf16[128,80]{1,0:T(8,128)(2,1)S(1)}, bf16[128,80]{1,0:T(8,128)(2,1)S(1)}, u32[]{:S(2)}, u32[]{:S(2)}) collective-permute-start(bf16[128,80]{1,0:T(8,128)(2,1)S(1)} %get-tuple-element.33), channel_id=1, source_target_pairs={{0,1},{1,2},{2,3},{3,4},{4,5},{5,6},{6,7},{7,8},{8,9},{9,10},{10,1... | collective-permute-start | bytes 61448 | tf_op jit(solution)/shard_map/ppermute | solution.py:242
  27.2 0.8 copy-start.4
  29.4 6.1 %copy-start.5 = (bf16[4,512,256]{2,1,0:T(8,128)(2,1)}, bf16[4,512,256]{2,1,0:T(8,128)(2,1)S(1)}, u32[]{:S(2)}) copy-start(bf16[4,512,256]{2,1,0:T(8,128)(2,1)S(1)} %get-tuple-element.16.dband_ref.refs_4_) | copy-start | bytes 3145732
  29.4 28.5 %copy-start = (bf16[4,256,256]{2,1,0:T(8,128)(2,1)S(1)}, bf16[4,256,256]{2,1,0:T(8,128)(2,1)}, u32[]{:S(2)}) copy-start(bf16[4,256,256]{2,1,0:T(8,128)(2,1)} %refs_1_.1) | copy-start | bytes 1572868
  29.4 28.5 %copy-start.1 = (bf16[4,8,32,256]{3,2,1,0:T(8,128)(2,1)S(1)}, bf16[4,8,32,256]{3,2,1,0:T(8,128)(2,1)}, u32[]{:S(2)}) copy-start(bf16[4,8,32,256]{3,2,1,0:T(8,128)(2,1)} %param.15) | copy-start | bytes 1572868
  35.5 1.0 copy-start.9
  36.5 24.5 %copy-start.7 = (f32[4,512,256]{2,1,0:T(8,128)}, f32[4,512,256]{2,1,0:T(8,128)S(1)}, u32[]{:S(2)}) copy-start(f32[4,512,256]{2,1,0:T(8,128)S(1)} %get-tuple-element.22.refs_2_) | copy-start | bytes 6291460
  80.6 1.2 copy-start.6
  81.9 1.6 %copy-start.8 = (f32[4,512,256]{2,1,0:T(8,128)S(1)}, f32[4,512,256]{2,1,0:T(8,128)}, u32[]{:S(2)}) copy-start(f32[4,512,256]{2,1,0:T(8,128)} %copy-done.7) | copy-start | bytes 6291460
  83.5 1.2 copy-start.10
  90.1 1.3 collective-permute-start.4
  91.4 6.7 %collective-permute-start.5 = (f32[128,128]{1,0:T(8,128)S(1)}, f32[128,128]{1,0:T(8,128)S(1)}, u32[]{:S(2)}, u32[]{:S(2)}) collective-permute-start(f32[128,128]{1,0:T(8,128)S(1)} %add.23), channel_id=1, source_target_pairs={{0,2},{1,3},{2,0},{3,1},{4,6},{5,7},{6,4},{7,5},{8,10},{9,11},{10,... | collective-permute-start | bytes 196616 | tf_op jit(solution)/shard_map/ppermute | solution.py:210
  98.2 4.3 %collective-permute-start.6 = (f32[128,128]{1,0:T(8,128)S(1)}, f32[128,128]{1,0:T(8,128)S(1)}, u32[]{:S(2)}, u32[]{:S(2)}) collective-permute-start(f32[128,128]{1,0:T(8,128)S(1)} %add.24), channel_id=1, source_target_pairs={{0,4},{1,5},{2,6},{3,7},{4,0},{5,1},{6,2},{7,3},{8,12},{9,13},{10,... | collective-permute-start | bytes 196616 | tf_op jit(solution)/shard_map/ppermute | solution.py:210
  102.5 5.8 %collective-permute-start.7 = (f32[128,128]{1,0:T(8,128)S(1)}, f32[128,128]{1,0:T(8,128)S(1)}, u32[]{:S(2)}, u32[]{:S(2)}) collective-permute-start(f32[128,128]{1,0:T(8,128)S(1)} %add.25), channel_id=1, source_target_pairs={{0,8},{1,9},{2,10},{3,11},{4,12},{5,13},{6,14},{7,15},{8,0},{9,1},... | collective-permute-start | bytes 196616 | tf_op jit(solution)/shard_map/ppermute | solution.py:210
  108.4 6.1 %collective-permute-start.8 = (f32[128,128]{1,0:T(8,128)S(1)}, f32[128,128]{1,0:T(8,128)S(1)}, u32[]{:S(2)}, u32[]{:S(2)}) collective-permute-start(f32[128,128]{1,0:T(8,128)S(1)} %add.26), channel_id=1, source_target_pairs={{0,16},{16,0},{32,48},{48,32},{64,80},{80,64},{96,112},{112,96},{1... | collective-permute-start | bytes 196616 | tf_op jit(solution)/shard_map/ppermute | solution.py:210
  114.5 5.9 %collective-permute-start.9 = (f32[128,128]{1,0:T(8,128)S(1)}, f32[128,128]{1,0:T(8,128)S(1)}, u32[]{:S(2)}, u32[]{:S(2)}) collective-permute-start(f32[128,128]{1,0:T(8,128)S(1)} %add.27), channel_id=1, source_target_pairs={{0,32},{16,48},{32,0},{48,16},{64,96},{80,112},{96,64},{112,80},{1... | collective-permute-start | bytes 196616 | tf_op jit(solution)/shard_map/ppermute | solution.py:210
  120.4 5.8 %collective-permute-start.10 = (f32[128,128]{1,0:T(8,128)S(1)}, f32[128,128]{1,0:T(8,128)S(1)}, u32[]{:S(2)}, u32[]{:S(2)}) collective-permute-start(f32[128,128]{1,0:T(8,128)S(1)} %add.28), channel_id=1, source_target_pairs={{0,64},{16,80},{32,96},{48,112},{64,0},{80,16},{96,32},{112,48},{1... | collective-permute-start | bytes 196616 | tf_op jit(solution)/shard_map/ppermute | solution.py:210
Sparse Core Ops, SparseCore 0:
  61.1 38.2 reduce-scatter.1

commit v2 on v1

--- a/solution.py
+++ b/solution.py
@@ -10,6 +10,8 @@
 F32 = jnp.float32
 BF16 = jnp.bfloat16
 VMEM = pl.BlockSpec(memory_space=pltpu.VMEM)
+HBM = pl.BlockSpec(memory_space=pltpu.HBM)
+RUNS = ((64, 0, 32), (0, 32, 96))
 
 
 def dot(a, b, ca, cb):
@@ -20,23 +22,50 @@
     return lax.broadcasted_iota(jnp.int32, shape, dim)
 
 
-def feature_kernel(lab_ref, wd_ref, out_ref, lab_s, wd_s):
-    lab_s[...] = lab_ref[...]
-    wd_s[...] = wd_ref[...].astype(F32)
+def fetch(sources, targets, sem):
+    copies = [pltpu.make_async_copy(a, b, sem.at[k]) for k, (a, b) in enumerate(zip(sources, targets))]
+    for copy in copies:
+        copy.start()
+    return copies
+
+
+def feature_kernel(lab_hbm, wd_hbm, out_ref, first_ref, last_ref, lab_s, wd_b, wd_s, first_s, last_s, sem):
+    copies = fetch((lab_hbm, wd_hbm), (lab_s, wd_b), sem)
     row = iota((128, 64), 0)
     run, r = row // 32, row % 32
     y = jnp.where(run == 0, 2 * r, jnp.where(run == 1, 2 * r + 1, jnp.where(run == 2, 2 * r - 1, 2 * r + 2)))
     pick = (y == iota((128, 64), 1)).astype(BF16)
+    for copy in copies:
+        copy.wait()
+    wd_s[...] = wd_b[...].astype(F32)
     for z in range(out_ref.shape[0]):
         lab = lab_s[:, z, :]
         parts = [(lab == m).astype(F32).astype(BF16) for m in range(4)]
         parts.append(wd_s[:, z, :].astype(BF16))
-        out_ref[z] = dot(pick, jnp.concatenate(parts, axis=0), 1, 1).astype(BF16)
-
-
-def weight_kernel(conv_ref, down_ref, emb_ref, band_ref, dband_ref, table_ref):
+        rows = dot(pick, jnp.concatenate(parts, axis=0), 1, 1)
+        out_ref[z] = rows.astype(BF16)
+        first_s[z : z + 1, :] = rows[0:1, :]
+        last_s[z : z + 1, :] = rows[63:64, :]
+    first_ref[...] = first_s[...].astype(BF16)
+    last_ref[...] = last_s[...].astype(BF16)
+
+
+def weight_kernel(
+    conv_hbm, down_hbm, mat_hbm, dist_hbm, band_ref, dband_ref, table_ref,
+    conv_ref, down_ref, mat_ref, dist_ref, sem,
+):
+    copies = fetch(
+        (conv_hbm, down_hbm, mat_hbm, dist_hbm), (conv_ref, down_ref, mat_ref, dist_ref), sem
+    )
+    for copy in copies:
+        copy.wait()
     spread = (iota((256, 16), 0) % 16 == iota((256, 16), 1)).astype(BF16)
-    wide = dot(spread, conv_ref[...], 1, 0).astype(BF16)
+    taps = conv_ref[...].reshape(256, 27)
+    repeat = (iota((27, 432), 0) == iota((27, 432), 1) // 16).astype(BF16)
+    own = iota((256, 432), 0) // 16 == iota((256, 432), 1) % 16
+    apart = jnp.where(own, dot(taps, repeat, 1, 0), 0.0).astype(BF16)
+    gather = (iota((256, 256), 0) % 16 == iota((256, 256), 1) % 16).astype(BF16)
+    wide = dot(gather, apart, 1, 0).astype(BF16)
     offset = iota((256, 256), 0) // 16 - iota((256, 256), 1) // 16 + 1
     for t in range(9):
         total = jnp.zeros((256, 256), F32)
@@ -53,20 +82,25 @@
             dband_ref[bc, 64 * x2 : 64 * x2 + 64, :] = jnp.where(lane_x // 2 == x2, both, 0.0).astype(BF16)
     lane_e = iota((16, 256), 1) // 16
     row_e = iota((16, 256), 0)
-    rows = dot(emb_ref[...], spread, 1, 1)
+    mat = dot(mat_ref[...], spread, 1, 1)
+    dist = dot(dist_ref[...], spread, 1, 1)
     for m in range(5):
-        line = jnp.broadcast_to(rows[m : m + 1, :], (16, 256))
+        line = jnp.broadcast_to(mat[m : m + 1, :] if m < 4 else dist, (16, 256))
         table_ref[16 * m : 16 * m + 16, :] = jnp.where(lane_e == row_e, line, 0.0).astype(BF16)
 
 
-def forward_kernel(
-    feat_ref, zlo_ref, zhi_ref, ylo_ref, yhi_ref, table_ref, band_ref, dband_ref,
-    emb_ref, slope_ref, hidden_ref, coarse_ref, turn_a, turn_b,
+def activate(acc):
+    sigma = jax.nn.sigmoid(acc)
+    return (acc * sigma).astype(BF16), sigma * (1.0 + acc * (1.0 - sigma))
+
+
+def inner_kernel(
+    feat_ref, ylo_ref, yhi_ref, table_ref, band_ref, emb_ref, slope_ref, hidden_ref, edge_ref
 ):
     table = table_ref[...]
     row = iota((128, 80), 0)
-    emb_ref[0] = dot(zlo_ref[...], table, 1, 0).astype(BF16)
-    emb_ref[33] = dot(zhi_ref[...], table, 1, 0).astype(BF16)
+    emb_ref[0] = jnp.zeros((128, 256), BF16)
+    emb_ref[33] = jnp.zeros((128, 256), BF16)
     ylo = ylo_ref[...].astype(F32)
     yhi = yhi_ref[...].astype(F32)
     for z in range(32):
@@ -76,22 +110,42 @@
         emb_ref[z + 1] = dot(f.astype(BF16), table, 1, 0).astype(BF16)
     chunk = 8
     for b in range(2):
-        runs = (2, 0, 1) if b == 0 else (0, 1, 3)
         for z0 in range(0, 32, chunk):
             acc = None
             for ty in range(3):
                 for tz in range(3):
-                    run = 32 * runs[ty]
+                    run = RUNS[b][ty]
                     rows = emb_ref[z0 + tz : z0 + tz + chunk, run : run + 32, :].reshape(32 * chunk, 256)
                     part = dot(rows, band_ref[3 * ty + tz], 1, 0)
                     acc = part if acc is None else acc + part
-            sigma = jax.nn.sigmoid(acc)
-            hid = (acc * sigma).astype(BF16).reshape(chunk, 32, 256)
-            slope = (sigma * (1.0 + acc * (1.0 - sigma))).reshape(chunk, 32, 256)
+            hid, slope = activate(acc)
+            if z0 == 0:
+                edge_ref[0, 32 * b : 32 * b + 32, :] = acc[:32]
+            if z0 == 32 - chunk:
+                edge_ref[1, 32 * b : 32 * b + 32, :] = acc[32 * chunk - 32 :]
             for k in range(chunk):
                 z2, c = (z0 + k) // 2, k % 2
-                hidden_ref[2 * b + c, 32 * z2 : 32 * z2 + 32, :] = hid[k]
-                slope_ref[2 * b + c, 32 * z2 : 32 * z2 + 32, :] = slope[k]
+                hidden_ref[2 * b + c, 32 * z2 : 32 * z2 + 32, :] = hid[32 * k : 32 * k + 32]
+                slope_ref[2 * b + c, 32 * z2 : 32 * z2 + 32, :] = slope[32 * k : 32 * k + 32]
+
+
+def outer_kernel(
+    zlo_ref, zhi_ref, table_ref, band_ref, dband_ref, edge_ref, inner_ref,
+    emb_ref, slope_ref, hidden_ref, coarse_ref, turn_a, turn_b,
+):
+    table = table_ref[...]
+    hidden_ref[...] = inner_ref[...]
+    for side, face in enumerate((zlo_ref, zhi_ref)):
+        plane = dot(face[...], table, 1, 0).astype(BF16)
+        emb_ref[side] = plane
+        for b in range(2):
+            acc = edge_ref[side, 32 * b : 32 * b + 32, :]
+            for ty in range(3):
+                run = RUNS[b][ty]
+                acc = acc + dot(plane[run : run + 32], band_ref[3 * ty + 2 * side], 1, 0)
+            hid, slope = activate(acc)
+            hidden_ref[2 * b + side, 480 * side : 480 * side + 32, :] = hid
+            slope_ref[side, 32 * b : 32 * b + 32, :] = slope
     for x2 in range(8):
         at = slice(64 * x2, 64 * x2 + 64)
         acc = None
@@ -137,9 +191,10 @@
 
 
 def backward_kernel(
-    down_scale, conv_scale, cgrad_ref, emb_ref, slope_ref, hidden_ref, dband_ref,
-    out_ref, turn_a, turn_b, turned_pg,
+    down_scale, conv_scale, cgrad_ref, emb_ref, slope_hbm, hidden_hbm, dband_hbm, face_ref, edge_ref,
+    out_ref, turn_a, turn_b, turned_pg, hidden_ref, dband_ref, slope_ref, sem,
 ):
+    copies = fetch((hidden_hbm, dband_hbm, slope_hbm), (hidden_ref, dband_ref, slope_ref), sem)
     for half in range(2):
         turn_b[half] = cgrad_ref[:, 128 * half : 128 * half + 128].astype(F32)
     for half in range(2):
@@ -155,6 +210,7 @@
     lane = iota((64, 256), 1)
     low = iota((64, 128), 1)
     down = jnp.zeros((64, 128), F32)
+    copies[0].wait()
     for bc in range(4):
         total = jnp.zeros((64, 256), F32)
         for x2 in range(8):
@@ -162,21 +218,31 @@
             total = jnp.where(lane // 32 == x2, part, total)
         down = jnp.where(low // 32 == bc, fold(total, 32), down)
     out_ref[0:64, :] = down * down_scale
+    copies[1].wait()
+    copies[2].wait()
     for bc in range(4):
         hgrad = dot(cg, dband_ref[bc], 1, 0)
-        pgrad = (hgrad * slope_ref[bc]).astype(BF16)
+        edge = edge_ref[bc % 2, 32 * (bc // 2) : 32 * (bc // 2) + 32, :]
+        if bc % 2 == 0:
+            slope = jnp.concatenate([edge, slope_ref[bc, 32:, :]], axis=0)
+        else:
+            slope = jnp.concatenate([slope_ref[bc, :480, :], edge], axis=0)
+        pgrad = (hgrad * slope).astype(BF16)
         turned_pg[bc] = pgrad.T
     lane_x = iota((16, 256), 1) // 16
-    group = iota((16, 128), 1) // 16
-    blocks = [jnp.zeros((16, 128), F32) for _ in range(4)]
+    own = iota((8, 128), 1) // 16 == iota((8, 128), 0)
     for ty in range(3):
         for tz in range(3):
             acc = None
             for bc in range(4):
                 b, c = bc // 2, bc % 2
-                run = 32 * ((2, 0, 1) if b == 0 else (0, 1, 3))[ty]
+                run = RUNS[b][ty]
                 q, p = (c + tz) // 2, (c + tz) % 2
                 rows = emb_ref[q : q + 16, p, run : run + 32, :].reshape(512, 256)
+                if c + tz == 0:
+                    rows = jnp.concatenate([face_ref[0, run : run + 32, :], rows[32:]], axis=0)
+                if c + tz == 3:
+                    rows = jnp.concatenate([rows[:480], face_ref[1, run : run + 32, :]], axis=0)
                 part = dot(turned_pg[bc], rows, 1, 0)
                 acc = part if acc is None else acc + part
             for tx in range(3):
@@ -185,9 +251,29 @@
                     if 0 <= x + tx - 1 < 16:
                         total = jnp.where(lane_x == x + tx - 1, acc[16 * x : 16 * x + 16, :], total)
                 tap = 9 * tx + 3 * ty + tz
-                blocks[tap // 8] = jnp.where(group == tap % 8, fold(total, 16), blocks[tap // 8])
-    for k in range(4):
-        out_ref[64 + 16 * k : 80 + 16 * k, :] = blocks[k] * conv_scale
+                total = fold(total, 16) * conv_scale
+                for half in range(2):
+                    part = jnp.where(own, total[8 * half : 8 * half + 8], 0.0)
+                    line = 64 + 32 * half + tap
+                    out_ref[line : line + 1, :] = jnp.sum(part, axis=0, keepdims=True)
+    for half in range(2):
+        out_ref[91 + 32 * half : 96 + 32 * half, :] = jnp.zeros((5, 128), F32)
+
+
+def finish_kernel(a_ref, b_ref, c_ref, d_ref, down_ref, conv_ref):
+    total = (a_ref[...] + b_ref[...]) + (c_ref[...] + d_ref[...])
+    down = total[:64].T
+    for a in range(2):
+        for bc in range(4):
+            at = (2 * bc + a) * 16
+            down_ref[4 * a + bc] = down[at : at + 16, :]
+    for half in range(2):
+        conv = total[64 + 32 * half : 96 + 32 * half].T
+        conv_ref[128 * half : 128 * half + 128, :] = conv[:, :27]
+
+
+def kept(*values):
+    return [pltpu.with_memory_space_constraint(v, pltpu.HBM) for v in values]
 
 
 def params(mib):
@@ -202,14 +288,17 @@
     return jax.ShapeDtypeStruct(dims, dtype)
 
 
-def sum_everywhere(value, axes):
-    for axis in axes:
-        size = lax.axis_size(axis)
-        step = 1
-        while step < size:
-            value = value + lax.ppermute(value, axis, [(i, i ^ step) for i in range(size)])
-            step *= 2
-    return value
+def sum_rounds(count_y, count_z):
+    in_z = [1 << k for k in range(count_z.bit_length() - 1)]
+    in_y = [count_z << k for k in range(count_y.bit_length() - 1)]
+    order = in_z[:1] + in_z[1:2] + in_y[:1] + in_z[2:] + in_y[1:]
+    rounds, order = ([order[:1]] if len(order) % 2 else []), order[len(order) % 2 :]
+    return rounds + [order[k : k + 2] for k in range(0, len(order), 2)]
+
+
+def exchanged(value, masks, count):
+    masks = list(masks) + [masks[0] ^ masks[1]] if len(masks) == 2 else masks
+    return [lax.ppermute(value, ("sy", "sz"), [(i, i ^ m) for i in range(count)]) for m in masks]
 
 
 def per_device(
@@ -219,20 +308,51 @@
     count_z = lax.axis_size("sz")
     mine = 64 // count_z
     width = mix_weight.shape[1]
-    features = pl.pallas_call(
+    features, first, last = pl.pallas_call(
         feature_kernel,
-        out_shape=shape((32, 128, 80), BF16),
-        in_specs=[VMEM] * 2,
-        out_specs=VMEM,
-        scratch_shapes=[pltpu.VMEM((16, 32, 64), jnp.int32), pltpu.VMEM((16, 32, 64), F32)],
-        compiler_params=params(16),
+        out_shape=(shape((32, 128, 80), BF16), shape((32, 80), BF16), shape((32, 80), BF16)),
+        in_specs=[HBM] * 2,
+        out_specs=(VMEM,) * 3,
+        scratch_shapes=[
+            pltpu.VMEM((16, 32, 64), jnp.int32),
+            pltpu.VMEM((16, 32, 64), BF16),
+            pltpu.VMEM((16, 32, 64), F32),
+            pltpu.VMEM((32, 80), F32),
+            pltpu.VMEM((32, 80), F32),
+            pltpu.SemaphoreType.DMA((2,)),
+        ],
+        compiler_params=params(8),
         cost_estimate=cost(32 * 128 * 64 * 80 * 2, 2 << 20),
         name="features",
-    )(jnp.transpose(labels, (0, 2, 1)), jnp.transpose(wall_dist, (0, 2, 1)))
+    )(*kept(jnp.transpose(labels, (0, 2, 1)), jnp.transpose(wall_dist, (0, 2, 1))))
     up_y = [(i, i + 1) for i in range(count_y - 1)]
     up_z = [(i, i + 1) for i in range(count_z - 1)]
-    ylo = lax.ppermute(features[:, 63, :], "sy", up_y)
-    yhi = lax.ppermute(features[:, 0, :], "sy", [(j, i) for i, j in up_y])
+    ylo = lax.ppermute(last, "sy", up_y)
+    yhi = lax.ppermute(first, "sy", [(j, i) for i, j in up_y])
+    band, dband, table = pl.pallas_call(
+        weight_kernel,
+        out_shape=(shape((9, 256, 256), BF16), shape((4, 512, 256), BF16), shape((80, 256), BF16)),
+        in_specs=[HBM] * 4,
+        out_specs=(VMEM,) * 3,
+        scratch_shapes=[
+            pltpu.VMEM((16, 16, 27), BF16),
+            pltpu.VMEM((8, 16, 64), BF16),
+            pltpu.VMEM((4, 16), BF16),
+            pltpu.VMEM((1, 16), BF16),
+            pltpu.SemaphoreType.DMA((4,)),
+        ],
+        compiler_params=params(8),
+        cost_estimate=cost(27 * 256 * 16 * 256 * 2, 3 << 20),
+        name="weights",
+    )(
+        *kept(
+            jnp.transpose(conv_weight, (1, 2, 0)),
+            jnp.transpose(down_weight, (0, 2, 1)),
+            material_table,
+            dist_weight[None],
+        )
+    )
+    ylo, yhi, band, dband, table = lax.optimization_barrier((ylo, yhi, band, dband, table))
 
     def whole(z):
         row = lax.broadcasted_iota(jnp.int32, (128, 80), 0)
@@ -241,34 +361,35 @@
 
     zlo = lax.ppermute(whole(31), "sz", up_z)
     zhi = lax.ppermute(whole(0), "sz", [(j, i) for i, j in up_z])
-
-    flat_conv = jnp.transpose(conv_weight, (2, 0, 1)).reshape(16, 432)
-    rows = jnp.concatenate([material_table, dist_weight[None], jnp.zeros((3, 16), BF16)], axis=0)
-    band, dband, table = pl.pallas_call(
-        weight_kernel,
-        out_shape=(shape((9, 256, 256), BF16), shape((4, 512, 256), BF16), shape((80, 256), BF16)),
-        in_specs=[VMEM] * 3,
-        out_specs=(VMEM,) * 3,
-        compiler_params=params(16),
-        cost_estimate=cost(27 * 256 * 16 * 256 * 2, 3 << 20),
-        name="weights",
-    )(flat_conv, jnp.transpose(down_weight, (0, 2, 1)), rows)
-
-    embedded, slope, hidden, coarse = pl.pallas_call(
-        forward_kernel,
+    embedded, slope, hidden, edge = pl.pallas_call(
+        inner_kernel,
         out_shape=(
             shape((34, 128, 256), BF16),
             shape((4, 512, 256), F32),
             shape((4, 512, 256), BF16),
+            shape((2, 64, 256), F32),
+        ),
+        in_specs=[VMEM] * 5,
+        out_specs=(VMEM,) * 4,
+        compiler_params=params(8),
+        cost_estimate=cost(3 << 30, 10 << 20),
+        name="inner",
+    )(features, ylo, yhi, table, band)
+    faces, edge_slope, hidden, coarse = pl.pallas_call(
+        outer_kernel,
+        out_shape=(
+            shape((2, 128, 256), BF16),
+            shape((2, 64, 256), F32),
+            shape((4, 512, 256), BF16),
             shape((1024, 256), BF16),
         ),
-        in_specs=[VMEM] * 8,
+        in_specs=[VMEM] * 7,
         out_specs=(VMEM,) * 4,
         scratch_shapes=[pltpu.VMEM((512, 512), F32), pltpu.VMEM((2, 1024, 128), F32)],
-        compiler_params=params(32),
-        cost_estimate=cost(3 << 30, 10 << 20),
-        name="forward",
-    )(features, zlo, zhi, ylo, yhi, table, band, dband)
+        compiler_params=params(8),
+        cost_estimate=cost(1 << 30, 4 << 20),
+        name="outer",
+    )(zlo, zhi, table, band, dband, edge, hidden)
 
     sent = lax.all_to_all(
         coarse.reshape(count_z, mine * 16, 256), "sz", split_axis=0, concat_axis=0, tiled=True
@@ -292,7 +413,7 @@
             block(1, width, width),
             pl.BlockSpec((count_z, 16, 256), lambda c: (0, c, 0)),
         ),
-        compiler_params=params(16),
+        compiler_params=params(12),
         cost_estimate=cost(mine * 3 * 2 * 256 * width * width, 5 << 20),
         name="mix",
     )(sent, mix_weight, cotangent.reshape(mine, 256, width))
@@ -305,20 +426,36 @@
             1.0 / math.sqrt(cells // 8), 1.0 / math.sqrt(cells), *refs
         ),
         out_shape=shape((128, 128), F32),
-        in_specs=[VMEM] * 5,
+        in_specs=[VMEM, VMEM, HBM, HBM, HBM, VMEM, VMEM],
         out_specs=VMEM,
         scratch_shapes=[
             pltpu.VMEM((512, 512), F32),
             pltpu.VMEM((2, 1024, 128), F32),
             pltpu.VMEM((4, 256, 512), BF16),
+            pltpu.VMEM((4, 512, 256), BF16),
+            pltpu.VMEM((4, 512, 256), BF16),
+            pltpu.VMEM((4, 512, 256), F32),
+            pltpu.SemaphoreType.DMA((3,)),
         ],
-        compiler_params=params(32),
+        compiler_params=params(16),
         cost_estimate=cost(4 << 30, 8 << 20),
         name="backward",
-    )(coarse_grad.reshape(1024, 256), embedded.reshape(17, 2, 128, 256), slope, hidden, dband)
-    sums = sum_everywhere(sums, ("sz", "sy"))
-    down_grad = jnp.transpose(sums[:64].reshape(64, 4, 2, 16), (2, 1, 0, 3)).reshape(8, 64, 16)
-    conv_grad = jnp.transpose(sums[64:].reshape(4, 16, 8, 16), (0, 2, 1, 3)).reshape(32, 16, 16)[:27]
+    )(coarse_grad.reshape(1024, 256), embedded.reshape(17, 2, 128, 256), *kept(slope, hidden, dband), faces, edge_slope)
+    rounds = sum_rounds(count_y, count_z)
+    for masks in rounds[:-1]:
+        parts = [sums] + exchanged(sums, masks, count_y * count_z)
+        sums = parts[0] + parts[1] if len(parts) == 2 else (parts[0] + parts[1]) + (parts[2] + parts[3])
+    down_grad, conv_grad = pl.pallas_call(
+        finish_kernel,
+        out_shape=(shape((8, 16, 64), F32), shape((256, 27), F32)),
+        in_specs=[VMEM] * 4,
+        out_specs=(VMEM,) * 2,
+        compiler_params=params(8),
+        cost_estimate=cost(1 << 20, 1 << 18),
+        name="finish",
+    )(sums, *exchanged(sums, rounds[-1], count_y * count_z))
+    down_grad = jnp.transpose(down_grad, (0, 2, 1))
+    conv_grad = jnp.transpose(conv_grad.reshape(16, 16, 27), (2, 0, 1))
     return (mid.reshape(cotangent.shape), mix_grad, down_grad, conv_grad)
 
 

time: 136 us -> 122 us (0.90)
  local copies, waits for them, and re-layouts: 10.8 us -> 0.98 us
  waiting for transfers between devices: 25.5 us -> 17.2 us
  Pallas kernels: 18.4 us -> 23.9 us
    ppermute x9 -> x12, waiting for transfers between devices: 25.5 us -> 17.2 us  [the longest x10 15.5 us: exchanged(): lax.ppermute(value, ('sy', 'sz'), [(i, i ^ m) for i in range(count)])]
    unnamed x25 -> x10, local copies, waits for them, and re-layouts: 8.51 us -> 0.98 us
    pallas_call x2 -> x4, Pallas kernels: 8.55 us -> 11.1 us  [the longest x1 3.51 us: per_device(): pl.pallas_call(feature_kernel, out_shape=(shape((32, 128, 80), BF16), sha...]
    pallas_call x1, Pallas kernels: 5.39 us -> 7.23 us  [per_device(): pl.pallas_call(lambda *refs: backward_kernel(1.0 / math.sqrt(cells // 8),...]
    transpose x2 -> x0, local copies, waits for them, and re-layouts: 1.67 us -> none  [the longest x1 1.03 us: per_device(): flat_conv = jnp.transpose(conv_weight, (2, 0, 1)).reshape(16, 432)]
    ppermute x9 -> x12, starting transfers between devices: 19.6 us -> 20.7 us  [the longest x10 15.8 us: exchanged(): lax.ppermute(value, ('sy', 'sz'), [(i, i ^ m) for i in range(count)])]
  transfers between devices with their start and end apart: 12 -> 15, of which waited for: 8 -> 8; matrix products, arithmetic and copies ran while one was open for 3% -> 0% of each run, Pallas kernels for 5% -> 11%
where the time goes in v2:
time: 122 us; the launch traced here: 121 us
  blocking collectives  39.9 us (33%)
  starting transfers between devices  25 us (20%)
  Pallas kernels  23.9 us (20%)
  waiting for transfers between devices  17.2 us (14%)
  between operations  14.2 us (12%)
    all_to_all x1, blocking collectives, per_device(): lax.all_to_all(coarse.reshape(count_z, mine * 16, 256), 'sz', split_axis=...  21.4 us
    all_to_all x1, blocking collectives, per_device(): lax.all_to_all(back, 'sz', split_axis=0, concat_axis=0, tiled=True)  18.5 us
    ppermute x10, starting transfers between devices, exchanged(): lax.ppermute(value, ('sy', 'sz'), [(i, i ^ m) for i in range(count)])  15.8 us
    ppermute x10, waiting for transfers between devices, exchanged(): lax.ppermute(value, ('sy', 'sz'), [(i, i ^ m) for i in range(count)])  15.5 us
    pallas_call x1, Pallas kernels, per_device(): pl.pallas_call(lambda *refs: backward_kernel(1.0 / math.sqrt(cells // 8),...  7.23 us
    ppermute x1, starting transfers between devices, per_device(): ylo = lax.ppermute(last, 'sy', up_y)  3.56 us
    pallas_call x1, Pallas kernels, per_device(): pl.pallas_call(feature_kernel, out_shape=(shape((32, 128, 80), BF16), sha...  3.51 us
    pallas_call x1, Pallas kernels, per_device(): pl.pallas_call(outer_kernel, out_shape=(shape((2, 128, 256), BF16), shape...  3.46 us
  transfers between devices with their start and end apart: 15, of which 8 were waited for; matrix products, arithmetic and copies ran while one was open for 0% of the time, Pallas kernels for 11%

profile of v2, /device:TPU:0, one launch (start us, length us, event | category | flops | bytes accessed | tf_op | source)
XLA Modules:
  0.0 121.3 jit_solution(14258384191315144548)
XLA Ops:
  7.2 0.0 reduce-scatter.2.cloned.1.call-start
  7.2 3.5 %features.1 = (bf16[32,128,80]{2,1,0:T(8,128)(2,1)S(1)}, bf16[32,80]{1,0:T(8,128)(2,1)S(1)}, bf16[32,80]{1,0:T(8,128)(2,1)S(1)}) custom-call(s32[16,32,64]{2,1,0:T(8,128)} %bitcast.34, bf16[16,32,64]{2,1,0:T(8,128)(2,1)} %bitcast.35), custom_call_target="tpu_custom_call" | custom-call | flops 41943040 | bytes 2097152 | tf_op jit(solution)/shard_map/features/pallas_call | solution.py:311
  10.7 3.6 %collective-permute-start = (bf16[32,80]{1,0:T(8,128)(2,1)S(1)}, bf16[32,80]{1,0:T(8,128)(2,1)S(1)}, u32[]{:S(2)}, u32[]{:S(2)}) collective-permute-start(bf16[32,80]{1,0:T(8,128)(2,1)S(1)} %get-tuple-element.28), channel_id=1, source_target_pairs={{0,16},{16,32},{32,48},{48,64},{64,80},{80,96},{96,112},{1,17},{17... | collective-permute-start | bytes 15368 | tf_op jit(solution)/shard_map/ppermute | solution.py:330
  14.3 1.3 %collective-permute-start.1 = (bf16[32,80]{1,0:T(8,128)(2,1)S(1)}, bf16[32,80]{1,0:T(8,128)(2,1)S(1)}, u32[]{:S(2)}, u32[]{:S(2)}) collective-permute-start(bf16[32,80]{1,0:T(8,128)(2,1)S(1)} %get-tuple-element.29), channel_id=1, source_target_pairs={{16,0},{32,16},{48,32},{64,48},{80,64},{96,80},{112,96},{17,1},{33... | collective-permute-start | bytes 15368 | tf_op jit(solution)/shard_map/ppermute | solution.py:331
  15.6 2.5 %weights.1 = (bf16[9,256,256]{2,1,0:T(8,128)(2,1)S(1)}, bf16[4,512,256]{2,1,0:T(8,128)(2,1)S(1)}, bf16[80,256]{1,0:T(8,128)(2,1)S(1)}) custom-call(bf16[16,16,27]{2,1,0:T(8,128)(2,1)} %bitcast.38, bf16[8,16,64]{2,1,0:T(8,128)(2,1)} %bitcast.40, bf16[4,16]{1,0:T(4,128)(2,1)} %mat_hbm.1, bf16[1,16]{1,0:T(2,128)(2,1)} %bitcast.41), custom_call_target="tpu_custom_call" | custom-call | flops 56623104 | bytes 3145728 | tf_op jit(solution)/shard_map/weights/pallas_call | solution.py:332
  18.1 0.0 copy-start.2
  18.1 0.0 collective-permute-done.ylo_ref
  18.1 1.7 %collective-permute-done.1.yhi_ref = bf16[32,80]{1,0:T(8,128)(2,1)S(1)} collective-permute-done((bf16[32,80]{1,0:T(8,128)(2,1)S(1)}, bf16[32,80]{1,0:T(8,128)(2,1)S(1)}, u32[]{:S(2)}, u32[]{:S(2)}) %collective-permute-start.1) | collective-permute-done | bytes 5152 | tf_op jit(solution)/shard_map/ppermute | solution.py:331
  19.8 0.1 fusion
  20.0 1.3 %collective-permute-start.3 = (bf16[128,80]{1,0:T(8,128)(2,1)S(1)}, bf16[128,80]{1,0:T(8,128)(2,1)S(1)}, u32[]{:S(2)}, u32[]{:S(2)}) collective-permute-start(bf16[128,80]{1,0:T(8,128)(2,1)S(1)} %get-tuple-element.52), channel_id=1, source_target_pairs={{1,0},{2,1},{3,2},{4,3},{5,4},{6,5},{7,6},{8,7},{9,8},{10,9},{11,1... | collective-permute-start | bytes 61448 | tf_op jit(solution)/shard_map/ppermute | solution.py:363
  21.3 3.0 %collective-permute-start.2 = (bf16[128,80]{1,0:T(8,128)(2,1)S(1)}, bf16[128,80]{1,0:T(8,128)(2,1)S(1)}, u32[]{:S(2)}, u32[]{:S(2)}) collective-permute-start(bf16[128,80]{1,0:T(8,128)(2,1)S(1)} %get-tuple-element.53), channel_id=1, source_target_pairs={{0,1},{1,2},{2,3},{3,4},{4,5},{5,6},{6,7},{7,8},{8,9},{9,10},{10,1... | collective-permute-start | bytes 61448 | tf_op jit(solution)/shard_map/ppermute | solution.py:362
  24.3 3.4 %inner.1 = (bf16[34,128,256]{2,1,0:T(8,128)(2,1)S(1)}, f32[4,512,256]{2,1,0:T(8,128)S(1)}, bf16[4,512,256]{2,1,0:T(8,128)(2,1)S(1)}, f32[2,64,256]{2,1,0:T(8,128)S(1)}) custom-call(bf16[32,128,80]{2,1,0:T(8,128)(2,1)S(1)} %get-tuple-element.35.feat_ref, bf16[32,80]{1,0:T(8,128)(2,1)S(1)} %collective-permute-done.ylo_ref, ...), custom_call_target="tpu_custom_call" | custom-call | flops 3221225472 | bytes 10485760 | tf_op jit(solution)/shard_map/inner/pallas_call | solution.py:364
  27.7 0.0 copy-start.4
  27.7 0.0 collective-permute-done.3.zhi_ref
  27.7 0.0 collective-permute-done.2.zlo_ref
  27.7 0.0 copy-done.2
  27.7 0.0 copy-start
  27.7 0.0 copy-start.1
  27.7 3.5 %outer.1 = (bf16[2,128,256]{2,1,0:T(8,128)(2,1)S(1)}, f32[2,64,256]{2,1,0:T(8,128)S(1)}, bf16[4,512,256]{2,1,0:T(8,128)(2,1)S(1)}, bf16[1024,256]{1,0:T(8,128)(2,1)S(1)}) custom-call(bf16[128,80]{1,0:T(8,128)(2,1)S(1)} %collective-permute-done.2.zlo_ref, bf16[128,80]{1,0:T(8,128)(2,1)S(1)} %collective-permute-done.3.zhi_ref, ...), custom_call_target="tpu_custom_call" | custom-call | flops 1073741824 | bytes 4194304 | tf_op jit(solution)/shard_map/outer/pallas_call | solution.py:378
  31.2 0.0 copy-start.3
  31.2 1.0 copy-done.3
  32.2 21.4 %all_to_all.10.refs_0_ = bf16[16,64,256]{2,1,0:T(8,128)(2,1)S(1)} all-to-all(bf16[16,64,256]{2,1,0:T(8,128)(2,1)S(1)} %bitcast.31), channel_id=1, replica_groups=mesh['sy'=8,'sz'=16] {'sz'}, dimensions={0} | all-to-all | bytes 1048576 | tf_op jit(solution)/shard_map/all_to_all | solution.py:394
  53.6 0.0 copy-done.4
  53.6 0.0 copy-done
  53.6 0.0 copy-done.1
  53.6 3.1 %mix.1 = (bf16[4,256,256]{2,1,0:T(8,128)(2,1)}, f32[4,256,256]{2,1,0:T(8,128)}, bf16[16,64,256]{2,1,0:T(8,128)(2,1)S(1)}) custom-call(bf16[16,64,256]{2,1,0:T(8,128)(2,1)S(1)} %all_to_all.10.refs_0_, bf16[4,256,256]{2,1,0:T(8,128)(2,1)S(1)} %copy-done, bf16[4,256,256]{2,1,0:T(8,128)(2,1)S(1)} %bitcast.30), custom_call_target="tpu_custom_call" | custom-call | flops 402653184 | bytes 5242880 | tf_op jit(solution)/shard_map/mix/pallas_call | solution.py:398
  56.6 0.0 reduce-scatter.2.cloned.1.call-update
  56.7 18.5 %all_to_all.11 = bf16[16,64,256]{2,1,0:T(8,128)(2,1)S(1)} all-to-all(bf16[16,64,256]{2,1,0:T(8,128)(2,1)S(1)} %get-tuple-element.44), channel_id=1, replica_groups=mesh['sy'=8,'sz'=16] {'sz'}, dimensions={0} | all-to-all | bytes 1048576 | tf_op jit(solution)/shard_map/all_to_all | solution.py:420
  75.1 7.2 %backward.1 = f32[128,128]{1,0:T(8,128)S(1)} custom-call(bf16[1024,256]{1,0:T(8,128)(2,1)S(1)} %bitcast.32, bf16[17,2,128,256]{3,2,1,0:T(8,128)(2,1)S(1)} %bitcast.33, f32[4,512,256]{2,1,0:T(8,128)} %copy-done.4, bf16[4,512,256]{2,1,0:T(8,128)(2,1)} %copy-done.3, bf16[4,512,256]{2,1,0:T(8,128)(2,1)} %copy-done.2, ...), custom_call_target="tpu_custom_call" | custom-call | flops 4294967296 | bytes 8388608 | tf_op jit(solution)/shard_map/backward/pallas_call | solution.py:424
  82.4 0.1 collective-permute-start.4
  82.4 1.2 %collective-permute-done.4 = f32[128,128]{1,0:T(8,128)S(1)} collective-permute-done((f32[128,128]{1,0:T(8,128)S(1)}, f32[128,128]{1,0:T(8,128)S(1)}, u32[]{:S(2)}, u32[]{:S(2)}) %collective-permute-start.4) | collective-permute-done | bytes 65568 | tf_op jit(solution)/shard_map/ppermute | solution.py:301
  83.7 1.5 %collective-permute-start.7 = (f32[128,128]{1,0:T(8,128)S(1)}, f32[128,128]{1,0:T(8,128)S(1)}, u32[]{:S(2)}, u32[]{:S(2)}) collective-permute-start(f32[128,128]{1,0:T(8,128)S(1)} %add.23), channel_id=1, source_target_pairs={{0,18},{1,19},{2,16},{3,17},{4,22},{5,23},{6,20},{7,21},{8,26},{9,... | collective-permute-start | bytes 196616 | tf_op jit(solution)/shard_map/ppermute | solution.py:301
  85.2 3.9 %collective-permute-start.6 = (f32[128,128]{1,0:T(8,128)S(1)}, f32[128,128]{1,0:T(8,128)S(1)}, u32[]{:S(2)}, u32[]{:S(2)}) collective-permute-start(f32[128,128]{1,0:T(8,128)S(1)} %add.23), channel_id=1, source_target_pairs={{0,16},{1,17},{2,18},{3,19},{4,20},{5,21},{6,22},{7,23},{8,24},{9,... | collective-permute-start | bytes 196616 | tf_op jit(solution)/shard_map/ppermute | solution.py:301
  89.1 2.0 %collective-permute-start.5 = (f32[128,128]{1,0:T(8,128)S(1)}, f32[128,128]{1,0:T(8,128)S(1)}, u32[]{:S(2)}, u32[]{:S(2)}) collective-permute-start(f32[128,128]{1,0:T(8,128)S(1)} %add.23), channel_id=1, source_target_pairs={{0,2},{1,3},{2,0},{3,1},{4,6},{5,7},{6,4},{7,5},{8,10},{9,11},{10,... | collective-permute-start | bytes 196616 | tf_op jit(solution)/shard_map/ppermute | solution.py:301
  91.1 0.0 collective-permute-done.7
  91.1 1.4 %collective-permute-done.6 = f32[128,128]{1,0:T(8,128)S(1)} collective-permute-done((f32[128,128]{1,0:T(8,128)S(1)}, f32[128,128]{1,0:T(8,128)S(1)}, u32[]{:S(2)}, u32[]{:S(2)}) %collective-permute-start.6) | collective-permute-done | bytes 65568 | tf_op jit(solution)/shard_map/ppermute | solution.py:301
  92.5 3.9 %collective-permute-done.5 = f32[128,128]{1,0:T(8,128)S(1)} collective-permute-done((f32[128,128]{1,0:T(8,128)S(1)}, f32[128,128]{1,0:T(8,128)S(1)}, u32[]{:S(2)}, u32[]{:S(2)}) %collective-permute-start.5) | collective-permute-done | bytes 65568 | tf_op jit(solution)/shard_map/ppermute | solution.py:301
  96.4 2.5 %collective-permute-start.10 = (f32[128,128]{1,0:T(8,128)S(1)}, f32[128,128]{1,0:T(8,128)S(1)}, u32[]{:S(2)}, u32[]{:S(2)}) collective-permute-start(f32[128,128]{1,0:T(8,128)S(1)} %add_add_fusion.1), channel_id=1, source_target_pairs={{0,12},{1,13},{2,14},{3,15},{4,8},{5,9},{6,10},{7,11},{8,4},{9,5},... | collective-permute-start | bytes 196616 | tf_op jit(solution)/shard_map/ppermute | solution.py:301
  99.0 0.9 collective-permute-start.9
  99.9 0.7 collective-permute-start.8
  100.6 1.4 %collective-permute-done.10 = f32[128,128]{1,0:T(8,128)S(1)} collective-permute-done((f32[128,128]{1,0:T(8,128)S(1)}, f32[128,128]{1,0:T(8,128)S(1)}, u32[]{:S(2)}, u32[]{:S(2)}) %collective-permute-start.10) | collective-permute-done | bytes 65568 | tf_op jit(solution)/shard_map/ppermute | solution.py:301
  102.0 2.8 %collective-permute-done.9 = f32[128,128]{1,0:T(8,128)S(1)} collective-permute-done((f32[128,128]{1,0:T(8,128)S(1)}, f32[128,128]{1,0:T(8,128)S(1)}, u32[]{:S(2)}, u32[]{:S(2)}) %collective-permute-start.9) | collective-permute-done | bytes 65568 | tf_op jit(solution)/shard_map/ppermute | solution.py:301
  104.8 0.0 collective-permute-done.8
  104.8 3.1 %collective-permute-start.13 = (f32[128,128]{1,0:T(8,128)S(1)}, f32[128,128]{1,0:T(8,128)S(1)}, u32[]{:S(2)}, u32[]{:S(2)}) collective-permute-start(f32[128,128]{1,0:T(8,128)S(1)} %add_add_fusion.a_ref), channel_id=1, source_target_pairs={{0,96},{1,97},{2,98},{3,99},{4,100},{5,101},{6,102},{7,103},{8,104... | collective-permute-start | bytes 196616 | tf_op jit(solution)/shard_map/ppermute | solution.py:301
  107.9 0.2 collective-permute-start.12
  108.1 0.9 collective-permute-start.11
  109.0 2.1 %collective-permute-done.13.d_ref = f32[128,128]{1,0:T(8,128)S(1)} collective-permute-done((f32[128,128]{1,0:T(8,128)S(1)}, f32[128,128]{1,0:T(8,128)S(1)}, u32[]{:S(2)}, u32[]{:S(2)}) %collective-permute-start.13) | collective-permute-done | bytes 65568 | tf_op jit(solution)/shard_map/ppermute | solution.py:301
  111.1 2.6 %collective-permute-done.12.c_ref = f32[128,128]{1,0:T(8,128)S(1)} collective-permute-done((f32[128,128]{1,0:T(8,128)S(1)}, f32[128,128]{1,0:T(8,128)S(1)}, u32[]{:S(2)}, u32[]{:S(2)}) %collective-permute-start.12) | collective-permute-done | bytes 65568 | tf_op jit(solution)/shard_map/ppermute | solution.py:301
  113.7 0.0 collective-permute-done.11.b_ref
  113.7 0.8 finish.1
  114.5 0.0 reduce-scatter.2.cloned.1.call-done
  (5 shorter events, 0.1 us)
Async XLA Ops:
  7.2 107.3 %reduce-scatter.2.cloned.1.call-start = ((), (), s32[]{:S(2)}) async-start(), calls=%async_computation.3 | async-start | bytes 1179648 | tf_op jit(solution)/shard_map/reduce_scatter | solution.py:421
  10.7 7.4 %collective-permute-start = (bf16[32,80]{1,0:T(8,128)(2,1)S(1)}, bf16[32,80]{1,0:T(8,128)(2,1)S(1)}, u32[]{:S(2)}, u32[]{:S(2)}) collective-permute-start(bf16[32,80]{1,0:T(8,128)(2,1)S(1)} %get-tuple-element.28), channel_id=1, source_target_pairs={{0,16},{16,32},{32,48},{48,64},{64,80},{80,96},{96,112},{1,17},{17... | collective-permute-start | bytes 15368 | tf_op jit(solution)/shard_map/ppermute | solution.py:330
  14.3 5.5 %collective-permute-start.1 = (bf16[32,80]{1,0:T(8,128)(2,1)S(1)}, bf16[32,80]{1,0:T(8,128)(2,1)S(1)}, u32[]{:S(2)}, u32[]{:S(2)}) collective-permute-start(bf16[32,80]{1,0:T(8,128)(2,1)S(1)} %get-tuple-element.29), channel_id=1, source_target_pairs={{16,0},{32,16},{48,32},{64,48},{80,64},{96,80},{112,96},{17,1},{33... | collective-permute-start | bytes 15368 | tf_op jit(solution)/shard_map/ppermute | solution.py:331
  18.1 9.6 %copy-start.2 = (bf16[4,512,256]{2,1,0:T(8,128)(2,1)}, bf16[4,512,256]{2,1,0:T(8,128)(2,1)S(1)}, u32[]{:S(2)}) copy-start(bf16[4,512,256]{2,1,0:T(8,128)(2,1)S(1)} %get-tuple-element.38.dband_ref.refs_4_) | copy-start | bytes 3145732
  20.0 7.7 %collective-permute-start.3 = (bf16[128,80]{1,0:T(8,128)(2,1)S(1)}, bf16[128,80]{1,0:T(8,128)(2,1)S(1)}, u32[]{:S(2)}, u32[]{:S(2)}) collective-permute-start(bf16[128,80]{1,0:T(8,128)(2,1)S(1)} %get-tuple-element.52), channel_id=1, source_target_pairs={{1,0},{2,1},{3,2},{4,3},{5,4},{6,5},{7,6},{8,7},{9,8},{10,9},{11,1... | collective-permute-start | bytes 61448 | tf_op jit(solution)/shard_map/ppermute | solution.py:363
  21.3 6.4 %collective-permute-start.2 = (bf16[128,80]{1,0:T(8,128)(2,1)S(1)}, bf16[128,80]{1,0:T(8,128)(2,1)S(1)}, u32[]{:S(2)}, u32[]{:S(2)}) collective-permute-start(bf16[128,80]{1,0:T(8,128)(2,1)S(1)} %get-tuple-element.53), channel_id=1, source_target_pairs={{0,1},{1,2},{2,3},{3,4},{4,5},{5,6},{6,7},{7,8},{8,9},{9,10},{10,1... | collective-permute-start | bytes 61448 | tf_op jit(solution)/shard_map/ppermute | solution.py:362
  27.7 25.9 %copy-start.4 = (f32[4,512,256]{2,1,0:T(8,128)}, f32[4,512,256]{2,1,0:T(8,128)S(1)}, u32[]{:S(2)}) copy-start(f32[4,512,256]{2,1,0:T(8,128)S(1)} %get-tuple-element.46.refs_2_) | copy-start | bytes 6291460
  27.7 25.9 %copy-start = (bf16[4,256,256]{2,1,0:T(8,128)(2,1)S(1)}, bf16[4,256,256]{2,1,0:T(8,128)(2,1)}, u32[]{:S(2)}) copy-start(bf16[4,256,256]{2,1,0:T(8,128)(2,1)} %refs_1_.1) | copy-start | bytes 1572868
  27.7 25.8 %copy-start.1 = (bf16[4,8,32,256]{3,2,1,0:T(8,128)(2,1)S(1)}, bf16[4,8,32,256]{3,2,1,0:T(8,128)(2,1)}, u32[]{:S(2)}) copy-start(bf16[4,8,32,256]{3,2,1,0:T(8,128)(2,1)} %param.15) | copy-start | bytes 1572868
  31.2 1.0 copy-start.3
  82.4 1.3 %collective-permute-start.4 = (f32[128,128]{1,0:T(8,128)S(1)}, f32[128,128]{1,0:T(8,128)S(1)}, u32[]{:S(2)}, u32[]{:S(2)}) collective-permute-start(f32[128,128]{1,0:T(8,128)S(1)} %backward.1), channel_id=1, source_target_pairs={{0,1},{1,0},{2,3},{3,2},{4,5},{5,4},{6,7},{7,6},{8,9},{9,8},{10,11... | collective-permute-start | bytes 196616 | tf_op jit(solution)/shard_map/ppermute | solution.py:301
  83.7 7.4 %collective-permute-start.7 = (f32[128,128]{1,0:T(8,128)S(1)}, f32[128,128]{1,0:T(8,128)S(1)}, u32[]{:S(2)}, u32[]{:S(2)}) collective-permute-start(f32[128,128]{1,0:T(8,128)S(1)} %add.23), channel_id=1, source_target_pairs={{0,18},{1,19},{2,16},{3,17},{4,22},{5,23},{6,20},{7,21},{8,26},{9,... | collective-permute-start | bytes 196616 | tf_op jit(solution)/shard_map/ppermute | solution.py:301
  85.2 7.3 %collective-permute-start.6 = (f32[128,128]{1,0:T(8,128)S(1)}, f32[128,128]{1,0:T(8,128)S(1)}, u32[]{:S(2)}, u32[]{:S(2)}) collective-permute-start(f32[128,128]{1,0:T(8,128)S(1)} %add.23), channel_id=1, source_target_pairs={{0,16},{1,17},{2,18},{3,19},{4,20},{5,21},{6,22},{7,23},{8,24},{9,... | collective-permute-start | bytes 196616 | tf_op jit(solution)/shard_map/ppermute | solution.py:301
  89.1 7.3 %collective-permute-start.5 = (f32[128,128]{1,0:T(8,128)S(1)}, f32[128,128]{1,0:T(8,128)S(1)}, u32[]{:S(2)}, u32[]{:S(2)}) collective-permute-start(f32[128,128]{1,0:T(8,128)S(1)} %add.23), channel_id=1, source_target_pairs={{0,2},{1,3},{2,0},{3,1},{4,6},{5,7},{6,4},{7,5},{8,10},{9,11},{10,... | collective-permute-start | bytes 196616 | tf_op jit(solution)/shard_map/ppermute | solution.py:301
  96.4 5.6 %collective-permute-start.10 = (f32[128,128]{1,0:T(8,128)S(1)}, f32[128,128]{1,0:T(8,128)S(1)}, u32[]{:S(2)}, u32[]{:S(2)}) collective-permute-start(f32[128,128]{1,0:T(8,128)S(1)} %add_add_fusion.1), channel_id=1, source_target_pairs={{0,12},{1,13},{2,14},{3,15},{4,8},{5,9},{6,10},{7,11},{8,4},{9,5},... | collective-permute-start | bytes 196616 | tf_op jit(solution)/shard_map/ppermute | solution.py:301
  99.0 5.8 %collective-permute-start.9 = (f32[128,128]{1,0:T(8,128)S(1)}, f32[128,128]{1,0:T(8,128)S(1)}, u32[]{:S(2)}, u32[]{:S(2)}) collective-permute-start(f32[128,128]{1,0:T(8,128)S(1)} %add_add_fusion.1), channel_id=1, source_target_pairs={{0,8},{1,9},{2,10},{3,11},{4,12},{5,13},{6,14},{7,15},{8,0},{9,1},... | collective-permute-start | bytes 196616 | tf_op jit(solution)/shard_map/ppermute | solution.py:301
  99.9 4.9 %collective-permute-start.8 = (f32[128,128]{1,0:T(8,128)S(1)}, f32[128,128]{1,0:T(8,128)S(1)}, u32[]{:S(2)}, u32[]{:S(2)}) collective-permute-start(f32[128,128]{1,0:T(8,128)S(1)} %add_add_fusion.1), channel_id=1, source_target_pairs={{0,4},{1,5},{2,6},{3,7},{4,0},{5,1},{6,2},{7,3},{8,12},{9,13},{10,... | collective-permute-start | bytes 196616 | tf_op jit(solution)/shard_map/ppermute | solution.py:301
  104.8 6.3 %collective-permute-start.13 = (f32[128,128]{1,0:T(8,128)S(1)}, f32[128,128]{1,0:T(8,128)S(1)}, u32[]{:S(2)}, u32[]{:S(2)}) collective-permute-start(f32[128,128]{1,0:T(8,128)S(1)} %add_add_fusion.a_ref), channel_id=1, source_target_pairs={{0,96},{1,97},{2,98},{3,99},{4,100},{5,101},{6,102},{7,103},{8,104... | collective-permute-start | bytes 196616 | tf_op jit(solution)/shard_map/ppermute | solution.py:301
  107.9 5.8 %collective-permute-start.12 = (f32[128,128]{1,0:T(8,128)S(1)}, f32[128,128]{1,0:T(8,128)S(1)}, u32[]{:S(2)}, u32[]{:S(2)}) collective-permute-start(f32[128,128]{1,0:T(8,128)S(1)} %add_add_fusion.a_ref), channel_id=1, source_target_pairs={{0,64},{1,65},{2,66},{3,67},{4,68},{5,69},{6,70},{7,71},{8,72},{9,... | collective-permute-start | bytes 196616 | tf_op jit(solution)/shard_map/ppermute | solution.py:301
  108.1 5.6 %collective-permute-start.11 = (f32[128,128]{1,0:T(8,128)S(1)}, f32[128,128]{1,0:T(8,128)S(1)}, u32[]{:S(2)}, u32[]{:S(2)}) collective-permute-start(f32[128,128]{1,0:T(8,128)S(1)} %add_add_fusion.a_ref), channel_id=1, source_target_pairs={{0,32},{1,33},{2,34},{3,35},{4,36},{5,37},{6,38},{7,39},{8,40},{9,... | collective-permute-start | bytes 196616 | tf_op jit(solution)/shard_map/ppermute | solution.py:301
Sparse Core Ops, SparseCore 0:
  56.8 39.2 reduce-scatter.1

commit v3 on v2

--- a/solution.py
+++ b/solution.py
@@ -95,7 +95,8 @@
 
 
 def inner_kernel(
-    feat_ref, ylo_ref, yhi_ref, table_ref, band_ref, emb_ref, slope_ref, hidden_ref, edge_ref
+    feat_ref, ylo_ref, yhi_ref, table_ref, band_ref, emb_hbm, slope_hbm, hidden_ref, edge_ref,
+    emb_ref, slope_ref, sem,
 ):
     table = table_ref[...]
     row = iota((128, 80), 0)
@@ -108,6 +109,8 @@
         f = jnp.where(row == 64, ylo[z : z + 1, :], f)
         f = jnp.where(row == 127, yhi[z : z + 1, :], f)
         emb_ref[z + 1] = dot(f.astype(BF16), table, 1, 0).astype(BF16)
+    copies = [pltpu.make_async_copy(emb_ref, emb_hbm, sem.at[0])]
+    copies[0].start()
     chunk = 8
     for b in range(2):
         for z0 in range(0, 32, chunk):
@@ -127,11 +130,16 @@
                 z2, c = (z0 + k) // 2, k % 2
                 hidden_ref[2 * b + c, 32 * z2 : 32 * z2 + 32, :] = hid[32 * k : 32 * k + 32]
                 slope_ref[2 * b + c, 32 * z2 : 32 * z2 + 32, :] = slope[32 * k : 32 * k + 32]
+            at = (pl.ds(2 * b, 2), pl.ds(16 * z0, 16 * chunk))
+            copies.append(pltpu.make_async_copy(slope_ref.at[at], slope_hbm.at[at], sem.at[len(copies)]))
+            copies[-1].start()
+    for copy in copies:
+        copy.wait()
 
 
 def outer_kernel(
     zlo_ref, zhi_ref, table_ref, band_ref, dband_ref, edge_ref, inner_ref,
-    emb_ref, slope_ref, hidden_ref, coarse_ref, turn_a, turn_b,
+    emb_ref, slope_ref, hidden_hbm, coarse_ref, turn_a, turn_b, hidden_ref, sem,
 ):
     table = table_ref[...]
     hidden_ref[...] = inner_ref[...]
@@ -146,6 +154,8 @@
             hid, slope = activate(acc)
             hidden_ref[2 * b + side, 480 * side : 480 * side + 32, :] = hid
             slope_ref[side, 32 * b : 32 * b + 32, :] = slope
+    copy = pltpu.make_async_copy(hidden_ref, hidden_hbm, sem)
+    copy.start()
     for x2 in range(8):
         at = slice(64 * x2, 64 * x2 + 64)
         acc = None
@@ -162,9 +172,11 @@
             turn_b[half, pl.ds(z2, 64, stride=16), :] = jnp.concatenate(pieces, axis=1)
     for half in range(2):
         coarse_ref[:, 128 * half : 128 * half + 128] = turn_b[half].astype(BF16)
-
-
-def mix_kernel(scale, coarse_ref, mix_ref, cot_ref, mid_ref, mixg_ref, grad_ref):
+    copy.wait()
+
+
+def mix_kernel(scale, me_ref, coarse_ref, mix_ref, cot_ref, mid_ref, grad_ref, *more_refs):
+    *share_refs, total_ref = more_refs
     width = mix_ref.shape[1]
     coarse = coarse_ref[...].reshape(width, 256)
     mix = mix_ref[0]
@@ -174,7 +186,12 @@
     mid_ref[0] = (pre * sigma).astype(BF16)
     grad = (cot_ref[0].astype(F32) * (sigma * (1.0 + pre * (1.0 - sigma)))).astype(BF16)
     turned = grad.T
-    mixg_ref[0] = dot(turned, flat, 1, 0) * scale
+    total_ref[...] = dot(turned, flat, 1, 0) * scale
+    rows = width // (2 * len(share_refs))
+    for place in range(2 * len(share_refs)):
+        start = pl.multiple_of(jnp.bitwise_xor(me_ref[0], place) * rows, rows)
+        at = place % 2 * rows
+        share_refs[place // 2][0, at : at + rows, :] = total_ref[pl.ds(start, rows), :]
     out = dot(mix.T, turned, 1, 0)
     grad_ref[...] = out.astype(BF16).reshape(grad_ref.shape)
 
@@ -191,10 +208,10 @@
 
 
 def backward_kernel(
-    down_scale, conv_scale, cgrad_ref, emb_ref, slope_hbm, hidden_hbm, dband_hbm, face_ref, edge_ref,
-    out_ref, turn_a, turn_b, turned_pg, hidden_ref, dband_ref, slope_ref, sem,
+    down_scale, conv_scale, cgrad_ref, emb_hbm, slope_hbm, hidden_ref, dband_ref, face_ref, edge_ref,
+    out_ref, turn_a, turn_b, turned_pg, emb_ref, slope_ref, sem,
 ):
-    copies = fetch((hidden_hbm, dband_hbm, slope_hbm), (hidden_ref, dband_ref, slope_ref), sem)
+    copies = fetch((slope_hbm, emb_hbm), (slope_ref, emb_ref), sem)
     for half in range(2):
         turn_b[half] = cgrad_ref[:, 128 * half : 128 * half + 128].astype(F32)
     for half in range(2):
@@ -210,7 +227,6 @@
     lane = iota((64, 256), 1)
     low = iota((64, 128), 1)
     down = jnp.zeros((64, 128), F32)
-    copies[0].wait()
     for bc in range(4):
         total = jnp.zeros((64, 256), F32)
         for x2 in range(8):
@@ -218,8 +234,7 @@
             total = jnp.where(lane // 32 == x2, part, total)
         down = jnp.where(low // 32 == bc, fold(total, 32), down)
     out_ref[0:64, :] = down * down_scale
-    copies[1].wait()
-    copies[2].wait()
+    copies[0].wait()
     for bc in range(4):
         hgrad = dot(cg, dband_ref[bc], 1, 0)
         edge = edge_ref[bc % 2, 32 * (bc // 2) : 32 * (bc // 2) + 32, :]
@@ -229,6 +244,7 @@
             slope = jnp.concatenate([slope_ref[bc, :480, :], edge], axis=0)
         pgrad = (hgrad * slope).astype(BF16)
         turned_pg[bc] = pgrad.T
+    copies[1].wait()
     lane_x = iota((16, 256), 1) // 16
     own = iota((8, 128), 1) // 16 == iota((8, 128), 0)
     for ty in range(3):
@@ -364,14 +380,19 @@
     embedded, slope, hidden, edge = pl.pallas_call(
         inner_kernel,
         out_shape=(
-            shape((34, 128, 256), BF16),
-            shape((4, 512, 256), F32),
+            pltpu.HBM((34, 128, 256), BF16),
+            pltpu.HBM((4, 512, 256), F32),
             shape((4, 512, 256), BF16),
             shape((2, 64, 256), F32),
         ),
         in_specs=[VMEM] * 5,
-        out_specs=(VMEM,) * 4,
-        compiler_params=params(8),
+        out_specs=(HBM, HBM, VMEM, VMEM),
+        scratch_shapes=[
+            pltpu.VMEM((34, 128, 256), BF16),
+            pltpu.VMEM((4, 512, 256), F32),
+            pltpu.SemaphoreType.DMA((9,)),
+        ],
+        compiler_params=params(12),
         cost_estimate=cost(3 << 30, 10 << 20),
         name="inner",
     )(features, ylo, yhi, table, band)
@@ -380,12 +401,17 @@
         out_shape=(
             shape((2, 128, 256), BF16),
             shape((2, 64, 256), F32),
-            shape((4, 512, 256), BF16),
+            pltpu.HBM((4, 512, 256), BF16),
             shape((1024, 256), BF16),
         ),
         in_specs=[VMEM] * 7,
-        out_specs=(VMEM,) * 4,
-        scratch_shapes=[pltpu.VMEM((512, 512), F32), pltpu.VMEM((2, 1024, 128), F32)],
+        out_specs=(VMEM, VMEM, HBM, VMEM),
+        scratch_shapes=[
+            pltpu.VMEM((512, 512), F32),
+            pltpu.VMEM((2, 1024, 128), F32),
+            pltpu.VMEM((4, 512, 256), BF16),
+            pltpu.SemaphoreType.DMA,
+        ],
         compiler_params=params(8),
         cost_estimate=cost(1 << 30, 4 << 20),
         name="outer",
@@ -395,30 +421,32 @@
         coarse.reshape(count_z, mine * 16, 256), "sz", split_axis=0, concat_axis=0, tiled=True
     )
     block = lambda *dims: pl.BlockSpec(dims, lambda c: (c,) + (0,) * (len(dims) - 1))
-    mid, mix_partial, back = pl.pallas_call(
+    shares = count_y // 2
+    mid, back, *mix_parts = pl.pallas_call(
         lambda *refs: mix_kernel(1.0 / math.sqrt(8 * 32 * count_y), *refs),
         grid=(mine,),
-        out_shape=(
-            shape((mine, 256, width), BF16),
-            shape((mine, width, width), F32),
-            shape((count_z, mine * 16, 256), BF16),
-        ),
+        out_shape=[shape((mine, 256, width), BF16), shape((count_z, mine * 16, 256), BF16)]
+        + [pltpu.HBM((mine, width // shares, width), F32)] * shares,
         in_specs=[
+            pl.BlockSpec(memory_space=pltpu.SMEM),
             pl.BlockSpec((count_z, 16, 256), lambda c: (0, c, 0)),
             block(1, width, width),
             block(1, 256, width),
         ],
-        out_specs=(
-            block(1, 256, width),
-            block(1, width, width),
-            pl.BlockSpec((count_z, 16, 256), lambda c: (0, c, 0)),
-        ),
+        out_specs=[block(1, 256, width), pl.BlockSpec((count_z, 16, 256), lambda c: (0, c, 0))]
+        + [block(1, width // shares, width)] * shares,
+        scratch_shapes=[pltpu.VMEM((width, width), F32)],
         compiler_params=params(12),
         cost_estimate=cost(mine * 3 * 2 * 256 * width * width, 5 << 20),
         name="mix",
-    )(sent, mix_weight, cotangent.reshape(mine, 256, width))
+    )(lax.axis_index("sy")[None], sent, mix_weight, cotangent.reshape(mine, 256, width))
+    mix_sum = mix_parts[0]
+    for k, part in enumerate(mix_parts[1:], 1):
+        mix_sum = mix_sum + lax.ppermute(part, "sy", [(i, i ^ (2 * k)) for i in range(count_y)])
     coarse_grad = lax.all_to_all(back, "sz", split_axis=0, concat_axis=0, tiled=True)
-    mix_grad = lax.psum_scatter(mix_partial, "sy", scatter_dimension=1, tiled=True)
+    mix_sum, coarse_grad = lax.optimization_barrier((mix_sum, coarse_grad))
+    mine_last, other = jnp.split(mix_sum, 2, axis=1)
+    mix_grad = mine_last + lax.ppermute(other, "sy", [(i, i ^ 1) for i in range(count_y)])
 
     cells = 16 * 64 * count_y * 32 * count_z
     sums = pl.pallas_call(
@@ -426,21 +454,27 @@
             1.0 / math.sqrt(cells // 8), 1.0 / math.sqrt(cells), *refs
         ),
         out_shape=shape((128, 128), F32),
-        in_specs=[VMEM, VMEM, HBM, HBM, HBM, VMEM, VMEM],
+        in_specs=[VMEM, HBM, HBM, VMEM, VMEM, VMEM, VMEM],
         out_specs=VMEM,
         scratch_shapes=[
             pltpu.VMEM((512, 512), F32),
             pltpu.VMEM((2, 1024, 128), F32),
             pltpu.VMEM((4, 256, 512), BF16),
-            pltpu.VMEM((4, 512, 256), BF16),
-            pltpu.VMEM((4, 512, 256), BF16),
+            pltpu.VMEM((17, 2, 128, 256), BF16),
             pltpu.VMEM((4, 512, 256), F32),
-            pltpu.SemaphoreType.DMA((3,)),
+            pltpu.SemaphoreType.DMA((2,)),
         ],
         compiler_params=params(16),
         cost_estimate=cost(4 << 30, 8 << 20),
         name="backward",
-    )(coarse_grad.reshape(1024, 256), embedded.reshape(17, 2, 128, 256), *kept(slope, hidden, dband), faces, edge_slope)
+    )(
+        coarse_grad.reshape(1024, 256),
+        *kept(embedded.reshape(17, 2, 128, 256), slope),
+        hidden,
+        dband,
+        faces,
+        edge_slope,
+    )
     rounds = sum_rounds(count_y, count_z)
     for masks in rounds[:-1]:
         parts = [sums] + exchanged(sums, masks, count_y * count_z)

time: 122 us -> 109 us (0.89)
  blocking collectives: 39.9 us -> 0 us
  waiting for transfers between devices: 17.2 us -> 36.8 us
  starting transfers between devices: 25 us -> 42.2 us
  between operations: 14.2 us -> 0.8 us
  Pallas kernels: 23.9 us -> 27 us
  other arithmetic: 0.15 us -> 2 us
    all_to_all x2 -> x0, blocking collectives: 39.9 us -> none  [the longest x1 21.4 us: per_device(): lax.all_to_all(coarse.reshape(count_z, mine * 16, 256), 'sz', split_axis=...]
    all_to_all x0 -> x2, starting transfers between devices: none -> 15.4 us  [the longest x1 11.6 us: per_device(): lax.all_to_all(coarse.reshape(count_z, mine * 16, 256), 'sz', split_axis=...]
    all_to_all x0 -> x2, waiting for transfers between devices: none -> 13 us  [the longest x1 12.4 us: per_device(): lax.all_to_all(coarse.reshape(count_z, mine * 16, 256), 'sz', split_axis=...]
    ppermute x0 -> x4, waiting for transfers between devices: none -> 10.4 us  [the longest x3 10.4 us: per_device(): lax.ppermute(part, 'sy', [(i, i ^ 2 * k) for i in range(count_y)])]
    ppermute x0 -> x4, starting transfers between devices: none -> 5.54 us  [the longest x3 4.87 us: per_device(): lax.ppermute(part, 'sy', [(i, i ^ 2 * k) for i in range(count_y)])]
    ppermute x10, waiting for transfers between devices: 15.5 us -> 11.2 us  [exchanged(): lax.ppermute(value, ('sy', 'sz'), [(i, i ^ m) for i in range(count)])]
    ppermute x10, starting transfers between devices: 15.8 us -> 13.8 us  [exchanged(): lax.ppermute(value, ('sy', 'sz'), [(i, i ^ m) for i in range(count)])]
    add x0 -> x2, other arithmetic: none -> 1.85 us  [the longest x1 1.18 us: per_device(): mix_sum + lax.ppermute(part, 'sy', [(i, i ^ 2 * k) for i in range(count_y)])]
  transfers between devices with their start and end apart: 15 -> 20, of which waited for: 8 -> 14; matrix products, arithmetic and copies ran while one was open for 0% -> 2% of each run, Pallas kernels for 11% -> 6%
where the time goes in v3:
time: 109 us
  starting transfers between devices  42.2 us (39%)
  waiting for transfers between devices  36.8 us (34%)
  Pallas kernels  27 us (25%)
  other arithmetic  2 us (2%)
    ppermute x10, starting transfers between devices, exchanged(): lax.ppermute(value, ('sy', 'sz'), [(i, i ^ m) for i in range(count)])  13.8 us
    all_to_all x1, waiting for transfers between devices, per_device(): lax.all_to_all(coarse.reshape(count_z, mine * 16, 256), 'sz', split_axis=...  12.4 us
    all_to_all x1, starting transfers between devices, per_device(): lax.all_to_all(coarse.reshape(count_z, mine * 16, 256), 'sz', split_axis=...  11.6 us
    ppermute x10, waiting for transfers between devices, exchanged(): lax.ppermute(value, ('sy', 'sz'), [(i, i ^ m) for i in range(count)])  11.2 us
    ppermute x3, waiting for transfers between devices, per_device(): lax.ppermute(part, 'sy', [(i, i ^ 2 * k) for i in range(count_y)])  10.4 us
    pallas_call x1, Pallas kernels, per_device(): pl.pallas_call(lambda *refs: backward_kernel(1.0 / math.sqrt(cells // 8),...  7.51 us
    pallas_call x1, Pallas kernels, per_device(): pl.pallas_call(outer_kernel, out_shape=(shape((2, 128, 256), BF16), shape...  5.14 us
    ppermute x3, starting transfers between devices, per_device(): lax.ppermute(part, 'sy', [(i, i ^ 2 * k) for i in range(count_y)])  4.87 us
  transfers between devices with their start and end apart: 20, of which 14 were waited for; matrix products, arithmetic and copies ran while one was open for 2% of the time, Pallas kernels for 6%

profile of v3, /device:TPU:0, one launch (start us, length us, event | category | flops | bytes accessed | tf_op | source)
XLA Modules:
  0.0 108.9 jit_solution(6341906523856359171)
XLA Ops:
  0.6 3.5 %features.1 = (bf16[32,128,80]{2,1,0:T(8,128)(2,1)S(1)}, bf16[32,80]{1,0:T(8,128)(2,1)S(1)}, bf16[32,80]{1,0:T(8,128)(2,1)S(1)}) custom-call(s32[16,32,64]{2,1,0:T(8,128)} %bitcast.33, bf16[16,32,64]{2,1,0:T(8,128)(2,1)} %bitcast.34), custom_call_target="tpu_custom_call" | custom-call | flops 41943040 | bytes 2097152 | tf_op jit(solution)/shard_map/features/pallas_call | solution.py:327
  4.1 3.6 %collective-permute-start = (bf16[32,80]{1,0:T(8,128)(2,1)S(1)}, bf16[32,80]{1,0:T(8,128)(2,1)S(1)}, u32[]{:S(2)}, u32[]{:S(2)}) collective-permute-start(bf16[32,80]{1,0:T(8,128)(2,1)S(1)} %get-tuple-element.33), channel_id=1, source_target_pairs={{0,16},{16,32},{32,48},{48,64},{64,80},{80,96},{96,112},{1,17},{17... | collective-permute-start | bytes 15368 | tf_op jit(solution)/shard_map/ppermute | solution.py:346
  7.7 1.3 %collective-permute-start.1 = (bf16[32,80]{1,0:T(8,128)(2,1)S(1)}, bf16[32,80]{1,0:T(8,128)(2,1)S(1)}, u32[]{:S(2)}, u32[]{:S(2)}) collective-permute-start(bf16[32,80]{1,0:T(8,128)(2,1)S(1)} %get-tuple-element.34), channel_id=1, source_target_pairs={{16,0},{32,16},{48,32},{64,48},{80,64},{96,80},{112,96},{17,1},{33... | collective-permute-start | bytes 15368 | tf_op jit(solution)/shard_map/ppermute | solution.py:347
  9.0 2.5 %weights.1 = (bf16[9,256,256]{2,1,0:T(8,128)(2,1)S(1)}, bf16[4,512,256]{2,1,0:T(8,128)(2,1)S(1)}, bf16[80,256]{1,0:T(8,128)(2,1)S(1)}) custom-call(bf16[16,16,27]{2,1,0:T(8,128)(2,1)} %bitcast.37, bf16[8,16,64]{2,1,0:T(8,128)(2,1)} %bitcast.39, bf16[4,16]{1,0:T(4,128)(2,1)} %mat_hbm.1, bf16[1,16]{1,0:T(2,128)(2,1)} %bitcast.40), custom_call_target="tpu_custom_call" | custom-call | flops 56623104 | bytes 3145728 | tf_op jit(solution)/shard_map/weights/pallas_call | solution.py:348
  11.5 0.0 collective-permute-done.ylo_ref
  11.6 1.7 %collective-permute-done.1.yhi_ref = bf16[32,80]{1,0:T(8,128)(2,1)S(1)} collective-permute-done((bf16[32,80]{1,0:T(8,128)(2,1)S(1)}, bf16[32,80]{1,0:T(8,128)(2,1)S(1)}, u32[]{:S(2)}, u32[]{:S(2)}) %collective-permute-start.1) | collective-permute-done | bytes 5152 | tf_op jit(solution)/shard_map/ppermute | solution.py:347
  13.3 0.1 fusion
  13.4 1.3 %collective-permute-start.2 = (bf16[128,80]{1,0:T(8,128)(2,1)S(1)}, bf16[128,80]{1,0:T(8,128)(2,1)S(1)}, u32[]{:S(2)}, u32[]{:S(2)}) collective-permute-start(bf16[128,80]{1,0:T(8,128)(2,1)S(1)} %get-tuple-element.63), channel_id=1, source_target_pairs={{0,1},{1,2},{2,3},{3,4},{4,5},{5,6},{6,7},{7,8},{8,9},{9,10},{10,1... | collective-permute-start | bytes 61448 | tf_op jit(solution)/shard_map/ppermute | solution.py:378
  14.7 1.3 %collective-permute-start.3 = (bf16[128,80]{1,0:T(8,128)(2,1)S(1)}, bf16[128,80]{1,0:T(8,128)(2,1)S(1)}, u32[]{:S(2)}, u32[]{:S(2)}) collective-permute-start(bf16[128,80]{1,0:T(8,128)(2,1)S(1)} %get-tuple-element.62), channel_id=1, source_target_pairs={{1,0},{2,1},{3,2},{4,3},{5,4},{6,5},{7,6},{8,7},{9,8},{10,9},{11,1... | collective-permute-start | bytes 61448 | tf_op jit(solution)/shard_map/ppermute | solution.py:379
  16.0 4.3 %inner.1 = (bf16[34,128,256]{2,1,0:T(8,128)(2,1)}, f32[4,512,256]{2,1,0:T(8,128)}, bf16[4,512,256]{2,1,0:T(8,128)(2,1)S(1)}, f32[2,64,256]{2,1,0:T(8,128)S(1)}) custom-call(bf16[32,128,80]{2,1,0:T(8,128)(2,1)S(1)} %get-tuple-element.40.feat_ref, bf16[32,80]{1,0:T(8,128)(2,1)S(1)} %collective-permute-done.ylo_ref, ...), custom_call_target="tpu_custom_call" | custom-call | flops 3221225472 | bytes 10485760 | tf_op jit(solution)/shard_map/inner/pallas_call | solution.py:380
  20.3 0.0 collective-permute-done.2.zlo_ref
  20.3 0.6 collective-permute-done.3.zhi_ref
  20.9 0.0 copy-start
  20.9 0.0 copy-start.1
  20.9 5.1 %outer.1 = (bf16[2,128,256]{2,1,0:T(8,128)(2,1)S(1)}, f32[2,64,256]{2,1,0:T(8,128)S(1)}, bf16[4,512,256]{2,1,0:T(8,128)(2,1)}, bf16[1024,256]{1,0:T(8,128)(2,1)}) custom-call(bf16[128,80]{1,0:T(8,128)(2,1)S(1)} %collective-permute-done.2.zlo_ref, bf16[128,80]{1,0:T(8,128)(2,1)S(1)} %collective-permute-done.3.zhi_ref, ...), custom_call_target="tpu_custom_call" | custom-call | flops 1073741824 | bytes 4194304 | tf_op jit(solution)/shard_map/outer/pallas_call | solution.py:399
  26.1 11.6 %all-to-all-start = ((bf16[16,64,256]{2,1,0:T(8,128)(2,1)}), bf16[16,64,256]{2,1,0:T(8,128)(2,1)S(1)}, u32[]{:S(2)}, u32[]{:S(2)}) async-start(bf16[16,64,256]{2,1,0:T(8,128)(2,1)} %bitcast.12), calls=%async_computation | async-start | bytes 1048576 | tf_op jit(solution)/shard_map/all_to_all | solution.py:420
  37.7 12.4 %all-to-all-done.refs_1_ = bf16[16,64,256]{2,1,0:T(8,128)(2,1)S(1)} async-done(((bf16[16,64,256]{2,1,0:T(8,128)(2,1)}), bf16[16,64,256]{2,1,0:T(8,128)(2,1)S(1)}, u32[]{:S(2)}, u32[]{:S(2)}) %all-to-all-start) | async-done | bytes 524320 | tf_op jit(solution)/shard_map/all_to_all | solution.py:420
  50.1 0.0 copy-done
  50.1 0.0 copy-done.1
  50.1 3.3 %mix.1 = (bf16[4,256,256]{2,1,0:T(8,128)(2,1)}, bf16[16,64,256]{2,1,0:T(8,128)(2,1)}, f32[4,64,256]{2,1,0:T(8,128)}, f32[4,64,256]{2,1,0:T(8,128)}, f32[4,64,256]{2,1,0:T(8,128)}, /*index=5*/f32[4,64,256]{2,1,0:T(8,128)}) custom-call(s32[1]{0:T(128)} %bitcast.refs_0_, bf16[16,64,256]{2,1,0:T(8,128)(2,1)S(1)} %all-to-all-done.refs_1_, ...), custom_call_target="tpu_custom_call" | custom-call | flops 402653184 | bytes 5242880 | tf_op jit(solution)/shard_map/mix/pallas_call | solution.py:425
  53.4 0.0 copy-start.2
  53.4 2.1 %collective-permute-start.4 = (f32[4,64,256]{2,1,0:T(8,128)}, f32[4,64,256]{2,1,0:T(8,128)S(1)}, u32[]{:S(2)}, u32[]{:S(2)}) collective-permute-start(f32[4,64,256]{2,1,0:T(8,128)} %get-tuple-element.49), channel_id=1, source_target_pairs={{0,32},{16,48},{32,0},{48,16},{64,96},{80,112},{96,64},{112,80},{1... | collective-permute-start | bytes 786440 | tf_op jit(solution)/shard_map/ppermute | solution.py:445
  55.5 2.7 %collective-permute-start.5 = (f32[4,64,256]{2,1,0:T(8,128)}, f32[4,64,256]{2,1,0:T(8,128)}, u32[]{:S(2)}, u32[]{:S(2)}) collective-permute-start(f32[4,64,256]{2,1,0:T(8,128)} %get-tuple-element.50), channel_id=1, source_target_pairs={{0,64},{16,80},{32,96},{48,112},{64,0},{80,16},{96,32},{112,48},{1... | collective-permute-start | bytes 786440 | tf_op jit(solution)/shard_map/ppermute | solution.py:445
  58.2 0.0 collective-permute-start.6
  58.2 3.8 %all-to-all-start.1 = ((bf16[16,64,256]{2,1,0:T(8,128)(2,1)}), bf16[16,64,256]{2,1,0:T(8,128)(2,1)S(1)}, u32[]{:S(2)}, u32[]{:S(2)}) async-start(bf16[16,64,256]{2,1,0:T(8,128)(2,1)} %get-tuple-element.52), calls=%async_computation.1 | async-start | bytes 1048576 | tf_op jit(solution)/shard_map/all_to_all | solution.py:446
  62.0 0.9 collective-permute-done.4
  62.9 6.9 %collective-permute-done.5 = f32[4,64,256]{2,1,0:T(8,128)} collective-permute-done((f32[4,64,256]{2,1,0:T(8,128)}, f32[4,64,256]{2,1,0:T(8,128)}, u32[]{:S(2)}, u32[]{:S(2)}) %collective-permute-start.5) | collective-permute-done | bytes 262176 | tf_op jit(solution)/shard_map/ppermute | solution.py:445
  69.8 2.6 %collective-permute-done.6 = f32[4,64,256]{2,1,0:T(8,128)} collective-permute-done((f32[4,64,256]{2,1,0:T(8,128)}, f32[4,64,256]{2,1,0:T(8,128)}, u32[]{:S(2)}, u32[]{:S(2)}) %collective-permute-start.6) | collective-permute-done | bytes 262176 | tf_op jit(solution)/shard_map/ppermute | solution.py:445
  72.3 1.2 %add_add_fusion = f32[4,64,256]{2,1,0:T(8,128)S(1)} fusion(f32[4,64,256]{2,1,0:T(8,128)} %collective-permute-done.6, f32[4,64,256]{2,1,0:T(8,128)} %collective-permute-done.5, f32[4,64,256]{2,1,0:T(8,128)} %get-tuple-element.48, f32[4,64,256]{2,1,0:T(8,128)S(1)} %collective-permute-done.4), kind=kLoop, calls=%fused_computation | loop fusion | flops 196608 | bytes 1310720 | tf_op jit(solution)/shard_map/add | solution.py:445
  73.5 0.6 all-to-all-done.1
  74.1 0.0 copy-done.2
  74.1 7.5 %backward.1 = f32[128,128]{1,0:T(8,128)S(1)} custom-call(bf16[1024,256]{1,0:T(8,128)(2,1)S(1)} %bitcast.32, bf16[17,2,128,256]{3,2,1,0:T(8,128)(2,1)} %bitcast.41, f32[4,512,256]{2,1,0:T(8,128)} %get-tuple-element.56.refs_2_, bf16[4,512,256]{2,1,0:T(8,128)(2,1)S(1)} %copy-done.2, bf16[4,512,256]{2,1,0:T(8,128)(2,1)S(1)} %get-tuple-element.43.dband_ref.refs_4_, ...), custom_call_target="tpu_custom_call" | custom-call | flops 4294967296 | bytes 8388608 | tf_op jit(solution)/shard_map/backward/pallas_call | solution.py:452
  81.7 0.1 collective-permute-start.8
  81.7 1.2 %collective-permute-done.8 = f32[128,128]{1,0:T(8,128)S(1)} collective-permute-done((f32[128,128]{1,0:T(8,128)S(1)}, f32[128,128]{1,0:T(8,128)S(1)}, u32[]{:S(2)}, u32[]{:S(2)}) %collective-permute-start.8) | collective-permute-done | bytes 65568 | tf_op jit(solution)/shard_map/ppermute | solution.py:317
  83.0 1.9 %collective-permute-start.10 = (f32[128,128]{1,0:T(8,128)S(1)}, f32[128,128]{1,0:T(8,128)S(1)}, u32[]{:S(2)}, u32[]{:S(2)}) collective-permute-start(f32[128,128]{1,0:T(8,128)S(1)} %add.37), channel_id=1, source_target_pairs={{0,16},{1,17},{2,18},{3,19},{4,20},{5,21},{6,22},{7,23},{8,24},{9,... | collective-permute-start | bytes 196616 | tf_op jit(solution)/shard_map/ppermute | solution.py:317
  84.9 0.0 collective-permute-start.11
  84.9 2.2 %collective-permute-start.9 = (f32[128,128]{1,0:T(8,128)S(1)}, f32[128,128]{1,0:T(8,128)S(1)}, u32[]{:S(2)}, u32[]{:S(2)}) collective-permute-start(f32[128,128]{1,0:T(8,128)S(1)} %add.37), channel_id=1, source_target_pairs={{0,2},{1,3},{2,0},{3,1},{4,6},{5,7},{6,4},{7,5},{8,10},{9,11},{10,... | collective-permute-start | bytes 196616 | tf_op jit(solution)/shard_map/ppermute | solution.py:317
  87.2 0.2 collective-permute-done.10
  87.4 4.1 %collective-permute-done.11 = f32[128,128]{1,0:T(8,128)S(1)} collective-permute-done((f32[128,128]{1,0:T(8,128)S(1)}, f32[128,128]{1,0:T(8,128)S(1)}, u32[]{:S(2)}, u32[]{:S(2)}) %collective-permute-start.11) | collective-permute-done | bytes 65568 | tf_op jit(solution)/shard_map/ppermute | solution.py:317
  91.4 0.0 collective-permute-done.9
  91.5 0.1 collective-permute-start.12
  91.6 2.3 %collective-permute-start.13 = (f32[128,128]{1,0:T(8,128)S(1)}, f32[128,128]{1,0:T(8,128)S(1)}, u32[]{:S(2)}, u32[]{:S(2)}) collective-permute-start(f32[128,128]{1,0:T(8,128)S(1)} %add_add_fusion.2), channel_id=1, source_target_pairs={{0,8},{1,9},{2,10},{3,11},{4,12},{5,13},{6,14},{7,15},{8,0},{9,1},... | collective-permute-start | bytes 196616 | tf_op jit(solution)/shard_map/ppermute | solution.py:317
  93.8 2.4 %collective-permute-start.14 = (f32[128,128]{1,0:T(8,128)S(1)}, f32[128,128]{1,0:T(8,128)S(1)}, u32[]{:S(2)}, u32[]{:S(2)}) collective-permute-start(f32[128,128]{1,0:T(8,128)S(1)} %add_add_fusion.2), channel_id=1, source_target_pairs={{0,12},{1,13},{2,14},{3,15},{4,8},{5,9},{6,10},{7,11},{8,4},{9,5},... | collective-permute-start | bytes 196616 | tf_op jit(solution)/shard_map/ppermute | solution.py:317
  96.2 0.7 collective-permute-start.7
  96.9 0.0 collective-permute-done.12
  96.9 0.6 collective-permute-done.13
  97.5 1.8 %collective-permute-done.14 = f32[128,128]{1,0:T(8,128)S(1)} collective-permute-done((f32[128,128]{1,0:T(8,128)S(1)}, f32[128,128]{1,0:T(8,128)S(1)}, u32[]{:S(2)}, u32[]{:S(2)}) %collective-permute-start.14) | collective-permute-done | bytes 65568 | tf_op jit(solution)/shard_map/ppermute | solution.py:317
  99.3 0.4 collective-permute-start.15
  99.7 2.9 %collective-permute-start.16 = (f32[128,128]{1,0:T(8,128)S(1)}, f32[128,128]{1,0:T(8,128)S(1)}, u32[]{:S(2)}, u32[]{:S(2)}) collective-permute-start(f32[128,128]{1,0:T(8,128)S(1)} %add_add_fusion.1.a_ref), channel_id=1, source_target_pairs={{0,64},{1,65},{2,66},{3,67},{4,68},{5,69},{6,70},{7,71},{8,72},{9,... | collective-permute-start | bytes 196616 | tf_op jit(solution)/shard_map/ppermute | solution.py:317
  102.6 1.5 %collective-permute-start.17 = (f32[128,128]{1,0:T(8,128)S(1)}, f32[128,128]{1,0:T(8,128)S(1)}, u32[]{:S(2)}, u32[]{:S(2)}) collective-permute-start(f32[128,128]{1,0:T(8,128)S(1)} %add_add_fusion.1.a_ref), channel_id=1, source_target_pairs={{0,96},{1,97},{2,98},{3,99},{4,100},{5,101},{6,102},{7,103},{8,104... | collective-permute-start | bytes 196616 | tf_op jit(solution)/shard_map/ppermute | solution.py:317
  104.1 0.0 collective-permute-done.7
  104.1 0.7 slice_add_fusion
  104.8 0.0 collective-permute-done.15.b_ref
  104.8 0.7 collective-permute-done.16.c_ref
  105.5 2.5 %collective-permute-done.17.d_ref = f32[128,128]{1,0:T(8,128)S(1)} collective-permute-done((f32[128,128]{1,0:T(8,128)S(1)}, f32[128,128]{1,0:T(8,128)S(1)}, u32[]{:S(2)}, u32[]{:S(2)}) %collective-permute-start.17) | collective-permute-done | bytes 65568 | tf_op jit(solution)/shard_map/ppermute | solution.py:317
  108.1 0.8 finish.1
  (6 shorter events, 0.1 us)
Async XLA Ops:
  4.1 7.4 %collective-permute-start = (bf16[32,80]{1,0:T(8,128)(2,1)S(1)}, bf16[32,80]{1,0:T(8,128)(2,1)S(1)}, u32[]{:S(2)}, u32[]{:S(2)}) collective-permute-start(bf16[32,80]{1,0:T(8,128)(2,1)S(1)} %get-tuple-element.33), channel_id=1, source_target_pairs={{0,16},{16,32},{32,48},{48,64},{64,80},{80,96},{96,112},{1,17},{17... | collective-permute-start | bytes 15368 | tf_op jit(solution)/shard_map/ppermute | solution.py:346
  7.7 5.5 %collective-permute-start.1 = (bf16[32,80]{1,0:T(8,128)(2,1)S(1)}, bf16[32,80]{1,0:T(8,128)(2,1)S(1)}, u32[]{:S(2)}, u32[]{:S(2)}) collective-permute-start(bf16[32,80]{1,0:T(8,128)(2,1)S(1)} %get-tuple-element.34), channel_id=1, source_target_pairs={{16,0},{32,16},{48,32},{64,48},{80,64},{96,80},{112,96},{17,1},{33... | collective-permute-start | bytes 15368 | tf_op jit(solution)/shard_map/ppermute | solution.py:347
  13.4 6.9 %collective-permute-start.2 = (bf16[128,80]{1,0:T(8,128)(2,1)S(1)}, bf16[128,80]{1,0:T(8,128)(2,1)S(1)}, u32[]{:S(2)}, u32[]{:S(2)}) collective-permute-start(bf16[128,80]{1,0:T(8,128)(2,1)S(1)} %get-tuple-element.63), channel_id=1, source_target_pairs={{0,1},{1,2},{2,3},{3,4},{4,5},{5,6},{6,7},{7,8},{8,9},{9,10},{10,1... | collective-permute-start | bytes 61448 | tf_op jit(solution)/shard_map/ppermute | solution.py:378
  14.7 6.2 %collective-permute-start.3 = (bf16[128,80]{1,0:T(8,128)(2,1)S(1)}, bf16[128,80]{1,0:T(8,128)(2,1)S(1)}, u32[]{:S(2)}, u32[]{:S(2)}) collective-permute-start(bf16[128,80]{1,0:T(8,128)(2,1)S(1)} %get-tuple-element.62), channel_id=1, source_target_pairs={{1,0},{2,1},{3,2},{4,3},{5,4},{6,5},{7,6},{8,7},{9,8},{10,9},{11,1... | collective-permute-start | bytes 61448 | tf_op jit(solution)/shard_map/ppermute | solution.py:379
  20.9 29.2 %copy-start = (bf16[4,256,256]{2,1,0:T(8,128)(2,1)S(1)}, bf16[4,256,256]{2,1,0:T(8,128)(2,1)}, u32[]{:S(2)}) copy-start(bf16[4,256,256]{2,1,0:T(8,128)(2,1)} %refs_2_.1) | copy-start | bytes 1572868
  20.9 29.2 %copy-start.1 = (bf16[4,8,32,256]{3,2,1,0:T(8,128)(2,1)S(1)}, bf16[4,8,32,256]{3,2,1,0:T(8,128)(2,1)}, u32[]{:S(2)}) copy-start(bf16[4,8,32,256]{3,2,1,0:T(8,128)(2,1)} %param.15) | copy-start | bytes 1572868
  26.1 24.0 %all-to-all-start = ((bf16[16,64,256]{2,1,0:T(8,128)(2,1)}), bf16[16,64,256]{2,1,0:T(8,128)(2,1)S(1)}, u32[]{:S(2)}, u32[]{:S(2)}) async-start(bf16[16,64,256]{2,1,0:T(8,128)(2,1)} %bitcast.12), calls=%async_computation | async-start | bytes 1048576 | tf_op jit(solution)/shard_map/all_to_all | solution.py:420
  53.4 20.8 %copy-start.2 = (bf16[4,512,256]{2,1,0:T(8,128)(2,1)S(1)}, bf16[4,512,256]{2,1,0:T(8,128)(2,1)}, u32[]{:S(2)}) copy-start(bf16[4,512,256]{2,1,0:T(8,128)(2,1)} %get-tuple-element.57.refs_3_) | copy-start | bytes 3145732
  53.4 9.5 %collective-permute-start.4 = (f32[4,64,256]{2,1,0:T(8,128)}, f32[4,64,256]{2,1,0:T(8,128)S(1)}, u32[]{:S(2)}, u32[]{:S(2)}) collective-permute-start(f32[4,64,256]{2,1,0:T(8,128)} %get-tuple-element.49), channel_id=1, source_target_pairs={{0,32},{16,48},{32,0},{48,16},{64,96},{80,112},{96,64},{112,80},{1... | collective-permute-start | bytes 786440 | tf_op jit(solution)/shard_map/ppermute | solution.py:445
  55.5 14.3 %collective-permute-start.5 = (f32[4,64,256]{2,1,0:T(8,128)}, f32[4,64,256]{2,1,0:T(8,128)}, u32[]{:S(2)}, u32[]{:S(2)}) collective-permute-start(f32[4,64,256]{2,1,0:T(8,128)} %get-tuple-element.50), channel_id=1, source_target_pairs={{0,64},{16,80},{32,96},{48,112},{64,0},{80,16},{96,32},{112,48},{1... | collective-permute-start | bytes 786440 | tf_op jit(solution)/shard_map/ppermute | solution.py:445
  58.2 14.1 %collective-permute-start.6 = (f32[4,64,256]{2,1,0:T(8,128)}, f32[4,64,256]{2,1,0:T(8,128)}, u32[]{:S(2)}, u32[]{:S(2)}) collective-permute-start(f32[4,64,256]{2,1,0:T(8,128)} %get-tuple-element.51), channel_id=1, source_target_pairs={{0,96},{16,112},{32,64},{48,80},{64,32},{80,48},{96,0},{112,16},{1... | collective-permute-start | bytes 786440 | tf_op jit(solution)/shard_map/ppermute | solution.py:445
  58.2 15.9 %all-to-all-start.1 = ((bf16[16,64,256]{2,1,0:T(8,128)(2,1)}), bf16[16,64,256]{2,1,0:T(8,128)(2,1)S(1)}, u32[]{:S(2)}, u32[]{:S(2)}) async-start(bf16[16,64,256]{2,1,0:T(8,128)(2,1)} %get-tuple-element.52), calls=%async_computation.1 | async-start | bytes 1048576 | tf_op jit(solution)/shard_map/all_to_all | solution.py:446
  81.7 1.3 %collective-permute-start.8 = (f32[128,128]{1,0:T(8,128)S(1)}, f32[128,128]{1,0:T(8,128)S(1)}, u32[]{:S(2)}, u32[]{:S(2)}) collective-permute-start(f32[128,128]{1,0:T(8,128)S(1)} %backward.1), channel_id=1, source_target_pairs={{0,1},{1,0},{2,3},{3,2},{4,5},{5,4},{6,7},{7,6},{8,9},{9,8},{10,11... | collective-permute-start | bytes 196616 | tf_op jit(solution)/shard_map/ppermute | solution.py:317
  83.0 4.4 %collective-permute-start.10 = (f32[128,128]{1,0:T(8,128)S(1)}, f32[128,128]{1,0:T(8,128)S(1)}, u32[]{:S(2)}, u32[]{:S(2)}) collective-permute-start(f32[128,128]{1,0:T(8,128)S(1)} %add.37), channel_id=1, source_target_pairs={{0,16},{1,17},{2,18},{3,19},{4,20},{5,21},{6,22},{7,23},{8,24},{9,... | collective-permute-start | bytes 196616 | tf_op jit(solution)/shard_map/ppermute | solution.py:317
  84.9 6.5 %collective-permute-start.11 = (f32[128,128]{1,0:T(8,128)S(1)}, f32[128,128]{1,0:T(8,128)S(1)}, u32[]{:S(2)}, u32[]{:S(2)}) collective-permute-start(f32[128,128]{1,0:T(8,128)S(1)} %add.37), channel_id=1, source_target_pairs={{0,18},{1,19},{2,16},{3,17},{4,22},{5,23},{6,20},{7,21},{8,26},{9,... | collective-permute-start | bytes 196616 | tf_op jit(solution)/shard_map/ppermute | solution.py:317
  84.9 6.5 %collective-permute-start.9 = (f32[128,128]{1,0:T(8,128)S(1)}, f32[128,128]{1,0:T(8,128)S(1)}, u32[]{:S(2)}, u32[]{:S(2)}) collective-permute-start(f32[128,128]{1,0:T(8,128)S(1)} %add.37), channel_id=1, source_target_pairs={{0,2},{1,3},{2,0},{3,1},{4,6},{5,7},{6,4},{7,5},{8,10},{9,11},{10,... | collective-permute-start | bytes 196616 | tf_op jit(solution)/shard_map/ppermute | solution.py:317
  91.5 5.5 %collective-permute-start.12 = (f32[128,128]{1,0:T(8,128)S(1)}, f32[128,128]{1,0:T(8,128)S(1)}, u32[]{:S(2)}, u32[]{:S(2)}) collective-permute-start(f32[128,128]{1,0:T(8,128)S(1)} %add_add_fusion.2), channel_id=1, source_target_pairs={{0,4},{1,5},{2,6},{3,7},{4,0},{5,1},{6,2},{7,3},{8,12},{9,13},{10,... | collective-permute-start | bytes 196616 | tf_op jit(solution)/shard_map/ppermute | solution.py:317
  91.6 6.0 %collective-permute-start.13 = (f32[128,128]{1,0:T(8,128)S(1)}, f32[128,128]{1,0:T(8,128)S(1)}, u32[]{:S(2)}, u32[]{:S(2)}) collective-permute-start(f32[128,128]{1,0:T(8,128)S(1)} %add_add_fusion.2), channel_id=1, source_target_pairs={{0,8},{1,9},{2,10},{3,11},{4,12},{5,13},{6,14},{7,15},{8,0},{9,1},... | collective-permute-start | bytes 196616 | tf_op jit(solution)/shard_map/ppermute | solution.py:317
  93.8 5.5 %collective-permute-start.14 = (f32[128,128]{1,0:T(8,128)S(1)}, f32[128,128]{1,0:T(8,128)S(1)}, u32[]{:S(2)}, u32[]{:S(2)}) collective-permute-start(f32[128,128]{1,0:T(8,128)S(1)} %add_add_fusion.2), channel_id=1, source_target_pairs={{0,12},{1,13},{2,14},{3,15},{4,8},{5,9},{6,10},{7,11},{8,4},{9,5},... | collective-permute-start | bytes 196616 | tf_op jit(solution)/shard_map/ppermute | solution.py:317
  96.2 7.8 %collective-permute-start.7 = (f32[4,32,256]{2,1,0:T(8,128)S(1)}, f32[4,32,256]{2,1,0:T(8,128)S(1)}, u32[]{:S(2)}, u32[]{:S(2)}) collective-permute-start(f32[4,32,256]{2,1,0:T(8,128)S(1)} %split.7), channel_id=1, source_target_pairs={{0,16},{16,0},{32,48},{48,32},{64,80},{80,64},{96,112},{112,96},{1... | collective-permute-start | bytes 393224 | tf_op jit(solution)/shard_map/ppermute | solution.py:449
  99.3 5.5 %collective-permute-start.15 = (f32[128,128]{1,0:T(8,128)S(1)}, f32[128,128]{1,0:T(8,128)S(1)}, u32[]{:S(2)}, u32[]{:S(2)}) collective-permute-start(f32[128,128]{1,0:T(8,128)S(1)} %add_add_fusion.1.a_ref), channel_id=1, source_target_pairs={{0,32},{1,33},{2,34},{3,35},{4,36},{5,37},{6,38},{7,39},{8,40},{9,... | collective-permute-start | bytes 196616 | tf_op jit(solution)/shard_map/ppermute | solution.py:317
  99.7 5.9 %collective-permute-start.16 = (f32[128,128]{1,0:T(8,128)S(1)}, f32[128,128]{1,0:T(8,128)S(1)}, u32[]{:S(2)}, u32[]{:S(2)}) collective-permute-start(f32[128,128]{1,0:T(8,128)S(1)} %add_add_fusion.1.a_ref), channel_id=1, source_target_pairs={{0,64},{1,65},{2,66},{3,67},{4,68},{5,69},{6,70},{7,71},{8,72},{9,... | collective-permute-start | bytes 196616 | tf_op jit(solution)/shard_map/ppermute | solution.py:317
  102.6 5.5 %collective-permute-start.17 = (f32[128,128]{1,0:T(8,128)S(1)}, f32[128,128]{1,0:T(8,128)S(1)}, u32[]{:S(2)}, u32[]{:S(2)}) collective-permute-start(f32[128,128]{1,0:T(8,128)S(1)} %add_add_fusion.1.a_ref), channel_id=1, source_target_pairs={{0,96},{1,97},{2,98},{3,99},{4,100},{5,101},{6,102},{7,103},{8,104... | collective-permute-start | bytes 196616 | tf_op jit(solution)/shard_map/ppermute | solution.py:317

commit v4 on v3

--- a/solution.py
+++ b/solution.py
@@ -51,7 +51,7 @@
 
 
 def weight_kernel(
-    conv_hbm, down_hbm, mat_hbm, dist_hbm, band_ref, dband_ref, table_ref,
+    conv_hbm, down_hbm, mat_hbm, dist_hbm, band_ref, pair_ref, pair_t_ref, table_ref,
     conv_ref, down_ref, mat_ref, dist_ref, sem,
 ):
     copies = fetch(
@@ -62,11 +62,11 @@
     spread = (iota((256, 16), 0) % 16 == iota((256, 16), 1)).astype(BF16)
     taps = conv_ref[...].reshape(256, 27)
     repeat = (iota((27, 432), 0) == iota((27, 432), 1) // 16).astype(BF16)
-    own = iota((256, 432), 0) // 16 == iota((256, 432), 1) % 16
+    own = iota((256, 432), 0) % 16 == iota((256, 432), 1) % 16
     apart = jnp.where(own, dot(taps, repeat, 1, 0), 0.0).astype(BF16)
-    gather = (iota((256, 256), 0) % 16 == iota((256, 256), 1) % 16).astype(BF16)
+    gather = (iota((256, 256), 0) % 16 == iota((256, 256), 1) // 16).astype(BF16)
     wide = dot(gather, apart, 1, 0).astype(BF16)
-    offset = iota((256, 256), 0) // 16 - iota((256, 256), 1) // 16 + 1
+    offset = iota((256, 256), 1) // 16 - iota((256, 256), 0) // 16 + 1
     for t in range(9):
         total = jnp.zeros((256, 256), F32)
         for tx in range(3):
@@ -74,12 +74,14 @@
             tile = dot(wide[:, at : at + 16], spread, 1, 1)
             total = jnp.where(offset == tx, tile, total)
         band_ref[t] = total.astype(BF16)
-    lane_x = iota((64, 256), 1) // 16
     for bc in range(4):
-        tiles = [dot(down_ref[4 * a + bc], spread, 0, 1) for a in range(2)]
-        both = jnp.where(lane_x % 2 == 0, tiles[0], tiles[1])
-        for x2 in range(8):
-            dband_ref[bc, 64 * x2 : 64 * x2 + 64, :] = jnp.where(lane_x // 2 == x2, both, 0.0).astype(BF16)
+        for x2 in range(2):
+            for a in range(2):
+                tap = down_ref[4 * a + bc]
+                none = jnp.zeros_like(tap)
+                at = 64 * bc + 32 * x2 + 16 * a
+                pair_t_ref[at : at + 16, :] = jnp.concatenate([none, tap] if x2 else [tap, none], axis=1)
+    pair_ref[...] = pair_t_ref[...].T
     lane_e = iota((16, 256), 1) // 16
     row_e = iota((16, 256), 0)
     mat = dot(mat_ref[...], spread, 1, 1)
@@ -94,52 +96,56 @@
     return (acc * sigma).astype(BF16), sigma * (1.0 + acc * (1.0 - sigma))
 
 
+def cells_of(emb_ref, b, c, ty, tz, half):
+    run = RUNS[b][ty]
+    q = (c + tz) // 2 + 8 * half
+    return emb_ref[q : q + 8, (c + tz) % 2, run : run + 32, :].reshape(256, 256)
+
+
 def inner_kernel(
     feat_ref, ylo_ref, yhi_ref, table_ref, band_ref, emb_hbm, slope_hbm, hidden_ref, edge_ref,
     emb_ref, slope_ref, sem,
 ):
     table = table_ref[...]
     row = iota((128, 80), 0)
-    emb_ref[0] = jnp.zeros((128, 256), BF16)
-    emb_ref[33] = jnp.zeros((128, 256), BF16)
+    emb_ref[0, 0] = jnp.zeros((128, 256), BF16)
+    emb_ref[16, 1] = jnp.zeros((128, 256), BF16)
     ylo = ylo_ref[...].astype(F32)
     yhi = yhi_ref[...].astype(F32)
     for z in range(32):
         f = feat_ref[z].astype(F32)
         f = jnp.where(row == 64, ylo[z : z + 1, :], f)
         f = jnp.where(row == 127, yhi[z : z + 1, :], f)
-        emb_ref[z + 1] = dot(f.astype(BF16), table, 1, 0).astype(BF16)
+        emb_ref[(z + 1) // 2, (z + 1) % 2] = dot(f.astype(BF16), table, 1, 0).astype(BF16)
     copies = [pltpu.make_async_copy(emb_ref, emb_hbm, sem.at[0])]
     copies[0].start()
-    chunk = 8
-    for b in range(2):
-        for z0 in range(0, 32, chunk):
+    for bc in range(4):
+        b, c = bc // 2, bc % 2
+        for half in range(2):
             acc = None
             for ty in range(3):
                 for tz in range(3):
-                    run = RUNS[b][ty]
-                    rows = emb_ref[z0 + tz : z0 + tz + chunk, run : run + 32, :].reshape(32 * chunk, 256)
-                    part = dot(rows, band_ref[3 * ty + tz], 1, 0)
+                    part = dot(band_ref[3 * ty + tz], cells_of(emb_ref, b, c, ty, tz, half), 1, 1)
                     acc = part if acc is None else acc + part
-            hid, slope = activate(acc)
-            if z0 == 0:
-                edge_ref[0, 32 * b : 32 * b + 32, :] = acc[:32]
-            if z0 == 32 - chunk:
-                edge_ref[1, 32 * b : 32 * b + 32, :] = acc[32 * chunk - 32 :]
-            for k in range(chunk):
-                z2, c = (z0 + k) // 2, k % 2
-                hidden_ref[2 * b + c, 32 * z2 : 32 * z2 + 32, :] = hid[32 * k : 32 * k + 32]
-                slope_ref[2 * b + c, 32 * z2 : 32 * z2 + 32, :] = slope[32 * k : 32 * k + 32]
-            at = (pl.ds(2 * b, 2), pl.ds(16 * z0, 16 * chunk))
-            copies.append(pltpu.make_async_copy(slope_ref.at[at], slope_hbm.at[at], sem.at[len(copies)]))
-            copies[-1].start()
+            if half == 0 and c == 0:
+                edge_ref[0, b] = acc[:, :32]
+            if half == 1 and c == 1:
+                edge_ref[1, b] = acc[:, 224:]
+            at = slice(256 * half, 256 * half + 256)
+            hidden_ref[bc, :, at], slope_ref[bc, :, at] = activate(acc)
+        copies.append(pltpu.make_async_copy(slope_ref.at[bc], slope_hbm.at[bc], sem.at[1 + bc]))
+        copies[-1].start()
     for copy in copies:
         copy.wait()
 
 
+def pair_rows(hidden_ref, pair):
+    return jnp.concatenate([hidden_ref[bc, 64 * pair : 64 * pair + 64, :] for bc in range(4)], axis=0)
+
+
 def outer_kernel(
-    zlo_ref, zhi_ref, table_ref, band_ref, dband_ref, edge_ref, inner_ref,
-    emb_ref, slope_ref, hidden_hbm, coarse_ref, turn_a, turn_b, hidden_ref, sem,
+    zlo_ref, zhi_ref, table_ref, band_ref, pair_ref, edge_ref, inner_ref,
+    emb_ref, slope_ref, hidden_hbm, coarse_hbm, turn_a, turn_b, hidden_ref, coarse_ref, sem,
 ):
     table = table_ref[...]
     hidden_ref[...] = inner_ref[...]
@@ -147,32 +153,29 @@
         plane = dot(face[...], table, 1, 0).astype(BF16)
         emb_ref[side] = plane
         for b in range(2):
-            acc = edge_ref[side, 32 * b : 32 * b + 32, :]
+            acc = edge_ref[side, b]
             for ty in range(3):
                 run = RUNS[b][ty]
-                acc = acc + dot(plane[run : run + 32], band_ref[3 * ty + 2 * side], 1, 0)
-            hid, slope = activate(acc)
-            hidden_ref[2 * b + side, 480 * side : 480 * side + 32, :] = hid
-            slope_ref[side, 32 * b : 32 * b + 32, :] = slope
-    copy = pltpu.make_async_copy(hidden_ref, hidden_hbm, sem)
-    copy.start()
-    for x2 in range(8):
-        at = slice(64 * x2, 64 * x2 + 64)
-        acc = None
-        for bc in range(4):
-            part = dot(dband_ref[bc, at, :], hidden_ref[bc], 1, 1)
-            acc = part if acc is None else acc + part
-        turn_a[at, :] = acc
-    for z2 in range(16):
-        for half in range(2):
+                acc = acc + dot(band_ref[3 * ty + 2 * side], plane[run : run + 32], 1, 1)
+            at = slice(480 * side, 480 * side + 32)
+            hidden_ref[2 * b + side, :, at], slope_ref[side, b] = activate(acc)
+    copies = [pltpu.make_async_copy(hidden_ref, hidden_hbm, sem.at[0])]
+    copies[0].start()
+    for pair in range(4):
+        turn_a[128 * pair : 128 * pair + 128, :] = dot(pair_ref[...], pair_rows(hidden_ref, pair), 1, 0)
+    for half in range(2):
+        for z2 in range(16):
             pieces = [
                 turn_a[64 * x2 : 64 * x2 + 64, 32 * z2 : 32 * z2 + 32]
                 for x2 in range(4 * half, 4 * half + 4)
             ]
             turn_b[half, pl.ds(z2, 64, stride=16), :] = jnp.concatenate(pieces, axis=1)
-    for half in range(2):
-        coarse_ref[:, 128 * half : 128 * half + 128] = turn_b[half].astype(BF16)
-    copy.wait()
+        at = (slice(None), pl.ds(128 * half, 128))
+        coarse_ref[at] = turn_b[half].astype(BF16)
+        copies.append(pltpu.make_async_copy(coarse_ref.at[at], coarse_hbm.at[at], sem.at[1 + half]))
+        copies[-1].start()
+    for copy in copies:
+        copy.wait()
 
 
 def mix_kernel(scale, me_ref, coarse_ref, mix_ref, cot_ref, mid_ref, grad_ref, *more_refs):
@@ -208,7 +211,7 @@
 
 
 def backward_kernel(
-    down_scale, conv_scale, cgrad_ref, emb_hbm, slope_hbm, hidden_ref, dband_ref, face_ref, edge_ref,
+    down_scale, conv_scale, cgrad_ref, emb_hbm, slope_hbm, hidden_ref, pair_ref, pair_t_ref, face_ref, edge_ref,
     out_ref, turn_a, turn_b, turned_pg, emb_ref, slope_ref, sem,
 ):
     copies = fetch((slope_hbm, emb_hbm), (slope_ref, emb_ref), sem)
@@ -223,28 +226,28 @@
                     [p[:, 32 * k : 32 * k + 32] for p in pieces], axis=1
                 )
     cg_t = turn_a[...].astype(BF16)
-    cg = cg_t.T
-    lane = iota((64, 256), 1)
-    low = iota((64, 128), 1)
-    down = jnp.zeros((64, 128), F32)
-    for bc in range(4):
-        total = jnp.zeros((64, 256), F32)
-        for x2 in range(8):
-            part = dot(cg_t[64 * x2 : 64 * x2 + 64, :], hidden_ref[bc], 1, 0)
-            total = jnp.where(lane // 32 == x2, part, total)
-        down = jnp.where(low // 32 == bc, fold(total, 32), down)
-    out_ref[0:64, :] = down * down_scale
+    pairs = [cg_t[128 * pair : 128 * pair + 128, :] for pair in range(4)]
+    down = None
+    for pair in range(4):
+        part = dot(pairs[pair], pair_rows(hidden_ref, pair), 1, 1)
+        down = part if down is None else down + part
+    down = jnp.where(iota((64, 256), 1) // 32 % 2 == 0, down[:64], down[64:]) * down_scale
+    left = down[:, :128] + pltpu.roll(down[:, :128], 96, 1)
+    right = down[:, 128:] + pltpu.roll(down[:, 128:], 32, 1)
+    out_ref[0:64, :] = jnp.where(iota((64, 128), 1) // 32 % 2 == 0, left, right)
     copies[0].wait()
-    for bc in range(4):
-        hgrad = dot(cg, dband_ref[bc], 1, 0)
-        edge = edge_ref[bc % 2, 32 * (bc // 2) : 32 * (bc // 2) + 32, :]
-        if bc % 2 == 0:
-            slope = jnp.concatenate([edge, slope_ref[bc, 32:, :]], axis=0)
-        else:
-            slope = jnp.concatenate([slope_ref[bc, :480, :], edge], axis=0)
-        pgrad = (hgrad * slope).astype(BF16)
-        turned_pg[bc] = pgrad.T
+    for side in range(2):
+        for b in range(2):
+            slope_ref[2 * b + side, :, 480 * side : 480 * side + 32] = edge_ref[side, b]
+    for pair in range(4):
+        hgrad = dot(pair_t_ref[...], pairs[pair], 1, 0)
+        at = slice(64 * pair, 64 * pair + 64)
+        for bc in range(4):
+            grad = hgrad[64 * bc : 64 * bc + 64] * slope_ref[bc, at, :]
+            turned_pg[bc, at, :] = grad.astype(BF16)
     copies[1].wait()
+    emb_ref[0, 0] = face_ref[0]
+    emb_ref[16, 1] = face_ref[1]
     lane_x = iota((16, 256), 1) // 16
     own = iota((8, 128), 1) // 16 == iota((8, 128), 0)
     for ty in range(3):
@@ -252,15 +255,10 @@
             acc = None
             for bc in range(4):
                 b, c = bc // 2, bc % 2
-                run = RUNS[b][ty]
-                q, p = (c + tz) // 2, (c + tz) % 2
-                rows = emb_ref[q : q + 16, p, run : run + 32, :].reshape(512, 256)
-                if c + tz == 0:
-                    rows = jnp.concatenate([face_ref[0, run : run + 32, :], rows[32:]], axis=0)
-                if c + tz == 3:
-                    rows = jnp.concatenate([rows[:480], face_ref[1, run : run + 32, :]], axis=0)
-                part = dot(turned_pg[bc], rows, 1, 0)
-                acc = part if acc is None else acc + part
+                for half in range(2):
+                    rows = cells_of(emb_ref, b, c, ty, tz, half)
+                    part = dot(turned_pg[bc, :, 256 * half : 256 * half + 256], rows, 1, 0)
+                    acc = part if acc is None else acc + part
             for tx in range(3):
                 total = jnp.zeros((16, 256), F32)
                 for x in range(16):
@@ -281,7 +279,7 @@
     down = total[:64].T
     for a in range(2):
         for bc in range(4):
-            at = (2 * bc + a) * 16
+            at = (2 * (2 * (bc % 2) + bc // 2) + a) * 16
             down_ref[4 * a + bc] = down[at : at + 16, :]
     for half in range(2):
         conv = total[64 + 32 * half : 96 + 32 * half].T
@@ -345,11 +343,16 @@
     up_z = [(i, i + 1) for i in range(count_z - 1)]
     ylo = lax.ppermute(last, "sy", up_y)
     yhi = lax.ppermute(first, "sy", [(j, i) for i, j in up_y])
-    band, dband, table = pl.pallas_call(
+    band, pair, pair_t, table = pl.pallas_call(
         weight_kernel,
-        out_shape=(shape((9, 256, 256), BF16), shape((4, 512, 256), BF16), shape((80, 256), BF16)),
+        out_shape=(
+            shape((9, 256, 256), BF16),
+            shape((128, 256), BF16),
+            shape((256, 128), BF16),
+            shape((80, 256), BF16),
+        ),
         in_specs=[HBM] * 4,
-        out_specs=(VMEM,) * 3,
+        out_specs=(VMEM,) * 4,
         scratch_shapes=[
             pltpu.VMEM((16, 16, 27), BF16),
             pltpu.VMEM((8, 16, 64), BF16),
@@ -368,7 +371,9 @@
             dist_weight[None],
         )
     )
-    ylo, yhi, band, dband, table = lax.optimization_barrier((ylo, yhi, band, dband, table))
+    ylo, yhi, band, pair, pair_t, table = lax.optimization_barrier(
+        (ylo, yhi, band, pair, pair_t, table)
+    )
 
     def whole(z):
         row = lax.broadcasted_iota(jnp.int32, (128, 80), 0)
@@ -380,17 +385,17 @@
     embedded, slope, hidden, edge = pl.pallas_call(
         inner_kernel,
         out_shape=(
-            pltpu.HBM((34, 128, 256), BF16),
-            pltpu.HBM((4, 512, 256), F32),
-            shape((4, 512, 256), BF16),
-            shape((2, 64, 256), F32),
+            pltpu.HBM((17, 2, 128, 256), BF16),
+            pltpu.HBM((4, 256, 512), F32),
+            shape((4, 256, 512), BF16),
+            shape((2, 2, 256, 32), F32),
         ),
         in_specs=[VMEM] * 5,
         out_specs=(HBM, HBM, VMEM, VMEM),
         scratch_shapes=[
-            pltpu.VMEM((34, 128, 256), BF16),
-            pltpu.VMEM((4, 512, 256), F32),
-            pltpu.SemaphoreType.DMA((9,)),
+            pltpu.VMEM((17, 2, 128, 256), BF16),
+            pltpu.VMEM((4, 256, 512), F32),
+            pltpu.SemaphoreType.DMA((5,)),
         ],
         compiler_params=params(12),
         cost_estimate=cost(3 << 30, 10 << 20),
@@ -400,22 +405,23 @@
         outer_kernel,
         out_shape=(
             shape((2, 128, 256), BF16),
-            shape((2, 64, 256), F32),
-            pltpu.HBM((4, 512, 256), BF16),
-            shape((1024, 256), BF16),
+            shape((2, 2, 256, 32), F32),
+            pltpu.HBM((4, 256, 512), BF16),
+            pltpu.HBM((1024, 256), BF16),
         ),
         in_specs=[VMEM] * 7,
-        out_specs=(VMEM, VMEM, HBM, VMEM),
+        out_specs=(VMEM, VMEM, HBM, HBM),
         scratch_shapes=[
             pltpu.VMEM((512, 512), F32),
             pltpu.VMEM((2, 1024, 128), F32),
-            pltpu.VMEM((4, 512, 256), BF16),
-            pltpu.SemaphoreType.DMA,
+            pltpu.VMEM((4, 256, 512), BF16),
+            pltpu.VMEM((1024, 256), BF16),
+            pltpu.SemaphoreType.DMA((3,)),
         ],
         compiler_params=params(8),
         cost_estimate=cost(1 << 30, 4 << 20),
         name="outer",
-    )(zlo, zhi, table, band, dband, edge, hidden)
+    )(zlo, zhi, table, band, pair, edge, hidden)
 
     sent = lax.all_to_all(
         coarse.reshape(count_z, mine * 16, 256), "sz", split_axis=0, concat_axis=0, tiled=True
@@ -454,14 +460,14 @@
             1.0 / math.sqrt(cells // 8), 1.0 / math.sqrt(cells), *refs
         ),
         out_shape=shape((128, 128), F32),
-        in_specs=[VMEM, HBM, HBM, VMEM, VMEM, VMEM, VMEM],
+        in_specs=[VMEM, HBM, HBM] + [VMEM] * 5,
         out_specs=VMEM,
         scratch_shapes=[
             pltpu.VMEM((512, 512), F32),
             pltpu.VMEM((2, 1024, 128), F32),
             pltpu.VMEM((4, 256, 512), BF16),
             pltpu.VMEM((17, 2, 128, 256), BF16),
-            pltpu.VMEM((4, 512, 256), F32),
+            pltpu.VMEM((4, 256, 512), F32),
             pltpu.SemaphoreType.DMA((2,)),
         ],
         compiler_params=params(16),
@@ -469,9 +475,10 @@
         name="backward",
     )(
         coarse_grad.reshape(1024, 256),
-        *kept(embedded.reshape(17, 2, 128, 256), slope),
+        *kept(embedded, slope),
         hidden,
-        dband,
+        pair,
+        pair_t,
         faces,
         edge_slope,
     )

time: 109 us -> 105 us (0.963)
  Pallas kernels: 27 us -> 22.8 us
    pallas_call x1, Pallas kernels: 5.14 us -> 2.64 us  [per_device(): pl.pallas_call(outer_kernel, out_shape=(shape((2, 128, 256), BF16), shape...]
    pallas_call x1, Pallas kernels: 7.51 us -> 6.12 us  [per_device(): pl.pallas_call(lambda *refs: backward_kernel(1.0 / math.sqrt(cells // 8),...]
where the time goes in v4:
time: 105 us
  starting transfers between devices  42 us (40%)
  waiting for transfers between devices  37.2 us (35%)
  Pallas kernels  22.8 us (22%)
  other arithmetic  1.84 us (2%)
    ppermute x10, starting transfers between devices, exchanged(): lax.ppermute(value, ('sy', 'sz'), [(i, i ^ m) for i in range(count)])  13.9 us
    all_to_all x1, waiting for transfers between devices, per_device(): lax.all_to_all(coarse.reshape(count_z, mine * 16, 256), 'sz', split_axis=...  12.3 us
    all_to_all x1, starting transfers between devices, per_device(): lax.all_to_all(coarse.reshape(count_z, mine * 16, 256), 'sz', split_axis=...  11.5 us
    ppermute x10, waiting for transfers between devices, exchanged(): lax.ppermute(value, ('sy', 'sz'), [(i, i ^ m) for i in range(count)])  11.1 us
    ppermute x3, waiting for transfers between devices, per_device(): lax.ppermute(part, 'sy', [(i, i ^ 2 * k) for i in range(count_y)])  10.2 us
    pallas_call x1, Pallas kernels, per_device(): pl.pallas_call(lambda *refs: backward_kernel(1.0 / math.sqrt(cells // 8),...  6.12 us
    ppermute x3, starting transfers between devices, per_device(): lax.ppermute(part, 'sy', [(i, i ^ 2 * k) for i in range(count_y)])  4.73 us
    pallas_call x1, Pallas kernels, per_device(): pl.pallas_call(inner_kernel, out_shape=(pltpu.HBM((17, 2, 128, 256), BF16...  4.15 us
  transfers between devices with their start and end apart: 20, of which 14 were waited for; matrix products, arithmetic and copies ran while one was open for 2% of the time, Pallas kernels for 6%

profile of v4, /device:TPU:0, one launch (start us, length us, event | category | flops | bytes accessed | tf_op | source)
XLA Modules:
  0.0 104.7 jit_solution(4574165224908171401)
XLA Ops:
  0.6 3.5 %features.1 = (bf16[32,128,80]{2,1,0:T(8,128)(2,1)S(1)}, bf16[32,80]{1,0:T(8,128)(2,1)S(1)}, bf16[32,80]{1,0:T(8,128)(2,1)S(1)}) custom-call(s32[16,32,64]{2,1,0:T(8,128)} %bitcast.33, bf16[16,32,64]{2,1,0:T(8,128)(2,1)} %bitcast.34), custom_call_target="tpu_custom_call" | custom-call | flops 41943040 | bytes 2097152 | tf_op jit(solution)/shard_map/features/pallas_call | solution.py:325
  4.1 3.6 %collective-permute-start = (bf16[32,80]{1,0:T(8,128)(2,1)S(1)}, bf16[32,80]{1,0:T(8,128)(2,1)S(1)}, u32[]{:S(2)}, u32[]{:S(2)}) collective-permute-start(bf16[32,80]{1,0:T(8,128)(2,1)S(1)} %get-tuple-element.35), channel_id=1, source_target_pairs={{0,16},{16,32},{32,48},{48,64},{64,80},{80,96},{96,112},{1,17},{17... | collective-permute-start | bytes 15368 | tf_op jit(solution)/shard_map/ppermute | solution.py:344
  7.7 1.3 %collective-permute-start.1 = (bf16[32,80]{1,0:T(8,128)(2,1)S(1)}, bf16[32,80]{1,0:T(8,128)(2,1)S(1)}, u32[]{:S(2)}, u32[]{:S(2)}) collective-permute-start(bf16[32,80]{1,0:T(8,128)(2,1)S(1)} %get-tuple-element.36), channel_id=1, source_target_pairs={{16,0},{32,16},{48,32},{64,48},{80,64},{96,80},{112,96},{17,1},{33... | collective-permute-start | bytes 15368 | tf_op jit(solution)/shard_map/ppermute | solution.py:345
  9.0 2.3 %weights.1 = (bf16[9,256,256]{2,1,0:T(8,128)(2,1)S(1)}, bf16[128,256]{1,0:T(8,128)(2,1)S(1)}, bf16[256,128]{1,0:T(8,128)(2,1)S(1)}, bf16[80,256]{1,0:T(8,128)(2,1)S(1)}) custom-call(bf16[16,16,27]{2,1,0:T(8,128)(2,1)} %bitcast.37, bf16[8,16,64]{2,1,0:T(8,128)(2,1)} %bitcast.39, bf16[4,16]{1,0:T(4,128)(2,1)} %mat_hbm.1, bf16[1,16]{1,0:T(2,128)(2,1)} %bitcast.40), custom_call_target="tpu_custom_call" | custom-call | flops 56623104 | bytes 3145728 | tf_op jit(solution)/shard_map/weights/pallas_call | solution.py:346
  11.4 0.0 collective-permute-done.ylo_ref
  11.4 1.9 %collective-permute-done.1.yhi_ref = bf16[32,80]{1,0:T(8,128)(2,1)S(1)} collective-permute-done((bf16[32,80]{1,0:T(8,128)(2,1)S(1)}, bf16[32,80]{1,0:T(8,128)(2,1)S(1)}, u32[]{:S(2)}, u32[]{:S(2)}) %collective-permute-start.1) | collective-permute-done | bytes 5152 | tf_op jit(solution)/shard_map/ppermute | solution.py:345
  13.3 0.1 fusion
  13.4 1.3 %collective-permute-start.2 = (bf16[128,80]{1,0:T(8,128)(2,1)S(1)}, bf16[128,80]{1,0:T(8,128)(2,1)S(1)}, u32[]{:S(2)}, u32[]{:S(2)}) collective-permute-start(bf16[128,80]{1,0:T(8,128)(2,1)S(1)} %get-tuple-element.67), channel_id=1, source_target_pairs={{0,1},{1,2},{2,3},{3,4},{4,5},{5,6},{6,7},{7,8},{8,9},{9,10},{10,1... | collective-permute-start | bytes 61448 | tf_op jit(solution)/shard_map/ppermute | solution.py:383
  14.7 1.3 %collective-permute-start.3 = (bf16[128,80]{1,0:T(8,128)(2,1)S(1)}, bf16[128,80]{1,0:T(8,128)(2,1)S(1)}, u32[]{:S(2)}, u32[]{:S(2)}) collective-permute-start(bf16[128,80]{1,0:T(8,128)(2,1)S(1)} %get-tuple-element.66), channel_id=1, source_target_pairs={{1,0},{2,1},{3,2},{4,3},{5,4},{6,5},{7,6},{8,7},{9,8},{10,9},{11,1... | collective-permute-start | bytes 61448 | tf_op jit(solution)/shard_map/ppermute | solution.py:384
  16.0 4.1 %inner.1 = (bf16[17,2,128,256]{3,2,1,0:T(8,128)(2,1)}, f32[4,256,512]{2,1,0:T(8,128)}, bf16[4,256,512]{2,1,0:T(8,128)(2,1)S(1)}, f32[2,2,256,32]{3,2,1,0:T(8,128)S(1)}) custom-call(bf16[32,128,80]{2,1,0:T(8,128)(2,1)S(1)} %get-tuple-element.43.feat_ref, bf16[32,80]{1,0:T(8,128)(2,1)S(1)} %collective-permute-done.ylo_ref, ...), custom_call_target="tpu_custom_call" | custom-call | flops 3221225472 | bytes 10485760 | tf_op jit(solution)/shard_map/inner/pallas_call | solution.py:385
  20.1 0.0 collective-permute-done.2.zlo_ref
  20.1 0.8 collective-permute-done.3.zhi_ref
  20.9 0.0 copy-start
  20.9 0.0 copy-start.1
  20.9 2.6 %outer.1 = (bf16[2,128,256]{2,1,0:T(8,128)(2,1)S(1)}, f32[2,2,256,32]{3,2,1,0:T(8,128)S(1)}, bf16[4,256,512]{2,1,0:T(8,128)(2,1)}, bf16[1024,256]{1,0:T(8,128)(2,1)}) custom-call(bf16[128,80]{1,0:T(8,128)(2,1)S(1)} %collective-permute-done.2.zlo_ref, bf16[128,80]{1,0:T(8,128)(2,1)S(1)} %collective-permute-done.3.zhi_ref, ...), custom_call_target="tpu_custom_call" | custom-call | flops 1073741824 | bytes 4194304 | tf_op jit(solution)/shard_map/outer/pallas_call | solution.py:404
  23.6 11.5 %all-to-all-start = ((bf16[16,64,256]{2,1,0:T(8,128)(2,1)}), bf16[16,64,256]{2,1,0:T(8,128)(2,1)S(1)}, u32[]{:S(2)}, u32[]{:S(2)}) async-start(bf16[16,64,256]{2,1,0:T(8,128)(2,1)} %bitcast.32), calls=%async_computation | async-start | bytes 1048576 | tf_op jit(solution)/shard_map/all_to_all | solution.py:426
  35.1 0.0 copy-start.2
  35.1 12.3 %all-to-all-done.refs_1_ = bf16[16,64,256]{2,1,0:T(8,128)(2,1)S(1)} async-done(((bf16[16,64,256]{2,1,0:T(8,128)(2,1)}), bf16[16,64,256]{2,1,0:T(8,128)(2,1)S(1)}, u32[]{:S(2)}, u32[]{:S(2)}) %all-to-all-start) | async-done | bytes 524320 | tf_op jit(solution)/shard_map/all_to_all | solution.py:426
  47.5 0.0 copy-done
  47.5 0.0 copy-done.1
  47.5 3.3 %mix.1 = (bf16[4,256,256]{2,1,0:T(8,128)(2,1)}, bf16[16,64,256]{2,1,0:T(8,128)(2,1)}, f32[4,64,256]{2,1,0:T(8,128)}, f32[4,64,256]{2,1,0:T(8,128)}, f32[4,64,256]{2,1,0:T(8,128)}, /*index=5*/f32[4,64,256]{2,1,0:T(8,128)}) custom-call(s32[1]{0:T(128)} %bitcast.refs_0_, bf16[16,64,256]{2,1,0:T(8,128)(2,1)S(1)} %all-to-all-done.refs_1_, ...), custom_call_target="tpu_custom_call" | custom-call | flops 402653184 | bytes 5242880 | tf_op jit(solution)/shard_map/mix/pallas_call | solution.py:431
  50.7 1.9 %collective-permute-start.4 = (f32[4,64,256]{2,1,0:T(8,128)}, f32[4,64,256]{2,1,0:T(8,128)S(1)}, u32[]{:S(2)}, u32[]{:S(2)}) collective-permute-start(f32[4,64,256]{2,1,0:T(8,128)} %get-tuple-element.52), channel_id=1, source_target_pairs={{0,32},{16,48},{32,0},{48,16},{64,96},{80,112},{96,64},{112,80},{1... | collective-permute-start | bytes 786440 | tf_op jit(solution)/shard_map/ppermute | solution.py:451
  52.7 2.7 %collective-permute-start.5 = (f32[4,64,256]{2,1,0:T(8,128)}, f32[4,64,256]{2,1,0:T(8,128)S(1)}, u32[]{:S(2)}, u32[]{:S(2)}) collective-permute-start(f32[4,64,256]{2,1,0:T(8,128)} %get-tuple-element.53), channel_id=1, source_target_pairs={{0,64},{16,80},{32,96},{48,112},{64,0},{80,16},{96,32},{112,48},{1... | collective-permute-start | bytes 786440 | tf_op jit(solution)/shard_map/ppermute | solution.py:451
  55.4 0.1 collective-permute-start.6
  55.5 3.8 %all-to-all-start.1 = ((bf16[16,64,256]{2,1,0:T(8,128)(2,1)}), bf16[16,64,256]{2,1,0:T(8,128)(2,1)S(1)}, u32[]{:S(2)}, u32[]{:S(2)}) async-start(bf16[16,64,256]{2,1,0:T(8,128)(2,1)} %get-tuple-element.55), calls=%async_computation.1 | async-start | bytes 1048576 | tf_op jit(solution)/shard_map/all_to_all | solution.py:452
  59.2 1.0 collective-permute-done.4
  60.2 6.6 %collective-permute-done.5 = f32[4,64,256]{2,1,0:T(8,128)S(1)} collective-permute-done((f32[4,64,256]{2,1,0:T(8,128)}, f32[4,64,256]{2,1,0:T(8,128)S(1)}, u32[]{:S(2)}, u32[]{:S(2)}) %collective-permute-start.5) | collective-permute-done | bytes 262176 | tf_op jit(solution)/shard_map/ppermute | solution.py:451
  66.8 2.6 %collective-permute-done.6 = f32[4,64,256]{2,1,0:T(8,128)S(1)} collective-permute-done((f32[4,64,256]{2,1,0:T(8,128)}, f32[4,64,256]{2,1,0:T(8,128)S(1)}, u32[]{:S(2)}, u32[]{:S(2)}) %collective-permute-start.6) | collective-permute-done | bytes 262176 | tf_op jit(solution)/shard_map/ppermute | solution.py:451
  69.4 1.0 add_add_fusion
  70.4 0.9 all-to-all-done.1
  71.4 0.0 copy-done.2
  71.4 6.1 %backward.1 = f32[128,128]{1,0:T(8,128)S(1)} custom-call(bf16[1024,256]{1,0:T(8,128)(2,1)S(1)} %bitcast.31, bf16[17,2,128,256]{3,2,1,0:T(8,128)(2,1)} %get-tuple-element.58.refs_1_, f32[4,256,512]{2,1,0:T(8,128)} %get-tuple-element.59.refs_2_, bf16[4,256,512]{2,1,0:T(8,128)(2,1)S(1)} %copy-done.2, bf16[128,256]{1,0:T(8,128)(2,1)S(1)} %get-tuple-element.46.pair_ref.refs_4_, ...), custom_call_target="tpu_custom_call" | custom-call | flops 4294967296 | bytes 8388608 | tf_op jit(solution)/shard_map/backward/pallas_call | solution.py:458
  77.5 0.1 collective-permute-start.8
  77.6 1.2 %collective-permute-done.8 = f32[128,128]{1,0:T(8,128)S(1)} collective-permute-done((f32[128,128]{1,0:T(8,128)S(1)}, f32[128,128]{1,0:T(8,128)S(1)}, u32[]{:S(2)}, u32[]{:S(2)}) %collective-permute-start.8) | collective-permute-done | bytes 65568 | tf_op jit(solution)/shard_map/ppermute | solution.py:315
  78.8 2.1 %collective-permute-start.10 = (f32[128,128]{1,0:T(8,128)S(1)}, f32[128,128]{1,0:T(8,128)S(1)}, u32[]{:S(2)}, u32[]{:S(2)}) collective-permute-start(f32[128,128]{1,0:T(8,128)S(1)} %add.37), channel_id=1, source_target_pairs={{0,16},{1,17},{2,18},{3,19},{4,20},{5,21},{6,22},{7,23},{8,24},{9,... | collective-permute-start | bytes 196616 | tf_op jit(solution)/shard_map/ppermute | solution.py:315
  80.9 0.0 collective-permute-start.11
  80.9 2.2 %collective-permute-start.9 = (f32[128,128]{1,0:T(8,128)S(1)}, f32[128,128]{1,0:T(8,128)S(1)}, u32[]{:S(2)}, u32[]{:S(2)}) collective-permute-start(f32[128,128]{1,0:T(8,128)S(1)} %add.37), channel_id=1, source_target_pairs={{0,2},{1,3},{2,0},{3,1},{4,6},{5,7},{6,4},{7,5},{8,10},{9,11},{10,... | collective-permute-start | bytes 196616 | tf_op jit(solution)/shard_map/ppermute | solution.py:315
  83.1 0.3 collective-permute-done.10
  83.3 4.1 %collective-permute-done.11 = f32[128,128]{1,0:T(8,128)S(1)} collective-permute-done((f32[128,128]{1,0:T(8,128)S(1)}, f32[128,128]{1,0:T(8,128)S(1)}, u32[]{:S(2)}, u32[]{:S(2)}) %collective-permute-start.11) | collective-permute-done | bytes 65568 | tf_op jit(solution)/shard_map/ppermute | solution.py:315
  87.4 0.0 collective-permute-done.9
  87.4 0.1 collective-permute-start.12
  87.5 2.3 %collective-permute-start.13 = (f32[128,128]{1,0:T(8,128)S(1)}, f32[128,128]{1,0:T(8,128)S(1)}, u32[]{:S(2)}, u32[]{:S(2)}) collective-permute-start(f32[128,128]{1,0:T(8,128)S(1)} %add_add_fusion.2), channel_id=1, source_target_pairs={{0,8},{1,9},{2,10},{3,11},{4,12},{5,13},{6,14},{7,15},{8,0},{9,1},... | collective-permute-start | bytes 196616 | tf_op jit(solution)/shard_map/ppermute | solution.py:315
  89.8 2.4 %collective-permute-start.14 = (f32[128,128]{1,0:T(8,128)S(1)}, f32[128,128]{1,0:T(8,128)S(1)}, u32[]{:S(2)}, u32[]{:S(2)}) collective-permute-start(f32[128,128]{1,0:T(8,128)S(1)} %add_add_fusion.2), channel_id=1, source_target_pairs={{0,12},{1,13},{2,14},{3,15},{4,8},{5,9},{6,10},{7,11},{8,4},{9,5},... | collective-permute-start | bytes 196616 | tf_op jit(solution)/shard_map/ppermute | solution.py:315
  92.2 0.7 collective-permute-start.7
  92.9 0.0 collective-permute-done.12
  92.9 0.6 collective-permute-done.13
  93.5 1.8 %collective-permute-done.14 = f32[128,128]{1,0:T(8,128)S(1)} collective-permute-done((f32[128,128]{1,0:T(8,128)S(1)}, f32[128,128]{1,0:T(8,128)S(1)}, u32[]{:S(2)}, u32[]{:S(2)}) %collective-permute-start.14) | collective-permute-done | bytes 65568 | tf_op jit(solution)/shard_map/ppermute | solution.py:315
  95.3 0.4 collective-permute-start.15
  95.6 2.7 %collective-permute-start.16 = (f32[128,128]{1,0:T(8,128)S(1)}, f32[128,128]{1,0:T(8,128)S(1)}, u32[]{:S(2)}, u32[]{:S(2)}) collective-permute-start(f32[128,128]{1,0:T(8,128)S(1)} %add_add_fusion.1.a_ref), channel_id=1, source_target_pairs={{0,64},{1,65},{2,66},{3,67},{4,68},{5,69},{6,70},{7,71},{8,72},{9,... | collective-permute-start | bytes 196616 | tf_op jit(solution)/shard_map/ppermute | solution.py:315
  98.4 1.7 %collective-permute-start.17 = (f32[128,128]{1,0:T(8,128)S(1)}, f32[128,128]{1,0:T(8,128)S(1)}, u32[]{:S(2)}, u32[]{:S(2)}) collective-permute-start(f32[128,128]{1,0:T(8,128)S(1)} %add_add_fusion.1.a_ref), channel_id=1, source_target_pairs={{0,96},{1,97},{2,98},{3,99},{4,100},{5,101},{6,102},{7,103},{8,104... | collective-permute-start | bytes 196616 | tf_op jit(solution)/shard_map/ppermute | solution.py:315
  100.1 0.0 collective-permute-done.7
  100.1 0.7 slice_add_fusion
  100.7 0.0 collective-permute-done.15.b_ref
  100.8 0.7 collective-permute-done.16.c_ref
  101.4 2.4 %collective-permute-done.17.d_ref = f32[128,128]{1,0:T(8,128)S(1)} collective-permute-done((f32[128,128]{1,0:T(8,128)S(1)}, f32[128,128]{1,0:T(8,128)S(1)}, u32[]{:S(2)}, u32[]{:S(2)}) %collective-permute-start.17) | collective-permute-done | bytes 65568 | tf_op jit(solution)/shard_map/ppermute | solution.py:315
  103.9 0.8 finish.1
  (6 shorter events, 0.1 us)
Async XLA Ops:
  4.1 7.2 %collective-permute-start = (bf16[32,80]{1,0:T(8,128)(2,1)S(1)}, bf16[32,80]{1,0:T(8,128)(2,1)S(1)}, u32[]{:S(2)}, u32[]{:S(2)}) collective-permute-start(bf16[32,80]{1,0:T(8,128)(2,1)S(1)} %get-tuple-element.35), channel_id=1, source_target_pairs={{0,16},{16,32},{32,48},{48,64},{64,80},{80,96},{96,112},{1,17},{17... | collective-permute-start | bytes 15368 | tf_op jit(solution)/shard_map/ppermute | solution.py:344
  7.7 5.5 %collective-permute-start.1 = (bf16[32,80]{1,0:T(8,128)(2,1)S(1)}, bf16[32,80]{1,0:T(8,128)(2,1)S(1)}, u32[]{:S(2)}, u32[]{:S(2)}) collective-permute-start(bf16[32,80]{1,0:T(8,128)(2,1)S(1)} %get-tuple-element.36), channel_id=1, source_target_pairs={{16,0},{32,16},{48,32},{64,48},{80,64},{96,80},{112,96},{17,1},{33... | collective-permute-start | bytes 15368 | tf_op jit(solution)/shard_map/ppermute | solution.py:345
  13.4 6.8 %collective-permute-start.2 = (bf16[128,80]{1,0:T(8,128)(2,1)S(1)}, bf16[128,80]{1,0:T(8,128)(2,1)S(1)}, u32[]{:S(2)}, u32[]{:S(2)}) collective-permute-start(bf16[128,80]{1,0:T(8,128)(2,1)S(1)} %get-tuple-element.67), channel_id=1, source_target_pairs={{0,1},{1,2},{2,3},{3,4},{4,5},{5,6},{6,7},{7,8},{8,9},{9,10},{10,1... | collective-permute-start | bytes 61448 | tf_op jit(solution)/shard_map/ppermute | solution.py:383
  14.7 6.2 %collective-permute-start.3 = (bf16[128,80]{1,0:T(8,128)(2,1)S(1)}, bf16[128,80]{1,0:T(8,128)(2,1)S(1)}, u32[]{:S(2)}, u32[]{:S(2)}) collective-permute-start(bf16[128,80]{1,0:T(8,128)(2,1)S(1)} %get-tuple-element.66), channel_id=1, source_target_pairs={{1,0},{2,1},{3,2},{4,3},{5,4},{6,5},{7,6},{8,7},{9,8},{10,9},{11,1... | collective-permute-start | bytes 61448 | tf_op jit(solution)/shard_map/ppermute | solution.py:384
  20.9 26.5 %copy-start = (bf16[4,256,256]{2,1,0:T(8,128)(2,1)S(1)}, bf16[4,256,256]{2,1,0:T(8,128)(2,1)}, u32[]{:S(2)}) copy-start(bf16[4,256,256]{2,1,0:T(8,128)(2,1)} %refs_2_.1) | copy-start | bytes 1572868
  20.9 26.5 %copy-start.1 = (bf16[4,8,32,256]{3,2,1,0:T(8,128)(2,1)S(1)}, bf16[4,8,32,256]{3,2,1,0:T(8,128)(2,1)}, u32[]{:S(2)}) copy-start(bf16[4,8,32,256]{3,2,1,0:T(8,128)(2,1)} %param.15) | copy-start | bytes 1572868
  23.6 23.9 %all-to-all-start = ((bf16[16,64,256]{2,1,0:T(8,128)(2,1)}), bf16[16,64,256]{2,1,0:T(8,128)(2,1)S(1)}, u32[]{:S(2)}, u32[]{:S(2)}) async-start(bf16[16,64,256]{2,1,0:T(8,128)(2,1)} %bitcast.32), calls=%async_computation | async-start | bytes 1048576 | tf_op jit(solution)/shard_map/all_to_all | solution.py:426
  35.1 36.3 %copy-start.2 = (bf16[4,256,512]{2,1,0:T(8,128)(2,1)S(1)}, bf16[4,256,512]{2,1,0:T(8,128)(2,1)}, u32[]{:S(2)}) copy-start(bf16[4,256,512]{2,1,0:T(8,128)(2,1)} %get-tuple-element.60.refs_3_) | copy-start | bytes 3145732
  50.7 9.5 %collective-permute-start.4 = (f32[4,64,256]{2,1,0:T(8,128)}, f32[4,64,256]{2,1,0:T(8,128)S(1)}, u32[]{:S(2)}, u32[]{:S(2)}) collective-permute-start(f32[4,64,256]{2,1,0:T(8,128)} %get-tuple-element.52), channel_id=1, source_target_pairs={{0,32},{16,48},{32,0},{48,16},{64,96},{80,112},{96,64},{112,80},{1... | collective-permute-start | bytes 786440 | tf_op jit(solution)/shard_map/ppermute | solution.py:451
  52.7 14.2 %collective-permute-start.5 = (f32[4,64,256]{2,1,0:T(8,128)}, f32[4,64,256]{2,1,0:T(8,128)S(1)}, u32[]{:S(2)}, u32[]{:S(2)}) collective-permute-start(f32[4,64,256]{2,1,0:T(8,128)} %get-tuple-element.53), channel_id=1, source_target_pairs={{0,64},{16,80},{32,96},{48,112},{64,0},{80,16},{96,32},{112,48},{1... | collective-permute-start | bytes 786440 | tf_op jit(solution)/shard_map/ppermute | solution.py:451
  55.4 14.0 %collective-permute-start.6 = (f32[4,64,256]{2,1,0:T(8,128)}, f32[4,64,256]{2,1,0:T(8,128)S(1)}, u32[]{:S(2)}, u32[]{:S(2)}) collective-permute-start(f32[4,64,256]{2,1,0:T(8,128)} %get-tuple-element.54), channel_id=1, source_target_pairs={{0,96},{16,112},{32,64},{48,80},{64,32},{80,48},{96,0},{112,16},{1... | collective-permute-start | bytes 786440 | tf_op jit(solution)/shard_map/ppermute | solution.py:451
  55.5 15.9 %all-to-all-start.1 = ((bf16[16,64,256]{2,1,0:T(8,128)(2,1)}), bf16[16,64,256]{2,1,0:T(8,128)(2,1)S(1)}, u32[]{:S(2)}, u32[]{:S(2)}) async-start(bf16[16,64,256]{2,1,0:T(8,128)(2,1)} %get-tuple-element.55), calls=%async_computation.1 | async-start | bytes 1048576 | tf_op jit(solution)/shard_map/all_to_all | solution.py:452
  77.5 1.3 %collective-permute-start.8 = (f32[128,128]{1,0:T(8,128)S(1)}, f32[128,128]{1,0:T(8,128)S(1)}, u32[]{:S(2)}, u32[]{:S(2)}) collective-permute-start(f32[128,128]{1,0:T(8,128)S(1)} %backward.1), channel_id=1, source_target_pairs={{0,1},{1,0},{2,3},{3,2},{4,5},{5,4},{6,7},{7,6},{8,9},{9,8},{10,11... | collective-permute-start | bytes 196616 | tf_op jit(solution)/shard_map/ppermute | solution.py:315
  78.8 4.5 %collective-permute-start.10 = (f32[128,128]{1,0:T(8,128)S(1)}, f32[128,128]{1,0:T(8,128)S(1)}, u32[]{:S(2)}, u32[]{:S(2)}) collective-permute-start(f32[128,128]{1,0:T(8,128)S(1)} %add.37), channel_id=1, source_target_pairs={{0,16},{1,17},{2,18},{3,19},{4,20},{5,21},{6,22},{7,23},{8,24},{9,... | collective-permute-start | bytes 196616 | tf_op jit(solution)/shard_map/ppermute | solution.py:315
  80.9 6.5 %collective-permute-start.11 = (f32[128,128]{1,0:T(8,128)S(1)}, f32[128,128]{1,0:T(8,128)S(1)}, u32[]{:S(2)}, u32[]{:S(2)}) collective-permute-start(f32[128,128]{1,0:T(8,128)S(1)} %add.37), channel_id=1, source_target_pairs={{0,18},{1,19},{2,16},{3,17},{4,22},{5,23},{6,20},{7,21},{8,26},{9,... | collective-permute-start | bytes 196616 | tf_op jit(solution)/shard_map/ppermute | solution.py:315
  80.9 6.5 %collective-permute-start.9 = (f32[128,128]{1,0:T(8,128)S(1)}, f32[128,128]{1,0:T(8,128)S(1)}, u32[]{:S(2)}, u32[]{:S(2)}) collective-permute-start(f32[128,128]{1,0:T(8,128)S(1)} %add.37), channel_id=1, source_target_pairs={{0,2},{1,3},{2,0},{3,1},{4,6},{5,7},{6,4},{7,5},{8,10},{9,11},{10,... | collective-permute-start | bytes 196616 | tf_op jit(solution)/shard_map/ppermute | solution.py:315
  87.4 5.5 %collective-permute-start.12 = (f32[128,128]{1,0:T(8,128)S(1)}, f32[128,128]{1,0:T(8,128)S(1)}, u32[]{:S(2)}, u32[]{:S(2)}) collective-permute-start(f32[128,128]{1,0:T(8,128)S(1)} %add_add_fusion.2), channel_id=1, source_target_pairs={{0,4},{1,5},{2,6},{3,7},{4,0},{5,1},{6,2},{7,3},{8,12},{9,13},{10,... | collective-permute-start | bytes 196616 | tf_op jit(solution)/shard_map/ppermute | solution.py:315
  87.5 6.0 %collective-permute-start.13 = (f32[128,128]{1,0:T(8,128)S(1)}, f32[128,128]{1,0:T(8,128)S(1)}, u32[]{:S(2)}, u32[]{:S(2)}) collective-permute-start(f32[128,128]{1,0:T(8,128)S(1)} %add_add_fusion.2), channel_id=1, source_target_pairs={{0,8},{1,9},{2,10},{3,11},{4,12},{5,13},{6,14},{7,15},{8,0},{9,1},... | collective-permute-start | bytes 196616 | tf_op jit(solution)/shard_map/ppermute | solution.py:315
  89.8 5.5 %collective-permute-start.14 = (f32[128,128]{1,0:T(8,128)S(1)}, f32[128,128]{1,0:T(8,128)S(1)}, u32[]{:S(2)}, u32[]{:S(2)}) collective-permute-start(f32[128,128]{1,0:T(8,128)S(1)} %add_add_fusion.2), channel_id=1, source_target_pairs={{0,12},{1,13},{2,14},{3,15},{4,8},{5,9},{6,10},{7,11},{8,4},{9,5},... | collective-permute-start | bytes 196616 | tf_op jit(solution)/shard_map/ppermute | solution.py:315
  92.2 7.9 %collective-permute-start.7 = (f32[4,32,256]{2,1,0:T(8,128)S(1)}, f32[4,32,256]{2,1,0:T(8,128)S(1)}, u32[]{:S(2)}, u32[]{:S(2)}) collective-permute-start(f32[4,32,256]{2,1,0:T(8,128)S(1)} %split.7), channel_id=1, source_target_pairs={{0,16},{16,0},{32,48},{48,32},{64,80},{80,64},{96,112},{112,96},{1... | collective-permute-start | bytes 393224 | tf_op jit(solution)/shard_map/ppermute | solution.py:455
  95.3 5.5 %collective-permute-start.15 = (f32[128,128]{1,0:T(8,128)S(1)}, f32[128,128]{1,0:T(8,128)S(1)}, u32[]{:S(2)}, u32[]{:S(2)}) collective-permute-start(f32[128,128]{1,0:T(8,128)S(1)} %add_add_fusion.1.a_ref), channel_id=1, source_target_pairs={{0,32},{1,33},{2,34},{3,35},{4,36},{5,37},{6,38},{7,39},{8,40},{9,... | collective-permute-start | bytes 196616 | tf_op jit(solution)/shard_map/ppermute | solution.py:315
  95.6 5.8 %collective-permute-start.16 = (f32[128,128]{1,0:T(8,128)S(1)}, f32[128,128]{1,0:T(8,128)S(1)}, u32[]{:S(2)}, u32[]{:S(2)}) collective-permute-start(f32[128,128]{1,0:T(8,128)S(1)} %add_add_fusion.1.a_ref), channel_id=1, source_target_pairs={{0,64},{1,65},{2,66},{3,67},{4,68},{5,69},{6,70},{7,71},{8,72},{9,... | collective-permute-start | bytes 196616 | tf_op jit(solution)/shard_map/ppermute | solution.py:315
  98.4 5.5 %collective-permute-start.17 = (f32[128,128]{1,0:T(8,128)S(1)}, f32[128,128]{1,0:T(8,128)S(1)}, u32[]{:S(2)}, u32[]{:S(2)}) collective-permute-start(f32[128,128]{1,0:T(8,128)S(1)} %add_add_fusion.1.a_ref), channel_id=1, source_target_pairs={{0,96},{1,97},{2,98},{3,99},{4,100},{5,101},{6,102},{7,103},{8,104... | collective-permute-start | bytes 196616 | tf_op jit(solution)/shard_map/ppermute | solution.py:315

commit v5 on v4

--- a/solution.py
+++ b/solution.py
@@ -103,8 +103,7 @@
 
 
 def inner_kernel(
-    feat_ref, ylo_ref, yhi_ref, table_ref, band_ref, emb_hbm, slope_hbm, hidden_ref, edge_ref,
-    emb_ref, slope_ref, sem,
+    feat_ref, ylo_ref, yhi_ref, table_ref, band_ref, emb_ref, slope_ref, hidden_ref, edge_ref,
 ):
     table = table_ref[...]
     row = iota((128, 80), 0)
@@ -117,8 +116,6 @@
         f = jnp.where(row == 64, ylo[z : z + 1, :], f)
         f = jnp.where(row == 127, yhi[z : z + 1, :], f)
         emb_ref[(z + 1) // 2, (z + 1) % 2] = dot(f.astype(BF16), table, 1, 0).astype(BF16)
-    copies = [pltpu.make_async_copy(emb_ref, emb_hbm, sem.at[0])]
-    copies[0].start()
     for bc in range(4):
         b, c = bc // 2, bc % 2
         for half in range(2):
@@ -133,10 +130,6 @@
                 edge_ref[1, b] = acc[:, 224:]
             at = slice(256 * half, 256 * half + 256)
             hidden_ref[bc, :, at], slope_ref[bc, :, at] = activate(acc)
-        copies.append(pltpu.make_async_copy(slope_ref.at[bc], slope_hbm.at[bc], sem.at[1 + bc]))
-        copies[-1].start()
-    for copy in copies:
-        copy.wait()
 
 
 def pair_rows(hidden_ref, pair):
@@ -158,7 +151,7 @@
                 run = RUNS[b][ty]
                 acc = acc + dot(band_ref[3 * ty + 2 * side], plane[run : run + 32], 1, 1)
             at = slice(480 * side, 480 * side + 32)
-            hidden_ref[2 * b + side, :, at], slope_ref[side, b] = activate(acc)
+            hidden_ref[2 * b + side, :, at], slope_ref[:, 64 * side + 32 * b : 64 * side + 32 * b + 32] = activate(acc)
     copies = [pltpu.make_async_copy(hidden_ref, hidden_hbm, sem.at[0])]
     copies[0].start()
     for pair in range(4):
@@ -178,25 +171,30 @@
         copy.wait()
 
 
-def mix_kernel(scale, me_ref, coarse_ref, mix_ref, cot_ref, mid_ref, grad_ref, *more_refs):
+def mixed(coarse_ref, mix_ref, cot_ref):
+    width = mix_ref.shape[1]
+    flat = coarse_ref[...].reshape(width, 256).T
+    pre = dot(flat, mix_ref[0], 1, 1)
+    sigma = jax.nn.sigmoid(pre)
+    grad = cot_ref[0].astype(F32) * (sigma * (1.0 + pre * (1.0 - sigma)))
+    return flat, pre * sigma, grad.astype(BF16).T
+
+
+def mix_kernel(coarse_ref, mix_ref, cot_ref, grad_ref):
+    _, _, turned = mixed(coarse_ref, mix_ref, cot_ref)
+    grad_ref[...] = dot(mix_ref[0].T, turned, 1, 0).astype(BF16).reshape(grad_ref.shape)
+
+
+def mix_grad_kernel(scale, me_ref, coarse_ref, mix_ref, cot_ref, mid_ref, *more_refs):
     *share_refs, total_ref = more_refs
-    width = mix_ref.shape[1]
-    coarse = coarse_ref[...].reshape(width, 256)
-    mix = mix_ref[0]
-    flat = coarse.T
-    pre = dot(flat, mix, 1, 1)
-    sigma = jax.nn.sigmoid(pre)
-    mid_ref[0] = (pre * sigma).astype(BF16)
-    grad = (cot_ref[0].astype(F32) * (sigma * (1.0 + pre * (1.0 - sigma)))).astype(BF16)
-    turned = grad.T
+    flat, mid, turned = mixed(coarse_ref, mix_ref, cot_ref)
+    mid_ref[0] = mid.astype(BF16)
     total_ref[...] = dot(turned, flat, 1, 0) * scale
-    rows = width // (2 * len(share_refs))
+    rows = total_ref.shape[0] // (2 * len(share_refs))
     for place in range(2 * len(share_refs)):
         start = pl.multiple_of(jnp.bitwise_xor(me_ref[0], place) * rows, rows)
         at = place % 2 * rows
         share_refs[place // 2][0, at : at + rows, :] = total_ref[pl.ds(start, rows), :]
-    out = dot(mix.T, turned, 1, 0)
-    grad_ref[...] = out.astype(BF16).reshape(grad_ref.shape)
 
 
 def fold(value, step):
@@ -212,9 +210,13 @@
 
 def backward_kernel(
     down_scale, conv_scale, cgrad_ref, emb_hbm, slope_hbm, hidden_ref, pair_ref, pair_t_ref, face_ref, edge_ref,
-    out_ref, turn_a, turn_b, turned_pg, emb_ref, slope_ref, sem,
+    out_ref, turn_a, turn_b, turned_pg, emb_in, slope_in, sem,
 ):
-    copies = fetch((slope_hbm, emb_hbm), (slope_ref, emb_ref), sem)
+    copies = [
+        pltpu.make_async_copy(slope_hbm, slope_in, sem.at[0]),
+        pltpu.make_async_copy(emb_hbm, emb_in, sem.at[1]),
+    ]
+    copies[0].start()
     for half in range(2):
         turn_b[half] = cgrad_ref[:, 128 * half : 128 * half + 128].astype(F32)
     for half in range(2):
@@ -225,6 +227,7 @@
                 turn_a[64 * x2 : 64 * x2 + 64, 128 * quad : 128 * quad + 128] = jnp.concatenate(
                     [p[:, 32 * k : 32 * k + 32] for p in pieces], axis=1
                 )
+    copies[1].start()
     cg_t = turn_a[...].astype(BF16)
     pairs = [cg_t[128 * pair : 128 * pair + 128, :] for pair in range(4)]
     down = None
@@ -236,18 +239,16 @@
     right = down[:, 128:] + pltpu.roll(down[:, 128:], 32, 1)
     out_ref[0:64, :] = jnp.where(iota((64, 128), 1) // 32 % 2 == 0, left, right)
     copies[0].wait()
-    for side in range(2):
-        for b in range(2):
-            slope_ref[2 * b + side, :, 480 * side : 480 * side + 32] = edge_ref[side, b]
     for pair in range(4):
         hgrad = dot(pair_t_ref[...], pairs[pair], 1, 0)
         at = slice(64 * pair, 64 * pair + 64)
         for bc in range(4):
-            grad = hgrad[64 * bc : 64 * bc + 64] * slope_ref[bc, at, :]
-            turned_pg[bc, at, :] = grad.astype(BF16)
+            rows = hgrad[64 * bc : 64 * bc + 64]
+            turned_pg[bc, at, :] = (rows * slope_in[bc, at, :]).astype(BF16)
+            edge = slice(480 * (bc % 2), 480 * (bc % 2) + 32)
+            low = 64 * (bc % 2) + 32 * (bc // 2)
+            turned_pg[bc, at, edge] = (rows[:, edge] * edge_ref[at, low : low + 32]).astype(BF16)
     copies[1].wait()
-    emb_ref[0, 0] = face_ref[0]
-    emb_ref[16, 1] = face_ref[1]
     lane_x = iota((16, 256), 1) // 16
     own = iota((8, 128), 1) // 16 == iota((8, 128), 0)
     for ty in range(3):
@@ -256,7 +257,12 @@
             for bc in range(4):
                 b, c = bc // 2, bc % 2
                 for half in range(2):
-                    rows = cells_of(emb_ref, b, c, ty, tz, half)
+                    rows = cells_of(emb_in, b, c, ty, tz, half)
+                    run = RUNS[b][ty]
+                    if c + tz == 0 and half == 0:
+                        rows = jnp.concatenate([face_ref[0, run : run + 32, :], rows[32:]], axis=0)
+                    if c + tz == 3 and half == 1:
+                        rows = jnp.concatenate([rows[:224], face_ref[1, run : run + 32, :]], axis=0)
                     part = dot(turned_pg[bc, :, 256 * half : 256 * half + 256], rows, 1, 0)
                     acc = part if acc is None else acc + part
             for tx in range(3):
@@ -385,18 +391,13 @@
     embedded, slope, hidden, edge = pl.pallas_call(
         inner_kernel,
         out_shape=(
-            pltpu.HBM((17, 2, 128, 256), BF16),
-            pltpu.HBM((4, 256, 512), F32),
+            shape((17, 2, 128, 256), BF16),
+            shape((4, 256, 512), F32),
             shape((4, 256, 512), BF16),
             shape((2, 2, 256, 32), F32),
         ),
         in_specs=[VMEM] * 5,
-        out_specs=(HBM, HBM, VMEM, VMEM),
-        scratch_shapes=[
-            pltpu.VMEM((17, 2, 128, 256), BF16),
-            pltpu.VMEM((4, 256, 512), F32),
-            pltpu.SemaphoreType.DMA((5,)),
-        ],
+        out_specs=(VMEM,) * 4,
         compiler_params=params(12),
         cost_estimate=cost(3 << 30, 10 << 20),
         name="inner",
@@ -405,7 +406,7 @@
         outer_kernel,
         out_shape=(
             shape((2, 128, 256), BF16),
-            shape((2, 2, 256, 32), F32),
+            shape((256, 128), F32),
             pltpu.HBM((4, 256, 512), BF16),
             pltpu.HBM((1024, 256), BF16),
         ),
@@ -428,29 +429,40 @@
     )
     block = lambda *dims: pl.BlockSpec(dims, lambda c: (c,) + (0,) * (len(dims) - 1))
     shares = count_y // 2
-    mid, back, *mix_parts = pl.pallas_call(
-        lambda *refs: mix_kernel(1.0 / math.sqrt(8 * 32 * count_y), *refs),
+    mix_specs = [
+        pl.BlockSpec((count_z, 16, 256), lambda c: (0, c, 0)),
+        block(1, width, width),
+        block(1, 256, width),
+    ]
+    cotangent_rows = cotangent.reshape(mine, 256, width)
+    back = pl.pallas_call(
+        mix_kernel,
         grid=(mine,),
-        out_shape=[shape((mine, 256, width), BF16), shape((count_z, mine * 16, 256), BF16)]
+        out_shape=shape((count_z, mine * 16, 256), BF16),
+        in_specs=mix_specs,
+        out_specs=pl.BlockSpec((count_z, 16, 256), lambda c: (0, c, 0)),
+        compiler_params=params(8),
+        cost_estimate=cost(mine * 2 * 2 * 256 * width * width, 2 << 20),
+        name="mix",
+    )(sent, mix_weight, cotangent_rows)
+    coarse_grad = lax.all_to_all(back, "sz", split_axis=0, concat_axis=0, tiled=True)
+    sent, back = lax.optimization_barrier((sent, back))
+    mid, *mix_parts = pl.pallas_call(
+        lambda *refs: mix_grad_kernel(1.0 / math.sqrt(8 * 32 * count_y), *refs),
+        grid=(mine,),
+        out_shape=[shape((mine, 256, width), BF16)]
         + [pltpu.HBM((mine, width // shares, width), F32)] * shares,
-        in_specs=[
-            pl.BlockSpec(memory_space=pltpu.SMEM),
-            pl.BlockSpec((count_z, 16, 256), lambda c: (0, c, 0)),
-            block(1, width, width),
-            block(1, 256, width),
-        ],
-        out_specs=[block(1, 256, width), pl.BlockSpec((count_z, 16, 256), lambda c: (0, c, 0))]
-        + [block(1, width // shares, width)] * shares,
+        in_specs=[pl.BlockSpec(memory_space=pltpu.SMEM)] + mix_specs,
+        out_specs=[block(1, 256, width)] + [block(1, width // shares, width)] * shares,
         scratch_shapes=[pltpu.VMEM((width, width), F32)],
-        compiler_params=params(12),
-        cost_estimate=cost(mine * 3 * 2 * 256 * width * width, 5 << 20),
-        name="mix",
-    )(lax.axis_index("sy")[None], sent, mix_weight, cotangent.reshape(mine, 256, width))
+        compiler_params=params(8),
+        cost_estimate=cost(mine * 2 * 2 * 256 * width * width, 3 << 20),
+        name="mix_grad",
+    )(lax.axis_index("sy")[None], sent, mix_weight, cotangent_rows)
+    *mix_parts, coarse_grad = lax.optimization_barrier((*mix_parts, coarse_grad))
     mix_sum = mix_parts[0]
     for k, part in enumerate(mix_parts[1:], 1):
         mix_sum = mix_sum + lax.ppermute(part, "sy", [(i, i ^ (2 * k)) for i in range(count_y)])
-    coarse_grad = lax.all_to_all(back, "sz", split_axis=0, concat_axis=0, tiled=True)
-    mix_sum, coarse_grad = lax.optimization_barrier((mix_sum, coarse_grad))
     mine_last, other = jnp.split(mix_sum, 2, axis=1)
     mix_grad = mine_last + lax.ppermute(other, "sy", [(i, i ^ 1) for i in range(count_y)])
 
@@ -470,7 +482,7 @@
             pltpu.VMEM((4, 256, 512), F32),
             pltpu.SemaphoreType.DMA((2,)),
         ],
-        compiler_params=params(16),
+        compiler_params=params(12),
         cost_estimate=cost(4 << 30, 8 << 20),
         name="backward",
     )(

time: 105 us -> 107 us (1.019)
  blocking collectives: 0 us -> 23.4 us
  starting transfers between devices: 42 us -> 29.6 us
  waiting for transfers between devices: 37.2 us -> 27.5 us
  Pallas kernels: 22.8 us -> 24.6 us
    all_to_all x0 -> x1, blocking collectives: none -> 23.4 us  [per_device(): lax.all_to_all(coarse.reshape(count_z, mine * 16, 256), 'sz', split_axis=...]
    all_to_all x1 -> x0, waiting for transfers between devices: 12.3 us -> none  [per_device(): lax.all_to_all(coarse.reshape(count_z, mine * 16, 256), 'sz', split_axis=...]
    all_to_all x1 -> x0, starting transfers between devices: 11.5 us -> none  [per_device(): lax.all_to_all(coarse.reshape(count_z, mine * 16, 256), 'sz', split_axis=...]
    all_to_all x1, waiting for transfers between devices: 0.93 us -> 9.14 us  [per_device(): lax.all_to_all(back, 'sz', split_axis=0, concat_axis=0, tiled=True)]
    ppermute x10, waiting for transfers between devices: 11.1 us -> 5.1 us  [exchanged(): lax.ppermute(value, ('sy', 'sz'), [(i, i ^ m) for i in range(count)])]
    pallas_call x2 -> x3, Pallas kernels: 7.41 us -> 9.16 us  [the longest x1 3.35 us: per_device(): pl.pallas_call(inner_kernel, out_shape=(shape((17, 2, 128, 256), BF16), s...]
    ppermute x10, starting transfers between devices: 13.9 us -> 12.6 us  [exchanged(): lax.ppermute(value, ('sy', 'sz'), [(i, i ^ m) for i in range(count)])]
  transfers between devices with their start and end apart: 20 -> 19, of which waited for: 14 -> 9; matrix products, arithmetic and copies ran while one was open for 2% -> 0% of each run, Pallas kernels for 6% -> 9%
where the time goes in v5:
time: 107 us
  starting transfers between devices  29.6 us (28%)
  waiting for transfers between devices  27.5 us (26%)
  Pallas kernels  24.6 us (23%)
  blocking collectives  23.4 us (22%)
    all_to_all x1, blocking collectives, per_device(): lax.all_to_all(coarse.reshape(count_z, mine * 16, 256), 'sz', split_axis=...  23.4 us
    ppermute x10, starting transfers between devices, exchanged(): lax.ppermute(value, ('sy', 'sz'), [(i, i ^ m) for i in range(count)])  12.6 us
    ppermute x3, waiting for transfers between devices, per_device(): lax.ppermute(part, 'sy', [(i, i ^ 2 * k) for i in range(count_y)])  9.85 us
    all_to_all x1, waiting for transfers between devices, per_device(): lax.all_to_all(back, 'sz', split_axis=0, concat_axis=0, tiled=True)  9.14 us
    pallas_call x1, Pallas kernels, per_device(): pl.pallas_call(lambda *refs: backward_kernel(1.0 / math.sqrt(cells // 8),...  6.11 us
    ppermute x10, waiting for transfers between devices, exchanged(): lax.ppermute(value, ('sy', 'sz'), [(i, i ^ m) for i in range(count)])  5.1 us
    ppermute x3, starting transfers between devices, per_device(): lax.ppermute(part, 'sy', [(i, i ^ 2 * k) for i in range(count_y)])  4.7 us
    all_to_all x1, starting transfers between devices, per_device(): lax.all_to_all(back, 'sz', split_axis=0, concat_axis=0, tiled=True)  3.75 us
  transfers between devices with their start and end apart: 19, of which 9 were waited for; matrix products, arithmetic and copies ran while one was open for 0% of the time, Pallas kernels for 9%

profile of v5, /device:TPU:0, one launch (start us, length us, event | category | flops | bytes accessed | tf_op | source)
XLA Modules:
  0.0 107.0 jit_solution(17710400792158825136)
XLA Ops:
  0.6 3.5 %features.1 = (bf16[32,128,80]{2,1,0:T(8,128)(2,1)S(1)}, bf16[32,80]{1,0:T(8,128)(2,1)S(1)}, bf16[32,80]{1,0:T(8,128)(2,1)S(1)}) custom-call(s32[16,32,64]{2,1,0:T(8,128)} %bitcast.34, bf16[16,32,64]{2,1,0:T(8,128)(2,1)} %bitcast.35), custom_call_target="tpu_custom_call" | custom-call | flops 41943040 | bytes 2097152 | tf_op jit(solution)/shard_map/features/pallas_call | solution.py:331
  4.1 3.6 %collective-permute-start = (bf16[32,80]{1,0:T(8,128)(2,1)S(1)}, bf16[32,80]{1,0:T(8,128)(2,1)S(1)}, u32[]{:S(2)}, u32[]{:S(2)}) collective-permute-start(bf16[32,80]{1,0:T(8,128)(2,1)S(1)} %get-tuple-element.38), channel_id=1, source_target_pairs={{0,16},{16,32},{32,48},{48,64},{64,80},{80,96},{96,112},{1,17},{17... | collective-permute-start | bytes 15368 | tf_op jit(solution)/shard_map/ppermute | solution.py:350
  7.7 1.3 %collective-permute-start.1 = (bf16[32,80]{1,0:T(8,128)(2,1)S(1)}, bf16[32,80]{1,0:T(8,128)(2,1)S(1)}, u32[]{:S(2)}, u32[]{:S(2)}) collective-permute-start(bf16[32,80]{1,0:T(8,128)(2,1)S(1)} %get-tuple-element.39), channel_id=1, source_target_pairs={{16,0},{32,16},{48,32},{64,48},{80,64},{96,80},{112,96},{17,1},{33... | collective-permute-start | bytes 15368 | tf_op jit(solution)/shard_map/ppermute | solution.py:351
  9.0 2.3 %weights.1 = (bf16[9,256,256]{2,1,0:T(8,128)(2,1)S(1)}, bf16[128,256]{1,0:T(8,128)(2,1)S(1)}, bf16[256,128]{1,0:T(8,128)(2,1)S(1)}, bf16[80,256]{1,0:T(8,128)(2,1)S(1)}) custom-call(bf16[16,16,27]{2,1,0:T(8,128)(2,1)} %bitcast.38, bf16[8,16,64]{2,1,0:T(8,128)(2,1)} %bitcast.40, bf16[4,16]{1,0:T(4,128)(2,1)} %mat_hbm.1, bf16[1,16]{1,0:T(2,128)(2,1)} %bitcast.41), custom_call_target="tpu_custom_call" | custom-call | flops 56623104 | bytes 3145728 | tf_op jit(solution)/shard_map/weights/pallas_call | solution.py:352
  11.4 0.0 collective-permute-done.ylo_ref
  11.4 1.9 %collective-permute-done.1.yhi_ref = bf16[32,80]{1,0:T(8,128)(2,1)S(1)} collective-permute-done((bf16[32,80]{1,0:T(8,128)(2,1)S(1)}, bf16[32,80]{1,0:T(8,128)(2,1)S(1)}, u32[]{:S(2)}, u32[]{:S(2)}) %collective-permute-start.1) | collective-permute-done | bytes 5152 | tf_op jit(solution)/shard_map/ppermute | solution.py:351
  13.3 0.1 fusion
  13.4 1.3 %collective-permute-start.2 = (bf16[128,80]{1,0:T(8,128)(2,1)S(1)}, bf16[128,80]{1,0:T(8,128)(2,1)S(1)}, u32[]{:S(2)}, u32[]{:S(2)}) collective-permute-start(bf16[128,80]{1,0:T(8,128)(2,1)S(1)} %get-tuple-element.73), channel_id=1, source_target_pairs={{0,1},{1,2},{2,3},{3,4},{4,5},{5,6},{6,7},{7,8},{8,9},{9,10},{10,1... | collective-permute-start | bytes 61448 | tf_op jit(solution)/shard_map/ppermute | solution.py:389
  14.7 1.3 %collective-permute-start.3 = (bf16[128,80]{1,0:T(8,128)(2,1)S(1)}, bf16[128,80]{1,0:T(8,128)(2,1)S(1)}, u32[]{:S(2)}, u32[]{:S(2)}) collective-permute-start(bf16[128,80]{1,0:T(8,128)(2,1)S(1)} %get-tuple-element.72), channel_id=1, source_target_pairs={{1,0},{2,1},{3,2},{4,3},{5,4},{6,5},{7,6},{8,7},{9,8},{10,9},{11,1... | collective-permute-start | bytes 61448 | tf_op jit(solution)/shard_map/ppermute | solution.py:390
  16.0 3.3 %inner.1 = (bf16[17,2,128,256]{3,2,1,0:T(8,128)(2,1)S(1)}, f32[4,256,512]{2,1,0:T(8,128)S(1)}, bf16[4,256,512]{2,1,0:T(8,128)(2,1)S(1)}, f32[2,2,256,32]{3,2,1,0:T(8,128)S(1)}) custom-call(bf16[32,128,80]{2,1,0:T(8,128)(2,1)S(1)} %get-tuple-element.46.feat_ref, bf16[32,80]{1,0:T(8,128)(2,1)S(1)} %collective-permute-done.ylo_ref, ...), custom_call_target="tpu_custom_call" | custom-call | flops 3221225472 | bytes 10485760 | tf_op jit(solution)/shard_map/inner/pallas_call | solution.py:391
  19.3 0.0 copy-start.3
  19.3 0.0 copy-start.4
  19.3 0.0 collective-permute-done.2.zlo_ref
  19.4 1.6 %collective-permute-done.3.zhi_ref = bf16[128,80]{1,0:T(8,128)(2,1)S(1)} collective-permute-done((bf16[128,80]{1,0:T(8,128)(2,1)S(1)}, bf16[128,80]{1,0:T(8,128)(2,1)S(1)}, u32[]{:S(2)}, u32[]{:S(2)}) %collective-permute-start.3) | collective-permute-done | bytes 20512 | tf_op jit(solution)/shard_map/ppermute | solution.py:390
  20.9 0.0 copy-start
  20.9 2.7 %outer.1 = (bf16[2,128,256]{2,1,0:T(8,128)(2,1)S(1)}, f32[256,128]{1,0:T(8,128)S(1)}, bf16[4,256,512]{2,1,0:T(8,128)(2,1)}, bf16[1024,256]{1,0:T(8,128)(2,1)}) custom-call(bf16[128,80]{1,0:T(8,128)(2,1)S(1)} %collective-permute-done.2.zlo_ref, bf16[128,80]{1,0:T(8,128)(2,1)S(1)} %collective-permute-done.3.zhi_ref, ...), custom_call_target="tpu_custom_call" | custom-call | flops 1073741824 | bytes 4194304 | tf_op jit(solution)/shard_map/outer/pallas_call | solution.py:405
  23.6 23.4 %all_to_all.10.coarse_ref.refs_1_ = bf16[16,64,256]{2,1,0:T(8,128)(2,1)S(1)} all-to-all(bf16[16,64,256]{2,1,0:T(8,128)(2,1)} %bitcast.33), channel_id=1, replica_groups=mesh['sy'=8,'sz'=16] {'sz'}, dimensions={0} | all-to-all | bytes 1048576 | tf_op jit(solution)/shard_map/all_to_all | solution.py:427
  47.0 0.0 copy-done.3
  47.0 0.0 copy-done.4
  47.0 0.0 copy-done
  47.1 0.0 copy-done.1
  47.1 0.0 copy-start.2
  47.1 2.8 %mix.1 = bf16[16,64,256]{2,1,0:T(8,128)(2,1)} custom-call(bf16[16,64,256]{2,1,0:T(8,128)(2,1)S(1)} %all_to_all.10.coarse_ref.refs_1_, bf16[4,256,256]{2,1,0:T(8,128)(2,1)S(1)} %copy-done, bf16[4,256,256]{2,1,0:T(8,128)(2,1)S(1)} %bitcast.30), custom_call_target="tpu_custom_call" | custom-call | flops 268435456 | bytes 2097152 | tf_op jit(solution)/shard_map/mix/pallas_call | solution.py:438
  49.9 3.8 %all-to-all-start.1 = ((bf16[16,64,256]{2,1,0:T(8,128)(2,1)}), bf16[16,64,256]{2,1,0:T(8,128)(2,1)S(1)}, u32[]{:S(2)}, u32[]{:S(2)}) async-start(bf16[16,64,256]{2,1,0:T(8,128)(2,1)} %mix.1), calls=%async_computation.1 | async-start | bytes 1048576 | tf_op jit(solution)/shard_map/all_to_all | solution.py:448
  53.7 3.0 %mix_grad.1 = (bf16[4,256,256]{2,1,0:T(8,128)(2,1)}, f32[4,64,256]{2,1,0:T(8,128)}, f32[4,64,256]{2,1,0:T(8,128)}, f32[4,64,256]{2,1,0:T(8,128)}, f32[4,64,256]{2,1,0:T(8,128)}) custom-call(s32[1]{0:T(128)} %bitcast.refs_0_, bf16[16,64,256]{2,1,0:T(8,128)(2,1)S(1)} %all_to_all.10.coarse_ref.refs_1_, bf16[4,256,256]{2,1,0:T(8,128)(2,1)S(1)} %copy-done, ...), custom_call_target="tpu_custom_call" | custom-call | flops 268435456 | bytes 3145728 | tf_op jit(solution)/shard_map/mix_grad/pallas_call | solution.py:450
  56.7 9.1 %all-to-all-done.1 = bf16[16,64,256]{2,1,0:T(8,128)(2,1)S(1)} async-done(((bf16[16,64,256]{2,1,0:T(8,128)(2,1)}), bf16[16,64,256]{2,1,0:T(8,128)(2,1)S(1)}, u32[]{:S(2)}, u32[]{:S(2)}) %all-to-all-start.1) | async-done | bytes 524320 | tf_op jit(solution)/shard_map/all_to_all | solution.py:448
  65.8 0.0 copy-done.2
  65.8 0.0 copy-start.5
  65.8 6.1 %backward.1 = f32[128,128]{1,0:T(8,128)S(1)} custom-call(bf16[1024,256]{1,0:T(8,128)(2,1)S(1)} %bitcast.32, bf16[17,2,128,256]{3,2,1,0:T(8,128)(2,1)} %copy-done.3, f32[4,256,512]{2,1,0:T(8,128)} %copy-done.4, bf16[4,256,512]{2,1,0:T(8,128)(2,1)S(1)} %copy-done.2, bf16[128,256]{1,0:T(8,128)(2,1)S(1)} %get-tuple-element.49.pair_ref.refs_4_, ...), custom_call_target="tpu_custom_call" | custom-call | flops 4294967296 | bytes 8388608 | tf_op jit(solution)/shard_map/backward/pallas_call | solution.py:470
  71.9 0.1 collective-permute-start.8
  72.0 1.2 %collective-permute-done.8 = f32[128,128]{1,0:T(8,128)S(1)} collective-permute-done((f32[128,128]{1,0:T(8,128)S(1)}, f32[128,128]{1,0:T(8,128)S(1)}, u32[]{:S(2)}, u32[]{:S(2)}) %collective-permute-start.8) | collective-permute-done | bytes 65568 | tf_op jit(solution)/shard_map/ppermute | solution.py:321
  73.3 2.4 %collective-permute-start.10 = (f32[128,128]{1,0:T(8,128)S(1)}, f32[128,128]{1,0:T(8,128)S(1)}, u32[]{:S(2)}, u32[]{:S(2)}) collective-permute-start(f32[128,128]{1,0:T(8,128)S(1)} %add.37), channel_id=1, source_target_pairs={{0,16},{1,17},{2,18},{3,19},{4,20},{5,21},{6,22},{7,23},{8,24},{9,... | collective-permute-start | bytes 196616 | tf_op jit(solution)/shard_map/ppermute | solution.py:321
  75.7 0.0 collective-permute-start.11
  75.7 2.2 %collective-permute-start.9 = (f32[128,128]{1,0:T(8,128)S(1)}, f32[128,128]{1,0:T(8,128)S(1)}, u32[]{:S(2)}, u32[]{:S(2)}) collective-permute-start(f32[128,128]{1,0:T(8,128)S(1)} %add.37), channel_id=1, source_target_pairs={{0,2},{1,3},{2,0},{3,1},{4,6},{5,7},{6,4},{7,5},{8,10},{9,11},{10,... | collective-permute-start | bytes 196616 | tf_op jit(solution)/shard_map/ppermute | solution.py:321
  77.8 0.0 copy-done.8
  77.8 1.5 %collective-permute-start.4 = (f32[4,64,256]{2,1,0:T(8,128)S(1)}, f32[4,64,256]{2,1,0:T(8,128)S(1)}, u32[]{:S(2)}, u32[]{:S(2)}) collective-permute-start(f32[4,64,256]{2,1,0:T(8,128)S(1)} %copy-done.8), channel_id=1, source_target_pairs={{0,32},{16,48},{32,0},{48,16},{64,96},{80,112},{96,64},{112,80},{1... | collective-permute-start | bytes 786440 | tf_op jit(solution)/shard_map/ppermute | solution.py:465
  79.3 0.0 copy-done.7
  79.3 2.5 %collective-permute-start.5 = (f32[4,64,256]{2,1,0:T(8,128)S(1)}, f32[4,64,256]{2,1,0:T(8,128)S(1)}, u32[]{:S(2)}, u32[]{:S(2)}) collective-permute-start(f32[4,64,256]{2,1,0:T(8,128)S(1)} %copy-done.7), channel_id=1, source_target_pairs={{0,64},{16,80},{32,96},{48,112},{64,0},{80,16},{96,32},{112,48},{1... | collective-permute-start | bytes 786440 | tf_op jit(solution)/shard_map/ppermute | solution.py:465
  81.8 0.0 collective-permute-done.10
  81.8 0.0 copy-done.6
  81.8 0.7 collective-permute-start.6
  82.5 0.0 collective-permute-done.11
  82.5 0.0 collective-permute-done.9
  82.6 0.1 collective-permute-start.12
  82.7 2.3 %collective-permute-start.13 = (f32[128,128]{1,0:T(8,128)S(1)}, f32[128,128]{1,0:T(8,128)S(1)}, u32[]{:S(2)}, u32[]{:S(2)}) collective-permute-start(f32[128,128]{1,0:T(8,128)S(1)} %add_add_fusion.2), channel_id=1, source_target_pairs={{0,8},{1,9},{2,10},{3,11},{4,12},{5,13},{6,14},{7,15},{8,0},{9,1},... | collective-permute-start | bytes 196616 | tf_op jit(solution)/shard_map/ppermute | solution.py:321
  84.9 2.1 %collective-permute-done.4 = f32[4,64,256]{2,1,0:T(8,128)S(1)} collective-permute-done((f32[4,64,256]{2,1,0:T(8,128)S(1)}, f32[4,64,256]{2,1,0:T(8,128)S(1)}, u32[]{:S(2)}, u32[]{:S(2)}) %collective-permute-start.4) | collective-permute-done | bytes 262176 | tf_op jit(solution)/shard_map/ppermute | solution.py:465
  87.1 0.8 collective-permute-start.14
  87.9 5.1 %collective-permute-done.5 = f32[4,64,256]{2,1,0:T(8,128)S(1)} collective-permute-done((f32[4,64,256]{2,1,0:T(8,128)S(1)}, f32[4,64,256]{2,1,0:T(8,128)S(1)}, u32[]{:S(2)}, u32[]{:S(2)}) %collective-permute-start.5) | collective-permute-done | bytes 262176 | tf_op jit(solution)/shard_map/ppermute | solution.py:465
  93.0 2.6 %collective-permute-done.6 = f32[4,64,256]{2,1,0:T(8,128)S(1)} collective-permute-done((f32[4,64,256]{2,1,0:T(8,128)S(1)}, f32[4,64,256]{2,1,0:T(8,128)S(1)}, u32[]{:S(2)}, u32[]{:S(2)}) %collective-permute-start.6) | collective-permute-done | bytes 262176 | tf_op jit(solution)/shard_map/ppermute | solution.py:465
  95.6 0.0 copy-done.5
  95.6 0.1 add_add_fusion
  95.7 1.1 %collective-permute-start.7 = (f32[4,32,256]{2,1,0:T(8,128)S(1)}, f32[4,32,256]{2,1,0:T(8,128)S(1)}, u32[]{:S(2)}, u32[]{:S(2)}) collective-permute-start(f32[4,32,256]{2,1,0:T(8,128)S(1)} %split.9), channel_id=1, source_target_pairs={{0,16},{16,0},{32,48},{48,32},{64,80},{80,64},{96,112},{112,96},{1... | collective-permute-start | bytes 393224 | tf_op jit(solution)/shard_map/ppermute | solution.py:467
  96.8 0.0 collective-permute-done.12
  96.8 0.0 collective-permute-done.13
  96.8 0.0 collective-permute-done.14
  96.9 0.1 collective-permute-start.15
  97.0 3.0 %collective-permute-start.16 = (f32[128,128]{1,0:T(8,128)S(1)}, f32[128,128]{1,0:T(8,128)S(1)}, u32[]{:S(2)}, u32[]{:S(2)}) collective-permute-start(f32[128,128]{1,0:T(8,128)S(1)} %add_add_fusion.1.a_ref), channel_id=1, source_target_pairs={{0,64},{1,65},{2,66},{3,67},{4,68},{5,69},{6,70},{7,71},{8,72},{9,... | collective-permute-start | bytes 196616 | tf_op jit(solution)/shard_map/ppermute | solution.py:321
  100.0 1.6 %collective-permute-start.17 = (f32[128,128]{1,0:T(8,128)S(1)}, f32[128,128]{1,0:T(8,128)S(1)}, u32[]{:S(2)}, u32[]{:S(2)}) collective-permute-start(f32[128,128]{1,0:T(8,128)S(1)} %add_add_fusion.1.a_ref), channel_id=1, source_target_pairs={{0,96},{1,97},{2,98},{3,99},{4,100},{5,101},{6,102},{7,103},{8,104... | collective-permute-start | bytes 196616 | tf_op jit(solution)/shard_map/ppermute | solution.py:321
  101.7 0.0 collective-permute-done.15.b_ref
  101.7 1.3 %collective-permute-done.16.c_ref = f32[128,128]{1,0:T(8,128)S(1)} collective-permute-done((f32[128,128]{1,0:T(8,128)S(1)}, f32[128,128]{1,0:T(8,128)S(1)}, u32[]{:S(2)}, u32[]{:S(2)}) %collective-permute-start.16) | collective-permute-done | bytes 65568 | tf_op jit(solution)/shard_map/ppermute | solution.py:321
  103.0 2.5 %collective-permute-done.17.d_ref = f32[128,128]{1,0:T(8,128)S(1)} collective-permute-done((f32[128,128]{1,0:T(8,128)S(1)}, f32[128,128]{1,0:T(8,128)S(1)}, u32[]{:S(2)}, u32[]{:S(2)}) %collective-permute-start.17) | collective-permute-done | bytes 65568 | tf_op jit(solution)/shard_map/ppermute | solution.py:321
  105.5 0.8 finish.1
  106.3 0.0 collective-permute-done.7
  106.3 0.7 slice_add_fusion
  (10 shorter events, 0.1 us)
Async XLA Ops:
  4.1 7.2 %collective-permute-start = (bf16[32,80]{1,0:T(8,128)(2,1)S(1)}, bf16[32,80]{1,0:T(8,128)(2,1)S(1)}, u32[]{:S(2)}, u32[]{:S(2)}) collective-permute-start(bf16[32,80]{1,0:T(8,128)(2,1)S(1)} %get-tuple-element.38), channel_id=1, source_target_pairs={{0,16},{16,32},{32,48},{48,64},{64,80},{80,96},{96,112},{1,17},{17... | collective-permute-start | bytes 15368 | tf_op jit(solution)/shard_map/ppermute | solution.py:350
  7.7 5.5 %collective-permute-start.1 = (bf16[32,80]{1,0:T(8,128)(2,1)S(1)}, bf16[32,80]{1,0:T(8,128)(2,1)S(1)}, u32[]{:S(2)}, u32[]{:S(2)}) collective-permute-start(bf16[32,80]{1,0:T(8,128)(2,1)S(1)} %get-tuple-element.39), channel_id=1, source_target_pairs={{16,0},{32,16},{48,32},{64,48},{80,64},{96,80},{112,96},{17,1},{33... | collective-permute-start | bytes 15368 | tf_op jit(solution)/shard_map/ppermute | solution.py:351
  13.4 6.0 %collective-permute-start.2 = (bf16[128,80]{1,0:T(8,128)(2,1)S(1)}, bf16[128,80]{1,0:T(8,128)(2,1)S(1)}, u32[]{:S(2)}, u32[]{:S(2)}) collective-permute-start(bf16[128,80]{1,0:T(8,128)(2,1)S(1)} %get-tuple-element.73), channel_id=1, source_target_pairs={{0,1},{1,2},{2,3},{3,4},{4,5},{5,6},{6,7},{7,8},{8,9},{9,10},{10,1... | collective-permute-start | bytes 61448 | tf_op jit(solution)/shard_map/ppermute | solution.py:389
  14.7 6.2 %collective-permute-start.3 = (bf16[128,80]{1,0:T(8,128)(2,1)S(1)}, bf16[128,80]{1,0:T(8,128)(2,1)S(1)}, u32[]{:S(2)}, u32[]{:S(2)}) collective-permute-start(bf16[128,80]{1,0:T(8,128)(2,1)S(1)} %get-tuple-element.72), channel_id=1, source_target_pairs={{1,0},{2,1},{3,2},{4,3},{5,4},{6,5},{7,6},{8,7},{9,8},{10,9},{11,1... | collective-permute-start | bytes 61448 | tf_op jit(solution)/shard_map/ppermute | solution.py:390
  19.3 27.7 %copy-start.3 = (bf16[17,2,128,256]{3,2,1,0:T(8,128)(2,1)}, bf16[17,2,128,256]{3,2,1,0:T(8,128)(2,1)S(1)}, u32[]{:S(2)}) copy-start(bf16[17,2,128,256]{3,2,1,0:T(8,128)(2,1)S(1)} %get-tuple-element.64.refs_1_) | copy-start | bytes 6684676
  19.3 27.7 %copy-start.4 = (f32[4,256,512]{2,1,0:T(8,128)}, f32[4,256,512]{2,1,0:T(8,128)S(1)}, u32[]{:S(2)}) copy-start(f32[4,256,512]{2,1,0:T(8,128)S(1)} %get-tuple-element.65.refs_2_) | copy-start | bytes 6291460
  20.9 26.1 %copy-start = (bf16[4,256,256]{2,1,0:T(8,128)(2,1)S(1)}, bf16[4,256,256]{2,1,0:T(8,128)(2,1)}, u32[]{:S(2)}) copy-start(bf16[4,256,256]{2,1,0:T(8,128)(2,1)} %refs_2_.1) | copy-start | bytes 1572868
  20.9 26.1 %copy-start.1 = (bf16[4,8,32,256]{3,2,1,0:T(8,128)(2,1)S(1)}, bf16[4,8,32,256]{3,2,1,0:T(8,128)(2,1)}, u32[]{:S(2)}) copy-start(bf16[4,8,32,256]{3,2,1,0:T(8,128)(2,1)} %param.15) | copy-start | bytes 1572868
  47.1 18.7 %copy-start.2 = (bf16[4,256,512]{2,1,0:T(8,128)(2,1)S(1)}, bf16[4,256,512]{2,1,0:T(8,128)(2,1)}, u32[]{:S(2)}) copy-start(bf16[4,256,512]{2,1,0:T(8,128)(2,1)} %get-tuple-element.66.refs_3_) | copy-start | bytes 3145732
  49.9 15.9 %all-to-all-start.1 = ((bf16[16,64,256]{2,1,0:T(8,128)(2,1)}), bf16[16,64,256]{2,1,0:T(8,128)(2,1)S(1)}, u32[]{:S(2)}, u32[]{:S(2)}) async-start(bf16[16,64,256]{2,1,0:T(8,128)(2,1)} %mix.1), calls=%async_computation.1 | async-start | bytes 1048576 | tf_op jit(solution)/shard_map/all_to_all | solution.py:448
  65.8 12.0 %copy-start.8 = (f32[4,64,256]{2,1,0:T(8,128)S(1)}, f32[4,64,256]{2,1,0:T(8,128)}, u32[]{:S(2)}) copy-start(f32[4,64,256]{2,1,0:T(8,128)} %get-tuple-element.60) | copy-start | bytes 786436
  65.8 13.5 %copy-start.7 = (f32[4,64,256]{2,1,0:T(8,128)S(1)}, f32[4,64,256]{2,1,0:T(8,128)}, u32[]{:S(2)}) copy-start(f32[4,64,256]{2,1,0:T(8,128)} %get-tuple-element.61) | copy-start | bytes 786436
  65.8 16.0 %copy-start.6 = (f32[4,64,256]{2,1,0:T(8,128)S(1)}, f32[4,64,256]{2,1,0:T(8,128)}, u32[]{:S(2)}) copy-start(f32[4,64,256]{2,1,0:T(8,128)} %get-tuple-element.62) | copy-start | bytes 786436
  65.8 29.8 %copy-start.5 = (f32[4,64,256]{2,1,0:T(8,128)S(1)}, f32[4,64,256]{2,1,0:T(8,128)}, u32[]{:S(2)}) copy-start(f32[4,64,256]{2,1,0:T(8,128)} %get-tuple-element.59) | copy-start | bytes 786436
  71.9 1.3 %collective-permute-start.8 = (f32[128,128]{1,0:T(8,128)S(1)}, f32[128,128]{1,0:T(8,128)S(1)}, u32[]{:S(2)}, u32[]{:S(2)}) collective-permute-start(f32[128,128]{1,0:T(8,128)S(1)} %backward.1), channel_id=1, source_target_pairs={{0,1},{1,0},{2,3},{3,2},{4,5},{5,4},{6,7},{7,6},{8,9},{9,8},{10,11... | collective-permute-start | bytes 196616 | tf_op jit(solution)/shard_map/ppermute | solution.py:321
  73.3 8.5 %collective-permute-start.10 = (f32[128,128]{1,0:T(8,128)S(1)}, f32[128,128]{1,0:T(8,128)S(1)}, u32[]{:S(2)}, u32[]{:S(2)}) collective-permute-start(f32[128,128]{1,0:T(8,128)S(1)} %add.37), channel_id=1, source_target_pairs={{0,16},{1,17},{2,18},{3,19},{4,20},{5,21},{6,22},{7,23},{8,24},{9,... | collective-permute-start | bytes 196616 | tf_op jit(solution)/shard_map/ppermute | solution.py:321
  75.7 6.9 %collective-permute-start.11 = (f32[128,128]{1,0:T(8,128)S(1)}, f32[128,128]{1,0:T(8,128)S(1)}, u32[]{:S(2)}, u32[]{:S(2)}) collective-permute-start(f32[128,128]{1,0:T(8,128)S(1)} %add.37), channel_id=1, source_target_pairs={{0,18},{1,19},{2,16},{3,17},{4,22},{5,23},{6,20},{7,21},{8,26},{9,... | collective-permute-start | bytes 196616 | tf_op jit(solution)/shard_map/ppermute | solution.py:321
  75.7 6.9 %collective-permute-start.9 = (f32[128,128]{1,0:T(8,128)S(1)}, f32[128,128]{1,0:T(8,128)S(1)}, u32[]{:S(2)}, u32[]{:S(2)}) collective-permute-start(f32[128,128]{1,0:T(8,128)S(1)} %add.37), channel_id=1, source_target_pairs={{0,2},{1,3},{2,0},{3,1},{4,6},{5,7},{6,4},{7,5},{8,10},{9,11},{10,... | collective-permute-start | bytes 196616 | tf_op jit(solution)/shard_map/ppermute | solution.py:321
  77.8 9.2 %collective-permute-start.4 = (f32[4,64,256]{2,1,0:T(8,128)S(1)}, f32[4,64,256]{2,1,0:T(8,128)S(1)}, u32[]{:S(2)}, u32[]{:S(2)}) collective-permute-start(f32[4,64,256]{2,1,0:T(8,128)S(1)} %copy-done.8), channel_id=1, source_target_pairs={{0,32},{16,48},{32,0},{48,16},{64,96},{80,112},{96,64},{112,80},{1... | collective-permute-start | bytes 786440 | tf_op jit(solution)/shard_map/ppermute | solution.py:465
  79.3 13.7 %collective-permute-start.5 = (f32[4,64,256]{2,1,0:T(8,128)S(1)}, f32[4,64,256]{2,1,0:T(8,128)S(1)}, u32[]{:S(2)}, u32[]{:S(2)}) collective-permute-start(f32[4,64,256]{2,1,0:T(8,128)S(1)} %copy-done.7), channel_id=1, source_target_pairs={{0,64},{16,80},{32,96},{48,112},{64,0},{80,16},{96,32},{112,48},{1... | collective-permute-start | bytes 786440 | tf_op jit(solution)/shard_map/ppermute | solution.py:465
  81.8 13.8 %collective-permute-start.6 = (f32[4,64,256]{2,1,0:T(8,128)S(1)}, f32[4,64,256]{2,1,0:T(8,128)S(1)}, u32[]{:S(2)}, u32[]{:S(2)}) collective-permute-start(f32[4,64,256]{2,1,0:T(8,128)S(1)} %copy-done.6), channel_id=1, source_target_pairs={{0,96},{16,112},{32,64},{48,80},{64,32},{80,48},{96,0},{112,16},{1... | collective-permute-start | bytes 786440 | tf_op jit(solution)/shard_map/ppermute | solution.py:465
  82.6 14.3 %collective-permute-start.12 = (f32[128,128]{1,0:T(8,128)S(1)}, f32[128,128]{1,0:T(8,128)S(1)}, u32[]{:S(2)}, u32[]{:S(2)}) collective-permute-start(f32[128,128]{1,0:T(8,128)S(1)} %add_add_fusion.2), channel_id=1, source_target_pairs={{0,4},{1,5},{2,6},{3,7},{4,0},{5,1},{6,2},{7,3},{8,12},{9,13},{10,... | collective-permute-start | bytes 196616 | tf_op jit(solution)/shard_map/ppermute | solution.py:321
  82.7 14.2 %collective-permute-start.13 = (f32[128,128]{1,0:T(8,128)S(1)}, f32[128,128]{1,0:T(8,128)S(1)}, u32[]{:S(2)}, u32[]{:S(2)}) collective-permute-start(f32[128,128]{1,0:T(8,128)S(1)} %add_add_fusion.2), channel_id=1, source_target_pairs={{0,8},{1,9},{2,10},{3,11},{4,12},{5,13},{6,14},{7,15},{8,0},{9,1},... | collective-permute-start | bytes 196616 | tf_op jit(solution)/shard_map/ppermute | solution.py:321
  87.1 9.8 %collective-permute-start.14 = (f32[128,128]{1,0:T(8,128)S(1)}, f32[128,128]{1,0:T(8,128)S(1)}, u32[]{:S(2)}, u32[]{:S(2)}) collective-permute-start(f32[128,128]{1,0:T(8,128)S(1)} %add_add_fusion.2), channel_id=1, source_target_pairs={{0,12},{1,13},{2,14},{3,15},{4,8},{5,9},{6,10},{7,11},{8,4},{9,5},... | collective-permute-start | bytes 196616 | tf_op jit(solution)/shard_map/ppermute | solution.py:321
  95.7 10.6 %collective-permute-start.7 = (f32[4,32,256]{2,1,0:T(8,128)S(1)}, f32[4,32,256]{2,1,0:T(8,128)S(1)}, u32[]{:S(2)}, u32[]{:S(2)}) collective-permute-start(f32[4,32,256]{2,1,0:T(8,128)S(1)} %split.9), channel_id=1, source_target_pairs={{0,16},{16,0},{32,48},{48,32},{64,80},{80,64},{96,112},{112,96},{1... | collective-permute-start | bytes 393224 | tf_op jit(solution)/shard_map/ppermute | solution.py:467
  96.9 4.8 %collective-permute-start.15 = (f32[128,128]{1,0:T(8,128)S(1)}, f32[128,128]{1,0:T(8,128)S(1)}, u32[]{:S(2)}, u32[]{:S(2)}) collective-permute-start(f32[128,128]{1,0:T(8,128)S(1)} %add_add_fusion.1.a_ref), channel_id=1, source_target_pairs={{0,32},{1,33},{2,34},{3,35},{4,36},{5,37},{6,38},{7,39},{8,40},{9,... | collective-permute-start | bytes 196616 | tf_op jit(solution)/shard_map/ppermute | solution.py:321
  97.0 6.0 %collective-permute-start.16 = (f32[128,128]{1,0:T(8,128)S(1)}, f32[128,128]{1,0:T(8,128)S(1)}, u32[]{:S(2)}, u32[]{:S(2)}) collective-permute-start(f32[128,128]{1,0:T(8,128)S(1)} %add_add_fusion.1.a_ref), channel_id=1, source_target_pairs={{0,64},{1,65},{2,66},{3,67},{4,68},{5,69},{6,70},{7,71},{8,72},{9,... | collective-permute-start | bytes 196616 | tf_op jit(solution)/shard_map/ppermute | solution.py:321
  100.0 5.5 %collective-permute-start.17 = (f32[128,128]{1,0:T(8,128)S(1)}, f32[128,128]{1,0:T(8,128)S(1)}, u32[]{:S(2)}, u32[]{:S(2)}) collective-permute-start(f32[128,128]{1,0:T(8,128)S(1)} %add_add_fusion.1.a_ref), channel_id=1, source_target_pairs={{0,96},{1,97},{2,98},{3,99},{4,100},{5,101},{6,102},{7,103},{8,104... | collective-permute-start | bytes 196616 | tf_op jit(solution)/shard_map/ppermute | solution.py:321

commit v6 on v5

--- a/solution.py
+++ b/solution.py
@@ -459,13 +459,10 @@
         cost_estimate=cost(mine * 2 * 2 * 256 * width * width, 3 << 20),
         name="mix_grad",
     )(lax.axis_index("sy")[None], sent, mix_weight, cotangent_rows)
-    *mix_parts, coarse_grad = lax.optimization_barrier((*mix_parts, coarse_grad))
     mix_sum = mix_parts[0]
+    moved = []
     for k, part in enumerate(mix_parts[1:], 1):
-        mix_sum = mix_sum + lax.ppermute(part, "sy", [(i, i ^ (2 * k)) for i in range(count_y)])
-    mine_last, other = jnp.split(mix_sum, 2, axis=1)
-    mix_grad = mine_last + lax.ppermute(other, "sy", [(i, i ^ 1) for i in range(count_y)])
-
+        moved.append(lax.ppermute(part, "sy", [(i, i ^ (2 * k)) for i in range(count_y)]))
     cells = 16 * 64 * count_y * 32 * count_z
     sums = pl.pallas_call(
         lambda *refs: backward_kernel(
@@ -494,6 +491,12 @@
         faces,
         edge_slope,
     )
+    *moved, sums = lax.optimization_barrier((*moved, sums))
+    for part in moved:
+        mix_sum = mix_sum + part
+    mine_last, other = jnp.split(mix_sum, 2, axis=1)
+    mix_grad = mine_last + lax.ppermute(other, "sy", [(i, i ^ 1) for i in range(count_y)])
+
     rounds = sum_rounds(count_y, count_z)
     for masks in rounds[:-1]:
         parts = [sums] + exchanged(sums, masks, count_y * count_z)

time: 107 us -> 106 us (level)
  waiting for transfers between devices: 27.5 us -> 24.5 us
  starting transfers between devices: 29.6 us -> 31.3 us
    ppermute x10, waiting for transfers between devices: 5.1 us -> 12.6 us  [exchanged(): lax.ppermute(value, ('sy', 'sz'), [(i, i ^ m) for i in range(count)])]
    ppermute x3, waiting for transfers between devices: 9.85 us -> 3.86 us  [per_device(): lax.ppermute(part, 'sy', [(i, i ^ 2 * k) for i in range(count_y)])]
    all_to_all x1, waiting for transfers between devices: 9.14 us -> 4.61 us  [per_device(): lax.all_to_all(back, 'sz', split_axis=0, concat_axis=0, tiled=True)]
    ppermute x10, starting transfers between devices: 12.6 us -> 14.4 us  [exchanged(): lax.ppermute(value, ('sy', 'sz'), [(i, i ^ m) for i in range(count)])]
  transfers between devices with their start and end apart: 19 -> 19, of which waited for: 9 -> 12; matrix products, arithmetic and copies ran while one was open for 0% -> 1% of each run, Pallas kernels for 9% -> 14%
where the time goes in v6:
time: 106 us
  starting transfers between devices  31.3 us (30%)
  Pallas kernels  24.6 us (23%)
  waiting for transfers between devices  24.5 us (23%)
  blocking collectives  23.4 us (22%)
    all_to_all x1, blocking collectives, per_device(): lax.all_to_all(coarse.reshape(count_z, mine * 16, 256), 'sz', split_axis=...  23.4 us
    ppermute x10, starting transfers between devices, exchanged(): lax.ppermute(value, ('sy', 'sz'), [(i, i ^ m) for i in range(count)])  14.4 us
    ppermute x10, waiting for transfers between devices, exchanged(): lax.ppermute(value, ('sy', 'sz'), [(i, i ^ m) for i in range(count)])  12.6 us
    pallas_call x1, Pallas kernels, per_device(): pl.pallas_call(lambda *refs: backward_kernel(1.0 / math.sqrt(cells // 8),...  6.11 us
    ppermute x3, starting transfers between devices, per_device(): lax.ppermute(part, 'sy', [(i, i ^ 2 * k) for i in range(count_y)])  4.7 us
    all_to_all x1, waiting for transfers between devices, per_device(): lax.all_to_all(back, 'sz', split_axis=0, concat_axis=0, tiled=True)  4.61 us
    ppermute x3, waiting for transfers between devices, per_device(): lax.ppermute(part, 'sy', [(i, i ^ 2 * k) for i in range(count_y)])  3.86 us
    all_to_all x1, starting transfers between devices, per_device(): lax.all_to_all(back, 'sz', split_axis=0, concat_axis=0, tiled=True)  3.57 us
  transfers between devices with their start and end apart: 19, of which 12 were waited for; matrix products, arithmetic and copies ran while one was open for 1% of the time, Pallas kernels for 14%

profile of v6, /device:TPU:0, one launch (start us, length us, event | category | flops | bytes accessed | tf_op | source)
XLA Modules:
  0.0 105.6 jit_solution(11092542678781391793)
XLA Ops:
  0.6 3.5 %features.1 = (bf16[32,128,80]{2,1,0:T(8,128)(2,1)S(1)}, bf16[32,80]{1,0:T(8,128)(2,1)S(1)}, bf16[32,80]{1,0:T(8,128)(2,1)S(1)}) custom-call(s32[16,32,64]{2,1,0:T(8,128)} %bitcast.34, bf16[16,32,64]{2,1,0:T(8,128)(2,1)} %bitcast.35), custom_call_target="tpu_custom_call" | custom-call | flops 41943040 | bytes 2097152 | tf_op jit(solution)/shard_map/features/pallas_call | solution.py:331
  4.1 3.6 %collective-permute-start = (bf16[32,80]{1,0:T(8,128)(2,1)S(1)}, bf16[32,80]{1,0:T(8,128)(2,1)S(1)}, u32[]{:S(2)}, u32[]{:S(2)}) collective-permute-start(bf16[32,80]{1,0:T(8,128)(2,1)S(1)} %get-tuple-element.37), channel_id=1, source_target_pairs={{0,16},{16,32},{32,48},{48,64},{64,80},{80,96},{96,112},{1,17},{17... | collective-permute-start | bytes 15368 | tf_op jit(solution)/shard_map/ppermute | solution.py:350
  7.7 1.3 %collective-permute-start.1 = (bf16[32,80]{1,0:T(8,128)(2,1)S(1)}, bf16[32,80]{1,0:T(8,128)(2,1)S(1)}, u32[]{:S(2)}, u32[]{:S(2)}) collective-permute-start(bf16[32,80]{1,0:T(8,128)(2,1)S(1)} %get-tuple-element.38), channel_id=1, source_target_pairs={{16,0},{32,16},{48,32},{64,48},{80,64},{96,80},{112,96},{17,1},{33... | collective-permute-start | bytes 15368 | tf_op jit(solution)/shard_map/ppermute | solution.py:351
  9.0 2.3 %weights.1 = (bf16[9,256,256]{2,1,0:T(8,128)(2,1)S(1)}, bf16[128,256]{1,0:T(8,128)(2,1)S(1)}, bf16[256,128]{1,0:T(8,128)(2,1)S(1)}, bf16[80,256]{1,0:T(8,128)(2,1)S(1)}) custom-call(bf16[16,16,27]{2,1,0:T(8,128)(2,1)} %bitcast.38, bf16[8,16,64]{2,1,0:T(8,128)(2,1)} %bitcast.40, bf16[4,16]{1,0:T(4,128)(2,1)} %mat_hbm.1, bf16[1,16]{1,0:T(2,128)(2,1)} %bitcast.41), custom_call_target="tpu_custom_call" | custom-call | flops 56623104 | bytes 3145728 | tf_op jit(solution)/shard_map/weights/pallas_call | solution.py:352
  11.4 0.0 collective-permute-done.ylo_ref
  11.4 1.9 %collective-permute-done.1.yhi_ref = bf16[32,80]{1,0:T(8,128)(2,1)S(1)} collective-permute-done((bf16[32,80]{1,0:T(8,128)(2,1)S(1)}, bf16[32,80]{1,0:T(8,128)(2,1)S(1)}, u32[]{:S(2)}, u32[]{:S(2)}) %collective-permute-start.1) | collective-permute-done | bytes 5152 | tf_op jit(solution)/shard_map/ppermute | solution.py:351
  13.3 0.1 fusion
  13.4 1.3 %collective-permute-start.2 = (bf16[128,80]{1,0:T(8,128)(2,1)S(1)}, bf16[128,80]{1,0:T(8,128)(2,1)S(1)}, u32[]{:S(2)}, u32[]{:S(2)}) collective-permute-start(bf16[128,80]{1,0:T(8,128)(2,1)S(1)} %get-tuple-element.71), channel_id=1, source_target_pairs={{0,1},{1,2},{2,3},{3,4},{4,5},{5,6},{6,7},{7,8},{8,9},{9,10},{10,1... | collective-permute-start | bytes 61448 | tf_op jit(solution)/shard_map/ppermute | solution.py:389
  14.7 1.3 %collective-permute-start.3 = (bf16[128,80]{1,0:T(8,128)(2,1)S(1)}, bf16[128,80]{1,0:T(8,128)(2,1)S(1)}, u32[]{:S(2)}, u32[]{:S(2)}) collective-permute-start(bf16[128,80]{1,0:T(8,128)(2,1)S(1)} %get-tuple-element.70), channel_id=1, source_target_pairs={{1,0},{2,1},{3,2},{4,3},{5,4},{6,5},{7,6},{8,7},{9,8},{10,9},{11,1... | collective-permute-start | bytes 61448 | tf_op jit(solution)/shard_map/ppermute | solution.py:390
  16.0 3.3 %inner.1 = (bf16[17,2,128,256]{3,2,1,0:T(8,128)(2,1)S(1)}, f32[4,256,512]{2,1,0:T(8,128)S(1)}, bf16[4,256,512]{2,1,0:T(8,128)(2,1)S(1)}, f32[2,2,256,32]{3,2,1,0:T(8,128)S(1)}) custom-call(bf16[32,128,80]{2,1,0:T(8,128)(2,1)S(1)} %get-tuple-element.45.feat_ref, bf16[32,80]{1,0:T(8,128)(2,1)S(1)} %collective-permute-done.ylo_ref, ...), custom_call_target="tpu_custom_call" | custom-call | flops 3221225472 | bytes 10485760 | tf_op jit(solution)/shard_map/inner/pallas_call | solution.py:391
  19.3 0.0 copy-start.3
  19.3 0.0 copy-start.4
  19.3 0.0 collective-permute-done.2.zlo_ref
  19.4 1.6 %collective-permute-done.3.zhi_ref = bf16[128,80]{1,0:T(8,128)(2,1)S(1)} collective-permute-done((bf16[128,80]{1,0:T(8,128)(2,1)S(1)}, bf16[128,80]{1,0:T(8,128)(2,1)S(1)}, u32[]{:S(2)}, u32[]{:S(2)}) %collective-permute-start.3) | collective-permute-done | bytes 20512 | tf_op jit(solution)/shard_map/ppermute | solution.py:390
  20.9 0.0 copy-start
  20.9 0.0 copy-start.1
  20.9 2.7 %outer.1 = (bf16[2,128,256]{2,1,0:T(8,128)(2,1)S(1)}, f32[256,128]{1,0:T(8,128)S(1)}, bf16[4,256,512]{2,1,0:T(8,128)(2,1)}, bf16[1024,256]{1,0:T(8,128)(2,1)}) custom-call(bf16[128,80]{1,0:T(8,128)(2,1)S(1)} %collective-permute-done.2.zlo_ref, bf16[128,80]{1,0:T(8,128)(2,1)S(1)} %collective-permute-done.3.zhi_ref, ...), custom_call_target="tpu_custom_call" | custom-call | flops 1073741824 | bytes 4194304 | tf_op jit(solution)/shard_map/outer/pallas_call | solution.py:405
  23.6 23.4 %all_to_all.10.coarse_ref.refs_1_ = bf16[16,64,256]{2,1,0:T(8,128)(2,1)S(1)} all-to-all(bf16[16,64,256]{2,1,0:T(8,128)(2,1)} %bitcast.33), channel_id=1, replica_groups=mesh['sy'=8,'sz'=16] {'sz'}, dimensions={0} | all-to-all | bytes 1048576 | tf_op jit(solution)/shard_map/all_to_all | solution.py:427
  47.0 0.0 copy-done.3
  47.0 0.0 copy-done.4
  47.0 0.0 copy-done
  47.1 0.0 copy-done.1
  47.1 0.0 copy-start.2
  47.1 2.8 %mix.1 = bf16[16,64,256]{2,1,0:T(8,128)(2,1)} custom-call(bf16[16,64,256]{2,1,0:T(8,128)(2,1)S(1)} %all_to_all.10.coarse_ref.refs_1_, bf16[4,256,256]{2,1,0:T(8,128)(2,1)S(1)} %copy-done, bf16[4,256,256]{2,1,0:T(8,128)(2,1)S(1)} %bitcast.30), custom_call_target="tpu_custom_call" | custom-call | flops 268435456 | bytes 2097152 | tf_op jit(solution)/shard_map/mix/pallas_call | solution.py:438
  49.9 3.6 %all-to-all-start.1 = ((bf16[16,64,256]{2,1,0:T(8,128)(2,1)}), bf16[16,64,256]{2,1,0:T(8,128)(2,1)S(1)}, u32[]{:S(2)}, u32[]{:S(2)}) async-start(bf16[16,64,256]{2,1,0:T(8,128)(2,1)} %mix.1), calls=%async_computation.1 | async-start | bytes 1048576 | tf_op jit(solution)/shard_map/all_to_all | solution.py:448
  53.5 3.0 %mix_grad.1 = (bf16[4,256,256]{2,1,0:T(8,128)(2,1)}, f32[4,64,256]{2,1,0:T(8,128)}, f32[4,64,256]{2,1,0:T(8,128)}, f32[4,64,256]{2,1,0:T(8,128)}, f32[4,64,256]{2,1,0:T(8,128)}) custom-call(s32[1]{0:T(128)} %bitcast.refs_0_, bf16[16,64,256]{2,1,0:T(8,128)(2,1)S(1)} %all_to_all.10.coarse_ref.refs_1_, bf16[4,256,256]{2,1,0:T(8,128)(2,1)S(1)} %copy-done, ...), custom_call_target="tpu_custom_call" | custom-call | flops 268435456 | bytes 3145728 | tf_op jit(solution)/shard_map/mix_grad/pallas_call | solution.py:450
  56.5 1.6 %collective-permute-start.4 = (f32[4,64,256]{2,1,0:T(8,128)}, f32[4,64,256]{2,1,0:T(8,128)S(1)}, u32[]{:S(2)}, u32[]{:S(2)}) collective-permute-start(f32[4,64,256]{2,1,0:T(8,128)} %get-tuple-element.55), channel_id=1, source_target_pairs={{0,32},{16,48},{32,0},{48,16},{64,96},{80,112},{96,64},{112,80},{1... | collective-permute-start | bytes 786440 | tf_op jit(solution)/shard_map/ppermute | solution.py:465
  58.1 2.7 %collective-permute-start.5 = (f32[4,64,256]{2,1,0:T(8,128)}, f32[4,64,256]{2,1,0:T(8,128)S(1)}, u32[]{:S(2)}, u32[]{:S(2)}) collective-permute-start(f32[4,64,256]{2,1,0:T(8,128)} %get-tuple-element.56), channel_id=1, source_target_pairs={{0,64},{16,80},{32,96},{48,112},{64,0},{80,16},{96,32},{112,48},{1... | collective-permute-start | bytes 786440 | tf_op jit(solution)/shard_map/ppermute | solution.py:465
  60.8 0.4 collective-permute-start.6
  61.2 4.6 %all-to-all-done.1 = bf16[16,64,256]{2,1,0:T(8,128)(2,1)S(1)} async-done(((bf16[16,64,256]{2,1,0:T(8,128)(2,1)}), bf16[16,64,256]{2,1,0:T(8,128)(2,1)S(1)}, u32[]{:S(2)}, u32[]{:S(2)}) %all-to-all-start.1) | async-done | bytes 524320 | tf_op jit(solution)/shard_map/all_to_all | solution.py:448
  65.8 0.0 copy-done.2
  65.8 0.0 copy-start.5
  65.8 6.1 %backward.1 = f32[128,128]{1,0:T(8,128)S(1)} custom-call(bf16[1024,256]{1,0:T(8,128)(2,1)S(1)} %bitcast.32, bf16[17,2,128,256]{3,2,1,0:T(8,128)(2,1)} %copy-done.3, f32[4,256,512]{2,1,0:T(8,128)} %copy-done.4, bf16[4,256,512]{2,1,0:T(8,128)(2,1)S(1)} %copy-done.2, bf16[128,256]{1,0:T(8,128)(2,1)S(1)} %get-tuple-element.48.pair_ref.refs_4_, ...), custom_call_target="tpu_custom_call" | custom-call | flops 4294967296 | bytes 8388608 | tf_op jit(solution)/shard_map/backward/pallas_call | solution.py:467
  71.9 0.0 collective-permute-done.4
  71.9 1.3 %collective-permute-done.5 = f32[4,64,256]{2,1,0:T(8,128)S(1)} collective-permute-done((f32[4,64,256]{2,1,0:T(8,128)}, f32[4,64,256]{2,1,0:T(8,128)S(1)}, u32[]{:S(2)}, u32[]{:S(2)}) %collective-permute-start.5) | collective-permute-done | bytes 262176 | tf_op jit(solution)/shard_map/ppermute | solution.py:465
  73.2 2.6 %collective-permute-done.6 = f32[4,64,256]{2,1,0:T(8,128)S(1)} collective-permute-done((f32[4,64,256]{2,1,0:T(8,128)}, f32[4,64,256]{2,1,0:T(8,128)S(1)}, u32[]{:S(2)}, u32[]{:S(2)}) %collective-permute-start.6) | collective-permute-done | bytes 262176 | tf_op jit(solution)/shard_map/ppermute | solution.py:465
  75.8 0.0 collective-permute-start.8
  75.8 1.3 %collective-permute-done.8 = f32[128,128]{1,0:T(8,128)S(1)} collective-permute-done((f32[128,128]{1,0:T(8,128)S(1)}, f32[128,128]{1,0:T(8,128)S(1)}, u32[]{:S(2)}, u32[]{:S(2)}) %collective-permute-start.8) | collective-permute-done | bytes 65568 | tf_op jit(solution)/shard_map/ppermute | solution.py:321
  77.0 1.1 %collective-permute-start.10 = (f32[128,128]{1,0:T(8,128)S(1)}, f32[128,128]{1,0:T(8,128)S(1)}, u32[]{:S(2)}, u32[]{:S(2)}) collective-permute-start(f32[128,128]{1,0:T(8,128)S(1)} %add.37), channel_id=1, source_target_pairs={{0,16},{1,17},{2,18},{3,19},{4,20},{5,21},{6,22},{7,23},{8,24},{9,... | collective-permute-start | bytes 196616 | tf_op jit(solution)/shard_map/ppermute | solution.py:321
  78.1 2.7 %collective-permute-start.11 = (f32[128,128]{1,0:T(8,128)S(1)}, f32[128,128]{1,0:T(8,128)S(1)}, u32[]{:S(2)}, u32[]{:S(2)}) collective-permute-start(f32[128,128]{1,0:T(8,128)S(1)} %add.37), channel_id=1, source_target_pairs={{0,18},{1,19},{2,16},{3,17},{4,22},{5,23},{6,20},{7,21},{8,26},{9,... | collective-permute-start | bytes 196616 | tf_op jit(solution)/shard_map/ppermute | solution.py:321
  80.9 1.1 %collective-permute-start.9 = (f32[128,128]{1,0:T(8,128)S(1)}, f32[128,128]{1,0:T(8,128)S(1)}, u32[]{:S(2)}, u32[]{:S(2)}) collective-permute-start(f32[128,128]{1,0:T(8,128)S(1)} %add.37), channel_id=1, source_target_pairs={{0,2},{1,3},{2,0},{3,1},{4,6},{5,7},{6,4},{7,5},{8,10},{9,11},{10,... | collective-permute-start | bytes 196616 | tf_op jit(solution)/shard_map/ppermute | solution.py:321
  81.9 0.0 collective-permute-done.10
  81.9 1.7 %collective-permute-done.11 = f32[128,128]{1,0:T(8,128)S(1)} collective-permute-done((f32[128,128]{1,0:T(8,128)S(1)}, f32[128,128]{1,0:T(8,128)S(1)}, u32[]{:S(2)}, u32[]{:S(2)}) %collective-permute-start.11) | collective-permute-done | bytes 65568 | tf_op jit(solution)/shard_map/ppermute | solution.py:321
  83.6 3.0 %collective-permute-done.9 = f32[128,128]{1,0:T(8,128)S(1)} collective-permute-done((f32[128,128]{1,0:T(8,128)S(1)}, f32[128,128]{1,0:T(8,128)S(1)}, u32[]{:S(2)}, u32[]{:S(2)}) %collective-permute-start.9) | collective-permute-done | bytes 65568 | tf_op jit(solution)/shard_map/ppermute | solution.py:321
  86.6 1.6 %collective-permute-start.12 = (f32[128,128]{1,0:T(8,128)S(1)}, f32[128,128]{1,0:T(8,128)S(1)}, u32[]{:S(2)}, u32[]{:S(2)}) collective-permute-start(f32[128,128]{1,0:T(8,128)S(1)} %add_add_fusion.2), channel_id=1, source_target_pairs={{0,4},{1,5},{2,6},{3,7},{4,0},{5,1},{6,2},{7,3},{8,12},{9,13},{10,... | collective-permute-start | bytes 196616 | tf_op jit(solution)/shard_map/ppermute | solution.py:321
  88.2 2.7 %collective-permute-start.13 = (f32[128,128]{1,0:T(8,128)S(1)}, f32[128,128]{1,0:T(8,128)S(1)}, u32[]{:S(2)}, u32[]{:S(2)}) collective-permute-start(f32[128,128]{1,0:T(8,128)S(1)} %add_add_fusion.2), channel_id=1, source_target_pairs={{0,8},{1,9},{2,10},{3,11},{4,12},{5,13},{6,14},{7,15},{8,0},{9,1},... | collective-permute-start | bytes 196616 | tf_op jit(solution)/shard_map/ppermute | solution.py:321
  90.9 0.5 collective-permute-start.14
  91.4 0.0 copy-done.5
  91.4 0.1 add_add_fusion
  91.5 1.1 %collective-permute-start.7 = (f32[4,32,256]{2,1,0:T(8,128)S(1)}, f32[4,32,256]{2,1,0:T(8,128)S(1)}, u32[]{:S(2)}, u32[]{:S(2)}) collective-permute-start(f32[4,32,256]{2,1,0:T(8,128)S(1)} %split.9), channel_id=1, source_target_pairs={{0,16},{16,0},{32,48},{48,32},{64,80},{80,64},{96,112},{112,96},{1... | collective-permute-start | bytes 393224 | tf_op jit(solution)/shard_map/ppermute | solution.py:498
  92.6 0.0 collective-permute-done.12
  92.6 1.4 %collective-permute-done.13 = f32[128,128]{1,0:T(8,128)S(1)} collective-permute-done((f32[128,128]{1,0:T(8,128)S(1)}, f32[128,128]{1,0:T(8,128)S(1)}, u32[]{:S(2)}, u32[]{:S(2)}) %collective-permute-start.13) | collective-permute-done | bytes 65568 | tf_op jit(solution)/shard_map/ppermute | solution.py:321
  94.0 2.4 %collective-permute-done.14 = f32[128,128]{1,0:T(8,128)S(1)} collective-permute-done((f32[128,128]{1,0:T(8,128)S(1)}, f32[128,128]{1,0:T(8,128)S(1)}, u32[]{:S(2)}, u32[]{:S(2)}) %collective-permute-start.14) | collective-permute-done | bytes 65568 | tf_op jit(solution)/shard_map/ppermute | solution.py:321
  96.4 0.1 collective-permute-start.15
  96.5 2.8 %collective-permute-start.16 = (f32[128,128]{1,0:T(8,128)S(1)}, f32[128,128]{1,0:T(8,128)S(1)}, u32[]{:S(2)}, u32[]{:S(2)}) collective-permute-start(f32[128,128]{1,0:T(8,128)S(1)} %add_add_fusion.1.a_ref), channel_id=1, source_target_pairs={{0,64},{1,65},{2,66},{3,67},{4,68},{5,69},{6,70},{7,71},{8,72},{9,... | collective-permute-start | bytes 196616 | tf_op jit(solution)/shard_map/ppermute | solution.py:321
  99.3 1.9 %collective-permute-start.17 = (f32[128,128]{1,0:T(8,128)S(1)}, f32[128,128]{1,0:T(8,128)S(1)}, u32[]{:S(2)}, u32[]{:S(2)}) collective-permute-start(f32[128,128]{1,0:T(8,128)S(1)} %add_add_fusion.1.a_ref), channel_id=1, source_target_pairs={{0,96},{1,97},{2,98},{3,99},{4,100},{5,101},{6,102},{7,103},{8,104... | collective-permute-start | bytes 196616 | tf_op jit(solution)/shard_map/ppermute | solution.py:321
  101.2 0.0 collective-permute-done.7
  101.2 0.7 slice_add_fusion
  101.9 0.0 collective-permute-done.15.b_ref
  101.9 0.5 collective-permute-done.16.c_ref
  102.4 2.4 %collective-permute-done.17.d_ref = f32[128,128]{1,0:T(8,128)S(1)} collective-permute-done((f32[128,128]{1,0:T(8,128)S(1)}, f32[128,128]{1,0:T(8,128)S(1)}, u32[]{:S(2)}, u32[]{:S(2)}) %collective-permute-start.17) | collective-permute-done | bytes 65568 | tf_op jit(solution)/shard_map/ppermute | solution.py:321
  104.8 0.8 finish.1
  (6 shorter events, 0.1 us)
Async XLA Ops:
  4.1 7.2 %collective-permute-start = (bf16[32,80]{1,0:T(8,128)(2,1)S(1)}, bf16[32,80]{1,0:T(8,128)(2,1)S(1)}, u32[]{:S(2)}, u32[]{:S(2)}) collective-permute-start(bf16[32,80]{1,0:T(8,128)(2,1)S(1)} %get-tuple-element.37), channel_id=1, source_target_pairs={{0,16},{16,32},{32,48},{48,64},{64,80},{80,96},{96,112},{1,17},{17... | collective-permute-start | bytes 15368 | tf_op jit(solution)/shard_map/ppermute | solution.py:350
  7.7 5.5 %collective-permute-start.1 = (bf16[32,80]{1,0:T(8,128)(2,1)S(1)}, bf16[32,80]{1,0:T(8,128)(2,1)S(1)}, u32[]{:S(2)}, u32[]{:S(2)}) collective-permute-start(bf16[32,80]{1,0:T(8,128)(2,1)S(1)} %get-tuple-element.38), channel_id=1, source_target_pairs={{16,0},{32,16},{48,32},{64,48},{80,64},{96,80},{112,96},{17,1},{33... | collective-permute-start | bytes 15368 | tf_op jit(solution)/shard_map/ppermute | solution.py:351
  13.4 6.0 %collective-permute-start.2 = (bf16[128,80]{1,0:T(8,128)(2,1)S(1)}, bf16[128,80]{1,0:T(8,128)(2,1)S(1)}, u32[]{:S(2)}, u32[]{:S(2)}) collective-permute-start(bf16[128,80]{1,0:T(8,128)(2,1)S(1)} %get-tuple-element.71), channel_id=1, source_target_pairs={{0,1},{1,2},{2,3},{3,4},{4,5},{5,6},{6,7},{7,8},{8,9},{9,10},{10,1... | collective-permute-start | bytes 61448 | tf_op jit(solution)/shard_map/ppermute | solution.py:389
  14.7 6.2 %collective-permute-start.3 = (bf16[128,80]{1,0:T(8,128)(2,1)S(1)}, bf16[128,80]{1,0:T(8,128)(2,1)S(1)}, u32[]{:S(2)}, u32[]{:S(2)}) collective-permute-start(bf16[128,80]{1,0:T(8,128)(2,1)S(1)} %get-tuple-element.70), channel_id=1, source_target_pairs={{1,0},{2,1},{3,2},{4,3},{5,4},{6,5},{7,6},{8,7},{9,8},{10,9},{11,1... | collective-permute-start | bytes 61448 | tf_op jit(solution)/shard_map/ppermute | solution.py:390
  19.3 27.7 %copy-start.3 = (bf16[17,2,128,256]{3,2,1,0:T(8,128)(2,1)}, bf16[17,2,128,256]{3,2,1,0:T(8,128)(2,1)S(1)}, u32[]{:S(2)}) copy-start(bf16[17,2,128,256]{3,2,1,0:T(8,128)(2,1)S(1)} %get-tuple-element.58.refs_1_) | copy-start | bytes 6684676
  19.3 27.7 %copy-start.4 = (f32[4,256,512]{2,1,0:T(8,128)}, f32[4,256,512]{2,1,0:T(8,128)S(1)}, u32[]{:S(2)}) copy-start(f32[4,256,512]{2,1,0:T(8,128)S(1)} %get-tuple-element.59.refs_2_) | copy-start | bytes 6291460
  20.9 26.1 %copy-start = (bf16[4,256,256]{2,1,0:T(8,128)(2,1)S(1)}, bf16[4,256,256]{2,1,0:T(8,128)(2,1)}, u32[]{:S(2)}) copy-start(bf16[4,256,256]{2,1,0:T(8,128)(2,1)} %refs_2_.1) | copy-start | bytes 1572868
  20.9 26.1 %copy-start.1 = (bf16[4,8,32,256]{3,2,1,0:T(8,128)(2,1)S(1)}, bf16[4,8,32,256]{3,2,1,0:T(8,128)(2,1)}, u32[]{:S(2)}) copy-start(bf16[4,8,32,256]{3,2,1,0:T(8,128)(2,1)} %param.15) | copy-start | bytes 1572868
  47.1 18.7 %copy-start.2 = (bf16[4,256,512]{2,1,0:T(8,128)(2,1)S(1)}, bf16[4,256,512]{2,1,0:T(8,128)(2,1)}, u32[]{:S(2)}) copy-start(bf16[4,256,512]{2,1,0:T(8,128)(2,1)} %get-tuple-element.60.refs_3_) | copy-start | bytes 3145732
  49.9 15.9 %all-to-all-start.1 = ((bf16[16,64,256]{2,1,0:T(8,128)(2,1)}), bf16[16,64,256]{2,1,0:T(8,128)(2,1)S(1)}, u32[]{:S(2)}, u32[]{:S(2)}) async-start(bf16[16,64,256]{2,1,0:T(8,128)(2,1)} %mix.1), calls=%async_computation.1 | async-start | bytes 1048576 | tf_op jit(solution)/shard_map/all_to_all | solution.py:448
  56.5 15.4 %collective-permute-start.4 = (f32[4,64,256]{2,1,0:T(8,128)}, f32[4,64,256]{2,1,0:T(8,128)S(1)}, u32[]{:S(2)}, u32[]{:S(2)}) collective-permute-start(f32[4,64,256]{2,1,0:T(8,128)} %get-tuple-element.55), channel_id=1, source_target_pairs={{0,32},{16,48},{32,0},{48,16},{64,96},{80,112},{96,64},{112,80},{1... | collective-permute-start | bytes 786440 | tf_op jit(solution)/shard_map/ppermute | solution.py:465
  58.1 15.1 %collective-permute-start.5 = (f32[4,64,256]{2,1,0:T(8,128)}, f32[4,64,256]{2,1,0:T(8,128)S(1)}, u32[]{:S(2)}, u32[]{:S(2)}) collective-permute-start(f32[4,64,256]{2,1,0:T(8,128)} %get-tuple-element.56), channel_id=1, source_target_pairs={{0,64},{16,80},{32,96},{48,112},{64,0},{80,16},{96,32},{112,48},{1... | collective-permute-start | bytes 786440 | tf_op jit(solution)/shard_map/ppermute | solution.py:465
  60.8 15.0 %collective-permute-start.6 = (f32[4,64,256]{2,1,0:T(8,128)}, f32[4,64,256]{2,1,0:T(8,128)S(1)}, u32[]{:S(2)}, u32[]{:S(2)}) collective-permute-start(f32[4,64,256]{2,1,0:T(8,128)} %get-tuple-element.57), channel_id=1, source_target_pairs={{0,96},{16,112},{32,64},{48,80},{64,32},{80,48},{96,0},{112,16},{1... | collective-permute-start | bytes 786440 | tf_op jit(solution)/shard_map/ppermute | solution.py:465
  65.8 25.7 %copy-start.5 = (f32[4,64,256]{2,1,0:T(8,128)S(1)}, f32[4,64,256]{2,1,0:T(8,128)}, u32[]{:S(2)}) copy-start(f32[4,64,256]{2,1,0:T(8,128)} %get-tuple-element.54) | copy-start | bytes 786436
  75.8 1.3 %collective-permute-start.8 = (f32[128,128]{1,0:T(8,128)S(1)}, f32[128,128]{1,0:T(8,128)S(1)}, u32[]{:S(2)}, u32[]{:S(2)}) collective-permute-start(f32[128,128]{1,0:T(8,128)S(1)} %backward.1), channel_id=1, source_target_pairs={{0,1},{1,0},{2,3},{3,2},{4,5},{5,4},{6,7},{7,6},{8,9},{9,8},{10,11... | collective-permute-start | bytes 196616 | tf_op jit(solution)/shard_map/ppermute | solution.py:321
  77.0 4.9 %collective-permute-start.10 = (f32[128,128]{1,0:T(8,128)S(1)}, f32[128,128]{1,0:T(8,128)S(1)}, u32[]{:S(2)}, u32[]{:S(2)}) collective-permute-start(f32[128,128]{1,0:T(8,128)S(1)} %add.37), channel_id=1, source_target_pairs={{0,16},{1,17},{2,18},{3,19},{4,20},{5,21},{6,22},{7,23},{8,24},{9,... | collective-permute-start | bytes 196616 | tf_op jit(solution)/shard_map/ppermute | solution.py:321
  78.1 5.5 %collective-permute-start.11 = (f32[128,128]{1,0:T(8,128)S(1)}, f32[128,128]{1,0:T(8,128)S(1)}, u32[]{:S(2)}, u32[]{:S(2)}) collective-permute-start(f32[128,128]{1,0:T(8,128)S(1)} %add.37), channel_id=1, source_target_pairs={{0,18},{1,19},{2,16},{3,17},{4,22},{5,23},{6,20},{7,21},{8,26},{9,... | collective-permute-start | bytes 196616 | tf_op jit(solution)/shard_map/ppermute | solution.py:321
  80.9 5.8 %collective-permute-start.9 = (f32[128,128]{1,0:T(8,128)S(1)}, f32[128,128]{1,0:T(8,128)S(1)}, u32[]{:S(2)}, u32[]{:S(2)}) collective-permute-start(f32[128,128]{1,0:T(8,128)S(1)} %add.37), channel_id=1, source_target_pairs={{0,2},{1,3},{2,0},{3,1},{4,6},{5,7},{6,4},{7,5},{8,10},{9,11},{10,... | collective-permute-start | bytes 196616 | tf_op jit(solution)/shard_map/ppermute | solution.py:321
  86.6 6.0 %collective-permute-start.12 = (f32[128,128]{1,0:T(8,128)S(1)}, f32[128,128]{1,0:T(8,128)S(1)}, u32[]{:S(2)}, u32[]{:S(2)}) collective-permute-start(f32[128,128]{1,0:T(8,128)S(1)} %add_add_fusion.2), channel_id=1, source_target_pairs={{0,4},{1,5},{2,6},{3,7},{4,0},{5,1},{6,2},{7,3},{8,12},{9,13},{10,... | collective-permute-start | bytes 196616 | tf_op jit(solution)/shard_map/ppermute | solution.py:321
  88.2 5.8 %collective-permute-start.13 = (f32[128,128]{1,0:T(8,128)S(1)}, f32[128,128]{1,0:T(8,128)S(1)}, u32[]{:S(2)}, u32[]{:S(2)}) collective-permute-start(f32[128,128]{1,0:T(8,128)S(1)} %add_add_fusion.2), channel_id=1, source_target_pairs={{0,8},{1,9},{2,10},{3,11},{4,12},{5,13},{6,14},{7,15},{8,0},{9,1},... | collective-permute-start | bytes 196616 | tf_op jit(solution)/shard_map/ppermute | solution.py:321
  90.9 5.5 %collective-permute-start.14 = (f32[128,128]{1,0:T(8,128)S(1)}, f32[128,128]{1,0:T(8,128)S(1)}, u32[]{:S(2)}, u32[]{:S(2)}) collective-permute-start(f32[128,128]{1,0:T(8,128)S(1)} %add_add_fusion.2), channel_id=1, source_target_pairs={{0,12},{1,13},{2,14},{3,15},{4,8},{5,9},{6,10},{7,11},{8,4},{9,5},... | collective-permute-start | bytes 196616 | tf_op jit(solution)/shard_map/ppermute | solution.py:321
  91.5 9.7 %collective-permute-start.7 = (f32[4,32,256]{2,1,0:T(8,128)S(1)}, f32[4,32,256]{2,1,0:T(8,128)S(1)}, u32[]{:S(2)}, u32[]{:S(2)}) collective-permute-start(f32[4,32,256]{2,1,0:T(8,128)S(1)} %split.9), channel_id=1, source_target_pairs={{0,16},{16,0},{32,48},{48,32},{64,80},{80,64},{96,112},{112,96},{1... | collective-permute-start | bytes 393224 | tf_op jit(solution)/shard_map/ppermute | solution.py:498
  96.4 5.5 %collective-permute-start.15 = (f32[128,128]{1,0:T(8,128)S(1)}, f32[128,128]{1,0:T(8,128)S(1)}, u32[]{:S(2)}, u32[]{:S(2)}) collective-permute-start(f32[128,128]{1,0:T(8,128)S(1)} %add_add_fusion.1.a_ref), channel_id=1, source_target_pairs={{0,32},{1,33},{2,34},{3,35},{4,36},{5,37},{6,38},{7,39},{8,40},{9,... | collective-permute-start | bytes 196616 | tf_op jit(solution)/shard_map/ppermute | solution.py:321
  96.5 5.8 %collective-permute-start.16 = (f32[128,128]{1,0:T(8,128)S(1)}, f32[128,128]{1,0:T(8,128)S(1)}, u32[]{:S(2)}, u32[]{:S(2)}) collective-permute-start(f32[128,128]{1,0:T(8,128)S(1)} %add_add_fusion.1.a_ref), channel_id=1, source_target_pairs={{0,64},{1,65},{2,66},{3,67},{4,68},{5,69},{6,70},{7,71},{8,72},{9,... | collective-permute-start | bytes 196616 | tf_op jit(solution)/shard_map/ppermute | solution.py:321
  99.3 5.5 %collective-permute-start.17 = (f32[128,128]{1,0:T(8,128)S(1)}, f32[128,128]{1,0:T(8,128)S(1)}, u32[]{:S(2)}, u32[]{:S(2)}) collective-permute-start(f32[128,128]{1,0:T(8,128)S(1)} %add_add_fusion.1.a_ref), channel_id=1, source_target_pairs={{0,96},{1,97},{2,98},{3,99},{4,100},{5,101},{6,102},{7,103},{8,104... | collective-permute-start | bytes 196616 | tf_op jit(solution)/shard_map/ppermute | solution.py:321

commit v7 on v6

--- a/solution.py
+++ b/solution.py
@@ -103,7 +103,8 @@
 
 
 def inner_kernel(
-    feat_ref, ylo_ref, yhi_ref, table_ref, band_ref, emb_ref, slope_ref, hidden_ref, edge_ref,
+    feat_ref, ylo_ref, yhi_ref, table_ref, band_ref, emb_ref, slope_hbm, hidden_ref, edge_ref,
+    slope_ref, sem,
 ):
     table = table_ref[...]
     row = iota((128, 80), 0)
@@ -116,6 +117,7 @@
         f = jnp.where(row == 64, ylo[z : z + 1, :], f)
         f = jnp.where(row == 127, yhi[z : z + 1, :], f)
         emb_ref[(z + 1) // 2, (z + 1) % 2] = dot(f.astype(BF16), table, 1, 0).astype(BF16)
+    copies = []
     for bc in range(4):
         b, c = bc // 2, bc % 2
         for half in range(2):
@@ -130,6 +132,11 @@
                 edge_ref[1, b] = acc[:, 224:]
             at = slice(256 * half, 256 * half + 256)
             hidden_ref[bc, :, at], slope_ref[bc, :, at] = activate(acc)
+            part = (bc, slice(None), pl.ds(256 * half, 256))
+            copies.append(pltpu.make_async_copy(slope_ref.at[part], slope_hbm.at[part], sem.at[len(copies)]))
+            copies[-1].start()
+    for copy in copies:
+        copy.wait()
 
 
 def pair_rows(hidden_ref, pair):
@@ -171,30 +178,35 @@
         copy.wait()
 
 
-def mixed(coarse_ref, mix_ref, cot_ref):
-    width = mix_ref.shape[1]
-    flat = coarse_ref[...].reshape(width, 256).T
-    pre = dot(flat, mix_ref[0], 1, 1)
+def turn_kernel(mix_ref, cot_ref, mix_t_ref, cot_t_ref):
+    mix_t_ref[0] = mix_ref[0].T
+    cot_t_ref[0] = cot_ref[0].T
+
+
+def mixed(coarse_ref, mix_ref, cot_t_ref):
+    coarse = coarse_ref[...].reshape(mix_ref.shape[1], 256)
+    pre = dot(mix_ref[0], coarse, 1, 0)
     sigma = jax.nn.sigmoid(pre)
-    grad = cot_ref[0].astype(F32) * (sigma * (1.0 + pre * (1.0 - sigma)))
-    return flat, pre * sigma, grad.astype(BF16).T
-
-
-def mix_kernel(coarse_ref, mix_ref, cot_ref, grad_ref):
-    _, _, turned = mixed(coarse_ref, mix_ref, cot_ref)
-    grad_ref[...] = dot(mix_ref[0].T, turned, 1, 0).astype(BF16).reshape(grad_ref.shape)
-
-
-def mix_grad_kernel(scale, me_ref, coarse_ref, mix_ref, cot_ref, mid_ref, *more_refs):
+    grad = cot_t_ref[0].astype(F32) * (sigma * (1.0 + pre * (1.0 - sigma)))
+    return coarse, pre * sigma, grad.astype(BF16)
+
+
+def mix_kernel(coarse_ref, mix_ref, cot_t_ref, mix_t_ref, grad_ref):
+    _, _, grad = mixed(coarse_ref, mix_ref, cot_t_ref)
+    grad_ref[...] = dot(mix_t_ref[0], grad, 1, 0).astype(BF16).reshape(grad_ref.shape)
+
+
+def mix_grad_kernel(scale, me_ref, coarse_ref, mix_ref, cot_t_ref, mid_ref, *more_refs):
     *share_refs, total_ref = more_refs
-    flat, mid, turned = mixed(coarse_ref, mix_ref, cot_ref)
-    mid_ref[0] = mid.astype(BF16)
-    total_ref[...] = dot(turned, flat, 1, 0) * scale
+    coarse, mid, grad = mixed(coarse_ref, mix_ref, cot_t_ref)
+    mid_ref[0] = mid.astype(BF16).T
+    total_ref[...] = dot(grad, coarse, 1, 1) * scale
     rows = total_ref.shape[0] // (2 * len(share_refs))
     for place in range(2 * len(share_refs)):
         start = pl.multiple_of(jnp.bitwise_xor(me_ref[0], place) * rows, rows)
         at = place % 2 * rows
-        share_refs[place // 2][0, at : at + rows, :] = total_ref[pl.ds(start, rows), :]
+        share_ref = share_refs[place // 2]
+        share_ref[0, at : at + rows, :] = total_ref[pl.ds(start, rows), :].astype(share_ref.dtype)
 
 
 def fold(value, step):
@@ -209,13 +221,15 @@
 
 
 def backward_kernel(
-    down_scale, conv_scale, cgrad_ref, emb_hbm, slope_hbm, hidden_ref, pair_ref, pair_t_ref, face_ref, edge_ref,
-    out_ref, turn_a, turn_b, turned_pg, emb_in, slope_in, sem,
+    down_scale, conv_scale, cgrad_ref, emb_hbm, slope_hbm, hidden_hbm, pair_ref, pair_t_ref, face_ref, edge_ref,
+    out_ref, turn_a, turn_b, turned_pg, emb_in, slope_in, hidden_ref, sem,
 ):
     copies = [
         pltpu.make_async_copy(slope_hbm, slope_in, sem.at[0]),
         pltpu.make_async_copy(emb_hbm, emb_in, sem.at[1]),
+        pltpu.make_async_copy(hidden_hbm, hidden_ref, sem.at[2]),
     ]
+    copies[2].start()
     copies[0].start()
     for half in range(2):
         turn_b[half] = cgrad_ref[:, 128 * half : 128 * half + 128].astype(F32)
@@ -230,6 +244,7 @@
     copies[1].start()
     cg_t = turn_a[...].astype(BF16)
     pairs = [cg_t[128 * pair : 128 * pair + 128, :] for pair in range(4)]
+    copies[2].wait()
     down = None
     for pair in range(4):
         part = dot(pairs[pair], pair_rows(hidden_ref, pair), 1, 1)
@@ -392,12 +407,13 @@
         inner_kernel,
         out_shape=(
             shape((17, 2, 128, 256), BF16),
-            shape((4, 256, 512), F32),
+            pltpu.HBM((4, 256, 512), F32),
             shape((4, 256, 512), BF16),
             shape((2, 2, 256, 32), F32),
         ),
         in_specs=[VMEM] * 5,
-        out_specs=(VMEM,) * 4,
+        out_specs=(VMEM, HBM, VMEM, VMEM),
+        scratch_shapes=[pltpu.VMEM((4, 256, 512), F32), pltpu.SemaphoreType.DMA((8,))],
         compiler_params=params(12),
         cost_estimate=cost(3 << 30, 10 << 20),
         name="inner",
@@ -424,6 +440,9 @@
         name="outer",
     )(zlo, zhi, table, band, pair, edge, hidden)
 
+    mix_weight, cotangent_rows, coarse = lax.optimization_barrier(
+        (mix_weight, cotangent.reshape(mine, 256, width), coarse)
+    )
     sent = lax.all_to_all(
         coarse.reshape(count_z, mine * 16, 256), "sz", split_axis=0, concat_axis=0, tiled=True
     )
@@ -432,33 +451,44 @@
     mix_specs = [
         pl.BlockSpec((count_z, 16, 256), lambda c: (0, c, 0)),
         block(1, width, width),
-        block(1, 256, width),
+        block(1, width, 256),
     ]
-    cotangent_rows = cotangent.reshape(mine, 256, width)
+    mix_t, cotangent_t = pl.pallas_call(
+        turn_kernel,
+        grid=(mine,),
+        out_shape=(shape((mine, width, width), BF16), shape((mine, width, 256), BF16)),
+        in_specs=[block(1, width, width), block(1, 256, width)],
+        out_specs=(block(1, width, width), block(1, width, 256)),
+        compiler_params=params(4),
+        cost_estimate=cost(1 << 20, 2 << 20),
+        name="turn",
+    )(mix_weight, cotangent_rows)
     back = pl.pallas_call(
         mix_kernel,
         grid=(mine,),
         out_shape=shape((count_z, mine * 16, 256), BF16),
-        in_specs=mix_specs,
+        in_specs=mix_specs + [block(1, width, width)],
         out_specs=pl.BlockSpec((count_z, 16, 256), lambda c: (0, c, 0)),
         compiler_params=params(8),
         cost_estimate=cost(mine * 2 * 2 * 256 * width * width, 2 << 20),
         name="mix",
-    )(sent, mix_weight, cotangent_rows)
+    )(sent, mix_weight, cotangent_t, mix_t)
     coarse_grad = lax.all_to_all(back, "sz", split_axis=0, concat_axis=0, tiled=True)
     sent, back = lax.optimization_barrier((sent, back))
     mid, *mix_parts = pl.pallas_call(
         lambda *refs: mix_grad_kernel(1.0 / math.sqrt(8 * 32 * count_y), *refs),
         grid=(mine,),
         out_shape=[shape((mine, 256, width), BF16)]
-        + [pltpu.HBM((mine, width // shares, width), F32)] * shares,
+        + [
+            pltpu.HBM((mine, width // shares, width), BF16 if k else F32) for k in range(shares)
+        ],
         in_specs=[pl.BlockSpec(memory_space=pltpu.SMEM)] + mix_specs,
         out_specs=[block(1, 256, width)] + [block(1, width // shares, width)] * shares,
         scratch_shapes=[pltpu.VMEM((width, width), F32)],
         compiler_params=params(8),
         cost_estimate=cost(mine * 2 * 2 * 256 * width * width, 3 << 20),
         name="mix_grad",
-    )(lax.axis_index("sy")[None], sent, mix_weight, cotangent_rows)
+    )(lax.axis_index("sy")[None], sent, mix_weight, cotangent_t)
     mix_sum = mix_parts[0]
     moved = []
     for k, part in enumerate(mix_parts[1:], 1):
@@ -469,7 +499,7 @@
             1.0 / math.sqrt(cells // 8), 1.0 / math.sqrt(cells), *refs
         ),
         out_shape=shape((128, 128), F32),
-        in_specs=[VMEM, HBM, HBM] + [VMEM] * 5,
+        in_specs=[VMEM, HBM, HBM, HBM] + [VMEM] * 4,
         out_specs=VMEM,
         scratch_shapes=[
             pltpu.VMEM((512, 512), F32),
@@ -477,15 +507,15 @@
             pltpu.VMEM((4, 256, 512), BF16),
             pltpu.VMEM((17, 2, 128, 256), BF16),
             pltpu.VMEM((4, 256, 512), F32),
-            pltpu.SemaphoreType.DMA((2,)),
+            pltpu.VMEM((4, 256, 512), BF16),
+            pltpu.SemaphoreType.DMA((3,)),
         ],
         compiler_params=params(12),
         cost_estimate=cost(4 << 30, 8 << 20),
         name="backward",
     )(
         coarse_grad.reshape(1024, 256),
-        *kept(embedded, slope),
-        hidden,
+        *kept(embedded, slope, hidden),
         pair,
         pair_t,
         faces,
@@ -493,9 +523,10 @@
     )
     *moved, sums = lax.optimization_barrier((*moved, sums))
     for part in moved:
-        mix_sum = mix_sum + part
+        mix_sum = mix_sum + part.astype(F32)
     mine_last, other = jnp.split(mix_sum, 2, axis=1)
-    mix_grad = mine_last + lax.ppermute(other, "sy", [(i, i ^ 1) for i in range(count_y)])
+    other = lax.ppermute(other.astype(BF16), "sy", [(i, i ^ 1) for i in range(count_y)])
+    mix_grad = mine_last + other.astype(F32)
 
     rounds = sum_rounds(count_y, count_z)
     for masks in rounds[:-1]:

time: 106 us -> 99.9 us (0.942)
  blocking collectives: 23.4 us -> 0 us
  starting transfers between devices: 31.3 us -> 41.7 us
  waiting for transfers between devices: 24.5 us -> 30.7 us
    all_to_all x1 -> x0, blocking collectives: 23.4 us -> none  [per_device(): lax.all_to_all(coarse.reshape(count_z, mine * 16, 256), 'sz', split_axis=...]
    all_to_all x0 -> x1, waiting for transfers between devices: none -> 11.8 us  [per_device(): lax.all_to_all(coarse.reshape(count_z, mine * 16, 256), 'sz', split_axis=...]
    all_to_all x0 -> x1, starting transfers between devices: none -> 11.5 us  [per_device(): lax.all_to_all(coarse.reshape(count_z, mine * 16, 256), 'sz', split_axis=...]
    ppermute x3, waiting for transfers between devices: 3.86 us -> 0.01 us  [per_device(): lax.ppermute(part, 'sy', [(i, i ^ 2 * k) for i in range(count_y)])]
    ppermute x10, waiting for transfers between devices: 12.6 us -> 11.1 us  [exchanged(): lax.ppermute(value, ('sy', 'sz'), [(i, i ^ m) for i in range(count)])]
    pallas_call x1 -> x2, Pallas kernels: 3.35 us -> 4.61 us  [the longest x1 4.08 us: per_device(): pl.pallas_call(inner_kernel, out_shape=(shape((17, 2, 128, 256), BF16), p...]
  transfers between devices with their start and end apart: 19 -> 20, of which waited for: 12 -> 11; matrix products, arithmetic and copies ran while one was open for 1% -> 1% of each run, Pallas kernels for 14% -> 16%
where the time goes in v7:
time: 99.9 us; the launch traced here: 99.4 us
  starting transfers between devices  41.7 us (42%)
  waiting for transfers between devices  30.7 us (31%)
  Pallas kernels  25.2 us (25%)
    ppermute x10, starting transfers between devices, exchanged(): lax.ppermute(value, ('sy', 'sz'), [(i, i ^ m) for i in range(count)])  13.9 us
    all_to_all x1, waiting for transfers between devices, per_device(): lax.all_to_all(coarse.reshape(count_z, mine * 16, 256), 'sz', split_axis=...  11.8 us
    all_to_all x1, starting transfers between devices, per_device(): lax.all_to_all(coarse.reshape(count_z, mine * 16, 256), 'sz', split_axis=...  11.5 us
    ppermute x10, waiting for transfers between devices, exchanged(): lax.ppermute(value, ('sy', 'sz'), [(i, i ^ m) for i in range(count)])  11.1 us
    pallas_call x1, Pallas kernels, per_device(): pl.pallas_call(lambda *refs: backward_kernel(1.0 / math.sqrt(cells // 8),...  6.04 us
    all_to_all x1, waiting for transfers between devices, per_device(): lax.all_to_all(back, 'sz', split_axis=0, concat_axis=0, tiled=True)  5.1 us
    ppermute x3, starting transfers between devices, per_device(): lax.ppermute(part, 'sy', [(i, i ^ 2 * k) for i in range(count_y)])  4.7 us
    pallas_call x1, Pallas kernels, per_device(): pl.pallas_call(inner_kernel, out_shape=(shape((17, 2, 128, 256), BF16), p...  4.08 us
  transfers between devices with their start and end apart: 20, of which 11 were waited for; matrix products, arithmetic and copies ran while one was open for 1% of the time, Pallas kernels for 16%

profile of v7, /device:TPU:0, one launch (start us, length us, event | category | flops | bytes accessed | tf_op | source)
XLA Modules:
  0.0 99.4 jit_solution(8920401050221662577)
XLA Ops:
  0.6 3.5 %features.1 = (bf16[32,128,80]{2,1,0:T(8,128)(2,1)S(1)}, bf16[32,80]{1,0:T(8,128)(2,1)S(1)}, bf16[32,80]{1,0:T(8,128)(2,1)S(1)}) custom-call(s32[16,32,64]{2,1,0:T(8,128)} %bitcast.33, bf16[16,32,64]{2,1,0:T(8,128)(2,1)} %bitcast.34), custom_call_target="tpu_custom_call" | custom-call | flops 41943040 | bytes 2097152 | tf_op jit(solution)/shard_map/features/pallas_call | solution.py:346
  4.1 3.6 %collective-permute-start = (bf16[32,80]{1,0:T(8,128)(2,1)S(1)}, bf16[32,80]{1,0:T(8,128)(2,1)S(1)}, u32[]{:S(2)}, u32[]{:S(2)}) collective-permute-start(bf16[32,80]{1,0:T(8,128)(2,1)S(1)} %get-tuple-element.42), channel_id=1, source_target_pairs={{0,16},{16,32},{32,48},{48,64},{64,80},{80,96},{96,112},{1,17},{17... | collective-permute-start | bytes 15368 | tf_op jit(solution)/shard_map/ppermute | solution.py:365
  7.7 1.3 %collective-permute-start.1 = (bf16[32,80]{1,0:T(8,128)(2,1)S(1)}, bf16[32,80]{1,0:T(8,128)(2,1)S(1)}, u32[]{:S(2)}, u32[]{:S(2)}) collective-permute-start(bf16[32,80]{1,0:T(8,128)(2,1)S(1)} %get-tuple-element.43), channel_id=1, source_target_pairs={{16,0},{32,16},{48,32},{64,48},{80,64},{96,80},{112,96},{17,1},{33... | collective-permute-start | bytes 15368 | tf_op jit(solution)/shard_map/ppermute | solution.py:366
  9.0 2.3 %weights.1 = (bf16[9,256,256]{2,1,0:T(8,128)(2,1)S(1)}, bf16[128,256]{1,0:T(8,128)(2,1)S(1)}, bf16[256,128]{1,0:T(8,128)(2,1)S(1)}, bf16[80,256]{1,0:T(8,128)(2,1)S(1)}) custom-call(bf16[16,16,27]{2,1,0:T(8,128)(2,1)} %bitcast.37, bf16[8,16,64]{2,1,0:T(8,128)(2,1)} %bitcast.39, bf16[4,16]{1,0:T(4,128)(2,1)} %mat_hbm.1, bf16[1,16]{1,0:T(2,128)(2,1)} %bitcast.40), custom_call_target="tpu_custom_call" | custom-call | flops 56623104 | bytes 3145728 | tf_op jit(solution)/shard_map/weights/pallas_call | solution.py:367
  11.4 0.0 collective-permute-done.ylo_ref
  11.4 1.9 %collective-permute-done.1.yhi_ref = bf16[32,80]{1,0:T(8,128)(2,1)S(1)} collective-permute-done((bf16[32,80]{1,0:T(8,128)(2,1)S(1)}, bf16[32,80]{1,0:T(8,128)(2,1)S(1)}, u32[]{:S(2)}, u32[]{:S(2)}) %collective-permute-start.1) | collective-permute-done | bytes 5152 | tf_op jit(solution)/shard_map/ppermute | solution.py:366
  13.3 0.1 fusion
  13.4 1.3 %collective-permute-start.2 = (bf16[128,80]{1,0:T(8,128)(2,1)S(1)}, bf16[128,80]{1,0:T(8,128)(2,1)S(1)}, u32[]{:S(2)}, u32[]{:S(2)}) collective-permute-start(bf16[128,80]{1,0:T(8,128)(2,1)S(1)} %get-tuple-element.81), channel_id=1, source_target_pairs={{0,1},{1,2},{2,3},{3,4},{4,5},{5,6},{6,7},{7,8},{8,9},{9,10},{10,1... | collective-permute-start | bytes 61448 | tf_op jit(solution)/shard_map/ppermute | solution.py:404
  14.7 1.3 %collective-permute-start.3 = (bf16[128,80]{1,0:T(8,128)(2,1)S(1)}, bf16[128,80]{1,0:T(8,128)(2,1)S(1)}, u32[]{:S(2)}, u32[]{:S(2)}) collective-permute-start(bf16[128,80]{1,0:T(8,128)(2,1)S(1)} %get-tuple-element.80), channel_id=1, source_target_pairs={{1,0},{2,1},{3,2},{4,3},{5,4},{6,5},{7,6},{8,7},{9,8},{10,9},{11,1... | collective-permute-start | bytes 61448 | tf_op jit(solution)/shard_map/ppermute | solution.py:405
  16.0 4.1 %inner.1 = (bf16[17,2,128,256]{3,2,1,0:T(8,128)(2,1)S(1)}, f32[4,256,512]{2,1,0:T(8,128)}, bf16[4,256,512]{2,1,0:T(8,128)(2,1)S(1)}, f32[2,2,256,32]{3,2,1,0:T(8,128)S(1)}) custom-call(bf16[32,128,80]{2,1,0:T(8,128)(2,1)S(1)} %get-tuple-element.50.feat_ref, bf16[32,80]{1,0:T(8,128)(2,1)S(1)} %collective-permute-done.ylo_ref, ...), custom_call_target="tpu_custom_call" | custom-call | flops 3221225472 | bytes 10485760 | tf_op jit(solution)/shard_map/inner/pallas_call | solution.py:406
  20.1 0.0 copy-start.2
  20.1 0.0 collective-permute-done.2.zlo_ref
  20.1 0.8 collective-permute-done.3.zhi_ref
  20.9 0.0 copy-start
  20.9 0.0 copy-start.1
  20.9 2.7 %outer.1 = (bf16[2,128,256]{2,1,0:T(8,128)(2,1)S(1)}, f32[256,128]{1,0:T(8,128)S(1)}, bf16[4,256,512]{2,1,0:T(8,128)(2,1)}, bf16[1024,256]{1,0:T(8,128)(2,1)}) custom-call(bf16[128,80]{1,0:T(8,128)(2,1)S(1)} %collective-permute-done.2.zlo_ref, bf16[128,80]{1,0:T(8,128)(2,1)S(1)} %collective-permute-done.3.zhi_ref, ...), custom_call_target="tpu_custom_call" | custom-call | flops 1073741824 | bytes 4194304 | tf_op jit(solution)/shard_map/outer/pallas_call | solution.py:421
  23.6 0.0 copy-done.2
  23.7 11.5 %all-to-all-start = ((bf16[16,64,256]{2,1,0:T(8,128)(2,1)}), bf16[16,64,256]{2,1,0:T(8,128)(2,1)S(1)}, u32[]{:S(2)}, u32[]{:S(2)}) async-start(bf16[16,64,256]{2,1,0:T(8,128)(2,1)} %bitcast.32), calls=%async_computation | async-start | bytes 1048576 | tf_op jit(solution)/shard_map/all_to_all | solution.py:446
  35.1 0.0 copy-done
  35.1 0.0 copy-done.1
  35.1 0.5 turn.1
  35.7 11.8 %all-to-all-done.coarse_ref.refs_1_ = bf16[16,64,256]{2,1,0:T(8,128)(2,1)S(1)} async-done(((bf16[16,64,256]{2,1,0:T(8,128)(2,1)}), bf16[16,64,256]{2,1,0:T(8,128)(2,1)S(1)}, u32[]{:S(2)}, u32[]{:S(2)}) %all-to-all-start) | async-done | bytes 524320 | tf_op jit(solution)/shard_map/all_to_all | solution.py:446
  47.5 2.7 %mix.1 = bf16[16,64,256]{2,1,0:T(8,128)(2,1)} custom-call(bf16[16,64,256]{2,1,0:T(8,128)(2,1)S(1)} %all-to-all-done.coarse_ref.refs_1_, bf16[4,256,256]{2,1,0:T(8,128)(2,1)S(1)} %copy-done, bf16[4,256,256]{2,1,0:T(8,128)(2,1)S(1)} %get-tuple-element.60.cot_t_ref.refs_3_, bf16[4,256,256]{2,1,0:T(8,128)(2,1)S(1)} %get-tuple-element.61.mix_t_ref), custom_call_target="tpu_custom_call" | custom-call | flops 268435456 | bytes 2097152 | tf_op jit(solution)/shard_map/mix/pallas_call | solution.py:466
  50.2 3.6 %all-to-all-start.1 = ((bf16[16,64,256]{2,1,0:T(8,128)(2,1)}), bf16[16,64,256]{2,1,0:T(8,128)(2,1)S(1)}, u32[]{:S(2)}, u32[]{:S(2)}) async-start(bf16[16,64,256]{2,1,0:T(8,128)(2,1)} %mix.1), calls=%async_computation.1 | async-start | bytes 1048576 | tf_op jit(solution)/shard_map/all_to_all | solution.py:476
  53.7 2.5 %mix_grad.1 = (bf16[4,256,256]{2,1,0:T(8,128)(2,1)}, f32[4,64,256]{2,1,0:T(8,128)}, bf16[4,64,256]{2,1,0:T(8,128)(2,1)}, bf16[4,64,256]{2,1,0:T(8,128)(2,1)}, bf16[4,64,256]{2,1,0:T(8,128)(2,1)}) custom-call(s32[1]{0:T(128)} %bitcast.refs_0_, bf16[16,64,256]{2,1,0:T(8,128)(2,1)S(1)} %all-to-all-done.coarse_ref.refs_1_, bf16[4,256,256]{2,1,0:T(8,128)(2,1)S(1)} %copy-done, ...), custom_call_target="tpu_custom_call" | custom-call | flops 268435456 | bytes 3145728 | tf_op jit(solution)/shard_map/mix_grad/pallas_call | solution.py:478
  56.3 1.9 %collective-permute-start.4 = (bf16[4,64,256]{2,1,0:T(8,128)(2,1)}, bf16[4,64,256]{2,1,0:T(8,128)(2,1)S(1)}, u32[]{:S(2)}, u32[]{:S(2)}) collective-permute-start(bf16[4,64,256]{2,1,0:T(8,128)(2,1)} %get-tuple-element.65), channel_id=1, source_target_pairs={{0,32},{16,48},{32,0},{48,16},{64,96},{80,112},{96,64},{112,80},{1... | collective-permute-start | bytes 393224 | tf_op jit(solution)/shard_map/ppermute | solution.py:495
  58.2 2.7 %collective-permute-start.5 = (bf16[4,64,256]{2,1,0:T(8,128)(2,1)}, bf16[4,64,256]{2,1,0:T(8,128)(2,1)S(1)}, u32[]{:S(2)}, u32[]{:S(2)}) collective-permute-start(bf16[4,64,256]{2,1,0:T(8,128)(2,1)} %get-tuple-element.66), channel_id=1, source_target_pairs={{0,64},{16,80},{32,96},{48,112},{64,0},{80,16},{96,32},{112,48},{1... | collective-permute-start | bytes 393224 | tf_op jit(solution)/shard_map/ppermute | solution.py:495
  60.9 0.1 collective-permute-start.6
  61.0 5.1 %all-to-all-done.1 = bf16[16,64,256]{2,1,0:T(8,128)(2,1)S(1)} async-done(((bf16[16,64,256]{2,1,0:T(8,128)(2,1)}), bf16[16,64,256]{2,1,0:T(8,128)(2,1)S(1)}, u32[]{:S(2)}, u32[]{:S(2)}) %all-to-all-start.1) | async-done | bytes 524320 | tf_op jit(solution)/shard_map/all_to_all | solution.py:476
  66.1 0.0 copy-start.3
  66.1 6.0 %backward.1 = f32[128,128]{1,0:T(8,128)S(1)} custom-call(bf16[1024,256]{1,0:T(8,128)(2,1)S(1)} %bitcast.31, bf16[17,2,128,256]{3,2,1,0:T(8,128)(2,1)} %copy-done.2, f32[4,256,512]{2,1,0:T(8,128)} %get-tuple-element.69.refs_2_, bf16[4,256,512]{2,1,0:T(8,128)(2,1)} %get-tuple-element.70.refs_3_, bf16[128,256]{1,0:T(8,128)(2,1)S(1)} %get-tuple-element.53.pair_ref.refs_4_, ...), custom_call_target="tpu_custom_call" | custom-call | flops 4294967296 | bytes 8388608 | tf_op jit(solution)/shard_map/backward/pallas_call | solution.py:497
  72.1 0.0 collective-permute-done.4
  72.1 0.0 collective-permute-done.5
  72.1 0.0 collective-permute-done.6
  72.1 0.1 collective-permute-start.8
  72.2 1.2 %collective-permute-done.8 = f32[128,128]{1,0:T(8,128)S(1)} collective-permute-done((f32[128,128]{1,0:T(8,128)S(1)}, f32[128,128]{1,0:T(8,128)S(1)}, u32[]{:S(2)}, u32[]{:S(2)}) %collective-permute-start.8) | collective-permute-done | bytes 65568 | tf_op jit(solution)/shard_map/ppermute | solution.py:336
  73.5 2.1 %collective-permute-start.10 = (f32[128,128]{1,0:T(8,128)S(1)}, f32[128,128]{1,0:T(8,128)S(1)}, u32[]{:S(2)}, u32[]{:S(2)}) collective-permute-start(f32[128,128]{1,0:T(8,128)S(1)} %add.37), channel_id=1, source_target_pairs={{0,16},{1,17},{2,18},{3,19},{4,20},{5,21},{6,22},{7,23},{8,24},{9,... | collective-permute-start | bytes 196616 | tf_op jit(solution)/shard_map/ppermute | solution.py:336
  75.6 0.0 collective-permute-start.11
  75.6 2.2 %collective-permute-start.9 = (f32[128,128]{1,0:T(8,128)S(1)}, f32[128,128]{1,0:T(8,128)S(1)}, u32[]{:S(2)}, u32[]{:S(2)}) collective-permute-start(f32[128,128]{1,0:T(8,128)S(1)} %add.37), channel_id=1, source_target_pairs={{0,2},{1,3},{2,0},{3,1},{4,6},{5,7},{6,4},{7,5},{8,10},{9,11},{10,... | collective-permute-start | bytes 196616 | tf_op jit(solution)/shard_map/ppermute | solution.py:336
  77.7 0.3 collective-permute-done.10
  78.0 4.1 %collective-permute-done.11 = f32[128,128]{1,0:T(8,128)S(1)} collective-permute-done((f32[128,128]{1,0:T(8,128)S(1)}, f32[128,128]{1,0:T(8,128)S(1)}, u32[]{:S(2)}, u32[]{:S(2)}) %collective-permute-start.11) | collective-permute-done | bytes 65568 | tf_op jit(solution)/shard_map/ppermute | solution.py:336
  82.0 0.0 collective-permute-done.9
  82.1 0.3 collective-permute-start.12
  82.4 2.7 %collective-permute-start.13 = (f32[128,128]{1,0:T(8,128)S(1)}, f32[128,128]{1,0:T(8,128)S(1)}, u32[]{:S(2)}, u32[]{:S(2)}) collective-permute-start(f32[128,128]{1,0:T(8,128)S(1)} %add_add_fusion.1), channel_id=1, source_target_pairs={{0,8},{1,9},{2,10},{3,11},{4,12},{5,13},{6,14},{7,15},{8,0},{9,1},... | collective-permute-start | bytes 196616 | tf_op jit(solution)/shard_map/ppermute | solution.py:336
  85.1 1.8 %collective-permute-start.14 = (f32[128,128]{1,0:T(8,128)S(1)}, f32[128,128]{1,0:T(8,128)S(1)}, u32[]{:S(2)}, u32[]{:S(2)}) collective-permute-start(f32[128,128]{1,0:T(8,128)S(1)} %add_add_fusion.1), channel_id=1, source_target_pairs={{0,12},{1,13},{2,14},{3,15},{4,8},{5,9},{6,10},{7,11},{8,4},{9,5},... | collective-permute-start | bytes 196616 | tf_op jit(solution)/shard_map/ppermute | solution.py:336
  86.9 0.0 copy-done.3
  86.9 0.1 convert_add_fusion
  86.9 0.7 collective-permute-start.7
  87.6 0.0 collective-permute-done.12
  87.6 0.6 collective-permute-done.13
  88.3 2.3 %collective-permute-done.14 = f32[128,128]{1,0:T(8,128)S(1)} collective-permute-done((f32[128,128]{1,0:T(8,128)S(1)}, f32[128,128]{1,0:T(8,128)S(1)}, u32[]{:S(2)}, u32[]{:S(2)}) %collective-permute-start.14) | collective-permute-done | bytes 65568 | tf_op jit(solution)/shard_map/ppermute | solution.py:336
  90.6 0.9 collective-permute-start.15
  91.5 1.6 %collective-permute-start.16 = (f32[128,128]{1,0:T(8,128)S(1)}, f32[128,128]{1,0:T(8,128)S(1)}, u32[]{:S(2)}, u32[]{:S(2)}) collective-permute-start(f32[128,128]{1,0:T(8,128)S(1)} %add_add_fusion.a_ref), channel_id=1, source_target_pairs={{0,64},{1,65},{2,66},{3,67},{4,68},{5,69},{6,70},{7,71},{8,72},{9,... | collective-permute-start | bytes 196616 | tf_op jit(solution)/shard_map/ppermute | solution.py:336
  93.1 2.2 %collective-permute-start.17 = (f32[128,128]{1,0:T(8,128)S(1)}, f32[128,128]{1,0:T(8,128)S(1)}, u32[]{:S(2)}, u32[]{:S(2)}) collective-permute-start(f32[128,128]{1,0:T(8,128)S(1)} %add_add_fusion.a_ref), channel_id=1, source_target_pairs={{0,96},{1,97},{2,98},{3,99},{4,100},{5,101},{6,102},{7,103},{8,104... | collective-permute-start | bytes 196616 | tf_op jit(solution)/shard_map/ppermute | solution.py:336
  95.4 0.0 collective-permute-done.7
  95.4 0.7 slice_add_fusion
  96.0 0.0 collective-permute-done.15.b_ref
  96.0 1.2 %collective-permute-done.16.c_ref = f32[128,128]{1,0:T(8,128)S(1)} collective-permute-done((f32[128,128]{1,0:T(8,128)S(1)}, f32[128,128]{1,0:T(8,128)S(1)}, u32[]{:S(2)}, u32[]{:S(2)}) %collective-permute-start.16) | collective-permute-done | bytes 65568 | tf_op jit(solution)/shard_map/ppermute | solution.py:336
  97.3 1.3 %collective-permute-done.17.d_ref = f32[128,128]{1,0:T(8,128)S(1)} collective-permute-done((f32[128,128]{1,0:T(8,128)S(1)}, f32[128,128]{1,0:T(8,128)S(1)}, u32[]{:S(2)}, u32[]{:S(2)}) %collective-permute-start.17) | collective-permute-done | bytes 65568 | tf_op jit(solution)/shard_map/ppermute | solution.py:336
  98.6 0.8 finish.1
  (6 shorter events, 0.1 us)
Async XLA Ops:
  4.1 7.2 %collective-permute-start = (bf16[32,80]{1,0:T(8,128)(2,1)S(1)}, bf16[32,80]{1,0:T(8,128)(2,1)S(1)}, u32[]{:S(2)}, u32[]{:S(2)}) collective-permute-start(bf16[32,80]{1,0:T(8,128)(2,1)S(1)} %get-tuple-element.42), channel_id=1, source_target_pairs={{0,16},{16,32},{32,48},{48,64},{64,80},{80,96},{96,112},{1,17},{17... | collective-permute-start | bytes 15368 | tf_op jit(solution)/shard_map/ppermute | solution.py:365
  7.7 5.5 %collective-permute-start.1 = (bf16[32,80]{1,0:T(8,128)(2,1)S(1)}, bf16[32,80]{1,0:T(8,128)(2,1)S(1)}, u32[]{:S(2)}, u32[]{:S(2)}) collective-permute-start(bf16[32,80]{1,0:T(8,128)(2,1)S(1)} %get-tuple-element.43), channel_id=1, source_target_pairs={{16,0},{32,16},{48,32},{64,48},{80,64},{96,80},{112,96},{17,1},{33... | collective-permute-start | bytes 15368 | tf_op jit(solution)/shard_map/ppermute | solution.py:366
  13.4 6.7 %collective-permute-start.2 = (bf16[128,80]{1,0:T(8,128)(2,1)S(1)}, bf16[128,80]{1,0:T(8,128)(2,1)S(1)}, u32[]{:S(2)}, u32[]{:S(2)}) collective-permute-start(bf16[128,80]{1,0:T(8,128)(2,1)S(1)} %get-tuple-element.81), channel_id=1, source_target_pairs={{0,1},{1,2},{2,3},{3,4},{4,5},{5,6},{6,7},{7,8},{8,9},{9,10},{10,1... | collective-permute-start | bytes 61448 | tf_op jit(solution)/shard_map/ppermute | solution.py:404
  14.7 6.2 %collective-permute-start.3 = (bf16[128,80]{1,0:T(8,128)(2,1)S(1)}, bf16[128,80]{1,0:T(8,128)(2,1)S(1)}, u32[]{:S(2)}, u32[]{:S(2)}) collective-permute-start(bf16[128,80]{1,0:T(8,128)(2,1)S(1)} %get-tuple-element.80), channel_id=1, source_target_pairs={{1,0},{2,1},{3,2},{4,3},{5,4},{6,5},{7,6},{8,7},{9,8},{10,9},{11,1... | collective-permute-start | bytes 61448 | tf_op jit(solution)/shard_map/ppermute | solution.py:405
  20.1 3.6 %copy-start.2 = (bf16[17,2,128,256]{3,2,1,0:T(8,128)(2,1)}, bf16[17,2,128,256]{3,2,1,0:T(8,128)(2,1)S(1)}, u32[]{:S(2)}) copy-start(bf16[17,2,128,256]{3,2,1,0:T(8,128)(2,1)S(1)} %get-tuple-element.68.refs_1_) | copy-start | bytes 6684676
  20.9 14.2 %copy-start = (bf16[4,256,256]{2,1,0:T(8,128)(2,1)S(1)}, bf16[4,256,256]{2,1,0:T(8,128)(2,1)}, u32[]{:S(2)}) copy-start(bf16[4,256,256]{2,1,0:T(8,128)(2,1)} %refs_2_) | copy-start | bytes 1572868
  20.9 14.2 %copy-start.1 = (bf16[4,8,32,256]{3,2,1,0:T(8,128)(2,1)S(1)}, bf16[4,8,32,256]{3,2,1,0:T(8,128)(2,1)}, u32[]{:S(2)}) copy-start(bf16[4,8,32,256]{3,2,1,0:T(8,128)(2,1)} %param.15) | copy-start | bytes 1572868
  23.7 23.8 %all-to-all-start = ((bf16[16,64,256]{2,1,0:T(8,128)(2,1)}), bf16[16,64,256]{2,1,0:T(8,128)(2,1)S(1)}, u32[]{:S(2)}, u32[]{:S(2)}) async-start(bf16[16,64,256]{2,1,0:T(8,128)(2,1)} %bitcast.32), calls=%async_computation | async-start | bytes 1048576 | tf_op jit(solution)/shard_map/all_to_all | solution.py:446
  50.2 15.9 %all-to-all-start.1 = ((bf16[16,64,256]{2,1,0:T(8,128)(2,1)}), bf16[16,64,256]{2,1,0:T(8,128)(2,1)S(1)}, u32[]{:S(2)}, u32[]{:S(2)}) async-start(bf16[16,64,256]{2,1,0:T(8,128)(2,1)} %mix.1), calls=%async_computation.1 | async-start | bytes 1048576 | tf_op jit(solution)/shard_map/all_to_all | solution.py:476
  56.3 15.9 %collective-permute-start.4 = (bf16[4,64,256]{2,1,0:T(8,128)(2,1)}, bf16[4,64,256]{2,1,0:T(8,128)(2,1)S(1)}, u32[]{:S(2)}, u32[]{:S(2)}) collective-permute-start(bf16[4,64,256]{2,1,0:T(8,128)(2,1)} %get-tuple-element.65), channel_id=1, source_target_pairs={{0,32},{16,48},{32,0},{48,16},{64,96},{80,112},{96,64},{112,80},{1... | collective-permute-start | bytes 393224 | tf_op jit(solution)/shard_map/ppermute | solution.py:495
  58.2 14.0 %collective-permute-start.5 = (bf16[4,64,256]{2,1,0:T(8,128)(2,1)}, bf16[4,64,256]{2,1,0:T(8,128)(2,1)S(1)}, u32[]{:S(2)}, u32[]{:S(2)}) collective-permute-start(bf16[4,64,256]{2,1,0:T(8,128)(2,1)} %get-tuple-element.66), channel_id=1, source_target_pairs={{0,64},{16,80},{32,96},{48,112},{64,0},{80,16},{96,32},{112,48},{1... | collective-permute-start | bytes 393224 | tf_op jit(solution)/shard_map/ppermute | solution.py:495
  60.9 11.2 %collective-permute-start.6 = (bf16[4,64,256]{2,1,0:T(8,128)(2,1)}, bf16[4,64,256]{2,1,0:T(8,128)(2,1)S(1)}, u32[]{:S(2)}, u32[]{:S(2)}) collective-permute-start(bf16[4,64,256]{2,1,0:T(8,128)(2,1)} %get-tuple-element.67), channel_id=1, source_target_pairs={{0,96},{16,112},{32,64},{48,80},{64,32},{80,48},{96,0},{112,16},{1... | collective-permute-start | bytes 393224 | tf_op jit(solution)/shard_map/ppermute | solution.py:495
  66.1 20.8 %copy-start.3 = (f32[4,64,256]{2,1,0:T(8,128)S(1)}, f32[4,64,256]{2,1,0:T(8,128)}, u32[]{:S(2)}) copy-start(f32[4,64,256]{2,1,0:T(8,128)} %get-tuple-element.64) | copy-start | bytes 786436
  72.1 1.3 %collective-permute-start.8 = (f32[128,128]{1,0:T(8,128)S(1)}, f32[128,128]{1,0:T(8,128)S(1)}, u32[]{:S(2)}, u32[]{:S(2)}) collective-permute-start(f32[128,128]{1,0:T(8,128)S(1)} %backward.1), channel_id=1, source_target_pairs={{0,1},{1,0},{2,3},{3,2},{4,5},{5,4},{6,7},{7,6},{8,9},{9,8},{10,11... | collective-permute-start | bytes 196616 | tf_op jit(solution)/shard_map/ppermute | solution.py:336
  73.5 4.5 %collective-permute-start.10 = (f32[128,128]{1,0:T(8,128)S(1)}, f32[128,128]{1,0:T(8,128)S(1)}, u32[]{:S(2)}, u32[]{:S(2)}) collective-permute-start(f32[128,128]{1,0:T(8,128)S(1)} %add.37), channel_id=1, source_target_pairs={{0,16},{1,17},{2,18},{3,19},{4,20},{5,21},{6,22},{7,23},{8,24},{9,... | collective-permute-start | bytes 196616 | tf_op jit(solution)/shard_map/ppermute | solution.py:336
  75.6 6.5 %collective-permute-start.11 = (f32[128,128]{1,0:T(8,128)S(1)}, f32[128,128]{1,0:T(8,128)S(1)}, u32[]{:S(2)}, u32[]{:S(2)}) collective-permute-start(f32[128,128]{1,0:T(8,128)S(1)} %add.37), channel_id=1, source_target_pairs={{0,18},{1,19},{2,16},{3,17},{4,22},{5,23},{6,20},{7,21},{8,26},{9,... | collective-permute-start | bytes 196616 | tf_op jit(solution)/shard_map/ppermute | solution.py:336
  75.6 6.5 %collective-permute-start.9 = (f32[128,128]{1,0:T(8,128)S(1)}, f32[128,128]{1,0:T(8,128)S(1)}, u32[]{:S(2)}, u32[]{:S(2)}) collective-permute-start(f32[128,128]{1,0:T(8,128)S(1)} %add.37), channel_id=1, source_target_pairs={{0,2},{1,3},{2,0},{3,1},{4,6},{5,7},{6,4},{7,5},{8,10},{9,11},{10,... | collective-permute-start | bytes 196616 | tf_op jit(solution)/shard_map/ppermute | solution.py:336
  82.1 5.5 %collective-permute-start.12 = (f32[128,128]{1,0:T(8,128)S(1)}, f32[128,128]{1,0:T(8,128)S(1)}, u32[]{:S(2)}, u32[]{:S(2)}) collective-permute-start(f32[128,128]{1,0:T(8,128)S(1)} %add_add_fusion.1), channel_id=1, source_target_pairs={{0,4},{1,5},{2,6},{3,7},{4,0},{5,1},{6,2},{7,3},{8,12},{9,13},{10,... | collective-permute-start | bytes 196616 | tf_op jit(solution)/shard_map/ppermute | solution.py:336
  82.4 5.9 %collective-permute-start.13 = (f32[128,128]{1,0:T(8,128)S(1)}, f32[128,128]{1,0:T(8,128)S(1)}, u32[]{:S(2)}, u32[]{:S(2)}) collective-permute-start(f32[128,128]{1,0:T(8,128)S(1)} %add_add_fusion.1), channel_id=1, source_target_pairs={{0,8},{1,9},{2,10},{3,11},{4,12},{5,13},{6,14},{7,15},{8,0},{9,1},... | collective-permute-start | bytes 196616 | tf_op jit(solution)/shard_map/ppermute | solution.py:336
  85.1 5.5 %collective-permute-start.14 = (f32[128,128]{1,0:T(8,128)S(1)}, f32[128,128]{1,0:T(8,128)S(1)}, u32[]{:S(2)}, u32[]{:S(2)}) collective-permute-start(f32[128,128]{1,0:T(8,128)S(1)} %add_add_fusion.1), channel_id=1, source_target_pairs={{0,12},{1,13},{2,14},{3,15},{4,8},{5,9},{6,10},{7,11},{8,4},{9,5},... | collective-permute-start | bytes 196616 | tf_op jit(solution)/shard_map/ppermute | solution.py:336
  86.9 8.4 %collective-permute-start.7 = (bf16[4,32,256]{2,1,0:T(8,128)(2,1)S(1)}, bf16[4,32,256]{2,1,0:T(8,128)(2,1)S(1)}, u32[]{:S(2)}, u32[]{:S(2)}) collective-permute-start(bf16[4,32,256]{2,1,0:T(8,128)(2,1)S(1)} %split.13), channel_id=1, source_target_pairs={{0,16},{16,0},{32,48},{48,32},{64,80},{80,64},{96,112},{112,96},{1... | collective-permute-start | bytes 196616 | tf_op jit(solution)/shard_map/ppermute | solution.py:528
  90.6 5.5 %collective-permute-start.15 = (f32[128,128]{1,0:T(8,128)S(1)}, f32[128,128]{1,0:T(8,128)S(1)}, u32[]{:S(2)}, u32[]{:S(2)}) collective-permute-start(f32[128,128]{1,0:T(8,128)S(1)} %add_add_fusion.a_ref), channel_id=1, source_target_pairs={{0,32},{1,33},{2,34},{3,35},{4,36},{5,37},{6,38},{7,39},{8,40},{9,... | collective-permute-start | bytes 196616 | tf_op jit(solution)/shard_map/ppermute | solution.py:336
  91.5 5.8 %collective-permute-start.16 = (f32[128,128]{1,0:T(8,128)S(1)}, f32[128,128]{1,0:T(8,128)S(1)}, u32[]{:S(2)}, u32[]{:S(2)}) collective-permute-start(f32[128,128]{1,0:T(8,128)S(1)} %add_add_fusion.a_ref), channel_id=1, source_target_pairs={{0,64},{1,65},{2,66},{3,67},{4,68},{5,69},{6,70},{7,71},{8,72},{9,... | collective-permute-start | bytes 196616 | tf_op jit(solution)/shard_map/ppermute | solution.py:336
  93.1 5.5 %collective-permute-start.17 = (f32[128,128]{1,0:T(8,128)S(1)}, f32[128,128]{1,0:T(8,128)S(1)}, u32[]{:S(2)}, u32[]{:S(2)}) collective-permute-start(f32[128,128]{1,0:T(8,128)S(1)} %add_add_fusion.a_ref), channel_id=1, source_target_pairs={{0,96},{1,97},{2,98},{3,99},{4,100},{5,101},{6,102},{7,103},{8,104... | collective-permute-start | bytes 196616 | tf_op jit(solution)/shard_map/ppermute | solution.py:336

commit v8 on v7

--- a/solution.py
+++ b/solution.py
@@ -39,9 +39,9 @@
         copy.wait()
     wd_s[...] = wd_b[...].astype(F32)
     for z in range(out_ref.shape[0]):
-        lab = lab_s[:, z, :]
+        lab = lab_s[pl.ds(z, 16, stride=32), :]
         parts = [(lab == m).astype(F32).astype(BF16) for m in range(4)]
-        parts.append(wd_s[:, z, :].astype(BF16))
+        parts.append(wd_s[pl.ds(z, 16, stride=32), :].astype(BF16))
         rows = dot(pick, jnp.concatenate(parts, axis=0), 1, 1)
         out_ref[z] = rows.astype(BF16)
         first_s[z : z + 1, :] = rows[0:1, :]
@@ -183,22 +183,30 @@
     cot_t_ref[0] = cot_ref[0].T
 
 
-def mixed(coarse_ref, mix_ref, cot_t_ref):
-    coarse = coarse_ref[...].reshape(mix_ref.shape[1], 256)
-    pre = dot(mix_ref[0], coarse, 1, 0)
+def mixed(coarse, mix, cot_t):
+    pre = dot(mix, coarse, 1, 0)
     sigma = jax.nn.sigmoid(pre)
-    grad = cot_t_ref[0].astype(F32) * (sigma * (1.0 + pre * (1.0 - sigma)))
-    return coarse, pre * sigma, grad.astype(BF16)
-
-
-def mix_kernel(coarse_ref, mix_ref, cot_t_ref, mix_t_ref, grad_ref):
-    _, _, grad = mixed(coarse_ref, mix_ref, cot_t_ref)
-    grad_ref[...] = dot(mix_t_ref[0], grad, 1, 0).astype(BF16).reshape(grad_ref.shape)
+    grad = cot_t.astype(F32) * (sigma * (1.0 + pre * (1.0 - sigma)))
+    return pre * sigma, grad.astype(BF16)
+
+
+def mix_kernel(coarse_ref, mix_ref, cot_t_ref, mix_t_ref, grad_hbm, grad_ref, sem):
+    copies = []
+    for c in range(mix_ref.shape[0]):
+        at = (slice(None), pl.ds(16 * c, 16), slice(None))
+        _, grad = mixed(coarse_ref[at].reshape(-1, 256), mix_ref[c], cot_t_ref[c])
+        part = dot(mix_t_ref[c], grad, 1, 0).astype(BF16)
+        grad_ref[at] = part.reshape(-1, 16, 256)
+        copies.append(pltpu.make_async_copy(grad_ref.at[at], grad_hbm.at[at], sem.at[c]))
+        copies[-1].start()
+    for copy in copies:
+        copy.wait()
 
 
 def mix_grad_kernel(scale, me_ref, coarse_ref, mix_ref, cot_t_ref, mid_ref, *more_refs):
     *share_refs, total_ref = more_refs
-    coarse, mid, grad = mixed(coarse_ref, mix_ref, cot_t_ref)
+    coarse = coarse_ref[...].reshape(-1, 256)
+    mid, grad = mixed(coarse, mix_ref[0], cot_t_ref[0])
     mid_ref[0] = mid.astype(BF16).T
     total_ref[...] = dot(grad, coarse, 1, 1) * scale
     rows = total_ref.shape[0] // (2 * len(share_refs))
@@ -264,7 +272,7 @@
             low = 64 * (bc % 2) + 32 * (bc // 2)
             turned_pg[bc, at, edge] = (rows[:, edge] * edge_ref[at, low : low + 32]).astype(BF16)
     copies[1].wait()
-    lane_x = iota((16, 256), 1) // 16
+    lane_x = iota((16, 128), 1) // 16
     own = iota((8, 128), 1) // 16 == iota((8, 128), 0)
     for ty in range(3):
         for tz in range(3):
@@ -281,10 +289,15 @@
                     part = dot(turned_pg[bc, :, 256 * half : 256 * half + 256], rows, 1, 0)
                     acc = part if acc is None else acc + part
             for tx in range(3):
-                total = jnp.zeros((16, 256), F32)
-                for x in range(16):
-                    if 0 <= x + tx - 1 < 16:
-                        total = jnp.where(lane_x == x + tx - 1, acc[16 * x : 16 * x + 16, :], total)
+                total = None
+                for side in range(2):
+                    half = jnp.zeros((16, 128), F32)
+                    for x in range(16):
+                        lane = x + tx - 1 - 8 * side
+                        if 0 <= lane < 8:
+                            part = acc[16 * x : 16 * x + 16, 128 * side : 128 * side + 128]
+                            half = jnp.where(lane_x == lane, part, half)
+                    total = half if total is None else total + half
                 tap = 9 * tx + 3 * ty + tz
                 total = fold(total, 16) * conv_scale
                 for half in range(2):
@@ -349,9 +362,9 @@
         in_specs=[HBM] * 2,
         out_specs=(VMEM,) * 3,
         scratch_shapes=[
-            pltpu.VMEM((16, 32, 64), jnp.int32),
-            pltpu.VMEM((16, 32, 64), BF16),
-            pltpu.VMEM((16, 32, 64), F32),
+            pltpu.VMEM((512, 64), jnp.int32),
+            pltpu.VMEM((512, 64), BF16),
+            pltpu.VMEM((512, 64), F32),
             pltpu.VMEM((32, 80), F32),
             pltpu.VMEM((32, 80), F32),
             pltpu.SemaphoreType.DMA((2,)),
@@ -359,7 +372,12 @@
         compiler_params=params(8),
         cost_estimate=cost(32 * 128 * 64 * 80 * 2, 2 << 20),
         name="features",
-    )(*kept(jnp.transpose(labels, (0, 2, 1)), jnp.transpose(wall_dist, (0, 2, 1))))
+    )(
+        *kept(
+            jnp.transpose(labels, (0, 2, 1)).reshape(512, 64),
+            jnp.transpose(wall_dist, (0, 2, 1)).reshape(512, 64),
+        )
+    )
     up_y = [(i, i + 1) for i in range(count_y - 1)]
     up_z = [(i, i + 1) for i in range(count_z - 1)]
     ylo = lax.ppermute(last, "sy", up_y)
@@ -465,10 +483,13 @@
     )(mix_weight, cotangent_rows)
     back = pl.pallas_call(
         mix_kernel,
-        grid=(mine,),
-        out_shape=shape((count_z, mine * 16, 256), BF16),
-        in_specs=mix_specs + [block(1, width, width)],
-        out_specs=pl.BlockSpec((count_z, 16, 256), lambda c: (0, c, 0)),
+        out_shape=pltpu.HBM((count_z, mine * 16, 256), BF16),
+        in_specs=[VMEM] * 4,
+        out_specs=HBM,
+        scratch_shapes=[
+            pltpu.VMEM((count_z, mine * 16, 256), BF16),
+            pltpu.SemaphoreType.DMA((mine,)),
+        ],
         compiler_params=params(8),
         cost_estimate=cost(mine * 2 * 2 * 256 * width * width, 2 << 20),
         name="mix",

time: 99.9 us -> 96.7 us (0.968)
  Pallas kernels: 25.2 us -> 22 us
    pallas_call x1, Pallas kernels: 3.51 us -> 1.69 us  [per_device(): pl.pallas_call(feature_kernel, out_shape=(shape((32, 128, 80), BF16), sha...]
    pallas_call x1, Pallas kernels: 2.67 us -> 1.37 us  [per_device(): pl.pallas_call(mix_kernel, out_shape=pltpu.HBM((count_z, mine * 16, 256),...]
where the time goes in v8:
time: 96.7 us; the launch traced here: 96.3 us
  starting transfers between devices  41.7 us (43%)
  waiting for transfers between devices  30.7 us (32%)
  Pallas kernels  22 us (23%)
    ppermute x10, starting transfers between devices, exchanged(): lax.ppermute(value, ('sy', 'sz'), [(i, i ^ m) for i in range(count)])  13.9 us
    all_to_all x1, waiting for transfers between devices, per_device(): lax.all_to_all(coarse.reshape(count_z, mine * 16, 256), 'sz', split_axis=...  11.8 us
    all_to_all x1, starting transfers between devices, per_device(): lax.all_to_all(coarse.reshape(count_z, mine * 16, 256), 'sz', split_axis=...  11.5 us
    ppermute x10, waiting for transfers between devices, exchanged(): lax.ppermute(value, ('sy', 'sz'), [(i, i ^ m) for i in range(count)])  11.1 us
    pallas_call x1, Pallas kernels, per_device(): pl.pallas_call(lambda *refs: backward_kernel(1.0 / math.sqrt(cells // 8),...  6 us
    all_to_all x1, waiting for transfers between devices, per_device(): lax.all_to_all(back, 'sz', split_axis=0, concat_axis=0, tiled=True)  5.1 us
    ppermute x3, starting transfers between devices, per_device(): lax.ppermute(part, 'sy', [(i, i ^ 2 * k) for i in range(count_y)])  4.7 us
    pallas_call x1, Pallas kernels, per_device(): pl.pallas_call(inner_kernel, out_shape=(shape((17, 2, 128, 256), BF16), p...  4.08 us
  transfers between devices with their start and end apart: 20, of which 11 were waited for; matrix products, arithmetic and copies ran while one was open for 1% of the time, Pallas kernels for 16%

profile of v8, /device:TPU:0, one launch (start us, length us, event | category | flops | bytes accessed | tf_op | source)
XLA Modules:
  0.0 96.3 jit_solution(14539213910048320910)
XLA Ops:
  0.6 1.7 %features.1 = (bf16[32,128,80]{2,1,0:T(8,128)(2,1)S(1)}, bf16[32,80]{1,0:T(8,128)(2,1)S(1)}, bf16[32,80]{1,0:T(8,128)(2,1)S(1)}) custom-call(s32[512,64]{1,0:T(8,128)} %bitcast.37, bf16[512,64]{1,0:T(8,128)(2,1)} %bitcast.38), custom_call_target="tpu_custom_call" | custom-call | flops 41943040 | bytes 2097152 | tf_op jit(solution)/shard_map/features/pallas_call | solution.py:359
  2.3 3.6 %collective-permute-start = (bf16[32,80]{1,0:T(8,128)(2,1)S(1)}, bf16[32,80]{1,0:T(8,128)(2,1)S(1)}, u32[]{:S(2)}, u32[]{:S(2)}) collective-permute-start(bf16[32,80]{1,0:T(8,128)(2,1)S(1)} %get-tuple-element.42), channel_id=1, source_target_pairs={{0,16},{16,32},{32,48},{48,64},{64,80},{80,96},{96,112},{1,17},{17... | collective-permute-start | bytes 15368 | tf_op jit(solution)/shard_map/ppermute | solution.py:383
  5.9 1.3 %collective-permute-start.1 = (bf16[32,80]{1,0:T(8,128)(2,1)S(1)}, bf16[32,80]{1,0:T(8,128)(2,1)S(1)}, u32[]{:S(2)}, u32[]{:S(2)}) collective-permute-start(bf16[32,80]{1,0:T(8,128)(2,1)S(1)} %get-tuple-element.43), channel_id=1, source_target_pairs={{16,0},{32,16},{48,32},{64,48},{80,64},{96,80},{112,96},{17,1},{33... | collective-permute-start | bytes 15368 | tf_op jit(solution)/shard_map/ppermute | solution.py:384
  7.2 2.3 %weights.1 = (bf16[9,256,256]{2,1,0:T(8,128)(2,1)S(1)}, bf16[128,256]{1,0:T(8,128)(2,1)S(1)}, bf16[256,128]{1,0:T(8,128)(2,1)S(1)}, bf16[80,256]{1,0:T(8,128)(2,1)S(1)}) custom-call(bf16[16,16,27]{2,1,0:T(8,128)(2,1)} %bitcast.41, bf16[8,16,64]{2,1,0:T(8,128)(2,1)} %bitcast.43, bf16[4,16]{1,0:T(4,128)(2,1)} %mat_hbm.1, bf16[1,16]{1,0:T(2,128)(2,1)} %bitcast.44), custom_call_target="tpu_custom_call" | custom-call | flops 56623104 | bytes 3145728 | tf_op jit(solution)/shard_map/weights/pallas_call | solution.py:385
  9.6 0.0 collective-permute-done.ylo_ref
  9.6 1.9 %collective-permute-done.1.yhi_ref = bf16[32,80]{1,0:T(8,128)(2,1)S(1)} collective-permute-done((bf16[32,80]{1,0:T(8,128)(2,1)S(1)}, bf16[32,80]{1,0:T(8,128)(2,1)S(1)}, u32[]{:S(2)}, u32[]{:S(2)}) %collective-permute-start.1) | collective-permute-done | bytes 5152 | tf_op jit(solution)/shard_map/ppermute | solution.py:384
  11.5 0.1 fusion
  11.6 1.3 %collective-permute-start.2 = (bf16[128,80]{1,0:T(8,128)(2,1)S(1)}, bf16[128,80]{1,0:T(8,128)(2,1)S(1)}, u32[]{:S(2)}, u32[]{:S(2)}) collective-permute-start(bf16[128,80]{1,0:T(8,128)(2,1)S(1)} %get-tuple-element.81), channel_id=1, source_target_pairs={{0,1},{1,2},{2,3},{3,4},{4,5},{5,6},{6,7},{7,8},{8,9},{9,10},{10,1... | collective-permute-start | bytes 61448 | tf_op jit(solution)/shard_map/ppermute | solution.py:422
  12.9 1.3 %collective-permute-start.3 = (bf16[128,80]{1,0:T(8,128)(2,1)S(1)}, bf16[128,80]{1,0:T(8,128)(2,1)S(1)}, u32[]{:S(2)}, u32[]{:S(2)}) collective-permute-start(bf16[128,80]{1,0:T(8,128)(2,1)S(1)} %get-tuple-element.80), channel_id=1, source_target_pairs={{1,0},{2,1},{3,2},{4,3},{5,4},{6,5},{7,6},{8,7},{9,8},{10,9},{11,1... | collective-permute-start | bytes 61448 | tf_op jit(solution)/shard_map/ppermute | solution.py:423
  14.2 4.1 %inner.1 = (bf16[17,2,128,256]{3,2,1,0:T(8,128)(2,1)S(1)}, f32[4,256,512]{2,1,0:T(8,128)}, bf16[4,256,512]{2,1,0:T(8,128)(2,1)S(1)}, f32[2,2,256,32]{3,2,1,0:T(8,128)S(1)}) custom-call(bf16[32,128,80]{2,1,0:T(8,128)(2,1)S(1)} %get-tuple-element.50.feat_ref, bf16[32,80]{1,0:T(8,128)(2,1)S(1)} %collective-permute-done.ylo_ref, ...), custom_call_target="tpu_custom_call" | custom-call | flops 3221225472 | bytes 10485760 | tf_op jit(solution)/shard_map/inner/pallas_call | solution.py:424
  18.3 0.0 copy-start.2
  18.3 0.0 collective-permute-done.2.zlo_ref
  18.3 0.8 collective-permute-done.3.zhi_ref
  19.1 0.0 copy-start
  19.1 0.0 copy-start.1
  19.1 2.7 %outer.1 = (bf16[2,128,256]{2,1,0:T(8,128)(2,1)S(1)}, f32[256,128]{1,0:T(8,128)S(1)}, bf16[4,256,512]{2,1,0:T(8,128)(2,1)}, bf16[1024,256]{1,0:T(8,128)(2,1)}) custom-call(bf16[128,80]{1,0:T(8,128)(2,1)S(1)} %collective-permute-done.2.zlo_ref, bf16[128,80]{1,0:T(8,128)(2,1)S(1)} %collective-permute-done.3.zhi_ref, ...), custom_call_target="tpu_custom_call" | custom-call | flops 1073741824 | bytes 4194304 | tf_op jit(solution)/shard_map/outer/pallas_call | solution.py:439
  21.8 0.0 copy-done.2
  21.8 11.5 %all-to-all-start = ((bf16[16,64,256]{2,1,0:T(8,128)(2,1)}), bf16[16,64,256]{2,1,0:T(8,128)(2,1)S(1)}, u32[]{:S(2)}, u32[]{:S(2)}) async-start(bf16[16,64,256]{2,1,0:T(8,128)(2,1)} %bitcast.36), calls=%async_computation | async-start | bytes 1048576 | tf_op jit(solution)/shard_map/all_to_all | solution.py:464
  33.3 0.0 copy-done
  33.3 0.0 copy-done.1
  33.3 0.5 turn.1
  33.9 11.8 %all-to-all-done.coarse_ref.refs_1_ = bf16[16,64,256]{2,1,0:T(8,128)(2,1)S(1)} async-done(((bf16[16,64,256]{2,1,0:T(8,128)(2,1)}), bf16[16,64,256]{2,1,0:T(8,128)(2,1)S(1)}, u32[]{:S(2)}, u32[]{:S(2)}) %all-to-all-start) | async-done | bytes 524320 | tf_op jit(solution)/shard_map/all_to_all | solution.py:464
  45.7 1.4 %mix.1 = bf16[16,64,256]{2,1,0:T(8,128)(2,1)} custom-call(bf16[16,64,256]{2,1,0:T(8,128)(2,1)S(1)} %all-to-all-done.coarse_ref.refs_1_, bf16[4,256,256]{2,1,0:T(8,128)(2,1)S(1)} %copy-done, bf16[4,256,256]{2,1,0:T(8,128)(2,1)S(1)} %get-tuple-element.60.cot_t_ref.refs_3_, bf16[4,256,256]{2,1,0:T(8,128)(2,1)S(1)} %get-tuple-element.61.mix_t_ref), custom_call_target="tpu_custom_call" | custom-call | flops 268435456 | bytes 2097152 | tf_op jit(solution)/shard_map/mix/pallas_call | solution.py:484
  47.0 3.6 %all-to-all-start.1 = ((bf16[16,64,256]{2,1,0:T(8,128)(2,1)}), bf16[16,64,256]{2,1,0:T(8,128)(2,1)S(1)}, u32[]{:S(2)}, u32[]{:S(2)}) async-start(bf16[16,64,256]{2,1,0:T(8,128)(2,1)} %mix.1), calls=%async_computation.1 | async-start | bytes 1048576 | tf_op jit(solution)/shard_map/all_to_all | solution.py:497
  50.6 2.5 %mix_grad.1 = (bf16[4,256,256]{2,1,0:T(8,128)(2,1)}, f32[4,64,256]{2,1,0:T(8,128)}, bf16[4,64,256]{2,1,0:T(8,128)(2,1)}, bf16[4,64,256]{2,1,0:T(8,128)(2,1)}, bf16[4,64,256]{2,1,0:T(8,128)(2,1)}) custom-call(s32[1]{0:T(128)} %bitcast.refs_0_, bf16[16,64,256]{2,1,0:T(8,128)(2,1)S(1)} %all-to-all-done.coarse_ref.refs_1_, bf16[4,256,256]{2,1,0:T(8,128)(2,1)S(1)} %copy-done, ...), custom_call_target="tpu_custom_call" | custom-call | flops 268435456 | bytes 3145728 | tf_op jit(solution)/shard_map/mix_grad/pallas_call | solution.py:499
  53.2 1.9 %collective-permute-start.4 = (bf16[4,64,256]{2,1,0:T(8,128)(2,1)}, bf16[4,64,256]{2,1,0:T(8,128)(2,1)S(1)}, u32[]{:S(2)}, u32[]{:S(2)}) collective-permute-start(bf16[4,64,256]{2,1,0:T(8,128)(2,1)} %get-tuple-element.65), channel_id=1, source_target_pairs={{0,32},{16,48},{32,0},{48,16},{64,96},{80,112},{96,64},{112,80},{1... | collective-permute-start | bytes 393224 | tf_op jit(solution)/shard_map/ppermute | solution.py:516
  55.1 2.7 %collective-permute-start.5 = (bf16[4,64,256]{2,1,0:T(8,128)(2,1)}, bf16[4,64,256]{2,1,0:T(8,128)(2,1)S(1)}, u32[]{:S(2)}, u32[]{:S(2)}) collective-permute-start(bf16[4,64,256]{2,1,0:T(8,128)(2,1)} %get-tuple-element.66), channel_id=1, source_target_pairs={{0,64},{16,80},{32,96},{48,112},{64,0},{80,16},{96,32},{112,48},{1... | collective-permute-start | bytes 393224 | tf_op jit(solution)/shard_map/ppermute | solution.py:516
  57.8 0.1 collective-permute-start.6
  57.9 5.1 %all-to-all-done.1 = bf16[16,64,256]{2,1,0:T(8,128)(2,1)S(1)} async-done(((bf16[16,64,256]{2,1,0:T(8,128)(2,1)}), bf16[16,64,256]{2,1,0:T(8,128)(2,1)S(1)}, u32[]{:S(2)}, u32[]{:S(2)}) %all-to-all-start.1) | async-done | bytes 524320 | tf_op jit(solution)/shard_map/all_to_all | solution.py:497
  63.0 0.0 copy-start.3
  63.0 6.0 %backward.1 = f32[128,128]{1,0:T(8,128)S(1)} custom-call(bf16[1024,256]{1,0:T(8,128)(2,1)S(1)} %bitcast.35, bf16[17,2,128,256]{3,2,1,0:T(8,128)(2,1)} %copy-done.2, f32[4,256,512]{2,1,0:T(8,128)} %get-tuple-element.69.refs_2_, bf16[4,256,512]{2,1,0:T(8,128)(2,1)} %get-tuple-element.70.refs_3_, bf16[128,256]{1,0:T(8,128)(2,1)S(1)} %get-tuple-element.53.pair_ref.refs_4_, ...), custom_call_target="tpu_custom_call" | custom-call | flops 4294967296 | bytes 8388608 | tf_op jit(solution)/shard_map/backward/pallas_call | solution.py:518
  69.0 0.0 collective-permute-done.4
  69.0 0.0 collective-permute-done.5
  69.0 0.0 collective-permute-done.6
  69.0 0.1 collective-permute-start.8
  69.1 1.2 %collective-permute-done.8 = f32[128,128]{1,0:T(8,128)S(1)} collective-permute-done((f32[128,128]{1,0:T(8,128)S(1)}, f32[128,128]{1,0:T(8,128)S(1)}, u32[]{:S(2)}, u32[]{:S(2)}) %collective-permute-start.8) | collective-permute-done | bytes 65568 | tf_op jit(solution)/shard_map/ppermute | solution.py:349
  70.4 2.1 %collective-permute-start.10 = (f32[128,128]{1,0:T(8,128)S(1)}, f32[128,128]{1,0:T(8,128)S(1)}, u32[]{:S(2)}, u32[]{:S(2)}) collective-permute-start(f32[128,128]{1,0:T(8,128)S(1)} %add.37), channel_id=1, source_target_pairs={{0,16},{1,17},{2,18},{3,19},{4,20},{5,21},{6,22},{7,23},{8,24},{9,... | collective-permute-start | bytes 196616 | tf_op jit(solution)/shard_map/ppermute | solution.py:349
  72.4 0.0 collective-permute-start.11
  72.4 2.2 %collective-permute-start.9 = (f32[128,128]{1,0:T(8,128)S(1)}, f32[128,128]{1,0:T(8,128)S(1)}, u32[]{:S(2)}, u32[]{:S(2)}) collective-permute-start(f32[128,128]{1,0:T(8,128)S(1)} %add.37), channel_id=1, source_target_pairs={{0,2},{1,3},{2,0},{3,1},{4,6},{5,7},{6,4},{7,5},{8,10},{9,11},{10,... | collective-permute-start | bytes 196616 | tf_op jit(solution)/shard_map/ppermute | solution.py:349
  74.6 0.3 collective-permute-done.10
  74.8 4.1 %collective-permute-done.11 = f32[128,128]{1,0:T(8,128)S(1)} collective-permute-done((f32[128,128]{1,0:T(8,128)S(1)}, f32[128,128]{1,0:T(8,128)S(1)}, u32[]{:S(2)}, u32[]{:S(2)}) %collective-permute-start.11) | collective-permute-done | bytes 65568 | tf_op jit(solution)/shard_map/ppermute | solution.py:349
  78.9 0.0 collective-permute-done.9
  78.9 0.3 collective-permute-start.12
  79.3 2.7 %collective-permute-start.13 = (f32[128,128]{1,0:T(8,128)S(1)}, f32[128,128]{1,0:T(8,128)S(1)}, u32[]{:S(2)}, u32[]{:S(2)}) collective-permute-start(f32[128,128]{1,0:T(8,128)S(1)} %add_add_fusion.1), channel_id=1, source_target_pairs={{0,8},{1,9},{2,10},{3,11},{4,12},{5,13},{6,14},{7,15},{8,0},{9,1},... | collective-permute-start | bytes 196616 | tf_op jit(solution)/shard_map/ppermute | solution.py:349
  82.0 1.7 %collective-permute-start.14 = (f32[128,128]{1,0:T(8,128)S(1)}, f32[128,128]{1,0:T(8,128)S(1)}, u32[]{:S(2)}, u32[]{:S(2)}) collective-permute-start(f32[128,128]{1,0:T(8,128)S(1)} %add_add_fusion.1), channel_id=1, source_target_pairs={{0,12},{1,13},{2,14},{3,15},{4,8},{5,9},{6,10},{7,11},{8,4},{9,5},... | collective-permute-start | bytes 196616 | tf_op jit(solution)/shard_map/ppermute | solution.py:349
  83.7 0.0 copy-done.3
  83.7 0.1 convert_add_fusion
  83.8 0.7 collective-permute-start.7
  84.5 0.0 collective-permute-done.12
  84.5 0.7 collective-permute-done.13
  85.1 2.3 %collective-permute-done.14 = f32[128,128]{1,0:T(8,128)S(1)} collective-permute-done((f32[128,128]{1,0:T(8,128)S(1)}, f32[128,128]{1,0:T(8,128)S(1)}, u32[]{:S(2)}, u32[]{:S(2)}) %collective-permute-start.14) | collective-permute-done | bytes 65568 | tf_op jit(solution)/shard_map/ppermute | solution.py:349
  87.5 0.9 collective-permute-start.15
  88.4 1.6 %collective-permute-start.16 = (f32[128,128]{1,0:T(8,128)S(1)}, f32[128,128]{1,0:T(8,128)S(1)}, u32[]{:S(2)}, u32[]{:S(2)}) collective-permute-start(f32[128,128]{1,0:T(8,128)S(1)} %add_add_fusion.a_ref), channel_id=1, source_target_pairs={{0,64},{1,65},{2,66},{3,67},{4,68},{5,69},{6,70},{7,71},{8,72},{9,... | collective-permute-start | bytes 196616 | tf_op jit(solution)/shard_map/ppermute | solution.py:349
  90.0 2.3 %collective-permute-start.17 = (f32[128,128]{1,0:T(8,128)S(1)}, f32[128,128]{1,0:T(8,128)S(1)}, u32[]{:S(2)}, u32[]{:S(2)}) collective-permute-start(f32[128,128]{1,0:T(8,128)S(1)} %add_add_fusion.a_ref), channel_id=1, source_target_pairs={{0,96},{1,97},{2,98},{3,99},{4,100},{5,101},{6,102},{7,103},{8,104... | collective-permute-start | bytes 196616 | tf_op jit(solution)/shard_map/ppermute | solution.py:349
  92.3 0.0 collective-permute-done.7
  92.3 0.7 slice_add_fusion
  92.9 0.0 collective-permute-done.15.b_ref
  92.9 1.2 %collective-permute-done.16.c_ref = f32[128,128]{1,0:T(8,128)S(1)} collective-permute-done((f32[128,128]{1,0:T(8,128)S(1)}, f32[128,128]{1,0:T(8,128)S(1)}, u32[]{:S(2)}, u32[]{:S(2)}) %collective-permute-start.16) | collective-permute-done | bytes 65568 | tf_op jit(solution)/shard_map/ppermute | solution.py:349
  94.1 1.4 %collective-permute-done.17.d_ref = f32[128,128]{1,0:T(8,128)S(1)} collective-permute-done((f32[128,128]{1,0:T(8,128)S(1)}, f32[128,128]{1,0:T(8,128)S(1)}, u32[]{:S(2)}, u32[]{:S(2)}) %collective-permute-start.17) | collective-permute-done | bytes 65568 | tf_op jit(solution)/shard_map/ppermute | solution.py:349
  95.5 0.8 finish.1
  (6 shorter events, 0.1 us)
Async XLA Ops:
  2.3 7.2 %collective-permute-start = (bf16[32,80]{1,0:T(8,128)(2,1)S(1)}, bf16[32,80]{1,0:T(8,128)(2,1)S(1)}, u32[]{:S(2)}, u32[]{:S(2)}) collective-permute-start(bf16[32,80]{1,0:T(8,128)(2,1)S(1)} %get-tuple-element.42), channel_id=1, source_target_pairs={{0,16},{16,32},{32,48},{48,64},{64,80},{80,96},{96,112},{1,17},{17... | collective-permute-start | bytes 15368 | tf_op jit(solution)/shard_map/ppermute | solution.py:383
  5.9 5.5 %collective-permute-start.1 = (bf16[32,80]{1,0:T(8,128)(2,1)S(1)}, bf16[32,80]{1,0:T(8,128)(2,1)S(1)}, u32[]{:S(2)}, u32[]{:S(2)}) collective-permute-start(bf16[32,80]{1,0:T(8,128)(2,1)S(1)} %get-tuple-element.43), channel_id=1, source_target_pairs={{16,0},{32,16},{48,32},{64,48},{80,64},{96,80},{112,96},{17,1},{33... | collective-permute-start | bytes 15368 | tf_op jit(solution)/shard_map/ppermute | solution.py:384
  11.6 6.7 %collective-permute-start.2 = (bf16[128,80]{1,0:T(8,128)(2,1)S(1)}, bf16[128,80]{1,0:T(8,128)(2,1)S(1)}, u32[]{:S(2)}, u32[]{:S(2)}) collective-permute-start(bf16[128,80]{1,0:T(8,128)(2,1)S(1)} %get-tuple-element.81), channel_id=1, source_target_pairs={{0,1},{1,2},{2,3},{3,4},{4,5},{5,6},{6,7},{7,8},{8,9},{9,10},{10,1... | collective-permute-start | bytes 61448 | tf_op jit(solution)/shard_map/ppermute | solution.py:422
  12.9 6.2 %collective-permute-start.3 = (bf16[128,80]{1,0:T(8,128)(2,1)S(1)}, bf16[128,80]{1,0:T(8,128)(2,1)S(1)}, u32[]{:S(2)}, u32[]{:S(2)}) collective-permute-start(bf16[128,80]{1,0:T(8,128)(2,1)S(1)} %get-tuple-element.80), channel_id=1, source_target_pairs={{1,0},{2,1},{3,2},{4,3},{5,4},{6,5},{7,6},{8,7},{9,8},{10,9},{11,1... | collective-permute-start | bytes 61448 | tf_op jit(solution)/shard_map/ppermute | solution.py:423
  18.3 3.6 %copy-start.2 = (bf16[17,2,128,256]{3,2,1,0:T(8,128)(2,1)}, bf16[17,2,128,256]{3,2,1,0:T(8,128)(2,1)S(1)}, u32[]{:S(2)}) copy-start(bf16[17,2,128,256]{3,2,1,0:T(8,128)(2,1)S(1)} %get-tuple-element.68.refs_1_) | copy-start | bytes 6684676
  19.1 14.2 %copy-start = (bf16[4,256,256]{2,1,0:T(8,128)(2,1)S(1)}, bf16[4,256,256]{2,1,0:T(8,128)(2,1)}, u32[]{:S(2)}) copy-start(bf16[4,256,256]{2,1,0:T(8,128)(2,1)} %refs_2_) | copy-start | bytes 1572868
  19.1 14.2 %copy-start.1 = (bf16[4,8,32,256]{3,2,1,0:T(8,128)(2,1)S(1)}, bf16[4,8,32,256]{3,2,1,0:T(8,128)(2,1)}, u32[]{:S(2)}) copy-start(bf16[4,8,32,256]{3,2,1,0:T(8,128)(2,1)} %param.15) | copy-start | bytes 1572868
  21.8 23.8 %all-to-all-start = ((bf16[16,64,256]{2,1,0:T(8,128)(2,1)}), bf16[16,64,256]{2,1,0:T(8,128)(2,1)S(1)}, u32[]{:S(2)}, u32[]{:S(2)}) async-start(bf16[16,64,256]{2,1,0:T(8,128)(2,1)} %bitcast.36), calls=%async_computation | async-start | bytes 1048576 | tf_op jit(solution)/shard_map/all_to_all | solution.py:464
  47.0 15.9 %all-to-all-start.1 = ((bf16[16,64,256]{2,1,0:T(8,128)(2,1)}), bf16[16,64,256]{2,1,0:T(8,128)(2,1)S(1)}, u32[]{:S(2)}, u32[]{:S(2)}) async-start(bf16[16,64,256]{2,1,0:T(8,128)(2,1)} %mix.1), calls=%async_computation.1 | async-start | bytes 1048576 | tf_op jit(solution)/shard_map/all_to_all | solution.py:497
  53.2 15.8 %collective-permute-start.4 = (bf16[4,64,256]{2,1,0:T(8,128)(2,1)}, bf16[4,64,256]{2,1,0:T(8,128)(2,1)S(1)}, u32[]{:S(2)}, u32[]{:S(2)}) collective-permute-start(bf16[4,64,256]{2,1,0:T(8,128)(2,1)} %get-tuple-element.65), channel_id=1, source_target_pairs={{0,32},{16,48},{32,0},{48,16},{64,96},{80,112},{96,64},{112,80},{1... | collective-permute-start | bytes 393224 | tf_op jit(solution)/shard_map/ppermute | solution.py:516
  55.1 13.9 %collective-permute-start.5 = (bf16[4,64,256]{2,1,0:T(8,128)(2,1)}, bf16[4,64,256]{2,1,0:T(8,128)(2,1)S(1)}, u32[]{:S(2)}, u32[]{:S(2)}) collective-permute-start(bf16[4,64,256]{2,1,0:T(8,128)(2,1)} %get-tuple-element.66), channel_id=1, source_target_pairs={{0,64},{16,80},{32,96},{48,112},{64,0},{80,16},{96,32},{112,48},{1... | collective-permute-start | bytes 393224 | tf_op jit(solution)/shard_map/ppermute | solution.py:516
  57.8 11.2 %collective-permute-start.6 = (bf16[4,64,256]{2,1,0:T(8,128)(2,1)}, bf16[4,64,256]{2,1,0:T(8,128)(2,1)S(1)}, u32[]{:S(2)}, u32[]{:S(2)}) collective-permute-start(bf16[4,64,256]{2,1,0:T(8,128)(2,1)} %get-tuple-element.67), channel_id=1, source_target_pairs={{0,96},{16,112},{32,64},{48,80},{64,32},{80,48},{96,0},{112,16},{1... | collective-permute-start | bytes 393224 | tf_op jit(solution)/shard_map/ppermute | solution.py:516
  63.0 20.8 %copy-start.3 = (f32[4,64,256]{2,1,0:T(8,128)S(1)}, f32[4,64,256]{2,1,0:T(8,128)}, u32[]{:S(2)}) copy-start(f32[4,64,256]{2,1,0:T(8,128)} %get-tuple-element.64) | copy-start | bytes 786436
  69.0 1.3 %collective-permute-start.8 = (f32[128,128]{1,0:T(8,128)S(1)}, f32[128,128]{1,0:T(8,128)S(1)}, u32[]{:S(2)}, u32[]{:S(2)}) collective-permute-start(f32[128,128]{1,0:T(8,128)S(1)} %backward.1), channel_id=1, source_target_pairs={{0,1},{1,0},{2,3},{3,2},{4,5},{5,4},{6,7},{7,6},{8,9},{9,8},{10,11... | collective-permute-start | bytes 196616 | tf_op jit(solution)/shard_map/ppermute | solution.py:349
  70.4 4.5 %collective-permute-start.10 = (f32[128,128]{1,0:T(8,128)S(1)}, f32[128,128]{1,0:T(8,128)S(1)}, u32[]{:S(2)}, u32[]{:S(2)}) collective-permute-start(f32[128,128]{1,0:T(8,128)S(1)} %add.37), channel_id=1, source_target_pairs={{0,16},{1,17},{2,18},{3,19},{4,20},{5,21},{6,22},{7,23},{8,24},{9,... | collective-permute-start | bytes 196616 | tf_op jit(solution)/shard_map/ppermute | solution.py:349
  72.4 6.5 %collective-permute-start.11 = (f32[128,128]{1,0:T(8,128)S(1)}, f32[128,128]{1,0:T(8,128)S(1)}, u32[]{:S(2)}, u32[]{:S(2)}) collective-permute-start(f32[128,128]{1,0:T(8,128)S(1)} %add.37), channel_id=1, source_target_pairs={{0,18},{1,19},{2,16},{3,17},{4,22},{5,23},{6,20},{7,21},{8,26},{9,... | collective-permute-start | bytes 196616 | tf_op jit(solution)/shard_map/ppermute | solution.py:349
  72.4 6.5 %collective-permute-start.9 = (f32[128,128]{1,0:T(8,128)S(1)}, f32[128,128]{1,0:T(8,128)S(1)}, u32[]{:S(2)}, u32[]{:S(2)}) collective-permute-start(f32[128,128]{1,0:T(8,128)S(1)} %add.37), channel_id=1, source_target_pairs={{0,2},{1,3},{2,0},{3,1},{4,6},{5,7},{6,4},{7,5},{8,10},{9,11},{10,... | collective-permute-start | bytes 196616 | tf_op jit(solution)/shard_map/ppermute | solution.py:349
  78.9 5.5 %collective-permute-start.12 = (f32[128,128]{1,0:T(8,128)S(1)}, f32[128,128]{1,0:T(8,128)S(1)}, u32[]{:S(2)}, u32[]{:S(2)}) collective-permute-start(f32[128,128]{1,0:T(8,128)S(1)} %add_add_fusion.1), channel_id=1, source_target_pairs={{0,4},{1,5},{2,6},{3,7},{4,0},{5,1},{6,2},{7,3},{8,12},{9,13},{10,... | collective-permute-start | bytes 196616 | tf_op jit(solution)/shard_map/ppermute | solution.py:349
  79.3 5.9 %collective-permute-start.13 = (f32[128,128]{1,0:T(8,128)S(1)}, f32[128,128]{1,0:T(8,128)S(1)}, u32[]{:S(2)}, u32[]{:S(2)}) collective-permute-start(f32[128,128]{1,0:T(8,128)S(1)} %add_add_fusion.1), channel_id=1, source_target_pairs={{0,8},{1,9},{2,10},{3,11},{4,12},{5,13},{6,14},{7,15},{8,0},{9,1},... | collective-permute-start | bytes 196616 | tf_op jit(solution)/shard_map/ppermute | solution.py:349
  82.0 5.5 %collective-permute-start.14 = (f32[128,128]{1,0:T(8,128)S(1)}, f32[128,128]{1,0:T(8,128)S(1)}, u32[]{:S(2)}, u32[]{:S(2)}) collective-permute-start(f32[128,128]{1,0:T(8,128)S(1)} %add_add_fusion.1), channel_id=1, source_target_pairs={{0,12},{1,13},{2,14},{3,15},{4,8},{5,9},{6,10},{7,11},{8,4},{9,5},... | collective-permute-start | bytes 196616 | tf_op jit(solution)/shard_map/ppermute | solution.py:349
  83.8 8.5 %collective-permute-start.7 = (bf16[4,32,256]{2,1,0:T(8,128)(2,1)S(1)}, bf16[4,32,256]{2,1,0:T(8,128)(2,1)S(1)}, u32[]{:S(2)}, u32[]{:S(2)}) collective-permute-start(bf16[4,32,256]{2,1,0:T(8,128)(2,1)S(1)} %split.13), channel_id=1, source_target_pairs={{0,16},{16,0},{32,48},{48,32},{64,80},{80,64},{96,112},{112,96},{1... | collective-permute-start | bytes 196616 | tf_op jit(solution)/shard_map/ppermute | solution.py:549
  87.5 5.5 %collective-permute-start.15 = (f32[128,128]{1,0:T(8,128)S(1)}, f32[128,128]{1,0:T(8,128)S(1)}, u32[]{:S(2)}, u32[]{:S(2)}) collective-permute-start(f32[128,128]{1,0:T(8,128)S(1)} %add_add_fusion.a_ref), channel_id=1, source_target_pairs={{0,32},{1,33},{2,34},{3,35},{4,36},{5,37},{6,38},{7,39},{8,40},{9,... | collective-permute-start | bytes 196616 | tf_op jit(solution)/shard_map/ppermute | solution.py:349
  88.4 5.8 %collective-permute-start.16 = (f32[128,128]{1,0:T(8,128)S(1)}, f32[128,128]{1,0:T(8,128)S(1)}, u32[]{:S(2)}, u32[]{:S(2)}) collective-permute-start(f32[128,128]{1,0:T(8,128)S(1)} %add_add_fusion.a_ref), channel_id=1, source_target_pairs={{0,64},{1,65},{2,66},{3,67},{4,68},{5,69},{6,70},{7,71},{8,72},{9,... | collective-permute-start | bytes 196616 | tf_op jit(solution)/shard_map/ppermute | solution.py:349
  90.0 5.5 %collective-permute-start.17 = (f32[128,128]{1,0:T(8,128)S(1)}, f32[128,128]{1,0:T(8,128)S(1)}, u32[]{:S(2)}, u32[]{:S(2)}) collective-permute-start(f32[128,128]{1,0:T(8,128)S(1)} %add_add_fusion.a_ref), channel_id=1, source_target_pairs={{0,96},{1,97},{2,98},{3,99},{4,100},{5,101},{6,102},{7,103},{8,104... | collective-permute-start | bytes 196616 | tf_op jit(solution)/shard_map/ppermute | solution.py:349

commit v9 on v8

--- a/solution.py
+++ b/solution.py
@@ -29,14 +29,22 @@
     return copies
 
 
-def feature_kernel(lab_hbm, wd_hbm, out_ref, first_ref, last_ref, lab_s, wd_b, wd_s, first_s, last_s, sem):
-    copies = fetch((lab_hbm, wd_hbm), (lab_s, wd_b), sem)
+def feature_kernel(
+    lab_hbm, wd_hbm, conv_hbm, down_hbm, mat_hbm, dist_hbm,
+    out_ref, first_ref, last_ref, conv_ref, down_ref, mat_ref, dist_ref,
+    lab_s, wd_b, wd_s, first_s, last_s, sem,
+):
+    copies = fetch(
+        (lab_hbm, wd_hbm, conv_hbm, down_hbm, mat_hbm, dist_hbm),
+        (lab_s, wd_b, conv_ref, down_ref, mat_ref, dist_ref),
+        sem,
+    )
     row = iota((128, 64), 0)
     run, r = row // 32, row % 32
     y = jnp.where(run == 0, 2 * r, jnp.where(run == 1, 2 * r + 1, jnp.where(run == 2, 2 * r - 1, 2 * r + 2)))
     pick = (y == iota((128, 64), 1)).astype(BF16)
-    for copy in copies:
-        copy.wait()
+    copies[0].wait()
+    copies[1].wait()
     wd_s[...] = wd_b[...].astype(F32)
     for z in range(out_ref.shape[0]):
         lab = lab_s[pl.ds(z, 16, stride=32), :]
@@ -48,17 +56,13 @@
         last_s[z : z + 1, :] = rows[63:64, :]
     first_ref[...] = first_s[...].astype(BF16)
     last_ref[...] = last_s[...].astype(BF16)
+    for copy in copies[2:]:
+        copy.wait()
 
 
 def weight_kernel(
-    conv_hbm, down_hbm, mat_hbm, dist_hbm, band_ref, pair_ref, pair_t_ref, table_ref,
-    conv_ref, down_ref, mat_ref, dist_ref, sem,
+    conv_ref, down_ref, mat_ref, dist_ref, band_ref, pair_ref, pair_t_ref, table_ref
 ):
-    copies = fetch(
-        (conv_hbm, down_hbm, mat_hbm, dist_hbm), (conv_ref, down_ref, mat_ref, dist_ref), sem
-    )
-    for copy in copies:
-        copy.wait()
     spread = (iota((256, 16), 0) % 16 == iota((256, 16), 1)).astype(BF16)
     taps = conv_ref[...].reshape(256, 27)
     repeat = (iota((27, 432), 0) == iota((27, 432), 1) // 16).astype(BF16)
@@ -150,7 +154,9 @@
     table = table_ref[...]
     hidden_ref[...] = inner_ref[...]
     for side, face in enumerate((zlo_ref, zhi_ref)):
-        plane = dot(face[...], table, 1, 0).astype(BF16)
+        f = face[...].astype(F32)
+        runs = [f[:64], f[64:65], f[32:63], f[1:32], f[65:66]]
+        plane = dot(jnp.concatenate(runs, axis=0).astype(BF16), table, 1, 0).astype(BF16)
         emb_ref[side] = plane
         for b in range(2):
             acc = edge_ref[side, b]
@@ -356,18 +362,26 @@
     count_z = lax.axis_size("sz")
     mine = 64 // count_z
     width = mix_weight.shape[1]
-    features, first, last = pl.pallas_call(
+    features, first, last, *weights = pl.pallas_call(
         feature_kernel,
-        out_shape=(shape((32, 128, 80), BF16), shape((32, 80), BF16), shape((32, 80), BF16)),
-        in_specs=[HBM] * 2,
-        out_specs=(VMEM,) * 3,
+        out_shape=(
+            shape((32, 128, 80), BF16),
+            shape((32, 80), BF16),
+            shape((32, 80), BF16),
+            shape((16, 16, 27), BF16),
+            shape((8, 16, 64), BF16),
+            shape((4, 16), BF16),
+            shape((1, 16), BF16),
+        ),
+        in_specs=[HBM] * 6,
+        out_specs=(VMEM,) * 7,
         scratch_shapes=[
             pltpu.VMEM((512, 64), jnp.int32),
             pltpu.VMEM((512, 64), BF16),
             pltpu.VMEM((512, 64), F32),
             pltpu.VMEM((32, 80), F32),
             pltpu.VMEM((32, 80), F32),
-            pltpu.SemaphoreType.DMA((2,)),
+            pltpu.SemaphoreType.DMA((6,)),
         ],
         compiler_params=params(8),
         cost_estimate=cost(32 * 128 * 64 * 80 * 2, 2 << 20),
@@ -376,6 +390,10 @@
         *kept(
             jnp.transpose(labels, (0, 2, 1)).reshape(512, 64),
             jnp.transpose(wall_dist, (0, 2, 1)).reshape(512, 64),
+            jnp.transpose(conv_weight, (1, 2, 0)),
+            jnp.transpose(down_weight, (0, 2, 1)),
+            material_table,
+            dist_weight[None],
         )
     )
     up_y = [(i, i + 1) for i in range(count_y - 1)]
@@ -390,34 +408,20 @@
             shape((256, 128), BF16),
             shape((80, 256), BF16),
         ),
-        in_specs=[HBM] * 4,
+        in_specs=[VMEM] * 4,
         out_specs=(VMEM,) * 4,
-        scratch_shapes=[
-            pltpu.VMEM((16, 16, 27), BF16),
-            pltpu.VMEM((8, 16, 64), BF16),
-            pltpu.VMEM((4, 16), BF16),
-            pltpu.VMEM((1, 16), BF16),
-            pltpu.SemaphoreType.DMA((4,)),
-        ],
         compiler_params=params(8),
         cost_estimate=cost(27 * 256 * 16 * 256 * 2, 3 << 20),
         name="weights",
-    )(
-        *kept(
-            jnp.transpose(conv_weight, (1, 2, 0)),
-            jnp.transpose(down_weight, (0, 2, 1)),
-            material_table,
-            dist_weight[None],
-        )
-    )
+    )(*weights)
     ylo, yhi, band, pair, pair_t, table = lax.optimization_barrier(
         (ylo, yhi, band, pair, pair_t, table)
     )
 
     def whole(z):
-        row = lax.broadcasted_iota(jnp.int32, (128, 80), 0)
-        face = jnp.where(row == 64, ylo[z][None], features[z])
-        return jnp.where(row == 127, yhi[z][None], face)
+        row = lax.broadcasted_iota(jnp.int32, (80, 80), 0)
+        face = jnp.where(row == 64, ylo[z][None], features[z, :80])
+        return jnp.where(row == 65, yhi[z][None], face)
 
     zlo = lax.ppermute(whole(31), "sz", up_z)
     zhi = lax.ppermute(whole(0), "sz", [(j, i) for i, j in up_z])

time: 96.7 us -> 96.5 us (level)
  transfers between devices with their start and end apart: 20 -> 20, of which waited for: 11 -> 11; matrix products, arithmetic and copies ran while one was open for 1% -> 1% of each run, Pallas kernels for 16% -> 15%
where the time goes in v9:
time: 96.5 us; the launch traced here: 96.1 us
  starting transfers between devices  41.8 us (43%)
  waiting for transfers between devices  31.3 us (32%)
  Pallas kernels  21.2 us (22%)
    ppermute x10, starting transfers between devices, exchanged(): lax.ppermute(value, ('sy', 'sz'), [(i, i ^ m) for i in range(count)])  13.9 us
    all_to_all x1, waiting for transfers between devices, per_device(): lax.all_to_all(coarse.reshape(count_z, mine * 16, 256), 'sz', split_axis=...  11.8 us
    all_to_all x1, starting transfers between devices, per_device(): lax.all_to_all(coarse.reshape(count_z, mine * 16, 256), 'sz', split_axis=...  11.5 us
    ppermute x10, waiting for transfers between devices, exchanged(): lax.ppermute(value, ('sy', 'sz'), [(i, i ^ m) for i in range(count)])  10.8 us
    pallas_call x1, Pallas kernels, per_device(): pl.pallas_call(lambda *refs: backward_kernel(1.0 / math.sqrt(cells // 8),...  6 us
    all_to_all x1, waiting for transfers between devices, per_device(): lax.all_to_all(back, 'sz', split_axis=0, concat_axis=0, tiled=True)  5.1 us
    ppermute x3, starting transfers between devices, per_device(): lax.ppermute(part, 'sy', [(i, i ^ 2 * k) for i in range(count_y)])  4.7 us
    pallas_call x1, Pallas kernels, per_device(): pl.pallas_call(inner_kernel, out_shape=(shape((17, 2, 128, 256), BF16), p...  4.12 us
  transfers between devices with their start and end apart: 20, of which 11 were waited for; matrix products, arithmetic and copies ran while one was open for 1% of the time, Pallas kernels for 15%

profile of v9, /device:TPU:0, one launch (start us, length us, event | category | flops | bytes accessed | tf_op | source)
XLA Modules:
  0.0 96.1 jit_solution(786901944160833945)
XLA Ops:
  0.6 1.7 %features.1 = (bf16[32,128,80]{2,1,0:T(8,128)(2,1)S(1)}, bf16[32,80]{1,0:T(8,128)(2,1)S(1)}, bf16[32,80]{1,0:T(8,128)(2,1)S(1)}, bf16[16,16,27]{2,1,0:T(8,128)(2...) custom-call(s32[512,64]{1,0:T(8,128)} %bitcast.37, ...), custom_call_target="tpu_custom_call" | custom-call | flops 41943040 | bytes 2097152 | tf_op jit(solution)/shard_map/features/pallas_call | solution.py:365
  2.4 3.6 %collective-permute-start = (bf16[32,80]{1,0:T(8,128)(2,1)S(1)}, bf16[32,80]{1,0:T(8,128)(2,1)S(1)}, u32[]{:S(2)}, u32[]{:S(2)}) collective-permute-start(bf16[32,80]{1,0:T(8,128)(2,1)S(1)} %get-tuple-element.46), channel_id=1, source_target_pairs={{0,16},{16,32},{32,48},{48,64},{64,80},{80,96},{96,112},{1,17},{17... | collective-permute-start | bytes 15368 | tf_op jit(solution)/shard_map/ppermute | solution.py:401
  5.9 1.3 %collective-permute-start.1 = (bf16[32,80]{1,0:T(8,128)(2,1)S(1)}, bf16[32,80]{1,0:T(8,128)(2,1)S(1)}, u32[]{:S(2)}, u32[]{:S(2)}) collective-permute-start(bf16[32,80]{1,0:T(8,128)(2,1)S(1)} %get-tuple-element.47), channel_id=1, source_target_pairs={{16,0},{32,16},{48,32},{64,48},{80,64},{96,80},{112,96},{17,1},{33... | collective-permute-start | bytes 15368 | tf_op jit(solution)/shard_map/ppermute | solution.py:402
  7.3 1.4 %weights.1 = (bf16[9,256,256]{2,1,0:T(8,128)(2,1)S(1)}, bf16[128,256]{1,0:T(8,128)(2,1)S(1)}, bf16[256,128]{1,0:T(8,128)(2,1)S(1)}, bf16[80,256]{1,0:T(8,128)(2,1)S(1)}) custom-call(bf16[16,16,27]{2,1,0:T(8,128)(2,1)S(1)} %get-tuple-element.48.conv_ref, bf16[8,16,64]{2,1,0:T(8,128)(2,1)S(1)} %get-tuple-element.49.down_ref, ...), custom_call_target="tpu_custom_call" | custom-call | flops 56623104 | bytes 3145728 | tf_op jit(solution)/shard_map/weights/pallas_call | solution.py:403
  8.7 0.0 collective-permute-done.ylo_ref
  8.7 2.8 %collective-permute-done.1.yhi_ref = bf16[32,80]{1,0:T(8,128)(2,1)S(1)} collective-permute-done((bf16[32,80]{1,0:T(8,128)(2,1)S(1)}, bf16[32,80]{1,0:T(8,128)(2,1)S(1)}, u32[]{:S(2)}, u32[]{:S(2)}) %collective-permute-start.1) | collective-permute-done | bytes 5152 | tf_op jit(solution)/shard_map/ppermute | solution.py:402
  11.5 0.1 fusion
  11.6 1.3 %collective-permute-start.2 = (bf16[80,80]{1,0:T(8,128)(2,1)S(1)}, bf16[80,80]{1,0:T(8,128)(2,1)S(1)}, u32[]{:S(2)}, u32[]{:S(2)}) collective-permute-start(bf16[80,80]{1,0:T(8,128)(2,1)S(1)} %get-tuple-element.89), channel_id=1, source_target_pairs={{0,1},{1,2},{2,3},{3,4},{4,5},{5,6},{6,7},{7,8},{8,9},{9,10},{10,1... | collective-permute-start | bytes 38408 | tf_op jit(solution)/shard_map/ppermute | solution.py:426
  12.9 1.3 %collective-permute-start.3 = (bf16[80,80]{1,0:T(8,128)(2,1)S(1)}, bf16[80,80]{1,0:T(8,128)(2,1)S(1)}, u32[]{:S(2)}, u32[]{:S(2)}) collective-permute-start(bf16[80,80]{1,0:T(8,128)(2,1)S(1)} %get-tuple-element.88), channel_id=1, source_target_pairs={{1,0},{2,1},{3,2},{4,3},{5,4},{6,5},{7,6},{8,7},{9,8},{10,9},{11,1... | collective-permute-start | bytes 38408 | tf_op jit(solution)/shard_map/ppermute | solution.py:427
  14.2 4.1 %inner.1 = (bf16[17,2,128,256]{3,2,1,0:T(8,128)(2,1)S(1)}, f32[4,256,512]{2,1,0:T(8,128)}, bf16[4,256,512]{2,1,0:T(8,128)(2,1)S(1)}, f32[2,2,256,32]{3,2,1,0:T(8,128)S(1)}) custom-call(bf16[32,128,80]{2,1,0:T(8,128)(2,1)S(1)} %get-tuple-element.58.feat_ref, bf16[32,80]{1,0:T(8,128)(2,1)S(1)} %collective-permute-done.ylo_ref, ...), custom_call_target="tpu_custom_call" | custom-call | flops 3221225472 | bytes 10485760 | tf_op jit(solution)/shard_map/inner/pallas_call | solution.py:428
  18.3 0.0 copy-start.2
  18.3 0.0 collective-permute-done.2.zlo_ref
  18.3 0.8 collective-permute-done.3.zhi_ref
  19.1 0.0 copy-start
  19.1 0.0 copy-start.1
  19.1 2.7 %outer.1 = (bf16[2,128,256]{2,1,0:T(8,128)(2,1)S(1)}, f32[256,128]{1,0:T(8,128)S(1)}, bf16[4,256,512]{2,1,0:T(8,128)(2,1)}, bf16[1024,256]{1,0:T(8,128)(2,1)}) custom-call(bf16[80,80]{1,0:T(8,128)(2,1)S(1)} %collective-permute-done.2.zlo_ref, bf16[80,80]{1,0:T(8,128)(2,1)S(1)} %collective-permute-done.3.zhi_ref, ...), custom_call_target="tpu_custom_call" | custom-call | flops 1073741824 | bytes 4194304 | tf_op jit(solution)/shard_map/outer/pallas_call | solution.py:443
  21.8 0.0 copy-done.2
  21.8 11.5 %all-to-all-start = ((bf16[16,64,256]{2,1,0:T(8,128)(2,1)}), bf16[16,64,256]{2,1,0:T(8,128)(2,1)S(1)}, u32[]{:S(2)}, u32[]{:S(2)}) async-start(bf16[16,64,256]{2,1,0:T(8,128)(2,1)} %bitcast.36), calls=%async_computation | async-start | bytes 1048576 | tf_op jit(solution)/shard_map/all_to_all | solution.py:468
  33.4 0.0 copy-done
  33.4 0.0 copy-done.1
  33.4 0.5 turn.1
  33.9 11.8 %all-to-all-done.coarse_ref.refs_1_ = bf16[16,64,256]{2,1,0:T(8,128)(2,1)S(1)} async-done(((bf16[16,64,256]{2,1,0:T(8,128)(2,1)}), bf16[16,64,256]{2,1,0:T(8,128)(2,1)S(1)}, u32[]{:S(2)}, u32[]{:S(2)}) %all-to-all-start) | async-done | bytes 524320 | tf_op jit(solution)/shard_map/all_to_all | solution.py:468
  45.7 1.4 %mix.1 = bf16[16,64,256]{2,1,0:T(8,128)(2,1)} custom-call(bf16[16,64,256]{2,1,0:T(8,128)(2,1)S(1)} %all-to-all-done.coarse_ref.refs_1_, bf16[4,256,256]{2,1,0:T(8,128)(2,1)S(1)} %copy-done, bf16[4,256,256]{2,1,0:T(8,128)(2,1)S(1)} %get-tuple-element.68.cot_t_ref.refs_3_, bf16[4,256,256]{2,1,0:T(8,128)(2,1)S(1)} %get-tuple-element.69.mix_t_ref), custom_call_target="tpu_custom_call" | custom-call | flops 268435456 | bytes 2097152 | tf_op jit(solution)/shard_map/mix/pallas_call | solution.py:488
  47.1 3.6 %all-to-all-start.1 = ((bf16[16,64,256]{2,1,0:T(8,128)(2,1)}), bf16[16,64,256]{2,1,0:T(8,128)(2,1)S(1)}, u32[]{:S(2)}, u32[]{:S(2)}) async-start(bf16[16,64,256]{2,1,0:T(8,128)(2,1)} %mix.1), calls=%async_computation.1 | async-start | bytes 1048576 | tf_op jit(solution)/shard_map/all_to_all | solution.py:501
  50.7 2.5 %mix_grad.1 = (bf16[4,256,256]{2,1,0:T(8,128)(2,1)}, f32[4,64,256]{2,1,0:T(8,128)}, bf16[4,64,256]{2,1,0:T(8,128)(2,1)}, bf16[4,64,256]{2,1,0:T(8,128)(2,1)}, bf16[4,64,256]{2,1,0:T(8,128)(2,1)}) custom-call(s32[1]{0:T(128)} %bitcast.refs_0_, bf16[16,64,256]{2,1,0:T(8,128)(2,1)S(1)} %all-to-all-done.coarse_ref.refs_1_, bf16[4,256,256]{2,1,0:T(8,128)(2,1)S(1)} %copy-done, ...), custom_call_target="tpu_custom_call" | custom-call | flops 268435456 | bytes 3145728 | tf_op jit(solution)/shard_map/mix_grad/pallas_call | solution.py:503
  53.2 1.5 %collective-permute-start.4 = (bf16[4,64,256]{2,1,0:T(8,128)(2,1)}, bf16[4,64,256]{2,1,0:T(8,128)(2,1)S(1)}, u32[]{:S(2)}, u32[]{:S(2)}) collective-permute-start(bf16[4,64,256]{2,1,0:T(8,128)(2,1)} %get-tuple-element.73), channel_id=1, source_target_pairs={{0,32},{16,48},{32,0},{48,16},{64,96},{80,112},{96,64},{112,80},{1... | collective-permute-start | bytes 393224 | tf_op jit(solution)/shard_map/ppermute | solution.py:520
  54.7 2.7 %collective-permute-start.5 = (bf16[4,64,256]{2,1,0:T(8,128)(2,1)}, bf16[4,64,256]{2,1,0:T(8,128)(2,1)S(1)}, u32[]{:S(2)}, u32[]{:S(2)}) collective-permute-start(bf16[4,64,256]{2,1,0:T(8,128)(2,1)} %get-tuple-element.74), channel_id=1, source_target_pairs={{0,64},{16,80},{32,96},{48,112},{64,0},{80,16},{96,32},{112,48},{1... | collective-permute-start | bytes 393224 | tf_op jit(solution)/shard_map/ppermute | solution.py:520
  57.5 0.5 collective-permute-start.6
  57.9 5.1 %all-to-all-done.1 = bf16[16,64,256]{2,1,0:T(8,128)(2,1)S(1)} async-done(((bf16[16,64,256]{2,1,0:T(8,128)(2,1)}), bf16[16,64,256]{2,1,0:T(8,128)(2,1)S(1)}, u32[]{:S(2)}, u32[]{:S(2)}) %all-to-all-start.1) | async-done | bytes 524320 | tf_op jit(solution)/shard_map/all_to_all | solution.py:501
  63.0 0.0 copy-start.3
  63.0 6.0 %backward.1 = f32[128,128]{1,0:T(8,128)S(1)} custom-call(bf16[1024,256]{1,0:T(8,128)(2,1)S(1)} %bitcast.35, bf16[17,2,128,256]{3,2,1,0:T(8,128)(2,1)} %copy-done.2, f32[4,256,512]{2,1,0:T(8,128)} %get-tuple-element.77.refs_2_, bf16[4,256,512]{2,1,0:T(8,128)(2,1)} %get-tuple-element.78.refs_3_, bf16[128,256]{1,0:T(8,128)(2,1)S(1)} %get-tuple-element.61.pair_ref.refs_4_, ...), custom_call_target="tpu_custom_call" | custom-call | flops 4294967296 | bytes 8388608 | tf_op jit(solution)/shard_map/backward/pallas_call | solution.py:522
  69.0 0.0 collective-permute-done.4
  69.0 0.0 collective-permute-done.5
  69.1 0.0 collective-permute-done.6
  69.1 0.1 collective-permute-start.8
  69.2 1.2 %collective-permute-done.8 = f32[128,128]{1,0:T(8,128)S(1)} collective-permute-done((f32[128,128]{1,0:T(8,128)S(1)}, f32[128,128]{1,0:T(8,128)S(1)}, u32[]{:S(2)}, u32[]{:S(2)}) %collective-permute-start.8) | collective-permute-done | bytes 65568 | tf_op jit(solution)/shard_map/ppermute | solution.py:355
  70.4 2.1 %collective-permute-start.10 = (f32[128,128]{1,0:T(8,128)S(1)}, f32[128,128]{1,0:T(8,128)S(1)}, u32[]{:S(2)}, u32[]{:S(2)}) collective-permute-start(f32[128,128]{1,0:T(8,128)S(1)} %add.37), channel_id=1, source_target_pairs={{0,16},{1,17},{2,18},{3,19},{4,20},{5,21},{6,22},{7,23},{8,24},{9,... | collective-permute-start | bytes 196616 | tf_op jit(solution)/shard_map/ppermute | solution.py:355
  72.5 0.0 collective-permute-start.11
  72.5 2.2 %collective-permute-start.9 = (f32[128,128]{1,0:T(8,128)S(1)}, f32[128,128]{1,0:T(8,128)S(1)}, u32[]{:S(2)}, u32[]{:S(2)}) collective-permute-start(f32[128,128]{1,0:T(8,128)S(1)} %add.37), channel_id=1, source_target_pairs={{0,2},{1,3},{2,0},{3,1},{4,6},{5,7},{6,4},{7,5},{8,10},{9,11},{10,... | collective-permute-start | bytes 196616 | tf_op jit(solution)/shard_map/ppermute | solution.py:355
  74.6 0.3 collective-permute-done.10
  74.9 4.1 %collective-permute-done.11 = f32[128,128]{1,0:T(8,128)S(1)} collective-permute-done((f32[128,128]{1,0:T(8,128)S(1)}, f32[128,128]{1,0:T(8,128)S(1)}, u32[]{:S(2)}, u32[]{:S(2)}) %collective-permute-start.11) | collective-permute-done | bytes 65568 | tf_op jit(solution)/shard_map/ppermute | solution.py:355
  79.0 0.0 collective-permute-done.9
  79.0 0.1 collective-permute-start.12
  79.1 2.6 %collective-permute-start.13 = (f32[128,128]{1,0:T(8,128)S(1)}, f32[128,128]{1,0:T(8,128)S(1)}, u32[]{:S(2)}, u32[]{:S(2)}) collective-permute-start(f32[128,128]{1,0:T(8,128)S(1)} %add_add_fusion.1), channel_id=1, source_target_pairs={{0,8},{1,9},{2,10},{3,11},{4,12},{5,13},{6,14},{7,15},{8,0},{9,1},... | collective-permute-start | bytes 196616 | tf_op jit(solution)/shard_map/ppermute | solution.py:355
  81.7 2.1 %collective-permute-start.14 = (f32[128,128]{1,0:T(8,128)S(1)}, f32[128,128]{1,0:T(8,128)S(1)}, u32[]{:S(2)}, u32[]{:S(2)}) collective-permute-start(f32[128,128]{1,0:T(8,128)S(1)} %add_add_fusion.1), channel_id=1, source_target_pairs={{0,12},{1,13},{2,14},{3,15},{4,8},{5,9},{6,10},{7,11},{8,4},{9,5},... | collective-permute-start | bytes 196616 | tf_op jit(solution)/shard_map/ppermute | solution.py:355
  83.8 0.0 copy-done.3
  83.8 0.1 convert_add_fusion
  83.9 0.7 collective-permute-start.7
  84.5 0.0 collective-permute-done.12
  84.5 0.6 collective-permute-done.13
  85.2 2.0 %collective-permute-done.14 = f32[128,128]{1,0:T(8,128)S(1)} collective-permute-done((f32[128,128]{1,0:T(8,128)S(1)}, f32[128,128]{1,0:T(8,128)S(1)}, u32[]{:S(2)}, u32[]{:S(2)}) %collective-permute-start.14) | collective-permute-done | bytes 65568 | tf_op jit(solution)/shard_map/ppermute | solution.py:355
  87.2 1.3 %collective-permute-start.15 = (f32[128,128]{1,0:T(8,128)S(1)}, f32[128,128]{1,0:T(8,128)S(1)}, u32[]{:S(2)}, u32[]{:S(2)}) collective-permute-start(f32[128,128]{1,0:T(8,128)S(1)} %add_add_fusion.a_ref), channel_id=1, source_target_pairs={{0,32},{1,33},{2,34},{3,35},{4,36},{5,37},{6,38},{7,39},{8,40},{9,... | collective-permute-start | bytes 196616 | tf_op jit(solution)/shard_map/ppermute | solution.py:355
  88.4 1.4 %collective-permute-start.16 = (f32[128,128]{1,0:T(8,128)S(1)}, f32[128,128]{1,0:T(8,128)S(1)}, u32[]{:S(2)}, u32[]{:S(2)}) collective-permute-start(f32[128,128]{1,0:T(8,128)S(1)} %add_add_fusion.a_ref), channel_id=1, source_target_pairs={{0,64},{1,65},{2,66},{3,67},{4,68},{5,69},{6,70},{7,71},{8,72},{9,... | collective-permute-start | bytes 196616 | tf_op jit(solution)/shard_map/ppermute | solution.py:355
  89.8 2.2 %collective-permute-start.17 = (f32[128,128]{1,0:T(8,128)S(1)}, f32[128,128]{1,0:T(8,128)S(1)}, u32[]{:S(2)}, u32[]{:S(2)}) collective-permute-start(f32[128,128]{1,0:T(8,128)S(1)} %add_add_fusion.a_ref), channel_id=1, source_target_pairs={{0,96},{1,97},{2,98},{3,99},{4,100},{5,101},{6,102},{7,103},{8,104... | collective-permute-start | bytes 196616 | tf_op jit(solution)/shard_map/ppermute | solution.py:355
  92.0 0.0 collective-permute-done.7
  92.0 0.7 slice_add_fusion
  92.6 0.0 collective-permute-done.15.b_ref
  92.6 1.6 %collective-permute-done.16.c_ref = f32[128,128]{1,0:T(8,128)S(1)} collective-permute-done((f32[128,128]{1,0:T(8,128)S(1)}, f32[128,128]{1,0:T(8,128)S(1)}, u32[]{:S(2)}, u32[]{:S(2)}) %collective-permute-start.16) | collective-permute-done | bytes 65568 | tf_op jit(solution)/shard_map/ppermute | solution.py:355
  94.2 1.1 %collective-permute-done.17.d_ref = f32[128,128]{1,0:T(8,128)S(1)} collective-permute-done((f32[128,128]{1,0:T(8,128)S(1)}, f32[128,128]{1,0:T(8,128)S(1)}, u32[]{:S(2)}, u32[]{:S(2)}) %collective-permute-start.17) | collective-permute-done | bytes 65568 | tf_op jit(solution)/shard_map/ppermute | solution.py:355
  95.3 0.8 finish.1
  (6 shorter events, 0.1 us)
Async XLA Ops:
  2.4 6.3 %collective-permute-start = (bf16[32,80]{1,0:T(8,128)(2,1)S(1)}, bf16[32,80]{1,0:T(8,128)(2,1)S(1)}, u32[]{:S(2)}, u32[]{:S(2)}) collective-permute-start(bf16[32,80]{1,0:T(8,128)(2,1)S(1)} %get-tuple-element.46), channel_id=1, source_target_pairs={{0,16},{16,32},{32,48},{48,64},{64,80},{80,96},{96,112},{1,17},{17... | collective-permute-start | bytes 15368 | tf_op jit(solution)/shard_map/ppermute | solution.py:401
  5.9 5.5 %collective-permute-start.1 = (bf16[32,80]{1,0:T(8,128)(2,1)S(1)}, bf16[32,80]{1,0:T(8,128)(2,1)S(1)}, u32[]{:S(2)}, u32[]{:S(2)}) collective-permute-start(bf16[32,80]{1,0:T(8,128)(2,1)S(1)} %get-tuple-element.47), channel_id=1, source_target_pairs={{16,0},{32,16},{48,32},{64,48},{80,64},{96,80},{112,96},{17,1},{33... | collective-permute-start | bytes 15368 | tf_op jit(solution)/shard_map/ppermute | solution.py:402
  11.6 6.7 %collective-permute-start.2 = (bf16[80,80]{1,0:T(8,128)(2,1)S(1)}, bf16[80,80]{1,0:T(8,128)(2,1)S(1)}, u32[]{:S(2)}, u32[]{:S(2)}) collective-permute-start(bf16[80,80]{1,0:T(8,128)(2,1)S(1)} %get-tuple-element.89), channel_id=1, source_target_pairs={{0,1},{1,2},{2,3},{3,4},{4,5},{5,6},{6,7},{7,8},{8,9},{9,10},{10,1... | collective-permute-start | bytes 38408 | tf_op jit(solution)/shard_map/ppermute | solution.py:426
  12.9 6.2 %collective-permute-start.3 = (bf16[80,80]{1,0:T(8,128)(2,1)S(1)}, bf16[80,80]{1,0:T(8,128)(2,1)S(1)}, u32[]{:S(2)}, u32[]{:S(2)}) collective-permute-start(bf16[80,80]{1,0:T(8,128)(2,1)S(1)} %get-tuple-element.88), channel_id=1, source_target_pairs={{1,0},{2,1},{3,2},{4,3},{5,4},{6,5},{7,6},{8,7},{9,8},{10,9},{11,1... | collective-permute-start | bytes 38408 | tf_op jit(solution)/shard_map/ppermute | solution.py:427
  18.3 3.5 %copy-start.2 = (bf16[17,2,128,256]{3,2,1,0:T(8,128)(2,1)}, bf16[17,2,128,256]{3,2,1,0:T(8,128)(2,1)S(1)}, u32[]{:S(2)}) copy-start(bf16[17,2,128,256]{3,2,1,0:T(8,128)(2,1)S(1)} %get-tuple-element.76.refs_1_) | copy-start | bytes 6684676
  19.1 14.2 %copy-start = (bf16[4,256,256]{2,1,0:T(8,128)(2,1)S(1)}, bf16[4,256,256]{2,1,0:T(8,128)(2,1)}, u32[]{:S(2)}) copy-start(bf16[4,256,256]{2,1,0:T(8,128)(2,1)} %refs_2_) | copy-start | bytes 1572868
  19.1 14.3 %copy-start.1 = (bf16[4,8,32,256]{3,2,1,0:T(8,128)(2,1)S(1)}, bf16[4,8,32,256]{3,2,1,0:T(8,128)(2,1)}, u32[]{:S(2)}) copy-start(bf16[4,8,32,256]{3,2,1,0:T(8,128)(2,1)} %param.15) | copy-start | bytes 1572868
  21.8 23.9 %all-to-all-start = ((bf16[16,64,256]{2,1,0:T(8,128)(2,1)}), bf16[16,64,256]{2,1,0:T(8,128)(2,1)S(1)}, u32[]{:S(2)}, u32[]{:S(2)}) async-start(bf16[16,64,256]{2,1,0:T(8,128)(2,1)} %bitcast.36), calls=%async_computation | async-start | bytes 1048576 | tf_op jit(solution)/shard_map/all_to_all | solution.py:468
  47.1 15.9 %all-to-all-start.1 = ((bf16[16,64,256]{2,1,0:T(8,128)(2,1)}), bf16[16,64,256]{2,1,0:T(8,128)(2,1)S(1)}, u32[]{:S(2)}, u32[]{:S(2)}) async-start(bf16[16,64,256]{2,1,0:T(8,128)(2,1)} %mix.1), calls=%async_computation.1 | async-start | bytes 1048576 | tf_op jit(solution)/shard_map/all_to_all | solution.py:501
  53.2 15.8 %collective-permute-start.4 = (bf16[4,64,256]{2,1,0:T(8,128)(2,1)}, bf16[4,64,256]{2,1,0:T(8,128)(2,1)S(1)}, u32[]{:S(2)}, u32[]{:S(2)}) collective-permute-start(bf16[4,64,256]{2,1,0:T(8,128)(2,1)} %get-tuple-element.73), channel_id=1, source_target_pairs={{0,32},{16,48},{32,0},{48,16},{64,96},{80,112},{96,64},{112,80},{1... | collective-permute-start | bytes 393224 | tf_op jit(solution)/shard_map/ppermute | solution.py:520
  54.7 14.3 %collective-permute-start.5 = (bf16[4,64,256]{2,1,0:T(8,128)(2,1)}, bf16[4,64,256]{2,1,0:T(8,128)(2,1)S(1)}, u32[]{:S(2)}, u32[]{:S(2)}) collective-permute-start(bf16[4,64,256]{2,1,0:T(8,128)(2,1)} %get-tuple-element.74), channel_id=1, source_target_pairs={{0,64},{16,80},{32,96},{48,112},{64,0},{80,16},{96,32},{112,48},{1... | collective-permute-start | bytes 393224 | tf_op jit(solution)/shard_map/ppermute | solution.py:520
  57.5 11.6 %collective-permute-start.6 = (bf16[4,64,256]{2,1,0:T(8,128)(2,1)}, bf16[4,64,256]{2,1,0:T(8,128)(2,1)S(1)}, u32[]{:S(2)}, u32[]{:S(2)}) collective-permute-start(bf16[4,64,256]{2,1,0:T(8,128)(2,1)} %get-tuple-element.75), channel_id=1, source_target_pairs={{0,96},{16,112},{32,64},{48,80},{64,32},{80,48},{96,0},{112,16},{1... | collective-permute-start | bytes 393224 | tf_op jit(solution)/shard_map/ppermute | solution.py:520
  63.0 20.8 %copy-start.3 = (f32[4,64,256]{2,1,0:T(8,128)S(1)}, f32[4,64,256]{2,1,0:T(8,128)}, u32[]{:S(2)}) copy-start(f32[4,64,256]{2,1,0:T(8,128)} %get-tuple-element.72) | copy-start | bytes 786436
  69.1 1.3 %collective-permute-start.8 = (f32[128,128]{1,0:T(8,128)S(1)}, f32[128,128]{1,0:T(8,128)S(1)}, u32[]{:S(2)}, u32[]{:S(2)}) collective-permute-start(f32[128,128]{1,0:T(8,128)S(1)} %backward.1), channel_id=1, source_target_pairs={{0,1},{1,0},{2,3},{3,2},{4,5},{5,4},{6,7},{7,6},{8,9},{9,8},{10,11... | collective-permute-start | bytes 196616 | tf_op jit(solution)/shard_map/ppermute | solution.py:355
  70.4 4.5 %collective-permute-start.10 = (f32[128,128]{1,0:T(8,128)S(1)}, f32[128,128]{1,0:T(8,128)S(1)}, u32[]{:S(2)}, u32[]{:S(2)}) collective-permute-start(f32[128,128]{1,0:T(8,128)S(1)} %add.37), channel_id=1, source_target_pairs={{0,16},{1,17},{2,18},{3,19},{4,20},{5,21},{6,22},{7,23},{8,24},{9,... | collective-permute-start | bytes 196616 | tf_op jit(solution)/shard_map/ppermute | solution.py:355
  72.5 6.5 %collective-permute-start.11 = (f32[128,128]{1,0:T(8,128)S(1)}, f32[128,128]{1,0:T(8,128)S(1)}, u32[]{:S(2)}, u32[]{:S(2)}) collective-permute-start(f32[128,128]{1,0:T(8,128)S(1)} %add.37), channel_id=1, source_target_pairs={{0,18},{1,19},{2,16},{3,17},{4,22},{5,23},{6,20},{7,21},{8,26},{9,... | collective-permute-start | bytes 196616 | tf_op jit(solution)/shard_map/ppermute | solution.py:355
  72.5 6.5 %collective-permute-start.9 = (f32[128,128]{1,0:T(8,128)S(1)}, f32[128,128]{1,0:T(8,128)S(1)}, u32[]{:S(2)}, u32[]{:S(2)}) collective-permute-start(f32[128,128]{1,0:T(8,128)S(1)} %add.37), channel_id=1, source_target_pairs={{0,2},{1,3},{2,0},{3,1},{4,6},{5,7},{6,4},{7,5},{8,10},{9,11},{10,... | collective-permute-start | bytes 196616 | tf_op jit(solution)/shard_map/ppermute | solution.py:355
  79.0 5.5 %collective-permute-start.12 = (f32[128,128]{1,0:T(8,128)S(1)}, f32[128,128]{1,0:T(8,128)S(1)}, u32[]{:S(2)}, u32[]{:S(2)}) collective-permute-start(f32[128,128]{1,0:T(8,128)S(1)} %add_add_fusion.1), channel_id=1, source_target_pairs={{0,4},{1,5},{2,6},{3,7},{4,0},{5,1},{6,2},{7,3},{8,12},{9,13},{10,... | collective-permute-start | bytes 196616 | tf_op jit(solution)/shard_map/ppermute | solution.py:355
  79.1 6.1 %collective-permute-start.13 = (f32[128,128]{1,0:T(8,128)S(1)}, f32[128,128]{1,0:T(8,128)S(1)}, u32[]{:S(2)}, u32[]{:S(2)}) collective-permute-start(f32[128,128]{1,0:T(8,128)S(1)} %add_add_fusion.1), channel_id=1, source_target_pairs={{0,8},{1,9},{2,10},{3,11},{4,12},{5,13},{6,14},{7,15},{8,0},{9,1},... | collective-permute-start | bytes 196616 | tf_op jit(solution)/shard_map/ppermute | solution.py:355
  81.7 5.5 %collective-permute-start.14 = (f32[128,128]{1,0:T(8,128)S(1)}, f32[128,128]{1,0:T(8,128)S(1)}, u32[]{:S(2)}, u32[]{:S(2)}) collective-permute-start(f32[128,128]{1,0:T(8,128)S(1)} %add_add_fusion.1), channel_id=1, source_target_pairs={{0,12},{1,13},{2,14},{3,15},{4,8},{5,9},{6,10},{7,11},{8,4},{9,5},... | collective-permute-start | bytes 196616 | tf_op jit(solution)/shard_map/ppermute | solution.py:355
  83.9 8.1 %collective-permute-start.7 = (bf16[4,32,256]{2,1,0:T(8,128)(2,1)S(1)}, bf16[4,32,256]{2,1,0:T(8,128)(2,1)S(1)}, u32[]{:S(2)}, u32[]{:S(2)}) collective-permute-start(bf16[4,32,256]{2,1,0:T(8,128)(2,1)S(1)} %split.13), channel_id=1, source_target_pairs={{0,16},{16,0},{32,48},{48,32},{64,80},{80,64},{96,112},{112,96},{1... | collective-permute-start | bytes 196616 | tf_op jit(solution)/shard_map/ppermute | solution.py:553
  87.2 5.5 %collective-permute-start.15 = (f32[128,128]{1,0:T(8,128)S(1)}, f32[128,128]{1,0:T(8,128)S(1)}, u32[]{:S(2)}, u32[]{:S(2)}) collective-permute-start(f32[128,128]{1,0:T(8,128)S(1)} %add_add_fusion.a_ref), channel_id=1, source_target_pairs={{0,32},{1,33},{2,34},{3,35},{4,36},{5,37},{6,38},{7,39},{8,40},{9,... | collective-permute-start | bytes 196616 | tf_op jit(solution)/shard_map/ppermute | solution.py:355
  88.4 5.8 %collective-permute-start.16 = (f32[128,128]{1,0:T(8,128)S(1)}, f32[128,128]{1,0:T(8,128)S(1)}, u32[]{:S(2)}, u32[]{:S(2)}) collective-permute-start(f32[128,128]{1,0:T(8,128)S(1)} %add_add_fusion.a_ref), channel_id=1, source_target_pairs={{0,64},{1,65},{2,66},{3,67},{4,68},{5,69},{6,70},{7,71},{8,72},{9,... | collective-permute-start | bytes 196616 | tf_op jit(solution)/shard_map/ppermute | solution.py:355
  89.8 5.5 %collective-permute-start.17 = (f32[128,128]{1,0:T(8,128)S(1)}, f32[128,128]{1,0:T(8,128)S(1)}, u32[]{:S(2)}, u32[]{:S(2)}) collective-permute-start(f32[128,128]{1,0:T(8,128)S(1)} %add_add_fusion.a_ref), channel_id=1, source_target_pairs={{0,96},{1,97},{2,98},{3,99},{4,100},{5,101},{6,102},{7,103},{8,104... | collective-permute-start | bytes 196616 | tf_op jit(solution)/shard_map/ppermute | solution.py:355

commit v10 on v9

--- a/solution.py
+++ b/solution.py
@@ -238,13 +238,15 @@
     down_scale, conv_scale, cgrad_ref, emb_hbm, slope_hbm, hidden_hbm, pair_ref, pair_t_ref, face_ref, edge_ref,
     out_ref, turn_a, turn_b, turned_pg, emb_in, slope_in, hidden_ref, sem,
 ):
-    copies = [
-        pltpu.make_async_copy(slope_hbm, slope_in, sem.at[0]),
-        pltpu.make_async_copy(emb_hbm, emb_in, sem.at[1]),
-        pltpu.make_async_copy(hidden_hbm, hidden_ref, sem.at[2]),
-    ]
-    copies[2].start()
-    copies[0].start()
+    copies = []
+    for source, target in ((hidden_hbm, hidden_ref), (slope_hbm, slope_in)):
+        for bc in range(4):
+            copies.append(pltpu.make_async_copy(source.at[bc], target.at[bc], sem.at[len(copies)]))
+    for q in range(0, 17, 4):
+        part = pl.ds(q, min(4, 17 - q))
+        copies.append(pltpu.make_async_copy(emb_hbm.at[part], emb_in.at[part], sem.at[len(copies)]))
+    for copy in copies:
+        copy.start()
     for half in range(2):
         turn_b[half] = cgrad_ref[:, 128 * half : 128 * half + 128].astype(F32)
     for half in range(2):
@@ -255,10 +257,10 @@
                 turn_a[64 * x2 : 64 * x2 + 64, 128 * quad : 128 * quad + 128] = jnp.concatenate(
                     [p[:, 32 * k : 32 * k + 32] for p in pieces], axis=1
                 )
-    copies[1].start()
     cg_t = turn_a[...].astype(BF16)
     pairs = [cg_t[128 * pair : 128 * pair + 128, :] for pair in range(4)]
-    copies[2].wait()
+    for copy in copies[:4]:
+        copy.wait()
     down = None
     for pair in range(4):
         part = dot(pairs[pair], pair_rows(hidden_ref, pair), 1, 1)
@@ -267,7 +269,8 @@
     left = down[:, :128] + pltpu.roll(down[:, :128], 96, 1)
     right = down[:, 128:] + pltpu.roll(down[:, 128:], 32, 1)
     out_ref[0:64, :] = jnp.where(iota((64, 128), 1) // 32 % 2 == 0, left, right)
-    copies[0].wait()
+    for copy in copies[4:8]:
+        copy.wait()
     for pair in range(4):
         hgrad = dot(pair_t_ref[...], pairs[pair], 1, 0)
         at = slice(64 * pair, 64 * pair + 64)
@@ -277,7 +280,8 @@
             edge = slice(480 * (bc % 2), 480 * (bc % 2) + 32)
             low = 64 * (bc % 2) + 32 * (bc // 2)
             turned_pg[bc, at, edge] = (rows[:, edge] * edge_ref[at, low : low + 32]).astype(BF16)
-    copies[1].wait()
+    for copy in copies[8:]:
+        copy.wait()
     lane_x = iota((16, 128), 1) // 16
     own = iota((8, 128), 1) // 16 == iota((8, 128), 0)
     for ty in range(3):
@@ -533,7 +537,7 @@
             pltpu.VMEM((17, 2, 128, 256), BF16),
             pltpu.VMEM((4, 256, 512), F32),
             pltpu.VMEM((4, 256, 512), BF16),
-            pltpu.SemaphoreType.DMA((3,)),
+            pltpu.SemaphoreType.DMA((13,)),
         ],
         compiler_params=params(12),
         cost_estimate=cost(4 << 30, 8 << 20),

time: 96.5 us -> 96.5 us (level)
  no operation moved by 1% of the time
where the time goes in v10:
time: 96.5 us; the launch traced here: 96.1 us
  starting transfers between devices  41.8 us (43%)
  waiting for transfers between devices  31.3 us (32%)
  Pallas kernels  21.2 us (22%)
    ppermute x10, starting transfers between devices, exchanged(): lax.ppermute(value, ('sy', 'sz'), [(i, i ^ m) for i in range(count)])  13.9 us
    all_to_all x1, waiting for transfers between devices, per_device(): lax.all_to_all(coarse.reshape(count_z, mine * 16, 256), 'sz', split_axis=...  11.8 us
    all_to_all x1, starting transfers between devices, per_device(): lax.all_to_all(coarse.reshape(count_z, mine * 16, 256), 'sz', split_axis=...  11.5 us
    ppermute x10, waiting for transfers between devices, exchanged(): lax.ppermute(value, ('sy', 'sz'), [(i, i ^ m) for i in range(count)])  10.9 us
    pallas_call x1, Pallas kernels, per_device(): pl.pallas_call(lambda *refs: backward_kernel(1.0 / math.sqrt(cells // 8),...  5.98 us
    all_to_all x1, waiting for transfers between devices, per_device(): lax.all_to_all(back, 'sz', split_axis=0, concat_axis=0, tiled=True)  5.1 us
    ppermute x3, starting transfers between devices, per_device(): lax.ppermute(part, 'sy', [(i, i ^ 2 * k) for i in range(count_y)])  4.7 us
    pallas_call x1, Pallas kernels, per_device(): pl.pallas_call(inner_kernel, out_shape=(shape((17, 2, 128, 256), BF16), p...  4.12 us
  transfers between devices with their start and end apart: 20, of which 11 were waited for; matrix products, arithmetic and copies ran while one was open for 1% of the time, Pallas kernels for 15%

profile of v10, /device:TPU:0, one launch (start us, length us, event | category | flops | bytes accessed | tf_op | source)
XLA Modules:
  0.0 96.1 jit_solution(6531899835292036520)
XLA Ops:
  0.6 1.7 %features.1 = (bf16[32,128,80]{2,1,0:T(8,128)(2,1)S(1)}, bf16[32,80]{1,0:T(8,128)(2,1)S(1)}, bf16[32,80]{1,0:T(8,128)(2,1)S(1)}, bf16[16,16,27]{2,1,0:T(8,128)(2...) custom-call(s32[512,64]{1,0:T(8,128)} %bitcast.37, ...), custom_call_target="tpu_custom_call" | custom-call | flops 41943040 | bytes 2097152 | tf_op jit(solution)/shard_map/features/pallas_call | solution.py:369
  2.4 3.6 %collective-permute-start = (bf16[32,80]{1,0:T(8,128)(2,1)S(1)}, bf16[32,80]{1,0:T(8,128)(2,1)S(1)}, u32[]{:S(2)}, u32[]{:S(2)}) collective-permute-start(bf16[32,80]{1,0:T(8,128)(2,1)S(1)} %get-tuple-element.46), channel_id=1, source_target_pairs={{0,16},{16,32},{32,48},{48,64},{64,80},{80,96},{96,112},{1,17},{17... | collective-permute-start | bytes 15368 | tf_op jit(solution)/shard_map/ppermute | solution.py:405
  5.9 1.3 %collective-permute-start.1 = (bf16[32,80]{1,0:T(8,128)(2,1)S(1)}, bf16[32,80]{1,0:T(8,128)(2,1)S(1)}, u32[]{:S(2)}, u32[]{:S(2)}) collective-permute-start(bf16[32,80]{1,0:T(8,128)(2,1)S(1)} %get-tuple-element.47), channel_id=1, source_target_pairs={{16,0},{32,16},{48,32},{64,48},{80,64},{96,80},{112,96},{17,1},{33... | collective-permute-start | bytes 15368 | tf_op jit(solution)/shard_map/ppermute | solution.py:406
  7.3 1.4 %weights.1 = (bf16[9,256,256]{2,1,0:T(8,128)(2,1)S(1)}, bf16[128,256]{1,0:T(8,128)(2,1)S(1)}, bf16[256,128]{1,0:T(8,128)(2,1)S(1)}, bf16[80,256]{1,0:T(8,128)(2,1)S(1)}) custom-call(bf16[16,16,27]{2,1,0:T(8,128)(2,1)S(1)} %get-tuple-element.48.conv_ref, bf16[8,16,64]{2,1,0:T(8,128)(2,1)S(1)} %get-tuple-element.49.down_ref, ...), custom_call_target="tpu_custom_call" | custom-call | flops 56623104 | bytes 3145728 | tf_op jit(solution)/shard_map/weights/pallas_call | solution.py:407
  8.7 0.0 collective-permute-done.ylo_ref
  8.7 2.8 %collective-permute-done.1.yhi_ref = bf16[32,80]{1,0:T(8,128)(2,1)S(1)} collective-permute-done((bf16[32,80]{1,0:T(8,128)(2,1)S(1)}, bf16[32,80]{1,0:T(8,128)(2,1)S(1)}, u32[]{:S(2)}, u32[]{:S(2)}) %collective-permute-start.1) | collective-permute-done | bytes 5152 | tf_op jit(solution)/shard_map/ppermute | solution.py:406
  11.5 0.1 fusion
  11.6 1.3 %collective-permute-start.2 = (bf16[80,80]{1,0:T(8,128)(2,1)S(1)}, bf16[80,80]{1,0:T(8,128)(2,1)S(1)}, u32[]{:S(2)}, u32[]{:S(2)}) collective-permute-start(bf16[80,80]{1,0:T(8,128)(2,1)S(1)} %get-tuple-element.89), channel_id=1, source_target_pairs={{0,1},{1,2},{2,3},{3,4},{4,5},{5,6},{6,7},{7,8},{8,9},{9,10},{10,1... | collective-permute-start | bytes 38408 | tf_op jit(solution)/shard_map/ppermute | solution.py:430
  12.9 1.3 %collective-permute-start.3 = (bf16[80,80]{1,0:T(8,128)(2,1)S(1)}, bf16[80,80]{1,0:T(8,128)(2,1)S(1)}, u32[]{:S(2)}, u32[]{:S(2)}) collective-permute-start(bf16[80,80]{1,0:T(8,128)(2,1)S(1)} %get-tuple-element.88), channel_id=1, source_target_pairs={{1,0},{2,1},{3,2},{4,3},{5,4},{6,5},{7,6},{8,7},{9,8},{10,9},{11,1... | collective-permute-start | bytes 38408 | tf_op jit(solution)/shard_map/ppermute | solution.py:431
  14.2 4.1 %inner.1 = (bf16[17,2,128,256]{3,2,1,0:T(8,128)(2,1)S(1)}, f32[4,256,512]{2,1,0:T(8,128)}, bf16[4,256,512]{2,1,0:T(8,128)(2,1)S(1)}, f32[2,2,256,32]{3,2,1,0:T(8,128)S(1)}) custom-call(bf16[32,128,80]{2,1,0:T(8,128)(2,1)S(1)} %get-tuple-element.58.feat_ref, bf16[32,80]{1,0:T(8,128)(2,1)S(1)} %collective-permute-done.ylo_ref, ...), custom_call_target="tpu_custom_call" | custom-call | flops 3221225472 | bytes 10485760 | tf_op jit(solution)/shard_map/inner/pallas_call | solution.py:432
  18.3 0.0 copy-start.2
  18.3 0.0 collective-permute-done.2.zlo_ref
  18.3 0.8 collective-permute-done.3.zhi_ref
  19.1 0.0 copy-start
  19.1 0.0 copy-start.1
  19.1 2.7 %outer.1 = (bf16[2,128,256]{2,1,0:T(8,128)(2,1)S(1)}, f32[256,128]{1,0:T(8,128)S(1)}, bf16[4,256,512]{2,1,0:T(8,128)(2,1)}, bf16[1024,256]{1,0:T(8,128)(2,1)}) custom-call(bf16[80,80]{1,0:T(8,128)(2,1)S(1)} %collective-permute-done.2.zlo_ref, bf16[80,80]{1,0:T(8,128)(2,1)S(1)} %collective-permute-done.3.zhi_ref, ...), custom_call_target="tpu_custom_call" | custom-call | flops 1073741824 | bytes 4194304 | tf_op jit(solution)/shard_map/outer/pallas_call | solution.py:447
  21.8 0.0 copy-done.2
  21.8 11.5 %all-to-all-start = ((bf16[16,64,256]{2,1,0:T(8,128)(2,1)}), bf16[16,64,256]{2,1,0:T(8,128)(2,1)S(1)}, u32[]{:S(2)}, u32[]{:S(2)}) async-start(bf16[16,64,256]{2,1,0:T(8,128)(2,1)} %bitcast.36), calls=%async_computation | async-start | bytes 1048576 | tf_op jit(solution)/shard_map/all_to_all | solution.py:472
  33.4 0.0 copy-done
  33.4 0.0 copy-done.1
  33.4 0.5 turn.1
  33.9 11.8 %all-to-all-done.coarse_ref.refs_1_ = bf16[16,64,256]{2,1,0:T(8,128)(2,1)S(1)} async-done(((bf16[16,64,256]{2,1,0:T(8,128)(2,1)}), bf16[16,64,256]{2,1,0:T(8,128)(2,1)S(1)}, u32[]{:S(2)}, u32[]{:S(2)}) %all-to-all-start) | async-done | bytes 524320 | tf_op jit(solution)/shard_map/all_to_all | solution.py:472
  45.7 1.4 %mix.1 = bf16[16,64,256]{2,1,0:T(8,128)(2,1)} custom-call(bf16[16,64,256]{2,1,0:T(8,128)(2,1)S(1)} %all-to-all-done.coarse_ref.refs_1_, bf16[4,256,256]{2,1,0:T(8,128)(2,1)S(1)} %copy-done, bf16[4,256,256]{2,1,0:T(8,128)(2,1)S(1)} %get-tuple-element.68.cot_t_ref.refs_3_, bf16[4,256,256]{2,1,0:T(8,128)(2,1)S(1)} %get-tuple-element.69.mix_t_ref), custom_call_target="tpu_custom_call" | custom-call | flops 268435456 | bytes 2097152 | tf_op jit(solution)/shard_map/mix/pallas_call | solution.py:492
  47.1 3.6 %all-to-all-start.1 = ((bf16[16,64,256]{2,1,0:T(8,128)(2,1)}), bf16[16,64,256]{2,1,0:T(8,128)(2,1)S(1)}, u32[]{:S(2)}, u32[]{:S(2)}) async-start(bf16[16,64,256]{2,1,0:T(8,128)(2,1)} %mix.1), calls=%async_computation.1 | async-start | bytes 1048576 | tf_op jit(solution)/shard_map/all_to_all | solution.py:505
  50.7 2.5 %mix_grad.1 = (bf16[4,256,256]{2,1,0:T(8,128)(2,1)}, f32[4,64,256]{2,1,0:T(8,128)}, bf16[4,64,256]{2,1,0:T(8,128)(2,1)}, bf16[4,64,256]{2,1,0:T(8,128)(2,1)}, bf16[4,64,256]{2,1,0:T(8,128)(2,1)}) custom-call(s32[1]{0:T(128)} %bitcast.refs_0_, bf16[16,64,256]{2,1,0:T(8,128)(2,1)S(1)} %all-to-all-done.coarse_ref.refs_1_, bf16[4,256,256]{2,1,0:T(8,128)(2,1)S(1)} %copy-done, ...), custom_call_target="tpu_custom_call" | custom-call | flops 268435456 | bytes 3145728 | tf_op jit(solution)/shard_map/mix_grad/pallas_call | solution.py:507
  53.2 1.5 %collective-permute-start.4 = (bf16[4,64,256]{2,1,0:T(8,128)(2,1)}, bf16[4,64,256]{2,1,0:T(8,128)(2,1)S(1)}, u32[]{:S(2)}, u32[]{:S(2)}) collective-permute-start(bf16[4,64,256]{2,1,0:T(8,128)(2,1)} %get-tuple-element.73), channel_id=1, source_target_pairs={{0,32},{16,48},{32,0},{48,16},{64,96},{80,112},{96,64},{112,80},{1... | collective-permute-start | bytes 393224 | tf_op jit(solution)/shard_map/ppermute | solution.py:524
  54.7 2.7 %collective-permute-start.5 = (bf16[4,64,256]{2,1,0:T(8,128)(2,1)}, bf16[4,64,256]{2,1,0:T(8,128)(2,1)S(1)}, u32[]{:S(2)}, u32[]{:S(2)}) collective-permute-start(bf16[4,64,256]{2,1,0:T(8,128)(2,1)} %get-tuple-element.74), channel_id=1, source_target_pairs={{0,64},{16,80},{32,96},{48,112},{64,0},{80,16},{96,32},{112,48},{1... | collective-permute-start | bytes 393224 | tf_op jit(solution)/shard_map/ppermute | solution.py:524
  57.5 0.5 collective-permute-start.6
  57.9 5.1 %all-to-all-done.1 = bf16[16,64,256]{2,1,0:T(8,128)(2,1)S(1)} async-done(((bf16[16,64,256]{2,1,0:T(8,128)(2,1)}), bf16[16,64,256]{2,1,0:T(8,128)(2,1)S(1)}, u32[]{:S(2)}, u32[]{:S(2)}) %all-to-all-start.1) | async-done | bytes 524320 | tf_op jit(solution)/shard_map/all_to_all | solution.py:505
  63.0 0.0 copy-start.3
  63.0 6.0 %backward.1 = f32[128,128]{1,0:T(8,128)S(1)} custom-call(bf16[1024,256]{1,0:T(8,128)(2,1)S(1)} %bitcast.35, bf16[17,2,128,256]{3,2,1,0:T(8,128)(2,1)} %copy-done.2, f32[4,256,512]{2,1,0:T(8,128)} %get-tuple-element.77.refs_2_, bf16[4,256,512]{2,1,0:T(8,128)(2,1)} %get-tuple-element.78.refs_3_, bf16[128,256]{1,0:T(8,128)(2,1)S(1)} %get-tuple-element.61.pair_ref.refs_4_, ...), custom_call_target="tpu_custom_call" | custom-call | flops 4294967296 | bytes 8388608 | tf_op jit(solution)/shard_map/backward/pallas_call | solution.py:526
  69.0 0.0 collective-permute-done.4
  69.0 0.0 collective-permute-done.5
  69.0 0.0 collective-permute-done.6
  69.0 0.1 collective-permute-start.8
  69.1 1.2 %collective-permute-done.8 = f32[128,128]{1,0:T(8,128)S(1)} collective-permute-done((f32[128,128]{1,0:T(8,128)S(1)}, f32[128,128]{1,0:T(8,128)S(1)}, u32[]{:S(2)}, u32[]{:S(2)}) %collective-permute-start.8) | collective-permute-done | bytes 65568 | tf_op jit(solution)/shard_map/ppermute | solution.py:359
  70.4 2.1 %collective-permute-start.10 = (f32[128,128]{1,0:T(8,128)S(1)}, f32[128,128]{1,0:T(8,128)S(1)}, u32[]{:S(2)}, u32[]{:S(2)}) collective-permute-start(f32[128,128]{1,0:T(8,128)S(1)} %add.37), channel_id=1, source_target_pairs={{0,16},{1,17},{2,18},{3,19},{4,20},{5,21},{6,22},{7,23},{8,24},{9,... | collective-permute-start | bytes 196616 | tf_op jit(solution)/shard_map/ppermute | solution.py:359
  72.5 0.0 collective-permute-start.11
  72.5 2.2 %collective-permute-start.9 = (f32[128,128]{1,0:T(8,128)S(1)}, f32[128,128]{1,0:T(8,128)S(1)}, u32[]{:S(2)}, u32[]{:S(2)}) collective-permute-start(f32[128,128]{1,0:T(8,128)S(1)} %add.37), channel_id=1, source_target_pairs={{0,2},{1,3},{2,0},{3,1},{4,6},{5,7},{6,4},{7,5},{8,10},{9,11},{10,... | collective-permute-start | bytes 196616 | tf_op jit(solution)/shard_map/ppermute | solution.py:359
  74.6 0.3 collective-permute-done.10
  74.9 4.1 %collective-permute-done.11 = f32[128,128]{1,0:T(8,128)S(1)} collective-permute-done((f32[128,128]{1,0:T(8,128)S(1)}, f32[128,128]{1,0:T(8,128)S(1)}, u32[]{:S(2)}, u32[]{:S(2)}) %collective-permute-start.11) | collective-permute-done | bytes 65568 | tf_op jit(solution)/shard_map/ppermute | solution.py:359
  78.9 0.0 collective-permute-done.9
  79.0 0.1 collective-permute-start.12
  79.1 2.6 %collective-permute-start.13 = (f32[128,128]{1,0:T(8,128)S(1)}, f32[128,128]{1,0:T(8,128)S(1)}, u32[]{:S(2)}, u32[]{:S(2)}) collective-permute-start(f32[128,128]{1,0:T(8,128)S(1)} %add_add_fusion.1), channel_id=1, source_target_pairs={{0,8},{1,9},{2,10},{3,11},{4,12},{5,13},{6,14},{7,15},{8,0},{9,1},... | collective-permute-start | bytes 196616 | tf_op jit(solution)/shard_map/ppermute | solution.py:359
  81.7 2.1 %collective-permute-start.14 = (f32[128,128]{1,0:T(8,128)S(1)}, f32[128,128]{1,0:T(8,128)S(1)}, u32[]{:S(2)}, u32[]{:S(2)}) collective-permute-start(f32[128,128]{1,0:T(8,128)S(1)} %add_add_fusion.1), channel_id=1, source_target_pairs={{0,12},{1,13},{2,14},{3,15},{4,8},{5,9},{6,10},{7,11},{8,4},{9,5},... | collective-permute-start | bytes 196616 | tf_op jit(solution)/shard_map/ppermute | solution.py:359
  83.8 0.0 copy-done.3
  83.8 0.1 convert_add_fusion
  83.8 0.7 collective-permute-start.7
  84.5 0.0 collective-permute-done.12
  84.5 0.6 collective-permute-done.13
  85.2 2.0 %collective-permute-done.14 = f32[128,128]{1,0:T(8,128)S(1)} collective-permute-done((f32[128,128]{1,0:T(8,128)S(1)}, f32[128,128]{1,0:T(8,128)S(1)}, u32[]{:S(2)}, u32[]{:S(2)}) %collective-permute-start.14) | collective-permute-done | bytes 65568 | tf_op jit(solution)/shard_map/ppermute | solution.py:359
  87.2 1.2 %collective-permute-start.15 = (f32[128,128]{1,0:T(8,128)S(1)}, f32[128,128]{1,0:T(8,128)S(1)}, u32[]{:S(2)}, u32[]{:S(2)}) collective-permute-start(f32[128,128]{1,0:T(8,128)S(1)} %add_add_fusion.a_ref), channel_id=1, source_target_pairs={{0,32},{1,33},{2,34},{3,35},{4,36},{5,37},{6,38},{7,39},{8,40},{9,... | collective-permute-start | bytes 196616 | tf_op jit(solution)/shard_map/ppermute | solution.py:359
  88.4 1.4 %collective-permute-start.16 = (f32[128,128]{1,0:T(8,128)S(1)}, f32[128,128]{1,0:T(8,128)S(1)}, u32[]{:S(2)}, u32[]{:S(2)}) collective-permute-start(f32[128,128]{1,0:T(8,128)S(1)} %add_add_fusion.a_ref), channel_id=1, source_target_pairs={{0,64},{1,65},{2,66},{3,67},{4,68},{5,69},{6,70},{7,71},{8,72},{9,... | collective-permute-start | bytes 196616 | tf_op jit(solution)/shard_map/ppermute | solution.py:359
  89.8 2.2 %collective-permute-start.17 = (f32[128,128]{1,0:T(8,128)S(1)}, f32[128,128]{1,0:T(8,128)S(1)}, u32[]{:S(2)}, u32[]{:S(2)}) collective-permute-start(f32[128,128]{1,0:T(8,128)S(1)} %add_add_fusion.a_ref), channel_id=1, source_target_pairs={{0,96},{1,97},{2,98},{3,99},{4,100},{5,101},{6,102},{7,103},{8,104... | collective-permute-start | bytes 196616 | tf_op jit(solution)/shard_map/ppermute | solution.py:359
  92.0 0.0 collective-permute-done.7
  92.0 0.7 slice_add_fusion
  92.6 0.0 collective-permute-done.15.b_ref
  92.6 1.5 %collective-permute-done.16.c_ref = f32[128,128]{1,0:T(8,128)S(1)} collective-permute-done((f32[128,128]{1,0:T(8,128)S(1)}, f32[128,128]{1,0:T(8,128)S(1)}, u32[]{:S(2)}, u32[]{:S(2)}) %collective-permute-start.16) | collective-permute-done | bytes 65568 | tf_op jit(solution)/shard_map/ppermute | solution.py:359
  94.2 1.1 %collective-permute-done.17.d_ref = f32[128,128]{1,0:T(8,128)S(1)} collective-permute-done((f32[128,128]{1,0:T(8,128)S(1)}, f32[128,128]{1,0:T(8,128)S(1)}, u32[]{:S(2)}, u32[]{:S(2)}) %collective-permute-start.17) | collective-permute-done | bytes 65568 | tf_op jit(solution)/shard_map/ppermute | solution.py:359
  95.3 0.8 finish.1
  (6 shorter events, 0.1 us)
Async XLA Ops:
  2.4 6.3 %collective-permute-start = (bf16[32,80]{1,0:T(8,128)(2,1)S(1)}, bf16[32,80]{1,0:T(8,128)(2,1)S(1)}, u32[]{:S(2)}, u32[]{:S(2)}) collective-permute-start(bf16[32,80]{1,0:T(8,128)(2,1)S(1)} %get-tuple-element.46), channel_id=1, source_target_pairs={{0,16},{16,32},{32,48},{48,64},{64,80},{80,96},{96,112},{1,17},{17... | collective-permute-start | bytes 15368 | tf_op jit(solution)/shard_map/ppermute | solution.py:405
  5.9 5.5 %collective-permute-start.1 = (bf16[32,80]{1,0:T(8,128)(2,1)S(1)}, bf16[32,80]{1,0:T(8,128)(2,1)S(1)}, u32[]{:S(2)}, u32[]{:S(2)}) collective-permute-start(bf16[32,80]{1,0:T(8,128)(2,1)S(1)} %get-tuple-element.47), channel_id=1, source_target_pairs={{16,0},{32,16},{48,32},{64,48},{80,64},{96,80},{112,96},{17,1},{33... | collective-permute-start | bytes 15368 | tf_op jit(solution)/shard_map/ppermute | solution.py:406
  11.6 6.7 %collective-permute-start.2 = (bf16[80,80]{1,0:T(8,128)(2,1)S(1)}, bf16[80,80]{1,0:T(8,128)(2,1)S(1)}, u32[]{:S(2)}, u32[]{:S(2)}) collective-permute-start(bf16[80,80]{1,0:T(8,128)(2,1)S(1)} %get-tuple-element.89), channel_id=1, source_target_pairs={{0,1},{1,2},{2,3},{3,4},{4,5},{5,6},{6,7},{7,8},{8,9},{9,10},{10,1... | collective-permute-start | bytes 38408 | tf_op jit(solution)/shard_map/ppermute | solution.py:430
  12.9 6.2 %collective-permute-start.3 = (bf16[80,80]{1,0:T(8,128)(2,1)S(1)}, bf16[80,80]{1,0:T(8,128)(2,1)S(1)}, u32[]{:S(2)}, u32[]{:S(2)}) collective-permute-start(bf16[80,80]{1,0:T(8,128)(2,1)S(1)} %get-tuple-element.88), channel_id=1, source_target_pairs={{1,0},{2,1},{3,2},{4,3},{5,4},{6,5},{7,6},{8,7},{9,8},{10,9},{11,1... | collective-permute-start | bytes 38408 | tf_op jit(solution)/shard_map/ppermute | solution.py:431
  18.3 3.5 %copy-start.2 = (bf16[17,2,128,256]{3,2,1,0:T(8,128)(2,1)}, bf16[17,2,128,256]{3,2,1,0:T(8,128)(2,1)S(1)}, u32[]{:S(2)}) copy-start(bf16[17,2,128,256]{3,2,1,0:T(8,128)(2,1)S(1)} %get-tuple-element.76.refs_1_) | copy-start | bytes 6684676
  19.1 14.2 %copy-start = (bf16[4,256,256]{2,1,0:T(8,128)(2,1)S(1)}, bf16[4,256,256]{2,1,0:T(8,128)(2,1)}, u32[]{:S(2)}) copy-start(bf16[4,256,256]{2,1,0:T(8,128)(2,1)} %refs_2_) | copy-start | bytes 1572868
  19.1 14.3 %copy-start.1 = (bf16[4,8,32,256]{3,2,1,0:T(8,128)(2,1)S(1)}, bf16[4,8,32,256]{3,2,1,0:T(8,128)(2,1)}, u32[]{:S(2)}) copy-start(bf16[4,8,32,256]{3,2,1,0:T(8,128)(2,1)} %param.15) | copy-start | bytes 1572868
  21.8 23.9 %all-to-all-start = ((bf16[16,64,256]{2,1,0:T(8,128)(2,1)}), bf16[16,64,256]{2,1,0:T(8,128)(2,1)S(1)}, u32[]{:S(2)}, u32[]{:S(2)}) async-start(bf16[16,64,256]{2,1,0:T(8,128)(2,1)} %bitcast.36), calls=%async_computation | async-start | bytes 1048576 | tf_op jit(solution)/shard_map/all_to_all | solution.py:472
  47.1 15.9 %all-to-all-start.1 = ((bf16[16,64,256]{2,1,0:T(8,128)(2,1)}), bf16[16,64,256]{2,1,0:T(8,128)(2,1)S(1)}, u32[]{:S(2)}, u32[]{:S(2)}) async-start(bf16[16,64,256]{2,1,0:T(8,128)(2,1)} %mix.1), calls=%async_computation.1 | async-start | bytes 1048576 | tf_op jit(solution)/shard_map/all_to_all | solution.py:505
  53.2 15.8 %collective-permute-start.4 = (bf16[4,64,256]{2,1,0:T(8,128)(2,1)}, bf16[4,64,256]{2,1,0:T(8,128)(2,1)S(1)}, u32[]{:S(2)}, u32[]{:S(2)}) collective-permute-start(bf16[4,64,256]{2,1,0:T(8,128)(2,1)} %get-tuple-element.73), channel_id=1, source_target_pairs={{0,32},{16,48},{32,0},{48,16},{64,96},{80,112},{96,64},{112,80},{1... | collective-permute-start | bytes 393224 | tf_op jit(solution)/shard_map/ppermute | solution.py:524
  54.7 14.3 %collective-permute-start.5 = (bf16[4,64,256]{2,1,0:T(8,128)(2,1)}, bf16[4,64,256]{2,1,0:T(8,128)(2,1)S(1)}, u32[]{:S(2)}, u32[]{:S(2)}) collective-permute-start(bf16[4,64,256]{2,1,0:T(8,128)(2,1)} %get-tuple-element.74), channel_id=1, source_target_pairs={{0,64},{16,80},{32,96},{48,112},{64,0},{80,16},{96,32},{112,48},{1... | collective-permute-start | bytes 393224 | tf_op jit(solution)/shard_map/ppermute | solution.py:524
  57.5 11.6 %collective-permute-start.6 = (bf16[4,64,256]{2,1,0:T(8,128)(2,1)}, bf16[4,64,256]{2,1,0:T(8,128)(2,1)S(1)}, u32[]{:S(2)}, u32[]{:S(2)}) collective-permute-start(bf16[4,64,256]{2,1,0:T(8,128)(2,1)} %get-tuple-element.75), channel_id=1, source_target_pairs={{0,96},{16,112},{32,64},{48,80},{64,32},{80,48},{96,0},{112,16},{1... | collective-permute-start | bytes 393224 | tf_op jit(solution)/shard_map/ppermute | solution.py:524
  63.0 20.7 %copy-start.3 = (f32[4,64,256]{2,1,0:T(8,128)S(1)}, f32[4,64,256]{2,1,0:T(8,128)}, u32[]{:S(2)}) copy-start(f32[4,64,256]{2,1,0:T(8,128)} %get-tuple-element.72) | copy-start | bytes 786436
  69.0 1.3 %collective-permute-start.8 = (f32[128,128]{1,0:T(8,128)S(1)}, f32[128,128]{1,0:T(8,128)S(1)}, u32[]{:S(2)}, u32[]{:S(2)}) collective-permute-start(f32[128,128]{1,0:T(8,128)S(1)} %backward.1), channel_id=1, source_target_pairs={{0,1},{1,0},{2,3},{3,2},{4,5},{5,4},{6,7},{7,6},{8,9},{9,8},{10,11... | collective-permute-start | bytes 196616 | tf_op jit(solution)/shard_map/ppermute | solution.py:359
  70.4 4.5 %collective-permute-start.10 = (f32[128,128]{1,0:T(8,128)S(1)}, f32[128,128]{1,0:T(8,128)S(1)}, u32[]{:S(2)}, u32[]{:S(2)}) collective-permute-start(f32[128,128]{1,0:T(8,128)S(1)} %add.37), channel_id=1, source_target_pairs={{0,16},{1,17},{2,18},{3,19},{4,20},{5,21},{6,22},{7,23},{8,24},{9,... | collective-permute-start | bytes 196616 | tf_op jit(solution)/shard_map/ppermute | solution.py:359
  72.5 6.5 %collective-permute-start.11 = (f32[128,128]{1,0:T(8,128)S(1)}, f32[128,128]{1,0:T(8,128)S(1)}, u32[]{:S(2)}, u32[]{:S(2)}) collective-permute-start(f32[128,128]{1,0:T(8,128)S(1)} %add.37), channel_id=1, source_target_pairs={{0,18},{1,19},{2,16},{3,17},{4,22},{5,23},{6,20},{7,21},{8,26},{9,... | collective-permute-start | bytes 196616 | tf_op jit(solution)/shard_map/ppermute | solution.py:359
  72.5 6.5 %collective-permute-start.9 = (f32[128,128]{1,0:T(8,128)S(1)}, f32[128,128]{1,0:T(8,128)S(1)}, u32[]{:S(2)}, u32[]{:S(2)}) collective-permute-start(f32[128,128]{1,0:T(8,128)S(1)} %add.37), channel_id=1, source_target_pairs={{0,2},{1,3},{2,0},{3,1},{4,6},{5,7},{6,4},{7,5},{8,10},{9,11},{10,... | collective-permute-start | bytes 196616 | tf_op jit(solution)/shard_map/ppermute | solution.py:359
  79.0 5.5 %collective-permute-start.12 = (f32[128,128]{1,0:T(8,128)S(1)}, f32[128,128]{1,0:T(8,128)S(1)}, u32[]{:S(2)}, u32[]{:S(2)}) collective-permute-start(f32[128,128]{1,0:T(8,128)S(1)} %add_add_fusion.1), channel_id=1, source_target_pairs={{0,4},{1,5},{2,6},{3,7},{4,0},{5,1},{6,2},{7,3},{8,12},{9,13},{10,... | collective-permute-start | bytes 196616 | tf_op jit(solution)/shard_map/ppermute | solution.py:359
  79.1 6.1 %collective-permute-start.13 = (f32[128,128]{1,0:T(8,128)S(1)}, f32[128,128]{1,0:T(8,128)S(1)}, u32[]{:S(2)}, u32[]{:S(2)}) collective-permute-start(f32[128,128]{1,0:T(8,128)S(1)} %add_add_fusion.1), channel_id=1, source_target_pairs={{0,8},{1,9},{2,10},{3,11},{4,12},{5,13},{6,14},{7,15},{8,0},{9,1},... | collective-permute-start | bytes 196616 | tf_op jit(solution)/shard_map/ppermute | solution.py:359
  81.7 5.5 %collective-permute-start.14 = (f32[128,128]{1,0:T(8,128)S(1)}, f32[128,128]{1,0:T(8,128)S(1)}, u32[]{:S(2)}, u32[]{:S(2)}) collective-permute-start(f32[128,128]{1,0:T(8,128)S(1)} %add_add_fusion.1), channel_id=1, source_target_pairs={{0,12},{1,13},{2,14},{3,15},{4,8},{5,9},{6,10},{7,11},{8,4},{9,5},... | collective-permute-start | bytes 196616 | tf_op jit(solution)/shard_map/ppermute | solution.py:359
  83.8 8.1 %collective-permute-start.7 = (bf16[4,32,256]{2,1,0:T(8,128)(2,1)S(1)}, bf16[4,32,256]{2,1,0:T(8,128)(2,1)S(1)}, u32[]{:S(2)}, u32[]{:S(2)}) collective-permute-start(bf16[4,32,256]{2,1,0:T(8,128)(2,1)S(1)} %split.13), channel_id=1, source_target_pairs={{0,16},{16,0},{32,48},{48,32},{64,80},{80,64},{96,112},{112,96},{1... | collective-permute-start | bytes 196616 | tf_op jit(solution)/shard_map/ppermute | solution.py:557
  87.2 5.5 %collective-permute-start.15 = (f32[128,128]{1,0:T(8,128)S(1)}, f32[128,128]{1,0:T(8,128)S(1)}, u32[]{:S(2)}, u32[]{:S(2)}) collective-permute-start(f32[128,128]{1,0:T(8,128)S(1)} %add_add_fusion.a_ref), channel_id=1, source_target_pairs={{0,32},{1,33},{2,34},{3,35},{4,36},{5,37},{6,38},{7,39},{8,40},{9,... | collective-permute-start | bytes 196616 | tf_op jit(solution)/shard_map/ppermute | solution.py:359
  88.4 5.8 %collective-permute-start.16 = (f32[128,128]{1,0:T(8,128)S(1)}, f32[128,128]{1,0:T(8,128)S(1)}, u32[]{:S(2)}, u32[]{:S(2)}) collective-permute-start(f32[128,128]{1,0:T(8,128)S(1)} %add_add_fusion.a_ref), channel_id=1, source_target_pairs={{0,64},{1,65},{2,66},{3,67},{4,68},{5,69},{6,70},{7,71},{8,72},{9,... | collective-permute-start | bytes 196616 | tf_op jit(solution)/shard_map/ppermute | solution.py:359
  89.8 5.5 %collective-permute-start.17 = (f32[128,128]{1,0:T(8,128)S(1)}, f32[128,128]{1,0:T(8,128)S(1)}, u32[]{:S(2)}, u32[]{:S(2)}) collective-permute-start(f32[128,128]{1,0:T(8,128)S(1)} %add_add_fusion.a_ref), channel_id=1, source_target_pairs={{0,96},{1,97},{2,98},{3,99},{4,100},{5,101},{6,102},{7,103},{8,104... | collective-permute-start | bytes 196616 | tf_op jit(solution)/shard_map/ppermute | solution.py:359

commit v11 on v9

--- a/solution.py
+++ b/solution.py
@@ -273,27 +273,27 @@
         at = slice(64 * pair, 64 * pair + 64)
         for bc in range(4):
             rows = hgrad[64 * bc : 64 * bc + 64]
-            turned_pg[bc, at, :] = (rows * slope_in[bc, at, :]).astype(BF16)
-            edge = slice(480 * (bc % 2), 480 * (bc % 2) + 32)
+            turned_pg[at, 512 * bc : 512 * bc + 512] = (rows * slope_in[bc, at, :]).astype(BF16)
+            first = 480 * (bc % 2)
             low = 64 * (bc % 2) + 32 * (bc // 2)
-            turned_pg[bc, at, edge] = (rows[:, edge] * edge_ref[at, low : low + 32]).astype(BF16)
+            turned_pg[at, 512 * bc + first : 512 * bc + first + 32] = (rows[:, first : first + 32] * edge_ref[at, low : low + 32]).astype(BF16)
     copies[1].wait()
     lane_x = iota((16, 128), 1) // 16
     own = iota((8, 128), 1) // 16 == iota((8, 128), 0)
     for ty in range(3):
         for tz in range(3):
-            acc = None
+            pieces = []
             for bc in range(4):
                 b, c = bc // 2, bc % 2
+                run = RUNS[b][ty]
                 for half in range(2):
                     rows = cells_of(emb_in, b, c, ty, tz, half)
-                    run = RUNS[b][ty]
                     if c + tz == 0 and half == 0:
                         rows = jnp.concatenate([face_ref[0, run : run + 32, :], rows[32:]], axis=0)
                     if c + tz == 3 and half == 1:
                         rows = jnp.concatenate([rows[:224], face_ref[1, run : run + 32, :]], axis=0)
-                    part = dot(turned_pg[bc, :, 256 * half : 256 * half + 256], rows, 1, 0)
-                    acc = part if acc is None else acc + part
+                    pieces.append(rows)
+            acc = dot(turned_pg[...], jnp.concatenate(pieces, axis=0), 1, 0)
             for tx in range(3):
                 total = None
                 for side in range(2):
@@ -529,7 +529,7 @@
         scratch_shapes=[
             pltpu.VMEM((512, 512), F32),
             pltpu.VMEM((2, 1024, 128), F32),
-            pltpu.VMEM((4, 256, 512), BF16),
+            pltpu.VMEM((256, 2048), BF16),
             pltpu.VMEM((17, 2, 128, 256), BF16),
             pltpu.VMEM((4, 256, 512), F32),
             pltpu.VMEM((4, 256, 512), BF16),

time: 96.5 us -> 96.5 us (level)
  no operation moved by 1% of the time
where the time goes in v11:
time: 96.5 us; the launch traced here: 96.1 us
  starting transfers between devices  41.8 us (43%)
  waiting for transfers between devices  31.3 us (32%)
  Pallas kernels  21.2 us (22%)
    ppermute x10, starting transfers between devices, exchanged(): lax.ppermute(value, ('sy', 'sz'), [(i, i ^ m) for i in range(count)])  13.9 us
    all_to_all x1, waiting for transfers between devices, per_device(): lax.all_to_all(coarse.reshape(count_z, mine * 16, 256), 'sz', split_axis=...  11.8 us
    all_to_all x1, starting transfers between devices, per_device(): lax.all_to_all(coarse.reshape(count_z, mine * 16, 256), 'sz', split_axis=...  11.5 us
    ppermute x10, waiting for transfers between devices, exchanged(): lax.ppermute(value, ('sy', 'sz'), [(i, i ^ m) for i in range(count)])  10.9 us
    pallas_call x1, Pallas kernels, per_device(): pl.pallas_call(lambda *refs: backward_kernel(1.0 / math.sqrt(cells // 8),...  6 us
    all_to_all x1, waiting for transfers between devices, per_device(): lax.all_to_all(back, 'sz', split_axis=0, concat_axis=0, tiled=True)  5.1 us
    ppermute x3, starting transfers between devices, per_device(): lax.ppermute(part, 'sy', [(i, i ^ 2 * k) for i in range(count_y)])  4.7 us
    pallas_call x1, Pallas kernels, per_device(): pl.pallas_call(inner_kernel, out_shape=(shape((17, 2, 128, 256), BF16), p...  4.12 us
  transfers between devices with their start and end apart: 20, of which 11 were waited for; matrix products, arithmetic and copies ran while one was open for 1% of the time, Pallas kernels for 15%

profile of v11, /device:TPU:0, one launch (start us, length us, event | category | flops | bytes accessed | tf_op | source)
XLA Modules:
  0.0 96.1 jit_solution(682456785017794613)
XLA Ops:
  0.6 1.7 %features.1 = (bf16[32,128,80]{2,1,0:T(8,128)(2,1)S(1)}, bf16[32,80]{1,0:T(8,128)(2,1)S(1)}, bf16[32,80]{1,0:T(8,128)(2,1)S(1)}, bf16[16,16,27]{2,1,0:T(8,128)(2...) custom-call(s32[512,64]{1,0:T(8,128)} %bitcast.37, ...), custom_call_target="tpu_custom_call" | custom-call | flops 41943040 | bytes 2097152 | tf_op jit(solution)/shard_map/features/pallas_call | solution.py:365
  2.4 3.6 %collective-permute-start = (bf16[32,80]{1,0:T(8,128)(2,1)S(1)}, bf16[32,80]{1,0:T(8,128)(2,1)S(1)}, u32[]{:S(2)}, u32[]{:S(2)}) collective-permute-start(bf16[32,80]{1,0:T(8,128)(2,1)S(1)} %get-tuple-element.46), channel_id=1, source_target_pairs={{0,16},{16,32},{32,48},{48,64},{64,80},{80,96},{96,112},{1,17},{17... | collective-permute-start | bytes 15368 | tf_op jit(solution)/shard_map/ppermute | solution.py:401
  5.9 1.3 %collective-permute-start.1 = (bf16[32,80]{1,0:T(8,128)(2,1)S(1)}, bf16[32,80]{1,0:T(8,128)(2,1)S(1)}, u32[]{:S(2)}, u32[]{:S(2)}) collective-permute-start(bf16[32,80]{1,0:T(8,128)(2,1)S(1)} %get-tuple-element.47), channel_id=1, source_target_pairs={{16,0},{32,16},{48,32},{64,48},{80,64},{96,80},{112,96},{17,1},{33... | collective-permute-start | bytes 15368 | tf_op jit(solution)/shard_map/ppermute | solution.py:402
  7.3 1.4 %weights.1 = (bf16[9,256,256]{2,1,0:T(8,128)(2,1)S(1)}, bf16[128,256]{1,0:T(8,128)(2,1)S(1)}, bf16[256,128]{1,0:T(8,128)(2,1)S(1)}, bf16[80,256]{1,0:T(8,128)(2,1)S(1)}) custom-call(bf16[16,16,27]{2,1,0:T(8,128)(2,1)S(1)} %get-tuple-element.48.conv_ref, bf16[8,16,64]{2,1,0:T(8,128)(2,1)S(1)} %get-tuple-element.49.down_ref, ...), custom_call_target="tpu_custom_call" | custom-call | flops 56623104 | bytes 3145728 | tf_op jit(solution)/shard_map/weights/pallas_call | solution.py:403
  8.7 0.0 collective-permute-done.ylo_ref
  8.7 2.8 %collective-permute-done.1.yhi_ref = bf16[32,80]{1,0:T(8,128)(2,1)S(1)} collective-permute-done((bf16[32,80]{1,0:T(8,128)(2,1)S(1)}, bf16[32,80]{1,0:T(8,128)(2,1)S(1)}, u32[]{:S(2)}, u32[]{:S(2)}) %collective-permute-start.1) | collective-permute-done | bytes 5152 | tf_op jit(solution)/shard_map/ppermute | solution.py:402
  11.5 0.1 fusion
  11.6 1.3 %collective-permute-start.2 = (bf16[80,80]{1,0:T(8,128)(2,1)S(1)}, bf16[80,80]{1,0:T(8,128)(2,1)S(1)}, u32[]{:S(2)}, u32[]{:S(2)}) collective-permute-start(bf16[80,80]{1,0:T(8,128)(2,1)S(1)} %get-tuple-element.89), channel_id=1, source_target_pairs={{0,1},{1,2},{2,3},{3,4},{4,5},{5,6},{6,7},{7,8},{8,9},{9,10},{10,1... | collective-permute-start | bytes 38408 | tf_op jit(solution)/shard_map/ppermute | solution.py:426
  12.9 1.3 %collective-permute-start.3 = (bf16[80,80]{1,0:T(8,128)(2,1)S(1)}, bf16[80,80]{1,0:T(8,128)(2,1)S(1)}, u32[]{:S(2)}, u32[]{:S(2)}) collective-permute-start(bf16[80,80]{1,0:T(8,128)(2,1)S(1)} %get-tuple-element.88), channel_id=1, source_target_pairs={{1,0},{2,1},{3,2},{4,3},{5,4},{6,5},{7,6},{8,7},{9,8},{10,9},{11,1... | collective-permute-start | bytes 38408 | tf_op jit(solution)/shard_map/ppermute | solution.py:427
  14.2 4.1 %inner.1 = (bf16[17,2,128,256]{3,2,1,0:T(8,128)(2,1)S(1)}, f32[4,256,512]{2,1,0:T(8,128)}, bf16[4,256,512]{2,1,0:T(8,128)(2,1)S(1)}, f32[2,2,256,32]{3,2,1,0:T(8,128)S(1)}) custom-call(bf16[32,128,80]{2,1,0:T(8,128)(2,1)S(1)} %get-tuple-element.58.feat_ref, bf16[32,80]{1,0:T(8,128)(2,1)S(1)} %collective-permute-done.ylo_ref, ...), custom_call_target="tpu_custom_call" | custom-call | flops 3221225472 | bytes 10485760 | tf_op jit(solution)/shard_map/inner/pallas_call | solution.py:428
  18.3 0.0 copy-start.2
  18.3 0.0 collective-permute-done.2.zlo_ref
  18.3 0.8 collective-permute-done.3.zhi_ref
  19.1 0.0 copy-start
  19.1 0.0 copy-start.1
  19.1 2.7 %outer.1 = (bf16[2,128,256]{2,1,0:T(8,128)(2,1)S(1)}, f32[256,128]{1,0:T(8,128)S(1)}, bf16[4,256,512]{2,1,0:T(8,128)(2,1)}, bf16[1024,256]{1,0:T(8,128)(2,1)}) custom-call(bf16[80,80]{1,0:T(8,128)(2,1)S(1)} %collective-permute-done.2.zlo_ref, bf16[80,80]{1,0:T(8,128)(2,1)S(1)} %collective-permute-done.3.zhi_ref, ...), custom_call_target="tpu_custom_call" | custom-call | flops 1073741824 | bytes 4194304 | tf_op jit(solution)/shard_map/outer/pallas_call | solution.py:443
  21.8 0.0 copy-done.2
  21.8 11.5 %all-to-all-start = ((bf16[16,64,256]{2,1,0:T(8,128)(2,1)}), bf16[16,64,256]{2,1,0:T(8,128)(2,1)S(1)}, u32[]{:S(2)}, u32[]{:S(2)}) async-start(bf16[16,64,256]{2,1,0:T(8,128)(2,1)} %bitcast.36), calls=%async_computation | async-start | bytes 1048576 | tf_op jit(solution)/shard_map/all_to_all | solution.py:468
  33.4 0.0 copy-done
  33.4 0.0 copy-done.1
  33.4 0.5 turn.1
  33.9 11.8 %all-to-all-done.coarse_ref.refs_1_ = bf16[16,64,256]{2,1,0:T(8,128)(2,1)S(1)} async-done(((bf16[16,64,256]{2,1,0:T(8,128)(2,1)}), bf16[16,64,256]{2,1,0:T(8,128)(2,1)S(1)}, u32[]{:S(2)}, u32[]{:S(2)}) %all-to-all-start) | async-done | bytes 524320 | tf_op jit(solution)/shard_map/all_to_all | solution.py:468
  45.7 1.4 %mix.1 = bf16[16,64,256]{2,1,0:T(8,128)(2,1)} custom-call(bf16[16,64,256]{2,1,0:T(8,128)(2,1)S(1)} %all-to-all-done.coarse_ref.refs_1_, bf16[4,256,256]{2,1,0:T(8,128)(2,1)S(1)} %copy-done, bf16[4,256,256]{2,1,0:T(8,128)(2,1)S(1)} %get-tuple-element.68.cot_t_ref.refs_3_, bf16[4,256,256]{2,1,0:T(8,128)(2,1)S(1)} %get-tuple-element.69.mix_t_ref), custom_call_target="tpu_custom_call" | custom-call | flops 268435456 | bytes 2097152 | tf_op jit(solution)/shard_map/mix/pallas_call | solution.py:488
  47.1 3.6 %all-to-all-start.1 = ((bf16[16,64,256]{2,1,0:T(8,128)(2,1)}), bf16[16,64,256]{2,1,0:T(8,128)(2,1)S(1)}, u32[]{:S(2)}, u32[]{:S(2)}) async-start(bf16[16,64,256]{2,1,0:T(8,128)(2,1)} %mix.1), calls=%async_computation.1 | async-start | bytes 1048576 | tf_op jit(solution)/shard_map/all_to_all | solution.py:501
  50.7 2.5 %mix_grad.1 = (bf16[4,256,256]{2,1,0:T(8,128)(2,1)}, f32[4,64,256]{2,1,0:T(8,128)}, bf16[4,64,256]{2,1,0:T(8,128)(2,1)}, bf16[4,64,256]{2,1,0:T(8,128)(2,1)}, bf16[4,64,256]{2,1,0:T(8,128)(2,1)}) custom-call(s32[1]{0:T(128)} %bitcast.refs_0_, bf16[16,64,256]{2,1,0:T(8,128)(2,1)S(1)} %all-to-all-done.coarse_ref.refs_1_, bf16[4,256,256]{2,1,0:T(8,128)(2,1)S(1)} %copy-done, ...), custom_call_target="tpu_custom_call" | custom-call | flops 268435456 | bytes 3145728 | tf_op jit(solution)/shard_map/mix_grad/pallas_call | solution.py:503
  53.2 1.5 %collective-permute-start.4 = (bf16[4,64,256]{2,1,0:T(8,128)(2,1)}, bf16[4,64,256]{2,1,0:T(8,128)(2,1)S(1)}, u32[]{:S(2)}, u32[]{:S(2)}) collective-permute-start(bf16[4,64,256]{2,1,0:T(8,128)(2,1)} %get-tuple-element.73), channel_id=1, source_target_pairs={{0,32},{16,48},{32,0},{48,16},{64,96},{80,112},{96,64},{112,80},{1... | collective-permute-start | bytes 393224 | tf_op jit(solution)/shard_map/ppermute | solution.py:520
  54.7 2.7 %collective-permute-start.5 = (bf16[4,64,256]{2,1,0:T(8,128)(2,1)}, bf16[4,64,256]{2,1,0:T(8,128)(2,1)S(1)}, u32[]{:S(2)}, u32[]{:S(2)}) collective-permute-start(bf16[4,64,256]{2,1,0:T(8,128)(2,1)} %get-tuple-element.74), channel_id=1, source_target_pairs={{0,64},{16,80},{32,96},{48,112},{64,0},{80,16},{96,32},{112,48},{1... | collective-permute-start | bytes 393224 | tf_op jit(solution)/shard_map/ppermute | solution.py:520
  57.5 0.5 collective-permute-start.6
  57.9 5.1 %all-to-all-done.1 = bf16[16,64,256]{2,1,0:T(8,128)(2,1)S(1)} async-done(((bf16[16,64,256]{2,1,0:T(8,128)(2,1)}), bf16[16,64,256]{2,1,0:T(8,128)(2,1)S(1)}, u32[]{:S(2)}, u32[]{:S(2)}) %all-to-all-start.1) | async-done | bytes 524320 | tf_op jit(solution)/shard_map/all_to_all | solution.py:501
  63.0 0.0 copy-start.3
  63.0 6.0 %backward.1 = f32[128,128]{1,0:T(8,128)S(1)} custom-call(bf16[1024,256]{1,0:T(8,128)(2,1)S(1)} %bitcast.35, bf16[17,2,128,256]{3,2,1,0:T(8,128)(2,1)} %copy-done.2, f32[4,256,512]{2,1,0:T(8,128)} %get-tuple-element.77.refs_2_, bf16[4,256,512]{2,1,0:T(8,128)(2,1)} %get-tuple-element.78.refs_3_, bf16[128,256]{1,0:T(8,128)(2,1)S(1)} %get-tuple-element.61.pair_ref.refs_4_, ...), custom_call_target="tpu_custom_call" | custom-call | flops 4294967296 | bytes 8388608 | tf_op jit(solution)/shard_map/backward/pallas_call | solution.py:522
  69.0 0.0 collective-permute-done.4
  69.0 0.0 collective-permute-done.5
  69.1 0.0 collective-permute-done.6
  69.1 0.1 collective-permute-start.8
  69.2 1.2 %collective-permute-done.8 = f32[128,128]{1,0:T(8,128)S(1)} collective-permute-done((f32[128,128]{1,0:T(8,128)S(1)}, f32[128,128]{1,0:T(8,128)S(1)}, u32[]{:S(2)}, u32[]{:S(2)}) %collective-permute-start.8) | collective-permute-done | bytes 65568 | tf_op jit(solution)/shard_map/ppermute | solution.py:355
  70.4 2.1 %collective-permute-start.10 = (f32[128,128]{1,0:T(8,128)S(1)}, f32[128,128]{1,0:T(8,128)S(1)}, u32[]{:S(2)}, u32[]{:S(2)}) collective-permute-start(f32[128,128]{1,0:T(8,128)S(1)} %add.37), channel_id=1, source_target_pairs={{0,16},{1,17},{2,18},{3,19},{4,20},{5,21},{6,22},{7,23},{8,24},{9,... | collective-permute-start | bytes 196616 | tf_op jit(solution)/shard_map/ppermute | solution.py:355
  72.5 0.0 collective-permute-start.11
  72.5 2.2 %collective-permute-start.9 = (f32[128,128]{1,0:T(8,128)S(1)}, f32[128,128]{1,0:T(8,128)S(1)}, u32[]{:S(2)}, u32[]{:S(2)}) collective-permute-start(f32[128,128]{1,0:T(8,128)S(1)} %add.37), channel_id=1, source_target_pairs={{0,2},{1,3},{2,0},{3,1},{4,6},{5,7},{6,4},{7,5},{8,10},{9,11},{10,... | collective-permute-start | bytes 196616 | tf_op jit(solution)/shard_map/ppermute | solution.py:355
  74.6 0.3 collective-permute-done.10
  74.9 4.1 %collective-permute-done.11 = f32[128,128]{1,0:T(8,128)S(1)} collective-permute-done((f32[128,128]{1,0:T(8,128)S(1)}, f32[128,128]{1,0:T(8,128)S(1)}, u32[]{:S(2)}, u32[]{:S(2)}) %collective-permute-start.11) | collective-permute-done | bytes 65568 | tf_op jit(solution)/shard_map/ppermute | solution.py:355
  79.0 0.0 collective-permute-done.9
  79.0 0.1 collective-permute-start.12
  79.1 2.6 %collective-permute-start.13 = (f32[128,128]{1,0:T(8,128)S(1)}, f32[128,128]{1,0:T(8,128)S(1)}, u32[]{:S(2)}, u32[]{:S(2)}) collective-permute-start(f32[128,128]{1,0:T(8,128)S(1)} %add_add_fusion.1), channel_id=1, source_target_pairs={{0,8},{1,9},{2,10},{3,11},{4,12},{5,13},{6,14},{7,15},{8,0},{9,1},... | collective-permute-start | bytes 196616 | tf_op jit(solution)/shard_map/ppermute | solution.py:355
  81.7 2.1 %collective-permute-start.14 = (f32[128,128]{1,0:T(8,128)S(1)}, f32[128,128]{1,0:T(8,128)S(1)}, u32[]{:S(2)}, u32[]{:S(2)}) collective-permute-start(f32[128,128]{1,0:T(8,128)S(1)} %add_add_fusion.1), channel_id=1, source_target_pairs={{0,12},{1,13},{2,14},{3,15},{4,8},{5,9},{6,10},{7,11},{8,4},{9,5},... | collective-permute-start | bytes 196616 | tf_op jit(solution)/shard_map/ppermute | solution.py:355
  83.8 0.0 copy-done.3
  83.8 0.1 convert_add_fusion
  83.9 0.7 collective-permute-start.7
  84.5 0.0 collective-permute-done.12
  84.5 0.6 collective-permute-done.13
  85.2 2.0 %collective-permute-done.14 = f32[128,128]{1,0:T(8,128)S(1)} collective-permute-done((f32[128,128]{1,0:T(8,128)S(1)}, f32[128,128]{1,0:T(8,128)S(1)}, u32[]{:S(2)}, u32[]{:S(2)}) %collective-permute-start.14) | collective-permute-done | bytes 65568 | tf_op jit(solution)/shard_map/ppermute | solution.py:355
  87.2 1.3 %collective-permute-start.15 = (f32[128,128]{1,0:T(8,128)S(1)}, f32[128,128]{1,0:T(8,128)S(1)}, u32[]{:S(2)}, u32[]{:S(2)}) collective-permute-start(f32[128,128]{1,0:T(8,128)S(1)} %add_add_fusion.a_ref), channel_id=1, source_target_pairs={{0,32},{1,33},{2,34},{3,35},{4,36},{5,37},{6,38},{7,39},{8,40},{9,... | collective-permute-start | bytes 196616 | tf_op jit(solution)/shard_map/ppermute | solution.py:355
  88.4 1.4 %collective-permute-start.16 = (f32[128,128]{1,0:T(8,128)S(1)}, f32[128,128]{1,0:T(8,128)S(1)}, u32[]{:S(2)}, u32[]{:S(2)}) collective-permute-start(f32[128,128]{1,0:T(8,128)S(1)} %add_add_fusion.a_ref), channel_id=1, source_target_pairs={{0,64},{1,65},{2,66},{3,67},{4,68},{5,69},{6,70},{7,71},{8,72},{9,... | collective-permute-start | bytes 196616 | tf_op jit(solution)/shard_map/ppermute | solution.py:355
  89.8 2.2 %collective-permute-start.17 = (f32[128,128]{1,0:T(8,128)S(1)}, f32[128,128]{1,0:T(8,128)S(1)}, u32[]{:S(2)}, u32[]{:S(2)}) collective-permute-start(f32[128,128]{1,0:T(8,128)S(1)} %add_add_fusion.a_ref), channel_id=1, source_target_pairs={{0,96},{1,97},{2,98},{3,99},{4,100},{5,101},{6,102},{7,103},{8,104... | collective-permute-start | bytes 196616 | tf_op jit(solution)/shard_map/ppermute | solution.py:355
  92.0 0.0 collective-permute-done.7
  92.0 0.7 slice_add_fusion
  92.6 0.0 collective-permute-done.15.b_ref
  92.6 1.6 %collective-permute-done.16.c_ref = f32[128,128]{1,0:T(8,128)S(1)} collective-permute-done((f32[128,128]{1,0:T(8,128)S(1)}, f32[128,128]{1,0:T(8,128)S(1)}, u32[]{:S(2)}, u32[]{:S(2)}) %collective-permute-start.16) | collective-permute-done | bytes 65568 | tf_op jit(solution)/shard_map/ppermute | solution.py:355
  94.2 1.1 %collective-permute-done.17.d_ref = f32[128,128]{1,0:T(8,128)S(1)} collective-permute-done((f32[128,128]{1,0:T(8,128)S(1)}, f32[128,128]{1,0:T(8,128)S(1)}, u32[]{:S(2)}, u32[]{:S(2)}) %collective-permute-start.17) | collective-permute-done | bytes 65568 | tf_op jit(solution)/shard_map/ppermute | solution.py:355
  95.3 0.8 finish.1
  (6 shorter events, 0.1 us)
Async XLA Ops:
  2.4 6.3 %collective-permute-start = (bf16[32,80]{1,0:T(8,128)(2,1)S(1)}, bf16[32,80]{1,0:T(8,128)(2,1)S(1)}, u32[]{:S(2)}, u32[]{:S(2)}) collective-permute-start(bf16[32,80]{1,0:T(8,128)(2,1)S(1)} %get-tuple-element.46), channel_id=1, source_target_pairs={{0,16},{16,32},{32,48},{48,64},{64,80},{80,96},{96,112},{1,17},{17... | collective-permute-start | bytes 15368 | tf_op jit(solution)/shard_map/ppermute | solution.py:401
  5.9 5.5 %collective-permute-start.1 = (bf16[32,80]{1,0:T(8,128)(2,1)S(1)}, bf16[32,80]{1,0:T(8,128)(2,1)S(1)}, u32[]{:S(2)}, u32[]{:S(2)}) collective-permute-start(bf16[32,80]{1,0:T(8,128)(2,1)S(1)} %get-tuple-element.47), channel_id=1, source_target_pairs={{16,0},{32,16},{48,32},{64,48},{80,64},{96,80},{112,96},{17,1},{33... | collective-permute-start | bytes 15368 | tf_op jit(solution)/shard_map/ppermute | solution.py:402
  11.6 6.7 %collective-permute-start.2 = (bf16[80,80]{1,0:T(8,128)(2,1)S(1)}, bf16[80,80]{1,0:T(8,128)(2,1)S(1)}, u32[]{:S(2)}, u32[]{:S(2)}) collective-permute-start(bf16[80,80]{1,0:T(8,128)(2,1)S(1)} %get-tuple-element.89), channel_id=1, source_target_pairs={{0,1},{1,2},{2,3},{3,4},{4,5},{5,6},{6,7},{7,8},{8,9},{9,10},{10,1... | collective-permute-start | bytes 38408 | tf_op jit(solution)/shard_map/ppermute | solution.py:426
  12.9 6.2 %collective-permute-start.3 = (bf16[80,80]{1,0:T(8,128)(2,1)S(1)}, bf16[80,80]{1,0:T(8,128)(2,1)S(1)}, u32[]{:S(2)}, u32[]{:S(2)}) collective-permute-start(bf16[80,80]{1,0:T(8,128)(2,1)S(1)} %get-tuple-element.88), channel_id=1, source_target_pairs={{1,0},{2,1},{3,2},{4,3},{5,4},{6,5},{7,6},{8,7},{9,8},{10,9},{11,1... | collective-permute-start | bytes 38408 | tf_op jit(solution)/shard_map/ppermute | solution.py:427
  18.3 3.5 %copy-start.2 = (bf16[17,2,128,256]{3,2,1,0:T(8,128)(2,1)}, bf16[17,2,128,256]{3,2,1,0:T(8,128)(2,1)S(1)}, u32[]{:S(2)}) copy-start(bf16[17,2,128,256]{3,2,1,0:T(8,128)(2,1)S(1)} %get-tuple-element.76.refs_1_) | copy-start | bytes 6684676
  19.1 14.2 %copy-start = (bf16[4,256,256]{2,1,0:T(8,128)(2,1)S(1)}, bf16[4,256,256]{2,1,0:T(8,128)(2,1)}, u32[]{:S(2)}) copy-start(bf16[4,256,256]{2,1,0:T(8,128)(2,1)} %refs_2_) | copy-start | bytes 1572868
  19.1 14.3 %copy-start.1 = (bf16[4,8,32,256]{3,2,1,0:T(8,128)(2,1)S(1)}, bf16[4,8,32,256]{3,2,1,0:T(8,128)(2,1)}, u32[]{:S(2)}) copy-start(bf16[4,8,32,256]{3,2,1,0:T(8,128)(2,1)} %param.15) | copy-start | bytes 1572868
  21.8 23.9 %all-to-all-start = ((bf16[16,64,256]{2,1,0:T(8,128)(2,1)}), bf16[16,64,256]{2,1,0:T(8,128)(2,1)S(1)}, u32[]{:S(2)}, u32[]{:S(2)}) async-start(bf16[16,64,256]{2,1,0:T(8,128)(2,1)} %bitcast.36), calls=%async_computation | async-start | bytes 1048576 | tf_op jit(solution)/shard_map/all_to_all | solution.py:468
  47.1 15.9 %all-to-all-start.1 = ((bf16[16,64,256]{2,1,0:T(8,128)(2,1)}), bf16[16,64,256]{2,1,0:T(8,128)(2,1)S(1)}, u32[]{:S(2)}, u32[]{:S(2)}) async-start(bf16[16,64,256]{2,1,0:T(8,128)(2,1)} %mix.1), calls=%async_computation.1 | async-start | bytes 1048576 | tf_op jit(solution)/shard_map/all_to_all | solution.py:501
  53.2 15.8 %collective-permute-start.4 = (bf16[4,64,256]{2,1,0:T(8,128)(2,1)}, bf16[4,64,256]{2,1,0:T(8,128)(2,1)S(1)}, u32[]{:S(2)}, u32[]{:S(2)}) collective-permute-start(bf16[4,64,256]{2,1,0:T(8,128)(2,1)} %get-tuple-element.73), channel_id=1, source_target_pairs={{0,32},{16,48},{32,0},{48,16},{64,96},{80,112},{96,64},{112,80},{1... | collective-permute-start | bytes 393224 | tf_op jit(solution)/shard_map/ppermute | solution.py:520
  54.7 14.3 %collective-permute-start.5 = (bf16[4,64,256]{2,1,0:T(8,128)(2,1)}, bf16[4,64,256]{2,1,0:T(8,128)(2,1)S(1)}, u32[]{:S(2)}, u32[]{:S(2)}) collective-permute-start(bf16[4,64,256]{2,1,0:T(8,128)(2,1)} %get-tuple-element.74), channel_id=1, source_target_pairs={{0,64},{16,80},{32,96},{48,112},{64,0},{80,16},{96,32},{112,48},{1... | collective-permute-start | bytes 393224 | tf_op jit(solution)/shard_map/ppermute | solution.py:520
  57.5 11.6 %collective-permute-start.6 = (bf16[4,64,256]{2,1,0:T(8,128)(2,1)}, bf16[4,64,256]{2,1,0:T(8,128)(2,1)S(1)}, u32[]{:S(2)}, u32[]{:S(2)}) collective-permute-start(bf16[4,64,256]{2,1,0:T(8,128)(2,1)} %get-tuple-element.75), channel_id=1, source_target_pairs={{0,96},{16,112},{32,64},{48,80},{64,32},{80,48},{96,0},{112,16},{1... | collective-permute-start | bytes 393224 | tf_op jit(solution)/shard_map/ppermute | solution.py:520
  63.0 20.8 %copy-start.3 = (f32[4,64,256]{2,1,0:T(8,128)S(1)}, f32[4,64,256]{2,1,0:T(8,128)}, u32[]{:S(2)}) copy-start(f32[4,64,256]{2,1,0:T(8,128)} %get-tuple-element.72) | copy-start | bytes 786436
  69.1 1.3 %collective-permute-start.8 = (f32[128,128]{1,0:T(8,128)S(1)}, f32[128,128]{1,0:T(8,128)S(1)}, u32[]{:S(2)}, u32[]{:S(2)}) collective-permute-start(f32[128,128]{1,0:T(8,128)S(1)} %backward.1), channel_id=1, source_target_pairs={{0,1},{1,0},{2,3},{3,2},{4,5},{5,4},{6,7},{7,6},{8,9},{9,8},{10,11... | collective-permute-start | bytes 196616 | tf_op jit(solution)/shard_map/ppermute | solution.py:355
  70.4 4.5 %collective-permute-start.10 = (f32[128,128]{1,0:T(8,128)S(1)}, f32[128,128]{1,0:T(8,128)S(1)}, u32[]{:S(2)}, u32[]{:S(2)}) collective-permute-start(f32[128,128]{1,0:T(8,128)S(1)} %add.37), channel_id=1, source_target_pairs={{0,16},{1,17},{2,18},{3,19},{4,20},{5,21},{6,22},{7,23},{8,24},{9,... | collective-permute-start | bytes 196616 | tf_op jit(solution)/shard_map/ppermute | solution.py:355
  72.5 6.5 %collective-permute-start.11 = (f32[128,128]{1,0:T(8,128)S(1)}, f32[128,128]{1,0:T(8,128)S(1)}, u32[]{:S(2)}, u32[]{:S(2)}) collective-permute-start(f32[128,128]{1,0:T(8,128)S(1)} %add.37), channel_id=1, source_target_pairs={{0,18},{1,19},{2,16},{3,17},{4,22},{5,23},{6,20},{7,21},{8,26},{9,... | collective-permute-start | bytes 196616 | tf_op jit(solution)/shard_map/ppermute | solution.py:355
  72.5 6.5 %collective-permute-start.9 = (f32[128,128]{1,0:T(8,128)S(1)}, f32[128,128]{1,0:T(8,128)S(1)}, u32[]{:S(2)}, u32[]{:S(2)}) collective-permute-start(f32[128,128]{1,0:T(8,128)S(1)} %add.37), channel_id=1, source_target_pairs={{0,2},{1,3},{2,0},{3,1},{4,6},{5,7},{6,4},{7,5},{8,10},{9,11},{10,... | collective-permute-start | bytes 196616 | tf_op jit(solution)/shard_map/ppermute | solution.py:355
  79.0 5.5 %collective-permute-start.12 = (f32[128,128]{1,0:T(8,128)S(1)}, f32[128,128]{1,0:T(8,128)S(1)}, u32[]{:S(2)}, u32[]{:S(2)}) collective-permute-start(f32[128,128]{1,0:T(8,128)S(1)} %add_add_fusion.1), channel_id=1, source_target_pairs={{0,4},{1,5},{2,6},{3,7},{4,0},{5,1},{6,2},{7,3},{8,12},{9,13},{10,... | collective-permute-start | bytes 196616 | tf_op jit(solution)/shard_map/ppermute | solution.py:355
  79.1 6.1 %collective-permute-start.13 = (f32[128,128]{1,0:T(8,128)S(1)}, f32[128,128]{1,0:T(8,128)S(1)}, u32[]{:S(2)}, u32[]{:S(2)}) collective-permute-start(f32[128,128]{1,0:T(8,128)S(1)} %add_add_fusion.1), channel_id=1, source_target_pairs={{0,8},{1,9},{2,10},{3,11},{4,12},{5,13},{6,14},{7,15},{8,0},{9,1},... | collective-permute-start | bytes 196616 | tf_op jit(solution)/shard_map/ppermute | solution.py:355
  81.7 5.5 %collective-permute-start.14 = (f32[128,128]{1,0:T(8,128)S(1)}, f32[128,128]{1,0:T(8,128)S(1)}, u32[]{:S(2)}, u32[]{:S(2)}) collective-permute-start(f32[128,128]{1,0:T(8,128)S(1)} %add_add_fusion.1), channel_id=1, source_target_pairs={{0,12},{1,13},{2,14},{3,15},{4,8},{5,9},{6,10},{7,11},{8,4},{9,5},... | collective-permute-start | bytes 196616 | tf_op jit(solution)/shard_map/ppermute | solution.py:355
  83.9 8.1 %collective-permute-start.7 = (bf16[4,32,256]{2,1,0:T(8,128)(2,1)S(1)}, bf16[4,32,256]{2,1,0:T(8,128)(2,1)S(1)}, u32[]{:S(2)}, u32[]{:S(2)}) collective-permute-start(bf16[4,32,256]{2,1,0:T(8,128)(2,1)S(1)} %split.13), channel_id=1, source_target_pairs={{0,16},{16,0},{32,48},{48,32},{64,80},{80,64},{96,112},{112,96},{1... | collective-permute-start | bytes 196616 | tf_op jit(solution)/shard_map/ppermute | solution.py:553
  87.2 5.5 %collective-permute-start.15 = (f32[128,128]{1,0:T(8,128)S(1)}, f32[128,128]{1,0:T(8,128)S(1)}, u32[]{:S(2)}, u32[]{:S(2)}) collective-permute-start(f32[128,128]{1,0:T(8,128)S(1)} %add_add_fusion.a_ref), channel_id=1, source_target_pairs={{0,32},{1,33},{2,34},{3,35},{4,36},{5,37},{6,38},{7,39},{8,40},{9,... | collective-permute-start | bytes 196616 | tf_op jit(solution)/shard_map/ppermute | solution.py:355
  88.4 5.8 %collective-permute-start.16 = (f32[128,128]{1,0:T(8,128)S(1)}, f32[128,128]{1,0:T(8,128)S(1)}, u32[]{:S(2)}, u32[]{:S(2)}) collective-permute-start(f32[128,128]{1,0:T(8,128)S(1)} %add_add_fusion.a_ref), channel_id=1, source_target_pairs={{0,64},{1,65},{2,66},{3,67},{4,68},{5,69},{6,70},{7,71},{8,72},{9,... | collective-permute-start | bytes 196616 | tf_op jit(solution)/shard_map/ppermute | solution.py:355
  89.8 5.5 %collective-permute-start.17 = (f32[128,128]{1,0:T(8,128)S(1)}, f32[128,128]{1,0:T(8,128)S(1)}, u32[]{:S(2)}, u32[]{:S(2)}) collective-permute-start(f32[128,128]{1,0:T(8,128)S(1)} %add_add_fusion.a_ref), channel_id=1, source_target_pairs={{0,96},{1,97},{2,98},{3,99},{4,100},{5,101},{6,102},{7,103},{8,104... | collective-permute-start | bytes 196616 | tf_op jit(solution)/shard_map/ppermute | solution.py:355

commit v12 on v11

--- a/solution.py
+++ b/solution.py
@@ -236,7 +236,7 @@
 
 def backward_kernel(
     down_scale, conv_scale, cgrad_ref, emb_hbm, slope_hbm, hidden_hbm, pair_ref, pair_t_ref, face_ref, edge_ref,
-    out_ref, turn_a, turn_b, turned_pg, emb_in, slope_in, hidden_ref, sem,
+    out_ref, turn_a, turn_b, turned_pg, taps_ref, emb_in, slope_in, hidden_ref, sem,
 ):
     copies = [
         pltpu.make_async_copy(slope_hbm, slope_in, sem.at[0]),
@@ -279,7 +279,7 @@
             turned_pg[at, 512 * bc + first : 512 * bc + first + 32] = (rows[:, first : first + 32] * edge_ref[at, low : low + 32]).astype(BF16)
     copies[1].wait()
     lane_x = iota((16, 128), 1) // 16
-    own = iota((8, 128), 1) // 16 == iota((8, 128), 0)
+    own = iota((64, 8, 128), 2) // 16 == iota((64, 8, 128), 1)
     for ty in range(3):
         for tz in range(3):
             pieces = []
@@ -305,13 +305,13 @@
                             half = jnp.where(lane_x == lane, part, half)
                     total = half if total is None else total + half
                 tap = 9 * tx + 3 * ty + tz
-                total = fold(total, 16) * conv_scale
                 for half in range(2):
-                    part = jnp.where(own, total[8 * half : 8 * half + 8], 0.0)
-                    line = 64 + 32 * half + tap
-                    out_ref[line : line + 1, :] = jnp.sum(part, axis=0, keepdims=True)
+                    at = 8 * (32 * half + tap)
+                    taps_ref[at : at + 8, :] = total[8 * half : 8 * half + 8]
     for half in range(2):
-        out_ref[91 + 32 * half : 96 + 32 * half, :] = jnp.zeros((5, 128), F32)
+        taps_ref[256 * half + 216 : 256 * half + 256, :] = jnp.zeros((40, 128), F32)
+    total = fold(taps_ref[...], 16) * conv_scale
+    out_ref[64:128, :] = jnp.sum(jnp.where(own, total.reshape(64, 8, 128), 0.0), axis=1)
 
 
 def finish_kernel(a_ref, b_ref, c_ref, d_ref, down_ref, conv_ref):
@@ -530,6 +530,7 @@
             pltpu.VMEM((512, 512), F32),
             pltpu.VMEM((2, 1024, 128), F32),
             pltpu.VMEM((256, 2048), BF16),
+            pltpu.VMEM((512, 128), F32),
             pltpu.VMEM((17, 2, 128, 256), BF16),
             pltpu.VMEM((4, 256, 512), F32),
             pltpu.VMEM((4, 256, 512), BF16),

time: 96.5 us -> 96.5 us (level)
  no operation moved by 1% of the time
where the time goes in v12:
time: 96.5 us; the launch traced here: 96.1 us
  starting transfers between devices  41.8 us (43%)
  waiting for transfers between devices  31.3 us (32%)
  Pallas kernels  21.2 us (22%)
    ppermute x10, starting transfers between devices, exchanged(): lax.ppermute(value, ('sy', 'sz'), [(i, i ^ m) for i in range(count)])  13.9 us
    all_to_all x1, waiting for transfers between devices, per_device(): lax.all_to_all(coarse.reshape(count_z, mine * 16, 256), 'sz', split_axis=...  11.8 us
    all_to_all x1, starting transfers between devices, per_device(): lax.all_to_all(coarse.reshape(count_z, mine * 16, 256), 'sz', split_axis=...  11.5 us
    ppermute x10, waiting for transfers between devices, exchanged(): lax.ppermute(value, ('sy', 'sz'), [(i, i ^ m) for i in range(count)])  10.8 us
    pallas_call x1, Pallas kernels, per_device(): pl.pallas_call(lambda *refs: backward_kernel(1.0 / math.sqrt(cells // 8),...  6.01 us
    all_to_all x1, waiting for transfers between devices, per_device(): lax.all_to_all(back, 'sz', split_axis=0, concat_axis=0, tiled=True)  5.1 us
    ppermute x3, starting transfers between devices, per_device(): lax.ppermute(part, 'sy', [(i, i ^ 2 * k) for i in range(count_y)])  4.7 us
    pallas_call x1, Pallas kernels, per_device(): pl.pallas_call(inner_kernel, out_shape=(shape((17, 2, 128, 256), BF16), p...  4.12 us
  transfers between devices with their start and end apart: 20, of which 11 were waited for; matrix products, arithmetic and copies ran while one was open for 1% of the time, Pallas kernels for 15%

profile of v12, /device:TPU:0, one launch (start us, length us, event | category | flops | bytes accessed | tf_op | source)
XLA Modules:
  0.0 96.1 jit_solution(10841624491738609179)
XLA Ops:
  0.6 1.7 %features.1 = (bf16[32,128,80]{2,1,0:T(8,128)(2,1)S(1)}, bf16[32,80]{1,0:T(8,128)(2,1)S(1)}, bf16[32,80]{1,0:T(8,128)(2,1)S(1)}, bf16[16,16,27]{2,1,0:T(8,128)(2...) custom-call(s32[512,64]{1,0:T(8,128)} %bitcast.37, ...), custom_call_target="tpu_custom_call" | custom-call | flops 41943040 | bytes 2097152 | tf_op jit(solution)/shard_map/features/pallas_call | solution.py:365
  2.4 3.6 %collective-permute-start = (bf16[32,80]{1,0:T(8,128)(2,1)S(1)}, bf16[32,80]{1,0:T(8,128)(2,1)S(1)}, u32[]{:S(2)}, u32[]{:S(2)}) collective-permute-start(bf16[32,80]{1,0:T(8,128)(2,1)S(1)} %get-tuple-element.46), channel_id=1, source_target_pairs={{0,16},{16,32},{32,48},{48,64},{64,80},{80,96},{96,112},{1,17},{17... | collective-permute-start | bytes 15368 | tf_op jit(solution)/shard_map/ppermute | solution.py:401
  5.9 1.3 %collective-permute-start.1 = (bf16[32,80]{1,0:T(8,128)(2,1)S(1)}, bf16[32,80]{1,0:T(8,128)(2,1)S(1)}, u32[]{:S(2)}, u32[]{:S(2)}) collective-permute-start(bf16[32,80]{1,0:T(8,128)(2,1)S(1)} %get-tuple-element.47), channel_id=1, source_target_pairs={{16,0},{32,16},{48,32},{64,48},{80,64},{96,80},{112,96},{17,1},{33... | collective-permute-start | bytes 15368 | tf_op jit(solution)/shard_map/ppermute | solution.py:402
  7.3 1.4 %weights.1 = (bf16[9,256,256]{2,1,0:T(8,128)(2,1)S(1)}, bf16[128,256]{1,0:T(8,128)(2,1)S(1)}, bf16[256,128]{1,0:T(8,128)(2,1)S(1)}, bf16[80,256]{1,0:T(8,128)(2,1)S(1)}) custom-call(bf16[16,16,27]{2,1,0:T(8,128)(2,1)S(1)} %get-tuple-element.48.conv_ref, bf16[8,16,64]{2,1,0:T(8,128)(2,1)S(1)} %get-tuple-element.49.down_ref, ...), custom_call_target="tpu_custom_call" | custom-call | flops 56623104 | bytes 3145728 | tf_op jit(solution)/shard_map/weights/pallas_call | solution.py:403
  8.7 0.0 collective-permute-done.ylo_ref
  8.7 2.8 %collective-permute-done.1.yhi_ref = bf16[32,80]{1,0:T(8,128)(2,1)S(1)} collective-permute-done((bf16[32,80]{1,0:T(8,128)(2,1)S(1)}, bf16[32,80]{1,0:T(8,128)(2,1)S(1)}, u32[]{:S(2)}, u32[]{:S(2)}) %collective-permute-start.1) | collective-permute-done | bytes 5152 | tf_op jit(solution)/shard_map/ppermute | solution.py:402
  11.5 0.1 fusion
  11.6 1.3 %collective-permute-start.2 = (bf16[80,80]{1,0:T(8,128)(2,1)S(1)}, bf16[80,80]{1,0:T(8,128)(2,1)S(1)}, u32[]{:S(2)}, u32[]{:S(2)}) collective-permute-start(bf16[80,80]{1,0:T(8,128)(2,1)S(1)} %get-tuple-element.89), channel_id=1, source_target_pairs={{0,1},{1,2},{2,3},{3,4},{4,5},{5,6},{6,7},{7,8},{8,9},{9,10},{10,1... | collective-permute-start | bytes 38408 | tf_op jit(solution)/shard_map/ppermute | solution.py:426
  12.9 1.3 %collective-permute-start.3 = (bf16[80,80]{1,0:T(8,128)(2,1)S(1)}, bf16[80,80]{1,0:T(8,128)(2,1)S(1)}, u32[]{:S(2)}, u32[]{:S(2)}) collective-permute-start(bf16[80,80]{1,0:T(8,128)(2,1)S(1)} %get-tuple-element.88), channel_id=1, source_target_pairs={{1,0},{2,1},{3,2},{4,3},{5,4},{6,5},{7,6},{8,7},{9,8},{10,9},{11,1... | collective-permute-start | bytes 38408 | tf_op jit(solution)/shard_map/ppermute | solution.py:427
  14.2 4.1 %inner.1 = (bf16[17,2,128,256]{3,2,1,0:T(8,128)(2,1)S(1)}, f32[4,256,512]{2,1,0:T(8,128)}, bf16[4,256,512]{2,1,0:T(8,128)(2,1)S(1)}, f32[2,2,256,32]{3,2,1,0:T(8,128)S(1)}) custom-call(bf16[32,128,80]{2,1,0:T(8,128)(2,1)S(1)} %get-tuple-element.58.feat_ref, bf16[32,80]{1,0:T(8,128)(2,1)S(1)} %collective-permute-done.ylo_ref, ...), custom_call_target="tpu_custom_call" | custom-call | flops 3221225472 | bytes 10485760 | tf_op jit(solution)/shard_map/inner/pallas_call | solution.py:428
  18.3 0.0 copy-start.2
  18.3 0.0 collective-permute-done.2.zlo_ref
  18.3 0.8 collective-permute-done.3.zhi_ref
  19.1 0.0 copy-start
  19.1 0.0 copy-start.1
  19.1 2.7 %outer.1 = (bf16[2,128,256]{2,1,0:T(8,128)(2,1)S(1)}, f32[256,128]{1,0:T(8,128)S(1)}, bf16[4,256,512]{2,1,0:T(8,128)(2,1)}, bf16[1024,256]{1,0:T(8,128)(2,1)}) custom-call(bf16[80,80]{1,0:T(8,128)(2,1)S(1)} %collective-permute-done.2.zlo_ref, bf16[80,80]{1,0:T(8,128)(2,1)S(1)} %collective-permute-done.3.zhi_ref, ...), custom_call_target="tpu_custom_call" | custom-call | flops 1073741824 | bytes 4194304 | tf_op jit(solution)/shard_map/outer/pallas_call | solution.py:443
  21.8 0.0 copy-done.2
  21.8 11.5 %all-to-all-start = ((bf16[16,64,256]{2,1,0:T(8,128)(2,1)}), bf16[16,64,256]{2,1,0:T(8,128)(2,1)S(1)}, u32[]{:S(2)}, u32[]{:S(2)}) async-start(bf16[16,64,256]{2,1,0:T(8,128)(2,1)} %bitcast.36), calls=%async_computation | async-start | bytes 1048576 | tf_op jit(solution)/shard_map/all_to_all | solution.py:468
  33.4 0.0 copy-done
  33.4 0.0 copy-done.1
  33.4 0.5 turn.1
  33.9 11.8 %all-to-all-done.coarse_ref.refs_1_ = bf16[16,64,256]{2,1,0:T(8,128)(2,1)S(1)} async-done(((bf16[16,64,256]{2,1,0:T(8,128)(2,1)}), bf16[16,64,256]{2,1,0:T(8,128)(2,1)S(1)}, u32[]{:S(2)}, u32[]{:S(2)}) %all-to-all-start) | async-done | bytes 524320 | tf_op jit(solution)/shard_map/all_to_all | solution.py:468
  45.7 1.4 %mix.1 = bf16[16,64,256]{2,1,0:T(8,128)(2,1)} custom-call(bf16[16,64,256]{2,1,0:T(8,128)(2,1)S(1)} %all-to-all-done.coarse_ref.refs_1_, bf16[4,256,256]{2,1,0:T(8,128)(2,1)S(1)} %copy-done, bf16[4,256,256]{2,1,0:T(8,128)(2,1)S(1)} %get-tuple-element.68.cot_t_ref.refs_3_, bf16[4,256,256]{2,1,0:T(8,128)(2,1)S(1)} %get-tuple-element.69.mix_t_ref), custom_call_target="tpu_custom_call" | custom-call | flops 268435456 | bytes 2097152 | tf_op jit(solution)/shard_map/mix/pallas_call | solution.py:488
  47.1 3.6 %all-to-all-start.1 = ((bf16[16,64,256]{2,1,0:T(8,128)(2,1)}), bf16[16,64,256]{2,1,0:T(8,128)(2,1)S(1)}, u32[]{:S(2)}, u32[]{:S(2)}) async-start(bf16[16,64,256]{2,1,0:T(8,128)(2,1)} %mix.1), calls=%async_computation.1 | async-start | bytes 1048576 | tf_op jit(solution)/shard_map/all_to_all | solution.py:501
  50.7 2.5 %mix_grad.1 = (bf16[4,256,256]{2,1,0:T(8,128)(2,1)}, f32[4,64,256]{2,1,0:T(8,128)}, bf16[4,64,256]{2,1,0:T(8,128)(2,1)}, bf16[4,64,256]{2,1,0:T(8,128)(2,1)}, bf16[4,64,256]{2,1,0:T(8,128)(2,1)}) custom-call(s32[1]{0:T(128)} %bitcast.refs_0_, bf16[16,64,256]{2,1,0:T(8,128)(2,1)S(1)} %all-to-all-done.coarse_ref.refs_1_, bf16[4,256,256]{2,1,0:T(8,128)(2,1)S(1)} %copy-done, ...), custom_call_target="tpu_custom_call" | custom-call | flops 268435456 | bytes 3145728 | tf_op jit(solution)/shard_map/mix_grad/pallas_call | solution.py:503
  53.2 1.5 %collective-permute-start.4 = (bf16[4,64,256]{2,1,0:T(8,128)(2,1)}, bf16[4,64,256]{2,1,0:T(8,128)(2,1)S(1)}, u32[]{:S(2)}, u32[]{:S(2)}) collective-permute-start(bf16[4,64,256]{2,1,0:T(8,128)(2,1)} %get-tuple-element.73), channel_id=1, source_target_pairs={{0,32},{16,48},{32,0},{48,16},{64,96},{80,112},{96,64},{112,80},{1... | collective-permute-start | bytes 393224 | tf_op jit(solution)/shard_map/ppermute | solution.py:520
  54.7 2.7 %collective-permute-start.5 = (bf16[4,64,256]{2,1,0:T(8,128)(2,1)}, bf16[4,64,256]{2,1,0:T(8,128)(2,1)S(1)}, u32[]{:S(2)}, u32[]{:S(2)}) collective-permute-start(bf16[4,64,256]{2,1,0:T(8,128)(2,1)} %get-tuple-element.74), channel_id=1, source_target_pairs={{0,64},{16,80},{32,96},{48,112},{64,0},{80,16},{96,32},{112,48},{1... | collective-permute-start | bytes 393224 | tf_op jit(solution)/shard_map/ppermute | solution.py:520
  57.5 0.5 collective-permute-start.6
  57.9 5.1 %all-to-all-done.1 = bf16[16,64,256]{2,1,0:T(8,128)(2,1)S(1)} async-done(((bf16[16,64,256]{2,1,0:T(8,128)(2,1)}), bf16[16,64,256]{2,1,0:T(8,128)(2,1)S(1)}, u32[]{:S(2)}, u32[]{:S(2)}) %all-to-all-start.1) | async-done | bytes 524320 | tf_op jit(solution)/shard_map/all_to_all | solution.py:501
  63.0 0.0 copy-start.3
  63.0 6.0 %backward.1 = f32[128,128]{1,0:T(8,128)S(1)} custom-call(bf16[1024,256]{1,0:T(8,128)(2,1)S(1)} %bitcast.35, bf16[17,2,128,256]{3,2,1,0:T(8,128)(2,1)} %copy-done.2, f32[4,256,512]{2,1,0:T(8,128)} %get-tuple-element.77.refs_2_, bf16[4,256,512]{2,1,0:T(8,128)(2,1)} %get-tuple-element.78.refs_3_, bf16[128,256]{1,0:T(8,128)(2,1)S(1)} %get-tuple-element.61.pair_ref.refs_4_, ...), custom_call_target="tpu_custom_call" | custom-call | flops 4294967296 | bytes 8388608 | tf_op jit(solution)/shard_map/backward/pallas_call | solution.py:522
  69.0 0.0 collective-permute-done.4
  69.1 0.0 collective-permute-done.5
  69.1 0.0 collective-permute-done.6
  69.1 0.1 collective-permute-start.8
  69.2 1.2 %collective-permute-done.8 = f32[128,128]{1,0:T(8,128)S(1)} collective-permute-done((f32[128,128]{1,0:T(8,128)S(1)}, f32[128,128]{1,0:T(8,128)S(1)}, u32[]{:S(2)}, u32[]{:S(2)}) %collective-permute-start.8) | collective-permute-done | bytes 65568 | tf_op jit(solution)/shard_map/ppermute | solution.py:355
  70.4 2.1 %collective-permute-start.10 = (f32[128,128]{1,0:T(8,128)S(1)}, f32[128,128]{1,0:T(8,128)S(1)}, u32[]{:S(2)}, u32[]{:S(2)}) collective-permute-start(f32[128,128]{1,0:T(8,128)S(1)} %add.37), channel_id=1, source_target_pairs={{0,16},{1,17},{2,18},{3,19},{4,20},{5,21},{6,22},{7,23},{8,24},{9,... | collective-permute-start | bytes 196616 | tf_op jit(solution)/shard_map/ppermute | solution.py:355
  72.5 0.0 collective-permute-start.11
  72.5 2.2 %collective-permute-start.9 = (f32[128,128]{1,0:T(8,128)S(1)}, f32[128,128]{1,0:T(8,128)S(1)}, u32[]{:S(2)}, u32[]{:S(2)}) collective-permute-start(f32[128,128]{1,0:T(8,128)S(1)} %add.37), channel_id=1, source_target_pairs={{0,2},{1,3},{2,0},{3,1},{4,6},{5,7},{6,4},{7,5},{8,10},{9,11},{10,... | collective-permute-start | bytes 196616 | tf_op jit(solution)/shard_map/ppermute | solution.py:355
  74.7 0.3 collective-permute-done.10
  74.9 4.1 %collective-permute-done.11 = f32[128,128]{1,0:T(8,128)S(1)} collective-permute-done((f32[128,128]{1,0:T(8,128)S(1)}, f32[128,128]{1,0:T(8,128)S(1)}, u32[]{:S(2)}, u32[]{:S(2)}) %collective-permute-start.11) | collective-permute-done | bytes 65568 | tf_op jit(solution)/shard_map/ppermute | solution.py:355
  79.0 0.0 collective-permute-done.9
  79.0 0.1 collective-permute-start.12
  79.1 2.6 %collective-permute-start.13 = (f32[128,128]{1,0:T(8,128)S(1)}, f32[128,128]{1,0:T(8,128)S(1)}, u32[]{:S(2)}, u32[]{:S(2)}) collective-permute-start(f32[128,128]{1,0:T(8,128)S(1)} %add_add_fusion.1), channel_id=1, source_target_pairs={{0,8},{1,9},{2,10},{3,11},{4,12},{5,13},{6,14},{7,15},{8,0},{9,1},... | collective-permute-start | bytes 196616 | tf_op jit(solution)/shard_map/ppermute | solution.py:355
  81.7 2.1 %collective-permute-start.14 = (f32[128,128]{1,0:T(8,128)S(1)}, f32[128,128]{1,0:T(8,128)S(1)}, u32[]{:S(2)}, u32[]{:S(2)}) collective-permute-start(f32[128,128]{1,0:T(8,128)S(1)} %add_add_fusion.1), channel_id=1, source_target_pairs={{0,12},{1,13},{2,14},{3,15},{4,8},{5,9},{6,10},{7,11},{8,4},{9,5},... | collective-permute-start | bytes 196616 | tf_op jit(solution)/shard_map/ppermute | solution.py:355
  83.8 0.0 copy-done.3
  83.8 0.1 convert_add_fusion
  83.9 0.7 collective-permute-start.7
  84.5 0.0 collective-permute-done.12
  84.5 0.6 collective-permute-done.13
  85.2 2.0 %collective-permute-done.14 = f32[128,128]{1,0:T(8,128)S(1)} collective-permute-done((f32[128,128]{1,0:T(8,128)S(1)}, f32[128,128]{1,0:T(8,128)S(1)}, u32[]{:S(2)}, u32[]{:S(2)}) %collective-permute-start.14) | collective-permute-done | bytes 65568 | tf_op jit(solution)/shard_map/ppermute | solution.py:355
  87.2 1.3 %collective-permute-start.15 = (f32[128,128]{1,0:T(8,128)S(1)}, f32[128,128]{1,0:T(8,128)S(1)}, u32[]{:S(2)}, u32[]{:S(2)}) collective-permute-start(f32[128,128]{1,0:T(8,128)S(1)} %add_add_fusion.a_ref), channel_id=1, source_target_pairs={{0,32},{1,33},{2,34},{3,35},{4,36},{5,37},{6,38},{7,39},{8,40},{9,... | collective-permute-start | bytes 196616 | tf_op jit(solution)/shard_map/ppermute | solution.py:355
  88.4 1.4 %collective-permute-start.16 = (f32[128,128]{1,0:T(8,128)S(1)}, f32[128,128]{1,0:T(8,128)S(1)}, u32[]{:S(2)}, u32[]{:S(2)}) collective-permute-start(f32[128,128]{1,0:T(8,128)S(1)} %add_add_fusion.a_ref), channel_id=1, source_target_pairs={{0,64},{1,65},{2,66},{3,67},{4,68},{5,69},{6,70},{7,71},{8,72},{9,... | collective-permute-start | bytes 196616 | tf_op jit(solution)/shard_map/ppermute | solution.py:355
  89.8 2.2 %collective-permute-start.17 = (f32[128,128]{1,0:T(8,128)S(1)}, f32[128,128]{1,0:T(8,128)S(1)}, u32[]{:S(2)}, u32[]{:S(2)}) collective-permute-start(f32[128,128]{1,0:T(8,128)S(1)} %add_add_fusion.a_ref), channel_id=1, source_target_pairs={{0,96},{1,97},{2,98},{3,99},{4,100},{5,101},{6,102},{7,103},{8,104... | collective-permute-start | bytes 196616 | tf_op jit(solution)/shard_map/ppermute | solution.py:355
  92.0 0.0 collective-permute-done.7
  92.0 0.7 slice_add_fusion
  92.6 0.0 collective-permute-done.15.b_ref
  92.6 1.6 %collective-permute-done.16.c_ref = f32[128,128]{1,0:T(8,128)S(1)} collective-permute-done((f32[128,128]{1,0:T(8,128)S(1)}, f32[128,128]{1,0:T(8,128)S(1)}, u32[]{:S(2)}, u32[]{:S(2)}) %collective-permute-start.16) | collective-permute-done | bytes 65568 | tf_op jit(solution)/shard_map/ppermute | solution.py:355
  94.2 1.1 %collective-permute-done.17.d_ref = f32[128,128]{1,0:T(8,128)S(1)} collective-permute-done((f32[128,128]{1,0:T(8,128)S(1)}, f32[128,128]{1,0:T(8,128)S(1)}, u32[]{:S(2)}, u32[]{:S(2)}) %collective-permute-start.17) | collective-permute-done | bytes 65568 | tf_op jit(solution)/shard_map/ppermute | solution.py:355
  95.3 0.8 finish.1
  (6 shorter events, 0.1 us)
Async XLA Ops:
  2.4 6.3 %collective-permute-start = (bf16[32,80]{1,0:T(8,128)(2,1)S(1)}, bf16[32,80]{1,0:T(8,128)(2,1)S(1)}, u32[]{:S(2)}, u32[]{:S(2)}) collective-permute-start(bf16[32,80]{1,0:T(8,128)(2,1)S(1)} %get-tuple-element.46), channel_id=1, source_target_pairs={{0,16},{16,32},{32,48},{48,64},{64,80},{80,96},{96,112},{1,17},{17... | collective-permute-start | bytes 15368 | tf_op jit(solution)/shard_map/ppermute | solution.py:401
  5.9 5.5 %collective-permute-start.1 = (bf16[32,80]{1,0:T(8,128)(2,1)S(1)}, bf16[32,80]{1,0:T(8,128)(2,1)S(1)}, u32[]{:S(2)}, u32[]{:S(2)}) collective-permute-start(bf16[32,80]{1,0:T(8,128)(2,1)S(1)} %get-tuple-element.47), channel_id=1, source_target_pairs={{16,0},{32,16},{48,32},{64,48},{80,64},{96,80},{112,96},{17,1},{33... | collective-permute-start | bytes 15368 | tf_op jit(solution)/shard_map/ppermute | solution.py:402
  11.6 6.7 %collective-permute-start.2 = (bf16[80,80]{1,0:T(8,128)(2,1)S(1)}, bf16[80,80]{1,0:T(8,128)(2,1)S(1)}, u32[]{:S(2)}, u32[]{:S(2)}) collective-permute-start(bf16[80,80]{1,0:T(8,128)(2,1)S(1)} %get-tuple-element.89), channel_id=1, source_target_pairs={{0,1},{1,2},{2,3},{3,4},{4,5},{5,6},{6,7},{7,8},{8,9},{9,10},{10,1... | collective-permute-start | bytes 38408 | tf_op jit(solution)/shard_map/ppermute | solution.py:426
  12.9 6.2 %collective-permute-start.3 = (bf16[80,80]{1,0:T(8,128)(2,1)S(1)}, bf16[80,80]{1,0:T(8,128)(2,1)S(1)}, u32[]{:S(2)}, u32[]{:S(2)}) collective-permute-start(bf16[80,80]{1,0:T(8,128)(2,1)S(1)} %get-tuple-element.88), channel_id=1, source_target_pairs={{1,0},{2,1},{3,2},{4,3},{5,4},{6,5},{7,6},{8,7},{9,8},{10,9},{11,1... | collective-permute-start | bytes 38408 | tf_op jit(solution)/shard_map/ppermute | solution.py:427
  18.3 3.5 %copy-start.2 = (bf16[17,2,128,256]{3,2,1,0:T(8,128)(2,1)}, bf16[17,2,128,256]{3,2,1,0:T(8,128)(2,1)S(1)}, u32[]{:S(2)}) copy-start(bf16[17,2,128,256]{3,2,1,0:T(8,128)(2,1)S(1)} %get-tuple-element.76.refs_1_) | copy-start | bytes 6684676
  19.1 14.2 %copy-start = (bf16[4,256,256]{2,1,0:T(8,128)(2,1)S(1)}, bf16[4,256,256]{2,1,0:T(8,128)(2,1)}, u32[]{:S(2)}) copy-start(bf16[4,256,256]{2,1,0:T(8,128)(2,1)} %refs_2_) | copy-start | bytes 1572868
  19.1 14.3 %copy-start.1 = (bf16[4,8,32,256]{3,2,1,0:T(8,128)(2,1)S(1)}, bf16[4,8,32,256]{3,2,1,0:T(8,128)(2,1)}, u32[]{:S(2)}) copy-start(bf16[4,8,32,256]{3,2,1,0:T(8,128)(2,1)} %param.15) | copy-start | bytes 1572868
  21.8 23.9 %all-to-all-start = ((bf16[16,64,256]{2,1,0:T(8,128)(2,1)}), bf16[16,64,256]{2,1,0:T(8,128)(2,1)S(1)}, u32[]{:S(2)}, u32[]{:S(2)}) async-start(bf16[16,64,256]{2,1,0:T(8,128)(2,1)} %bitcast.36), calls=%async_computation | async-start | bytes 1048576 | tf_op jit(solution)/shard_map/all_to_all | solution.py:468
  47.1 15.9 %all-to-all-start.1 = ((bf16[16,64,256]{2,1,0:T(8,128)(2,1)}), bf16[16,64,256]{2,1,0:T(8,128)(2,1)S(1)}, u32[]{:S(2)}, u32[]{:S(2)}) async-start(bf16[16,64,256]{2,1,0:T(8,128)(2,1)} %mix.1), calls=%async_computation.1 | async-start | bytes 1048576 | tf_op jit(solution)/shard_map/all_to_all | solution.py:501
  53.2 15.8 %collective-permute-start.4 = (bf16[4,64,256]{2,1,0:T(8,128)(2,1)}, bf16[4,64,256]{2,1,0:T(8,128)(2,1)S(1)}, u32[]{:S(2)}, u32[]{:S(2)}) collective-permute-start(bf16[4,64,256]{2,1,0:T(8,128)(2,1)} %get-tuple-element.73), channel_id=1, source_target_pairs={{0,32},{16,48},{32,0},{48,16},{64,96},{80,112},{96,64},{112,80},{1... | collective-permute-start | bytes 393224 | tf_op jit(solution)/shard_map/ppermute | solution.py:520
  54.7 14.3 %collective-permute-start.5 = (bf16[4,64,256]{2,1,0:T(8,128)(2,1)}, bf16[4,64,256]{2,1,0:T(8,128)(2,1)S(1)}, u32[]{:S(2)}, u32[]{:S(2)}) collective-permute-start(bf16[4,64,256]{2,1,0:T(8,128)(2,1)} %get-tuple-element.74), channel_id=1, source_target_pairs={{0,64},{16,80},{32,96},{48,112},{64,0},{80,16},{96,32},{112,48},{1... | collective-permute-start | bytes 393224 | tf_op jit(solution)/shard_map/ppermute | solution.py:520
  57.5 11.6 %collective-permute-start.6 = (bf16[4,64,256]{2,1,0:T(8,128)(2,1)}, bf16[4,64,256]{2,1,0:T(8,128)(2,1)S(1)}, u32[]{:S(2)}, u32[]{:S(2)}) collective-permute-start(bf16[4,64,256]{2,1,0:T(8,128)(2,1)} %get-tuple-element.75), channel_id=1, source_target_pairs={{0,96},{16,112},{32,64},{48,80},{64,32},{80,48},{96,0},{112,16},{1... | collective-permute-start | bytes 393224 | tf_op jit(solution)/shard_map/ppermute | solution.py:520
  63.0 20.8 %copy-start.3 = (f32[4,64,256]{2,1,0:T(8,128)S(1)}, f32[4,64,256]{2,1,0:T(8,128)}, u32[]{:S(2)}) copy-start(f32[4,64,256]{2,1,0:T(8,128)} %get-tuple-element.72) | copy-start | bytes 786436
  69.1 1.3 %collective-permute-start.8 = (f32[128,128]{1,0:T(8,128)S(1)}, f32[128,128]{1,0:T(8,128)S(1)}, u32[]{:S(2)}, u32[]{:S(2)}) collective-permute-start(f32[128,128]{1,0:T(8,128)S(1)} %backward.1), channel_id=1, source_target_pairs={{0,1},{1,0},{2,3},{3,2},{4,5},{5,4},{6,7},{7,6},{8,9},{9,8},{10,11... | collective-permute-start | bytes 196616 | tf_op jit(solution)/shard_map/ppermute | solution.py:355
  70.4 4.5 %collective-permute-start.10 = (f32[128,128]{1,0:T(8,128)S(1)}, f32[128,128]{1,0:T(8,128)S(1)}, u32[]{:S(2)}, u32[]{:S(2)}) collective-permute-start(f32[128,128]{1,0:T(8,128)S(1)} %add.37), channel_id=1, source_target_pairs={{0,16},{1,17},{2,18},{3,19},{4,20},{5,21},{6,22},{7,23},{8,24},{9,... | collective-permute-start | bytes 196616 | tf_op jit(solution)/shard_map/ppermute | solution.py:355
  72.5 6.5 %collective-permute-start.11 = (f32[128,128]{1,0:T(8,128)S(1)}, f32[128,128]{1,0:T(8,128)S(1)}, u32[]{:S(2)}, u32[]{:S(2)}) collective-permute-start(f32[128,128]{1,0:T(8,128)S(1)} %add.37), channel_id=1, source_target_pairs={{0,18},{1,19},{2,16},{3,17},{4,22},{5,23},{6,20},{7,21},{8,26},{9,... | collective-permute-start | bytes 196616 | tf_op jit(solution)/shard_map/ppermute | solution.py:355
  72.5 6.5 %collective-permute-start.9 = (f32[128,128]{1,0:T(8,128)S(1)}, f32[128,128]{1,0:T(8,128)S(1)}, u32[]{:S(2)}, u32[]{:S(2)}) collective-permute-start(f32[128,128]{1,0:T(8,128)S(1)} %add.37), channel_id=1, source_target_pairs={{0,2},{1,3},{2,0},{3,1},{4,6},{5,7},{6,4},{7,5},{8,10},{9,11},{10,... | collective-permute-start | bytes 196616 | tf_op jit(solution)/shard_map/ppermute | solution.py:355
  79.0 5.5 %collective-permute-start.12 = (f32[128,128]{1,0:T(8,128)S(1)}, f32[128,128]{1,0:T(8,128)S(1)}, u32[]{:S(2)}, u32[]{:S(2)}) collective-permute-start(f32[128,128]{1,0:T(8,128)S(1)} %add_add_fusion.1), channel_id=1, source_target_pairs={{0,4},{1,5},{2,6},{3,7},{4,0},{5,1},{6,2},{7,3},{8,12},{9,13},{10,... | collective-permute-start | bytes 196616 | tf_op jit(solution)/shard_map/ppermute | solution.py:355
  79.1 6.1 %collective-permute-start.13 = (f32[128,128]{1,0:T(8,128)S(1)}, f32[128,128]{1,0:T(8,128)S(1)}, u32[]{:S(2)}, u32[]{:S(2)}) collective-permute-start(f32[128,128]{1,0:T(8,128)S(1)} %add_add_fusion.1), channel_id=1, source_target_pairs={{0,8},{1,9},{2,10},{3,11},{4,12},{5,13},{6,14},{7,15},{8,0},{9,1},... | collective-permute-start | bytes 196616 | tf_op jit(solution)/shard_map/ppermute | solution.py:355
  81.7 5.5 %collective-permute-start.14 = (f32[128,128]{1,0:T(8,128)S(1)}, f32[128,128]{1,0:T(8,128)S(1)}, u32[]{:S(2)}, u32[]{:S(2)}) collective-permute-start(f32[128,128]{1,0:T(8,128)S(1)} %add_add_fusion.1), channel_id=1, source_target_pairs={{0,12},{1,13},{2,14},{3,15},{4,8},{5,9},{6,10},{7,11},{8,4},{9,5},... | collective-permute-start | bytes 196616 | tf_op jit(solution)/shard_map/ppermute | solution.py:355
  83.9 8.1 %collective-permute-start.7 = (bf16[4,32,256]{2,1,0:T(8,128)(2,1)S(1)}, bf16[4,32,256]{2,1,0:T(8,128)(2,1)S(1)}, u32[]{:S(2)}, u32[]{:S(2)}) collective-permute-start(bf16[4,32,256]{2,1,0:T(8,128)(2,1)S(1)} %split.13), channel_id=1, source_target_pairs={{0,16},{16,0},{32,48},{48,32},{64,80},{80,64},{96,112},{112,96},{1... | collective-permute-start | bytes 196616 | tf_op jit(solution)/shard_map/ppermute | solution.py:554
  87.2 5.5 %collective-permute-start.15 = (f32[128,128]{1,0:T(8,128)S(1)}, f32[128,128]{1,0:T(8,128)S(1)}, u32[]{:S(2)}, u32[]{:S(2)}) collective-permute-start(f32[128,128]{1,0:T(8,128)S(1)} %add_add_fusion.a_ref), channel_id=1, source_target_pairs={{0,32},{1,33},{2,34},{3,35},{4,36},{5,37},{6,38},{7,39},{8,40},{9,... | collective-permute-start | bytes 196616 | tf_op jit(solution)/shard_map/ppermute | solution.py:355
  88.4 5.8 %collective-permute-start.16 = (f32[128,128]{1,0:T(8,128)S(1)}, f32[128,128]{1,0:T(8,128)S(1)}, u32[]{:S(2)}, u32[]{:S(2)}) collective-permute-start(f32[128,128]{1,0:T(8,128)S(1)} %add_add_fusion.a_ref), channel_id=1, source_target_pairs={{0,64},{1,65},{2,66},{3,67},{4,68},{5,69},{6,70},{7,71},{8,72},{9,... | collective-permute-start | bytes 196616 | tf_op jit(solution)/shard_map/ppermute | solution.py:355
  89.8 5.5 %collective-permute-start.17 = (f32[128,128]{1,0:T(8,128)S(1)}, f32[128,128]{1,0:T(8,128)S(1)}, u32[]{:S(2)}, u32[]{:S(2)}) collective-permute-start(f32[128,128]{1,0:T(8,128)S(1)} %add_add_fusion.a_ref), channel_id=1, source_target_pairs={{0,96},{1,97},{2,98},{3,99},{4,100},{5,101},{6,102},{7,103},{8,104... | collective-permute-start | bytes 196616 | tf_op jit(solution)/shard_map/ppermute | solution.py:355

commit v13 on v12

--- a/solution.py
+++ b/solution.py
@@ -345,7 +345,7 @@
 def sum_rounds(count_y, count_z):
     in_z = [1 << k for k in range(count_z.bit_length() - 1)]
     in_y = [count_z << k for k in range(count_y.bit_length() - 1)]
-    order = in_z[:1] + in_z[1:2] + in_y[:1] + in_z[2:] + in_y[1:]
+    order = in_z[:1] + in_z[2:] + in_y[1:] + in_z[1:2] + in_y[:1]
     rounds, order = ([order[:1]] if len(order) % 2 else []), order[len(order) % 2 :]
     return rounds + [order[k : k + 2] for k in range(0, len(order), 2)]
 

time: 96.5 us -> 95.8 us (level)
    ppermute x1, starting transfers between devices: 0.68 us -> 2.07 us  [per_device(): lax.ppermute(other.astype(BF16), 'sy', [(i, i ^ 1) for i in range(count_y)])]
    ppermute x10, starting transfers between devices: 13.9 us -> 12.6 us  [exchanged(): lax.ppermute(value, ('sy', 'sz'), [(i, i ^ m) for i in range(count)])]
where the time goes in v13:
time: 95.8 us; the launch traced here: 95.4 us
  starting transfers between devices  41.9 us (44%)
  waiting for transfers between devices  30.5 us (32%)
  Pallas kernels  21.2 us (22%)
    ppermute x10, starting transfers between devices, exchanged(): lax.ppermute(value, ('sy', 'sz'), [(i, i ^ m) for i in range(count)])  12.6 us
    all_to_all x1, waiting for transfers between devices, per_device(): lax.all_to_all(coarse.reshape(count_z, mine * 16, 256), 'sz', split_axis=...  11.8 us
    all_to_all x1, starting transfers between devices, per_device(): lax.all_to_all(coarse.reshape(count_z, mine * 16, 256), 'sz', split_axis=...  11.5 us
    ppermute x10, waiting for transfers between devices, exchanged(): lax.ppermute(value, ('sy', 'sz'), [(i, i ^ m) for i in range(count)])  9.99 us
    pallas_call x1, Pallas kernels, per_device(): pl.pallas_call(lambda *refs: backward_kernel(1.0 / math.sqrt(cells // 8),...  6.01 us
    all_to_all x1, waiting for transfers between devices, per_device(): lax.all_to_all(back, 'sz', split_axis=0, concat_axis=0, tiled=True)  5.1 us
    ppermute x3, starting transfers between devices, per_device(): lax.ppermute(part, 'sy', [(i, i ^ 2 * k) for i in range(count_y)])  4.7 us
    pallas_call x1, Pallas kernels, per_device(): pl.pallas_call(inner_kernel, out_shape=(shape((17, 2, 128, 256), BF16), p...  4.12 us
  transfers between devices with their start and end apart: 20, of which 11 were waited for; matrix products, arithmetic and copies ran while one was open for 1% of the time, Pallas kernels for 15%

profile of v13, /device:TPU:0, one launch (start us, length us, event | category | flops | bytes accessed | tf_op | source)
XLA Modules:
  0.0 95.4 jit_solution(8876413983352017601)
XLA Ops:
  0.6 1.7 %features.1 = (bf16[32,128,80]{2,1,0:T(8,128)(2,1)S(1)}, bf16[32,80]{1,0:T(8,128)(2,1)S(1)}, bf16[32,80]{1,0:T(8,128)(2,1)S(1)}, bf16[16,16,27]{2,1,0:T(8,128)(2...) custom-call(s32[512,64]{1,0:T(8,128)} %bitcast.37, ...), custom_call_target="tpu_custom_call" | custom-call | flops 41943040 | bytes 2097152 | tf_op jit(solution)/shard_map/features/pallas_call | solution.py:365
  2.4 3.6 %collective-permute-start = (bf16[32,80]{1,0:T(8,128)(2,1)S(1)}, bf16[32,80]{1,0:T(8,128)(2,1)S(1)}, u32[]{:S(2)}, u32[]{:S(2)}) collective-permute-start(bf16[32,80]{1,0:T(8,128)(2,1)S(1)} %get-tuple-element.46), channel_id=1, source_target_pairs={{0,16},{16,32},{32,48},{48,64},{64,80},{80,96},{96,112},{1,17},{17... | collective-permute-start | bytes 15368 | tf_op jit(solution)/shard_map/ppermute | solution.py:401
  5.9 1.3 %collective-permute-start.1 = (bf16[32,80]{1,0:T(8,128)(2,1)S(1)}, bf16[32,80]{1,0:T(8,128)(2,1)S(1)}, u32[]{:S(2)}, u32[]{:S(2)}) collective-permute-start(bf16[32,80]{1,0:T(8,128)(2,1)S(1)} %get-tuple-element.47), channel_id=1, source_target_pairs={{16,0},{32,16},{48,32},{64,48},{80,64},{96,80},{112,96},{17,1},{33... | collective-permute-start | bytes 15368 | tf_op jit(solution)/shard_map/ppermute | solution.py:402
  7.3 1.4 %weights.1 = (bf16[9,256,256]{2,1,0:T(8,128)(2,1)S(1)}, bf16[128,256]{1,0:T(8,128)(2,1)S(1)}, bf16[256,128]{1,0:T(8,128)(2,1)S(1)}, bf16[80,256]{1,0:T(8,128)(2,1)S(1)}) custom-call(bf16[16,16,27]{2,1,0:T(8,128)(2,1)S(1)} %get-tuple-element.48.conv_ref, bf16[8,16,64]{2,1,0:T(8,128)(2,1)S(1)} %get-tuple-element.49.down_ref, ...), custom_call_target="tpu_custom_call" | custom-call | flops 56623104 | bytes 3145728 | tf_op jit(solution)/shard_map/weights/pallas_call | solution.py:403
  8.7 0.0 collective-permute-done.ylo_ref
  8.7 2.8 %collective-permute-done.1.yhi_ref = bf16[32,80]{1,0:T(8,128)(2,1)S(1)} collective-permute-done((bf16[32,80]{1,0:T(8,128)(2,1)S(1)}, bf16[32,80]{1,0:T(8,128)(2,1)S(1)}, u32[]{:S(2)}, u32[]{:S(2)}) %collective-permute-start.1) | collective-permute-done | bytes 5152 | tf_op jit(solution)/shard_map/ppermute | solution.py:402
  11.5 0.1 fusion
  11.6 1.3 %collective-permute-start.2 = (bf16[80,80]{1,0:T(8,128)(2,1)S(1)}, bf16[80,80]{1,0:T(8,128)(2,1)S(1)}, u32[]{:S(2)}, u32[]{:S(2)}) collective-permute-start(bf16[80,80]{1,0:T(8,128)(2,1)S(1)} %get-tuple-element.89), channel_id=1, source_target_pairs={{0,1},{1,2},{2,3},{3,4},{4,5},{5,6},{6,7},{7,8},{8,9},{9,10},{10,1... | collective-permute-start | bytes 38408 | tf_op jit(solution)/shard_map/ppermute | solution.py:426
  12.9 1.3 %collective-permute-start.3 = (bf16[80,80]{1,0:T(8,128)(2,1)S(1)}, bf16[80,80]{1,0:T(8,128)(2,1)S(1)}, u32[]{:S(2)}, u32[]{:S(2)}) collective-permute-start(bf16[80,80]{1,0:T(8,128)(2,1)S(1)} %get-tuple-element.88), channel_id=1, source_target_pairs={{1,0},{2,1},{3,2},{4,3},{5,4},{6,5},{7,6},{8,7},{9,8},{10,9},{11,1... | collective-permute-start | bytes 38408 | tf_op jit(solution)/shard_map/ppermute | solution.py:427
  14.2 4.1 %inner.1 = (bf16[17,2,128,256]{3,2,1,0:T(8,128)(2,1)S(1)}, f32[4,256,512]{2,1,0:T(8,128)}, bf16[4,256,512]{2,1,0:T(8,128)(2,1)S(1)}, f32[2,2,256,32]{3,2,1,0:T(8,128)S(1)}) custom-call(bf16[32,128,80]{2,1,0:T(8,128)(2,1)S(1)} %get-tuple-element.58.feat_ref, bf16[32,80]{1,0:T(8,128)(2,1)S(1)} %collective-permute-done.ylo_ref, ...), custom_call_target="tpu_custom_call" | custom-call | flops 3221225472 | bytes 10485760 | tf_op jit(solution)/shard_map/inner/pallas_call | solution.py:428
  18.3 0.0 copy-start.2
  18.3 0.0 collective-permute-done.2.zlo_ref
  18.3 0.8 collective-permute-done.3.zhi_ref
  19.1 0.0 copy-start
  19.1 0.0 copy-start.1
  19.1 2.7 %outer.1 = (bf16[2,128,256]{2,1,0:T(8,128)(2,1)S(1)}, f32[256,128]{1,0:T(8,128)S(1)}, bf16[4,256,512]{2,1,0:T(8,128)(2,1)}, bf16[1024,256]{1,0:T(8,128)(2,1)}) custom-call(bf16[80,80]{1,0:T(8,128)(2,1)S(1)} %collective-permute-done.2.zlo_ref, bf16[80,80]{1,0:T(8,128)(2,1)S(1)} %collective-permute-done.3.zhi_ref, ...), custom_call_target="tpu_custom_call" | custom-call | flops 1073741824 | bytes 4194304 | tf_op jit(solution)/shard_map/outer/pallas_call | solution.py:443
  21.8 0.0 copy-done.2
  21.8 11.5 %all-to-all-start = ((bf16[16,64,256]{2,1,0:T(8,128)(2,1)}), bf16[16,64,256]{2,1,0:T(8,128)(2,1)S(1)}, u32[]{:S(2)}, u32[]{:S(2)}) async-start(bf16[16,64,256]{2,1,0:T(8,128)(2,1)} %bitcast.36), calls=%async_computation | async-start | bytes 1048576 | tf_op jit(solution)/shard_map/all_to_all | solution.py:468
  33.4 0.0 copy-done
  33.4 0.0 copy-done.1
  33.4 0.5 turn.1
  33.9 11.8 %all-to-all-done.coarse_ref.refs_1_ = bf16[16,64,256]{2,1,0:T(8,128)(2,1)S(1)} async-done(((bf16[16,64,256]{2,1,0:T(8,128)(2,1)}), bf16[16,64,256]{2,1,0:T(8,128)(2,1)S(1)}, u32[]{:S(2)}, u32[]{:S(2)}) %all-to-all-start) | async-done | bytes 524320 | tf_op jit(solution)/shard_map/all_to_all | solution.py:468
  45.7 1.4 %mix.1 = bf16[16,64,256]{2,1,0:T(8,128)(2,1)} custom-call(bf16[16,64,256]{2,1,0:T(8,128)(2,1)S(1)} %all-to-all-done.coarse_ref.refs_1_, bf16[4,256,256]{2,1,0:T(8,128)(2,1)S(1)} %copy-done, bf16[4,256,256]{2,1,0:T(8,128)(2,1)S(1)} %get-tuple-element.68.cot_t_ref.refs_3_, bf16[4,256,256]{2,1,0:T(8,128)(2,1)S(1)} %get-tuple-element.69.mix_t_ref), custom_call_target="tpu_custom_call" | custom-call | flops 268435456 | bytes 2097152 | tf_op jit(solution)/shard_map/mix/pallas_call | solution.py:488
  47.1 3.6 %all-to-all-start.1 = ((bf16[16,64,256]{2,1,0:T(8,128)(2,1)}), bf16[16,64,256]{2,1,0:T(8,128)(2,1)S(1)}, u32[]{:S(2)}, u32[]{:S(2)}) async-start(bf16[16,64,256]{2,1,0:T(8,128)(2,1)} %mix.1), calls=%async_computation.1 | async-start | bytes 1048576 | tf_op jit(solution)/shard_map/all_to_all | solution.py:501
  50.7 2.5 %mix_grad.1 = (bf16[4,256,256]{2,1,0:T(8,128)(2,1)}, f32[4,64,256]{2,1,0:T(8,128)}, bf16[4,64,256]{2,1,0:T(8,128)(2,1)}, bf16[4,64,256]{2,1,0:T(8,128)(2,1)}, bf16[4,64,256]{2,1,0:T(8,128)(2,1)}) custom-call(s32[1]{0:T(128)} %bitcast.refs_0_, bf16[16,64,256]{2,1,0:T(8,128)(2,1)S(1)} %all-to-all-done.coarse_ref.refs_1_, bf16[4,256,256]{2,1,0:T(8,128)(2,1)S(1)} %copy-done, ...), custom_call_target="tpu_custom_call" | custom-call | flops 268435456 | bytes 3145728 | tf_op jit(solution)/shard_map/mix_grad/pallas_call | solution.py:503
  53.2 1.5 %collective-permute-start.4 = (bf16[4,64,256]{2,1,0:T(8,128)(2,1)}, bf16[4,64,256]{2,1,0:T(8,128)(2,1)S(1)}, u32[]{:S(2)}, u32[]{:S(2)}) collective-permute-start(bf16[4,64,256]{2,1,0:T(8,128)(2,1)} %get-tuple-element.73), channel_id=1, source_target_pairs={{0,32},{16,48},{32,0},{48,16},{64,96},{80,112},{96,64},{112,80},{1... | collective-permute-start | bytes 393224 | tf_op jit(solution)/shard_map/ppermute | solution.py:520
  54.7 2.7 %collective-permute-start.5 = (bf16[4,64,256]{2,1,0:T(8,128)(2,1)}, bf16[4,64,256]{2,1,0:T(8,128)(2,1)S(1)}, u32[]{:S(2)}, u32[]{:S(2)}) collective-permute-start(bf16[4,64,256]{2,1,0:T(8,128)(2,1)} %get-tuple-element.74), channel_id=1, source_target_pairs={{0,64},{16,80},{32,96},{48,112},{64,0},{80,16},{96,32},{112,48},{1... | collective-permute-start | bytes 393224 | tf_op jit(solution)/shard_map/ppermute | solution.py:520
  57.5 0.5 collective-permute-start.6
  57.9 5.1 %all-to-all-done.1 = bf16[16,64,256]{2,1,0:T(8,128)(2,1)S(1)} async-done(((bf16[16,64,256]{2,1,0:T(8,128)(2,1)}), bf16[16,64,256]{2,1,0:T(8,128)(2,1)S(1)}, u32[]{:S(2)}, u32[]{:S(2)}) %all-to-all-start.1) | async-done | bytes 524320 | tf_op jit(solution)/shard_map/all_to_all | solution.py:501
  63.0 0.0 copy-start.3
  63.0 6.0 %backward.1 = f32[128,128]{1,0:T(8,128)S(1)} custom-call(bf16[1024,256]{1,0:T(8,128)(2,1)S(1)} %bitcast.35, bf16[17,2,128,256]{3,2,1,0:T(8,128)(2,1)} %copy-done.2, f32[4,256,512]{2,1,0:T(8,128)} %get-tuple-element.77.refs_2_, bf16[4,256,512]{2,1,0:T(8,128)(2,1)} %get-tuple-element.78.refs_3_, bf16[128,256]{1,0:T(8,128)(2,1)S(1)} %get-tuple-element.61.pair_ref.refs_4_, ...), custom_call_target="tpu_custom_call" | custom-call | flops 4294967296 | bytes 8388608 | tf_op jit(solution)/shard_map/backward/pallas_call | solution.py:522
  69.0 0.0 collective-permute-done.4
  69.1 0.0 collective-permute-done.5
  69.1 0.0 collective-permute-done.6
  69.1 0.1 collective-permute-start.8
  69.2 1.2 %collective-permute-done.8 = f32[128,128]{1,0:T(8,128)S(1)} collective-permute-done((f32[128,128]{1,0:T(8,128)S(1)}, f32[128,128]{1,0:T(8,128)S(1)}, u32[]{:S(2)}, u32[]{:S(2)}) %collective-permute-start.8) | collective-permute-done | bytes 65568 | tf_op jit(solution)/shard_map/ppermute | solution.py:355
  70.4 0.9 collective-permute-start.10
  71.3 1.1 %collective-permute-start.11 = (f32[128,128]{1,0:T(8,128)S(1)}, f32[128,128]{1,0:T(8,128)S(1)}, u32[]{:S(2)}, u32[]{:S(2)}) collective-permute-start(f32[128,128]{1,0:T(8,128)S(1)} %add.37), channel_id=1, source_target_pairs={{0,12},{1,13},{2,14},{3,15},{4,8},{5,9},{6,10},{7,11},{8,4},{9,5},... | collective-permute-start | bytes 196616 | tf_op jit(solution)/shard_map/ppermute | solution.py:355
  72.4 1.5 %collective-permute-start.9 = (f32[128,128]{1,0:T(8,128)S(1)}, f32[128,128]{1,0:T(8,128)S(1)}, u32[]{:S(2)}, u32[]{:S(2)}) collective-permute-start(f32[128,128]{1,0:T(8,128)S(1)} %add.37), channel_id=1, source_target_pairs={{0,4},{1,5},{2,6},{3,7},{4,0},{5,1},{6,2},{7,3},{8,12},{9,13},{10,... | collective-permute-start | bytes 196616 | tf_op jit(solution)/shard_map/ppermute | solution.py:355
  74.0 2.4 %collective-permute-done.10 = f32[128,128]{1,0:T(8,128)S(1)} collective-permute-done((f32[128,128]{1,0:T(8,128)S(1)}, f32[128,128]{1,0:T(8,128)S(1)}, u32[]{:S(2)}, u32[]{:S(2)}) %collective-permute-start.10) | collective-permute-done | bytes 65568 | tf_op jit(solution)/shard_map/ppermute | solution.py:355
  76.4 1.1 %collective-permute-done.11 = f32[128,128]{1,0:T(8,128)S(1)} collective-permute-done((f32[128,128]{1,0:T(8,128)S(1)}, f32[128,128]{1,0:T(8,128)S(1)}, u32[]{:S(2)}, u32[]{:S(2)}) %collective-permute-start.11) | collective-permute-done | bytes 65568 | tf_op jit(solution)/shard_map/ppermute | solution.py:355
  77.6 0.0 collective-permute-done.9
  77.6 1.6 %collective-permute-start.12 = (f32[128,128]{1,0:T(8,128)S(1)}, f32[128,128]{1,0:T(8,128)S(1)}, u32[]{:S(2)}, u32[]{:S(2)}) collective-permute-start(f32[128,128]{1,0:T(8,128)S(1)} %add_add_fusion.1), channel_id=1, source_target_pairs={{0,32},{1,33},{2,34},{3,35},{4,36},{5,37},{6,38},{7,39},{8,40},{9,... | collective-permute-start | bytes 196616 | tf_op jit(solution)/shard_map/ppermute | solution.py:355
  79.2 2.7 %collective-permute-start.13 = (f32[128,128]{1,0:T(8,128)S(1)}, f32[128,128]{1,0:T(8,128)S(1)}, u32[]{:S(2)}, u32[]{:S(2)}) collective-permute-start(f32[128,128]{1,0:T(8,128)S(1)} %add_add_fusion.1), channel_id=1, source_target_pairs={{0,64},{1,65},{2,66},{3,67},{4,68},{5,69},{6,70},{7,71},{8,72},{9,... | collective-permute-start | bytes 196616 | tf_op jit(solution)/shard_map/ppermute | solution.py:355
  81.9 0.5 collective-permute-start.14
  82.4 0.0 copy-done.3
  82.4 0.1 convert_add_fusion
  82.4 2.1 %collective-permute-start.7 = (bf16[4,32,256]{2,1,0:T(8,128)(2,1)S(1)}, bf16[4,32,256]{2,1,0:T(8,128)(2,1)S(1)}, u32[]{:S(2)}, u32[]{:S(2)}) collective-permute-start(bf16[4,32,256]{2,1,0:T(8,128)(2,1)S(1)} %split.13), channel_id=1, source_target_pairs={{0,16},{16,0},{32,48},{48,32},{64,80},{80,64},{96,112},{112,96},{1... | collective-permute-start | bytes 196616 | tf_op jit(solution)/shard_map/ppermute | solution.py:554
  84.5 0.0 collective-permute-done.12
  84.5 0.7 collective-permute-done.13
  85.2 2.1 %collective-permute-done.14 = f32[128,128]{1,0:T(8,128)S(1)} collective-permute-done((f32[128,128]{1,0:T(8,128)S(1)}, f32[128,128]{1,0:T(8,128)S(1)}, u32[]{:S(2)}, u32[]{:S(2)}) %collective-permute-start.14) | collective-permute-done | bytes 65568 | tf_op jit(solution)/shard_map/ppermute | solution.py:355
  87.4 0.9 collective-permute-start.15
  88.2 0.8 collective-permute-start.16
  89.1 2.5 %collective-permute-start.17 = (f32[128,128]{1,0:T(8,128)S(1)}, f32[128,128]{1,0:T(8,128)S(1)}, u32[]{:S(2)}, u32[]{:S(2)}) collective-permute-start(f32[128,128]{1,0:T(8,128)S(1)} %add_add_fusion.a_ref), channel_id=1, source_target_pairs={{0,18},{1,19},{2,16},{3,17},{4,22},{5,23},{6,20},{7,21},{8,26},{9,... | collective-permute-start | bytes 196616 | tf_op jit(solution)/shard_map/ppermute | solution.py:355
  91.6 0.0 collective-permute-done.7
  91.6 0.7 slice_add_fusion
  92.2 1.2 %collective-permute-done.15.b_ref = f32[128,128]{1,0:T(8,128)S(1)} collective-permute-done((f32[128,128]{1,0:T(8,128)S(1)}, f32[128,128]{1,0:T(8,128)S(1)}, u32[]{:S(2)}, u32[]{:S(2)}) %collective-permute-start.15) | collective-permute-done | bytes 65568 | tf_op jit(solution)/shard_map/ppermute | solution.py:355
  93.5 0.0 collective-permute-done.16.c_ref
  93.5 1.1 %collective-permute-done.17.d_ref = f32[128,128]{1,0:T(8,128)S(1)} collective-permute-done((f32[128,128]{1,0:T(8,128)S(1)}, f32[128,128]{1,0:T(8,128)S(1)}, u32[]{:S(2)}, u32[]{:S(2)}) %collective-permute-start.17) | collective-permute-done | bytes 65568 | tf_op jit(solution)/shard_map/ppermute | solution.py:355
  94.6 0.8 finish.1
  (6 shorter events, 0.1 us)
Async XLA Ops:
  2.4 6.3 %collective-permute-start = (bf16[32,80]{1,0:T(8,128)(2,1)S(1)}, bf16[32,80]{1,0:T(8,128)(2,1)S(1)}, u32[]{:S(2)}, u32[]{:S(2)}) collective-permute-start(bf16[32,80]{1,0:T(8,128)(2,1)S(1)} %get-tuple-element.46), channel_id=1, source_target_pairs={{0,16},{16,32},{32,48},{48,64},{64,80},{80,96},{96,112},{1,17},{17... | collective-permute-start | bytes 15368 | tf_op jit(solution)/shard_map/ppermute | solution.py:401
  5.9 5.5 %collective-permute-start.1 = (bf16[32,80]{1,0:T(8,128)(2,1)S(1)}, bf16[32,80]{1,0:T(8,128)(2,1)S(1)}, u32[]{:S(2)}, u32[]{:S(2)}) collective-permute-start(bf16[32,80]{1,0:T(8,128)(2,1)S(1)} %get-tuple-element.47), channel_id=1, source_target_pairs={{16,0},{32,16},{48,32},{64,48},{80,64},{96,80},{112,96},{17,1},{33... | collective-permute-start | bytes 15368 | tf_op jit(solution)/shard_map/ppermute | solution.py:402
  11.6 6.7 %collective-permute-start.2 = (bf16[80,80]{1,0:T(8,128)(2,1)S(1)}, bf16[80,80]{1,0:T(8,128)(2,1)S(1)}, u32[]{:S(2)}, u32[]{:S(2)}) collective-permute-start(bf16[80,80]{1,0:T(8,128)(2,1)S(1)} %get-tuple-element.89), channel_id=1, source_target_pairs={{0,1},{1,2},{2,3},{3,4},{4,5},{5,6},{6,7},{7,8},{8,9},{9,10},{10,1... | collective-permute-start | bytes 38408 | tf_op jit(solution)/shard_map/ppermute | solution.py:426
  12.9 6.2 %collective-permute-start.3 = (bf16[80,80]{1,0:T(8,128)(2,1)S(1)}, bf16[80,80]{1,0:T(8,128)(2,1)S(1)}, u32[]{:S(2)}, u32[]{:S(2)}) collective-permute-start(bf16[80,80]{1,0:T(8,128)(2,1)S(1)} %get-tuple-element.88), channel_id=1, source_target_pairs={{1,0},{2,1},{3,2},{4,3},{5,4},{6,5},{7,6},{8,7},{9,8},{10,9},{11,1... | collective-permute-start | bytes 38408 | tf_op jit(solution)/shard_map/ppermute | solution.py:427
  18.3 3.5 %copy-start.2 = (bf16[17,2,128,256]{3,2,1,0:T(8,128)(2,1)}, bf16[17,2,128,256]{3,2,1,0:T(8,128)(2,1)S(1)}, u32[]{:S(2)}) copy-start(bf16[17,2,128,256]{3,2,1,0:T(8,128)(2,1)S(1)} %get-tuple-element.76.refs_1_) | copy-start | bytes 6684676
  19.1 14.2 %copy-start = (bf16[4,256,256]{2,1,0:T(8,128)(2,1)S(1)}, bf16[4,256,256]{2,1,0:T(8,128)(2,1)}, u32[]{:S(2)}) copy-start(bf16[4,256,256]{2,1,0:T(8,128)(2,1)} %refs_2_) | copy-start | bytes 1572868
  19.1 14.3 %copy-start.1 = (bf16[4,8,32,256]{3,2,1,0:T(8,128)(2,1)S(1)}, bf16[4,8,32,256]{3,2,1,0:T(8,128)(2,1)}, u32[]{:S(2)}) copy-start(bf16[4,8,32,256]{3,2,1,0:T(8,128)(2,1)} %param.15) | copy-start | bytes 1572868
  21.8 23.9 %all-to-all-start = ((bf16[16,64,256]{2,1,0:T(8,128)(2,1)}), bf16[16,64,256]{2,1,0:T(8,128)(2,1)S(1)}, u32[]{:S(2)}, u32[]{:S(2)}) async-start(bf16[16,64,256]{2,1,0:T(8,128)(2,1)} %bitcast.36), calls=%async_computation | async-start | bytes 1048576 | tf_op jit(solution)/shard_map/all_to_all | solution.py:468
  47.1 15.9 %all-to-all-start.1 = ((bf16[16,64,256]{2,1,0:T(8,128)(2,1)}), bf16[16,64,256]{2,1,0:T(8,128)(2,1)S(1)}, u32[]{:S(2)}, u32[]{:S(2)}) async-start(bf16[16,64,256]{2,1,0:T(8,128)(2,1)} %mix.1), calls=%async_computation.1 | async-start | bytes 1048576 | tf_op jit(solution)/shard_map/all_to_all | solution.py:501
  53.2 15.8 %collective-permute-start.4 = (bf16[4,64,256]{2,1,0:T(8,128)(2,1)}, bf16[4,64,256]{2,1,0:T(8,128)(2,1)S(1)}, u32[]{:S(2)}, u32[]{:S(2)}) collective-permute-start(bf16[4,64,256]{2,1,0:T(8,128)(2,1)} %get-tuple-element.73), channel_id=1, source_target_pairs={{0,32},{16,48},{32,0},{48,16},{64,96},{80,112},{96,64},{112,80},{1... | collective-permute-start | bytes 393224 | tf_op jit(solution)/shard_map/ppermute | solution.py:520
  54.7 14.3 %collective-permute-start.5 = (bf16[4,64,256]{2,1,0:T(8,128)(2,1)}, bf16[4,64,256]{2,1,0:T(8,128)(2,1)S(1)}, u32[]{:S(2)}, u32[]{:S(2)}) collective-permute-start(bf16[4,64,256]{2,1,0:T(8,128)(2,1)} %get-tuple-element.74), channel_id=1, source_target_pairs={{0,64},{16,80},{32,96},{48,112},{64,0},{80,16},{96,32},{112,48},{1... | collective-permute-start | bytes 393224 | tf_op jit(solution)/shard_map/ppermute | solution.py:520
  57.5 11.6 %collective-permute-start.6 = (bf16[4,64,256]{2,1,0:T(8,128)(2,1)}, bf16[4,64,256]{2,1,0:T(8,128)(2,1)S(1)}, u32[]{:S(2)}, u32[]{:S(2)}) collective-permute-start(bf16[4,64,256]{2,1,0:T(8,128)(2,1)} %get-tuple-element.75), channel_id=1, source_target_pairs={{0,96},{16,112},{32,64},{48,80},{64,32},{80,48},{96,0},{112,16},{1... | collective-permute-start | bytes 393224 | tf_op jit(solution)/shard_map/ppermute | solution.py:520
  63.0 19.4 %copy-start.3 = (f32[4,64,256]{2,1,0:T(8,128)S(1)}, f32[4,64,256]{2,1,0:T(8,128)}, u32[]{:S(2)}) copy-start(f32[4,64,256]{2,1,0:T(8,128)} %get-tuple-element.72) | copy-start | bytes 786436
  69.1 1.3 %collective-permute-start.8 = (f32[128,128]{1,0:T(8,128)S(1)}, f32[128,128]{1,0:T(8,128)S(1)}, u32[]{:S(2)}, u32[]{:S(2)}) collective-permute-start(f32[128,128]{1,0:T(8,128)S(1)} %backward.1), channel_id=1, source_target_pairs={{0,1},{1,0},{2,3},{3,2},{4,5},{5,4},{6,7},{7,6},{8,9},{9,8},{10,11... | collective-permute-start | bytes 196616 | tf_op jit(solution)/shard_map/ppermute | solution.py:355
  70.4 6.0 %collective-permute-start.10 = (f32[128,128]{1,0:T(8,128)S(1)}, f32[128,128]{1,0:T(8,128)S(1)}, u32[]{:S(2)}, u32[]{:S(2)}) collective-permute-start(f32[128,128]{1,0:T(8,128)S(1)} %add.37), channel_id=1, source_target_pairs={{0,8},{1,9},{2,10},{3,11},{4,12},{5,13},{6,14},{7,15},{8,0},{9,1},... | collective-permute-start | bytes 196616 | tf_op jit(solution)/shard_map/ppermute | solution.py:355
  71.3 6.3 %collective-permute-start.11 = (f32[128,128]{1,0:T(8,128)S(1)}, f32[128,128]{1,0:T(8,128)S(1)}, u32[]{:S(2)}, u32[]{:S(2)}) collective-permute-start(f32[128,128]{1,0:T(8,128)S(1)} %add.37), channel_id=1, source_target_pairs={{0,12},{1,13},{2,14},{3,15},{4,8},{5,9},{6,10},{7,11},{8,4},{9,5},... | collective-permute-start | bytes 196616 | tf_op jit(solution)/shard_map/ppermute | solution.py:355
  72.4 5.1 %collective-permute-start.9 = (f32[128,128]{1,0:T(8,128)S(1)}, f32[128,128]{1,0:T(8,128)S(1)}, u32[]{:S(2)}, u32[]{:S(2)}) collective-permute-start(f32[128,128]{1,0:T(8,128)S(1)} %add.37), channel_id=1, source_target_pairs={{0,4},{1,5},{2,6},{3,7},{4,0},{5,1},{6,2},{7,3},{8,12},{9,13},{10,... | collective-permute-start | bytes 196616 | tf_op jit(solution)/shard_map/ppermute | solution.py:355
  77.6 6.9 %collective-permute-start.12 = (f32[128,128]{1,0:T(8,128)S(1)}, f32[128,128]{1,0:T(8,128)S(1)}, u32[]{:S(2)}, u32[]{:S(2)}) collective-permute-start(f32[128,128]{1,0:T(8,128)S(1)} %add_add_fusion.1), channel_id=1, source_target_pairs={{0,32},{1,33},{2,34},{3,35},{4,36},{5,37},{6,38},{7,39},{8,40},{9,... | collective-permute-start | bytes 196616 | tf_op jit(solution)/shard_map/ppermute | solution.py:355
  79.2 6.1 %collective-permute-start.13 = (f32[128,128]{1,0:T(8,128)S(1)}, f32[128,128]{1,0:T(8,128)S(1)}, u32[]{:S(2)}, u32[]{:S(2)}) collective-permute-start(f32[128,128]{1,0:T(8,128)S(1)} %add_add_fusion.1), channel_id=1, source_target_pairs={{0,64},{1,65},{2,66},{3,67},{4,68},{5,69},{6,70},{7,71},{8,72},{9,... | collective-permute-start | bytes 196616 | tf_op jit(solution)/shard_map/ppermute | solution.py:355
  81.9 5.5 %collective-permute-start.14 = (f32[128,128]{1,0:T(8,128)S(1)}, f32[128,128]{1,0:T(8,128)S(1)}, u32[]{:S(2)}, u32[]{:S(2)}) collective-permute-start(f32[128,128]{1,0:T(8,128)S(1)} %add_add_fusion.1), channel_id=1, source_target_pairs={{0,96},{1,97},{2,98},{3,99},{4,100},{5,101},{6,102},{7,103},{8,104... | collective-permute-start | bytes 196616 | tf_op jit(solution)/shard_map/ppermute | solution.py:355
  82.4 9.1 %collective-permute-start.7 = (bf16[4,32,256]{2,1,0:T(8,128)(2,1)S(1)}, bf16[4,32,256]{2,1,0:T(8,128)(2,1)S(1)}, u32[]{:S(2)}, u32[]{:S(2)}) collective-permute-start(bf16[4,32,256]{2,1,0:T(8,128)(2,1)S(1)} %split.13), channel_id=1, source_target_pairs={{0,16},{16,0},{32,48},{48,32},{64,80},{80,64},{96,112},{112,96},{1... | collective-permute-start | bytes 196616 | tf_op jit(solution)/shard_map/ppermute | solution.py:554
  87.4 6.1 %collective-permute-start.15 = (f32[128,128]{1,0:T(8,128)S(1)}, f32[128,128]{1,0:T(8,128)S(1)}, u32[]{:S(2)}, u32[]{:S(2)}) collective-permute-start(f32[128,128]{1,0:T(8,128)S(1)} %add_add_fusion.a_ref), channel_id=1, source_target_pairs={{0,2},{1,3},{2,0},{3,1},{4,6},{5,7},{6,4},{7,5},{8,10},{9,11},{10,... | collective-permute-start | bytes 196616 | tf_op jit(solution)/shard_map/ppermute | solution.py:355
  88.2 5.2 %collective-permute-start.16 = (f32[128,128]{1,0:T(8,128)S(1)}, f32[128,128]{1,0:T(8,128)S(1)}, u32[]{:S(2)}, u32[]{:S(2)}) collective-permute-start(f32[128,128]{1,0:T(8,128)S(1)} %add_add_fusion.a_ref), channel_id=1, source_target_pairs={{0,16},{1,17},{2,18},{3,19},{4,20},{5,21},{6,22},{7,23},{8,24},{9,... | collective-permute-start | bytes 196616 | tf_op jit(solution)/shard_map/ppermute | solution.py:355
  89.1 5.5 %collective-permute-start.17 = (f32[128,128]{1,0:T(8,128)S(1)}, f32[128,128]{1,0:T(8,128)S(1)}, u32[]{:S(2)}, u32[]{:S(2)}) collective-permute-start(f32[128,128]{1,0:T(8,128)S(1)} %add_add_fusion.a_ref), channel_id=1, source_target_pairs={{0,18},{1,19},{2,16},{3,17},{4,22},{5,23},{6,20},{7,21},{8,26},{9,... | collective-permute-start | bytes 196616 | tf_op jit(solution)/shard_map/ppermute | solution.py:355
